TPU v7x, 256 devices: a whole 4x4x8 slice. The times are simulated.
256 devices in a mesh: row: 4 (over y), col: 16 (over z, core), layer: 4 (over x).
Axes of the slice: x: 4, y: 4, z: 8, core: 2. Of those that a mesh axis runs over, the one named last changes fastest.
Arguments:
- blocks: bfloat16 [5632, 128, 128], P(('col', 'layer')), may hold values from -6 to 6
- block_aux: int32 [5632], P(('col', 'layer')), may hold values from 0 to 23
- block_row: int32 [5632], P(('col', 'layer')), may hold values from 0 to 15, as said below
- block_col: int32 [5632], P(('col', 'layer')), may hold values from 0 to 159, as said below
- extents: int32 [5632], P(('col', 'layer')), may hold values from 32 to 128
- occ_green: bfloat16 [20480, 2048], P('layer', 'row'), may hold values from -0.00390625 to 0.00390625
- virt_green: bfloat16 [20480, 2048], P('layer', 'row'), may hold values from -0.00390625 to 0.00390625
Outputs:
- chi: float32 [24, 24], replicated
Inputs may be any that keep to these rules, and one draw needn't show every extreme that they name: block_row[n] numbers the block of 128 window functions that tile n covers. The owner of tile n is the pair (block_row[n], block_col[n] // 40). Within each device's share of 88 consecutive entries no owner appears more than 2 times, and one owner, the same for every share, appears exactly 2 times in every share.
All inputs are finite; a program needn't handle non-finite values.
Results may differ from a plain program's by a relative error of at most 0.0003.
Values may be sent and summed in bfloat16 or wider, within the bound.
No kernel may reach another device: no remote copies, remote signals or barrier semaphores. Data moves between devices by JAX's collectives and lax.ppermute only.
A program may use at most 192 MiB of HBM per device.

v0:
```python
import jax
import jax.numpy as jnp
from jax import lax
from jax.sharding import PartitionSpec as P

NP = 24


def on_device(blocks, block_aux, block_row, block_col, extents, occ_green, virt_green):
    row_count = lax.axis_size("row")
    col_count = lax.axis_size("col")
    layer_count = lax.axis_size("layer")
    held_count = blocks.shape[0]
    tile_side = blocks.shape[1]
    aux_count = NP
    owner_count = col_count * layer_count
    capacity = max(2, held_count // owner_count + 1)
    layer_blocks = occ_green.shape[0] // tile_side
    columns = jnp.arange(tile_side, dtype=jnp.int32)
    masked_tiles = jnp.where(
        columns[None, None, :] < extents[:, None, None], blocks, jnp.zeros((), blocks.dtype)
    )
    layer_of = block_col // layer_blocks
    target = block_row * layer_count + layer_of
    kept_col = block_col - layer_of * layer_blocks
    marked = (target[:, None] == jnp.arange(owner_count, dtype=jnp.int32)[None, :]).astype(
        jnp.int32
    )
    earlier = jnp.cumsum(marked, axis=0) - marked
    placed = target * capacity + jnp.sum(earlier * marked, axis=1)
    send_tiles = (
        jnp.zeros((owner_count * capacity, tile_side, tile_side), blocks.dtype)
        .at[placed]
        .set(masked_tiles)
    )
    send_meta = (
        jnp.zeros((owner_count * capacity, 2), jnp.int32)
        .at[placed]
        .set(jnp.stack([block_aux, kept_col], axis=1))
    )
    send_tiles = send_tiles.reshape(col_count, layer_count, capacity, tile_side, tile_side)
    send_meta = send_meta.reshape(col_count, layer_count, capacity, 2)
    total_slots = col_count * layer_count * capacity
    got_tiles, got_meta = (
        lax.all_to_all(
            send_tiles.reshape(total_slots, tile_side, tile_side),
            ("col", "layer"),
            split_axis=0,
            concat_axis=0,
            tiled=True,
        ),
        lax.all_to_all(
            send_meta.reshape(total_slots, 2),
            ("col", "layer"),
            split_axis=0,
            concat_axis=0,
            tiled=True,
        ),
    )
    group_size = col_count * capacity
    got_tiles = got_tiles.reshape(layer_count, group_size, tile_side, tile_side)
    got_meta = got_meta.reshape(layer_count, group_size, 2)
    occ_cols, virt_cols = (occ_green, virt_green)
    width_here = occ_cols.shape[1]
    offsets = jnp.arange(tile_side, dtype=jnp.int32)

    def add_group(totals, record):
        occ_total, virt_total = totals
        tile_group, meta_group = record
        row_index = meta_group[:, 1][:, None] * tile_side + offsets[None, :]
        occ_rows = occ_cols[row_index]
        virt_rows = virt_cols[row_index]
        occ_term = jnp.einsum(
            "gsv,gls->gvl", occ_rows, tile_group, preferred_element_type=jnp.float32
        )
        virt_term = jnp.einsum(
            "gvs,gsl->gvl", tile_group, virt_rows, preferred_element_type=jnp.float32
        )
        aux_index = meta_group[:, 0]
        return (
            (occ_total.at[aux_index].add(occ_term), virt_total.at[aux_index].add(virt_term)),
            None,
        )

    start_totals = (
        jnp.zeros((aux_count, width_here, tile_side), jnp.float32),
        jnp.zeros((aux_count, tile_side, width_here), jnp.float32),
    )
    (occ_total, virt_total), _ = lax.scan(add_group, start_totals, (got_tiles, got_meta))
    occ_done, virt_done = (
        lax.psum_scatter(occ_total, "layer", scatter_dimension=1, tiled=True),
        lax.psum_scatter(virt_total, "layer", scatter_dimension=2, tiled=True),
    )
    mesh_count = row_count * layer_count
    thin_rows = tile_side // mesh_count
    stack_count = mesh_count // col_count
    narrow = occ_done.shape[1]
    occ_five = occ_done.reshape(aux_count, 1, col_count, thin_rows, tile_side)
    virt_five = virt_done.reshape(aux_count, stack_count, col_count, thin_rows, narrow)
    occ_moved, virt_moved = (
        lax.all_to_all(occ_five, "col", split_axis=2, concat_axis=1, tiled=True),
        lax.all_to_all(virt_five, "col", split_axis=2, concat_axis=1, tiled=True),
    )
    virt_four = virt_moved.reshape(aux_count, mesh_count, thin_rows, narrow)
    virt_back = lax.all_to_all(virt_four, ("row", "layer"), split_axis=1, concat_axis=3, tiled=True)
    occ_final = occ_moved.reshape(aux_count, col_count, thin_rows, tile_side)
    virt_final = virt_back.reshape(aux_count, thin_rows, col_count, tile_side)
    chi_part = jnp.einsum(
        "pcji,qjci->pq",
        occ_final,
        virt_final,
        precision=lax.Precision.HIGHEST,
        preferred_element_type=jnp.float32,
    )
    return lax.psum(chi_part, ("row", "col", "layer"))


def solution(mesh):
    in_specs = (
        P(("col", "layer"), None, None),
        P(("col", "layer")),
        P(("col", "layer")),
        P(("col", "layer")),
        P(("col", "layer")),
        P("layer", "row"),
        P("layer", "row"),
    )
    out_specs = P()
    return jax.shard_map(
        on_device, mesh=mesh, in_specs=in_specs, out_specs=out_specs, check_vma=False
    )
```

profile of v0, /device:TPU:1, one launch (start us, length us, event | category | flops | bytes accessed | tf_op | source)
XLA Modules:
  0.0 812.4 jit_solution(16769600088540931036)
XLA Ops:
  6.5 0.7 subtract_bitcast_fusion
  7.2 0.7 multiply_add_fusion
  8.3 0.7 pad_add_fusion
  9.0 0.8 scatter_custom_fusion.2
  9.9 1.1 copy.19
  11.0 13.0 %all-to-all-start = ((s32[64,2,2]{1,2,0:T(2,128)}), s32[64,2,2]{1,2,0:T(2,128)S(1)}, u32[]{:S(2)}, u32[]{:S(2)}) async-start(s32[64,2,2]{1,2,0:T(2,128)} %copy.19), calls=%async_computation | async-start | bytes 131072 | tf_op jit(solution)/shard_map/all_to_all | solution.py:52
  24.0 0.7 iota_compare_fusion
  24.7 2.1 broadcast_select_fusion
  26.8 3.0 broadcast_in_dim.41
  29.7 12.6 %scatter_fusion.2 = bf16[128,128,128]{2,1,0:T(8,128)(2,1)} fusion(bf16[128,128,128]{2,1,0:T(8,128)(2,1)} %broadcast_in_dim.41, s32[88]{0:T(128)S(1)} %compare_select_fusion.2, bf16[88,128,128]{2,1,0:T(8,128)(2,1)S(1)} %broadcast_select_fusion), kind=kCustom, calls=%fused_computation.5 | custom fusion | bytes 8651104 | tf_op jit(solution)/shard_map/scatter | solution.py:34
  42.3 10.5 %all-to-all-start.1 = ((bf16[128,128,128]{2,1,0:T(8,128)(2,1)}), bf16[128,128,128]{2,1,0:T(8,128)(2,1)}, u32[]{:S(2)}, u32[]{:S(2)}) async-start(bf16[128,128,128]{2,1,0:T(8,128)(2,1)} %scatter_fusion.2), calls=%async_computation.1 | async-start | bytes 8388608 | tf_op jit(solution)/shard_map/all_to_all | solution.py:45
  53.0 93.4 %all-to-all-done.1 = bf16[128,128,128]{2,1,0:T(8,128)(2,1)} async-done(((bf16[128,128,128]{2,1,0:T(8,128)(2,1)}), bf16[128,128,128]{2,1,0:T(8,128)(2,1)}, u32[]{:S(2)}, u32[]{:S(2)}) %all-to-all-start.1) | async-done | bytes 4194336 | tf_op jit(solution)/shard_map/all_to_all | solution.py:45
  146.3 3.4 broadcast_in_dim.22
  149.7 3.4 broadcast_in_dim.38
  153.1 367.4 %while.13 = (s32[]{:T(128)}, f32[24,512,128]{2,1,0:T(8,128)}, f32[24,128,512]{2,1,0:T(8,128)}, s32[4,32,2]{1,0,2:T(4,128)S(1)}, bf16[5120,512]{1,0:T(8,128)(2,1)...) while((s32[]{:T(128)}, f32[24,512,128]{2,1,0:T(8,128)}, ...), condition=%wide.region_7.8_spmd.clone, body=%wide.region_4.7_spmd.clone.sunk | while | flops 1077956736 | bytes 94423512 | solution.py:89
  153.2 20.6 %gather_fusion.1 = bf16[4096,512]{1,0:T(8,128)(2,1)} fusion(bf16[5120,512]{1,0:T(8,128)(2,1)} %get-tuple-element.167, s32[4096]{0:T(1024)S(1)} %fusion.37), kind=kCustom, calls=%fused_computation.1.clone.clone.1 | custom fusion | bytes 8404992 | tf_op jit(solution)/shard_map/while/body/eval_jaxpr/gather | solution.py:72
  173.8 7.0 fusion.39
  180.7 18.2 %scatter_fusion.1 = f32[24,128,512]{2,1,0:T(8,128)} fusion(f32[24,128,512]{2,1,0:T(8,128)} %get-tuple-element.155, s32[32]{0:T(128)S(1)} %get-tuple-element.143, f32[32,128,512]{2,1,0:T(8,128)} %fusion.39), kind=kCustom, calls=%fused_computation.3.clone.clone.1 | custom fusion | flops 2097152 | bytes 25165952 | tf_op jit(solution)/shard_map/while/body/eval_jaxpr/scatter-add | solution.py:81
  199.0 20.6 %gather_fusion = bf16[4096,512]{1,0:T(8,128)(2,1)} fusion(bf16[5120,512]{1,0:T(8,128)(2,1)} %get-tuple-element.165, s32[4096]{0:T(1024)S(1)} %fusion.37), kind=kCustom, calls=%fused_computation.clone.clone.1 | custom fusion | bytes 8404992 | tf_op jit(solution)/shard_map/while/body/eval_jaxpr/gather | solution.py:71
  219.6 7.0 fusion.38
  226.6 18.2 %scatter_fusion = f32[24,512,128]{2,1,0:T(8,128)} fusion(f32[24,512,128]{2,1,0:T(8,128)} %get-tuple-element.154, s32[32]{0:T(128)S(1)} %get-tuple-element.143, f32[32,512,128]{2,1,0:T(8,128)} %fusion.38), kind=kCustom, calls=%fused_computation.2.clone.clone.1 | custom fusion | flops 2097152 | bytes 25165952 | tf_op jit(solution)/shard_map/while/body/eval_jaxpr/scatter-add | solution.py:81
  244.9 20.6 %gather_fusion.1 = bf16[4096,512]{1,0:T(8,128)(2,1)} fusion(bf16[5120,512]{1,0:T(8,128)(2,1)} %get-tuple-element.167, s32[4096]{0:T(1024)S(1)} %fusion.37), kind=kCustom, calls=%fused_computation.1.clone.clone.1 | custom fusion | bytes 8404992 | tf_op jit(solution)/shard_map/while/body/eval_jaxpr/gather | solution.py:72
  265.5 7.0 fusion.39
  272.4 18.3 %scatter_fusion.1 = f32[24,128,512]{2,1,0:T(8,128)} fusion(f32[24,128,512]{2,1,0:T(8,128)} %get-tuple-element.155, s32[32]{0:T(128)S(1)} %get-tuple-element.143, f32[32,128,512]{2,1,0:T(8,128)} %fusion.39), kind=kCustom, calls=%fused_computation.3.clone.clone.1 | custom fusion | flops 2097152 | bytes 25165952 | tf_op jit(solution)/shard_map/while/body/eval_jaxpr/scatter-add | solution.py:81
  290.7 20.6 %gather_fusion = bf16[4096,512]{1,0:T(8,128)(2,1)} fusion(bf16[5120,512]{1,0:T(8,128)(2,1)} %get-tuple-element.165, s32[4096]{0:T(1024)S(1)} %fusion.37), kind=kCustom, calls=%fused_computation.clone.clone.1 | custom fusion | bytes 8404992 | tf_op jit(solution)/shard_map/while/body/eval_jaxpr/gather | solution.py:71
  311.3 7.0 fusion.38
  318.3 18.2 %scatter_fusion = f32[24,512,128]{2,1,0:T(8,128)} fusion(f32[24,512,128]{2,1,0:T(8,128)} %get-tuple-element.154, s32[32]{0:T(128)S(1)} %get-tuple-element.143, f32[32,512,128]{2,1,0:T(8,128)} %fusion.38), kind=kCustom, calls=%fused_computation.2.clone.clone.1 | custom fusion | flops 2097152 | bytes 25165952 | tf_op jit(solution)/shard_map/while/body/eval_jaxpr/scatter-add | solution.py:81
  336.6 20.6 %gather_fusion.1 = bf16[4096,512]{1,0:T(8,128)(2,1)} fusion(bf16[5120,512]{1,0:T(8,128)(2,1)} %get-tuple-element.167, s32[4096]{0:T(1024)S(1)} %fusion.37), kind=kCustom, calls=%fused_computation.1.clone.clone.1 | custom fusion | bytes 8404992 | tf_op jit(solution)/shard_map/while/body/eval_jaxpr/gather | solution.py:72
  357.2 7.0 fusion.39
  364.1 18.5 %scatter_fusion.1 = f32[24,128,512]{2,1,0:T(8,128)} fusion(f32[24,128,512]{2,1,0:T(8,128)} %get-tuple-element.155, s32[32]{0:T(128)S(1)} %get-tuple-element.143, f32[32,128,512]{2,1,0:T(8,128)} %fusion.39), kind=kCustom, calls=%fused_computation.3.clone.clone.1 | custom fusion | flops 2097152 | bytes 25165952 | tf_op jit(solution)/shard_map/while/body/eval_jaxpr/scatter-add | solution.py:81
  382.6 20.6 %gather_fusion = bf16[4096,512]{1,0:T(8,128)(2,1)} fusion(bf16[5120,512]{1,0:T(8,128)(2,1)} %get-tuple-element.165, s32[4096]{0:T(1024)S(1)} %fusion.37), kind=kCustom, calls=%fused_computation.clone.clone.1 | custom fusion | bytes 8404992 | tf_op jit(solution)/shard_map/while/body/eval_jaxpr/gather | solution.py:71
  403.2 7.0 fusion.38
  410.2 18.5 %scatter_fusion = f32[24,512,128]{2,1,0:T(8,128)} fusion(f32[24,512,128]{2,1,0:T(8,128)} %get-tuple-element.154, s32[32]{0:T(128)S(1)} %get-tuple-element.143, f32[32,512,128]{2,1,0:T(8,128)} %fusion.38), kind=kCustom, calls=%fused_computation.2.clone.clone.1 | custom fusion | flops 2097152 | bytes 25165952 | tf_op jit(solution)/shard_map/while/body/eval_jaxpr/scatter-add | solution.py:81
  428.9 20.6 %gather_fusion.1 = bf16[4096,512]{1,0:T(8,128)(2,1)} fusion(bf16[5120,512]{1,0:T(8,128)(2,1)} %get-tuple-element.167, s32[4096]{0:T(1024)S(1)} %fusion.37), kind=kCustom, calls=%fused_computation.1.clone.clone.1 | custom fusion | bytes 8404992 | tf_op jit(solution)/shard_map/while/body/eval_jaxpr/gather | solution.py:72
  449.4 7.0 fusion.39
  456.4 18.3 %scatter_fusion.1 = f32[24,128,512]{2,1,0:T(8,128)} fusion(f32[24,128,512]{2,1,0:T(8,128)} %get-tuple-element.155, s32[32]{0:T(128)S(1)} %get-tuple-element.143, f32[32,128,512]{2,1,0:T(8,128)} %fusion.39), kind=kCustom, calls=%fused_computation.3.clone.clone.1 | custom fusion | flops 2097152 | bytes 25165952 | tf_op jit(solution)/shard_map/while/body/eval_jaxpr/scatter-add | solution.py:81
  474.7 20.6 %gather_fusion = bf16[4096,512]{1,0:T(8,128)(2,1)} fusion(bf16[5120,512]{1,0:T(8,128)(2,1)} %get-tuple-element.165, s32[4096]{0:T(1024)S(1)} %fusion.37), kind=kCustom, calls=%fused_computation.clone.clone.1 | custom fusion | bytes 8404992 | tf_op jit(solution)/shard_map/while/body/eval_jaxpr/gather | solution.py:71
  495.3 7.0 fusion.38
  502.3 18.2 %scatter_fusion = f32[24,512,128]{2,1,0:T(8,128)} fusion(f32[24,512,128]{2,1,0:T(8,128)} %get-tuple-element.154, s32[32]{0:T(128)S(1)} %get-tuple-element.143, f32[32,512,128]{2,1,0:T(8,128)} %fusion.38), kind=kCustom, calls=%fused_computation.2.clone.clone.1 | custom fusion | flops 2097152 | bytes 25165952 | tf_op jit(solution)/shard_map/while/body/eval_jaxpr/scatter-add | solution.py:81
  521.3 64.1 %reduce-scatter.5.cloned.1.call-done = f32[24,128,128]{2,1,0:T(8,128)} async-done(((f32[24,128,512]{2,1,0:T(8,128)}), f32[24,128,128]{2,1,0:T(8,128)}) %reduce-scatter.5.cloned.1.call-update) | async-done | bytes 1572880 | tf_op jit(solution)/shard_map/reduce_scatter | solution.py:92
  585.4 3.5 copy.23
  588.9 7.6 all-to-all-start.3
  596.5 57.8 %reduce-scatter.3.cloned.1.call-done = f32[24,128,128]{2,1,0:T(8,128)} async-done(((f32[24,512,128]{2,1,0:T(8,128)}), f32[24,128,128]{2,1,0:T(8,128)}) %reduce-scatter.3.cloned.1.call-update) | async-done | bytes 1572880 | tf_op jit(solution)/shard_map/reduce_scatter | solution.py:91
  654.2 2.3 copy.22
  656.6 47.2 %all_to_all.47 = f32[24,1,16,8,128]{4,0,3,1,2:T(8,128)S(1)} all-to-all(f32[24,1,16,8,128]{4,0,3,1,2:T(8,128)S(1)} %bitcast.69), channel_id=1, replica_groups=mesh['row'=4,'col'=16,'layer'=4] {'col'}, dimensions={2} | all-to-all | bytes 3145728 | tf_op jit(solution)/shard_map/all_to_all | solution.py:101
  703.8 27.5 %all_to_all.48 = f32[24,16,8,128]{3,0,2,1:T(8,128)S(1)} all-to-all(f32[24,16,8,128]{3,0,2,1:T(8,128)S(1)} %bitcast.68), channel_id=1, replica_groups=mesh['row'=4,'col'=16,'layer'=4] {'row','layer'}, dimensions={1} | all-to-all | bytes 3145728 | tf_op jit(solution)/shard_map/all_to_all | solution.py:105
  731.3 1.6 fusion.16
  732.8 72.8 %psum.7 = f32[24,24]{1,0:T(8,128)} all-reduce(f32[24,24]{1,0:T(8,128)S(1)} %fusion.16), channel_id=1, replica_groups=mesh['row'=4,'col'=16,'layer'=4] {'row','col','layer'}, use_global_device_ids=true, to_apply=%region_10.11 | all-reduce | flops 576 | bytes 4608 | tf_op jit(solution)/shard_map/psum | solution.py:115
  (25 shorter events, 1.8 us)
Async XLA Ops:
  11.0 31.4 %all-to-all-start = ((s32[64,2,2]{1,2,0:T(2,128)}), s32[64,2,2]{1,2,0:T(2,128)S(1)}, u32[]{:S(2)}, u32[]{:S(2)}) async-start(s32[64,2,2]{1,2,0:T(2,128)} %copy.19), calls=%async_computation | async-start | bytes 131072 | tf_op jit(solution)/shard_map/all_to_all | solution.py:52
  42.3 104.0 %all-to-all-start.1 = ((bf16[128,128,128]{2,1,0:T(8,128)(2,1)}), bf16[128,128,128]{2,1,0:T(8,128)(2,1)}, u32[]{:S(2)}, u32[]{:S(2)}) async-start(bf16[128,128,128]{2,1,0:T(8,128)(2,1)} %scatter_fusion.2), calls=%async_computation.1 | async-start | bytes 8388608 | tf_op jit(solution)/shard_map/all_to_all | solution.py:45
  52.8 532.6 %reduce-scatter.5.cloned.1.call-start = ((), (), s32[]{:S(2)}) async-start(), calls=%async_computation.8 | async-start | bytes 7864320 | tf_op jit(solution)/shard_map/reduce_scatter | solution.py:92
  520.5 133.7 %reduce-scatter.3.cloned.1.call-start = ((), (), s32[]{:S(2)}) async-start(), calls=%async_computation.7 | async-start | bytes 7864320 | tf_op jit(solution)/shard_map/reduce_scatter | solution.py:91
  588.9 67.7 %all-to-all-start.3 = ((f32[24,1,16,8,128]{4,0,3,1,2:T(8,128)}), f32[24,1,16,8,128]{4,0,3,1,2:T(8,128)S(1)}, u32[]{:S(2)}, u32[]{:S(2)}) async-start(f32[24,1,16,8,128]{4,0,3,1,2:T(8,128)} %bitcast.6), calls=%async_computation.5 | async-start | bytes 3145728 | tf_op jit(solution)/shard_map/all_to_all | solution.py:102
Sparse Core Ops, SparseCore 0:
  520.6 64.7 reduce-scatter.4
  588.0 66.2 reduce-scatter.2
where the time goes:
time: 814 us; the launch traced here: 812 us
  waiting for transfers between devices  216 us (27%)
  local copies, waits for them, and re-layouts  195 us (24%)
  other arithmetic  152 us (19%)
  blocking collectives  147 us (18%)
  matrix products  57.5 us (7%)
  starting transfers between devices  31.3 us (4%)
  between operations  13.5 us (2%)
    all_to_all x1, waiting for transfers between devices, on_device(): lax.all_to_all(send_tiles.reshape(total_slots, tile_side, tile_side), ('c...  93.4 us
    gather x4, local copies, waits for them, and re-layouts, add_group(): virt_rows = virt_cols[row_index]  82.3 us
    gather x4, local copies, waits for them, and re-layouts, add_group(): occ_rows = occ_cols[row_index]  82.3 us
    scatter-add x4, other arithmetic, add_group(): virt_total.at[aux_index].add(virt_term)  73.3 us
    scatter-add x4, other arithmetic, add_group(): occ_total.at[aux_index].add(occ_term)  73.1 us
    psum x1, blocking collectives, on_device(): return lax.psum(chi_part, ('row', 'col', 'layer'))  72.8 us
    reduce_scatter x1, waiting for transfers between devices, on_device(): lax.psum_scatter(virt_total, 'layer', scatter_dimension=2, tiled=True)  64.1 us
    reduce_scatter x1, waiting for transfers between devices, on_device(): lax.psum_scatter(occ_total, 'layer', scatter_dimension=1, tiled=True)  57.8 us
  transfers between devices with their start and end apart: 5, of which 3 were waited for; matrix products, arithmetic and copies ran while one was open for 3% of the time, Pallas kernels for 0%

commit v1 on v0

v1 whole, which is shorter than its diff:
```python
import functools

import jax
import jax.numpy as jnp
from jax import lax
from jax.experimental import pallas as pl
from jax.experimental.pallas import tpu as pltpu
from jax.sharding import PartitionSpec as P

NP = 24
ROWS = 4
COLS = 16
LAYERS = 4
CAP = 2
OWNERS = COLS * LAYERS
BS = 128
QUARTER = BS // ROWS
WIDE = 512
HALF = NP // 2
TOP = 32700.0
STEPS = 64.0
ALL = ("row", "col", "layer")
F32 = jnp.float32
BF16 = jnp.bfloat16
S16 = jnp.int16


def params(mib):
    return pltpu.CompilerParams(vmem_limit_bytes=mib * 2**20)


def encode(block):
    peak = jnp.max(jnp.abs(block), axis=0, keepdims=True)
    level = jnp.ceil(jnp.log2(jnp.maximum(peak, 1e-30)) * STEPS)
    scaled = block * (jnp.exp2(level * (-1.0 / STEPS)) * TOP)
    return jnp.round(scaled).astype(jnp.int32).astype(S16), level


def decode(codes, level):
    return codes.astype(jnp.int32).astype(F32) * (jnp.exp2(level * (1.0 / STEPS)) * (1.0 / TOP))


def send_body(aux_ref, row_ref, col_ref, ext_ref, place_ref, blocks_ref, out_ref, count_ref, *, layer_blocks):
    del place_ref
    out_ref[...] = jnp.zeros(out_ref.shape, BF16)

    @pl.loop(0, OWNERS)
    def _(i):
        count_ref[i] = 0

    lane = lax.broadcasted_iota(jnp.int32, (QUARTER, BS), 1)
    meta_lane = lax.broadcasted_iota(jnp.int32, (8, BS), 1)

    @pl.loop(0, blocks_ref.shape[0])
    def _(i):
        col = col_ref[i]
        layer_of = col // layer_blocks
        kept = col - layer_of * layer_blocks
        owner = row_ref[i] * LAYERS + layer_of
        used = count_ref[owner]
        count_ref[owner] = used + 1
        tile = jnp.where(lane < ext_ref[i], blocks_ref[i].astype(F32), 0.0)
        out_ref[owner, pl.ds(pl.multiple_of(used * QUARTER, QUARTER), QUARTER), :] = tile.astype(BF16)
        old = out_ref[owner, 2 * QUARTER :, :].astype(F32)
        new = jnp.where(meta_lane == used * 2, aux_ref[i].astype(F32), old)
        new = jnp.where(meta_lane == used * 2 + 1, kept.astype(F32), new)
        out_ref[owner, 2 * QUARTER :, :] = new.astype(BF16)


def build_send(blocks, block_aux, block_row, block_col, extents, row_place, layer_blocks):
    held = blocks.shape[0]
    return pl.pallas_call(
        functools.partial(send_body, layer_blocks=layer_blocks),
        grid_spec=pltpu.PrefetchScalarGridSpec(
            num_scalar_prefetch=5,
            grid=(1,),
            in_specs=[pl.BlockSpec((held, QUARTER, BS), lambda i, a, r, c, e, p: (0, p[0], 0))],
            out_specs=pl.BlockSpec((OWNERS, 2 * QUARTER + 8, BS), lambda i, a, r, c, e, p: (0, 0, 0)),
            scratch_shapes=[pltpu.SMEM((OWNERS,), jnp.int32)],
        ),
        out_shape=jax.ShapeDtypeStruct((OWNERS, 2 * QUARTER + 8, BS), BF16),
        compiler_params=params(16),
        name="build_send",
    )(block_aux, block_row, block_col, extents, row_place, blocks)


def contract_body(meta_ref, place_ref, own_ref, prev_ref, next_ref, far_a_ref, far_b_ref, green_ref, *rest, transposed):
    if transposed:
        keep_ref, send0_ref, send1_ref, acc_ref, tile_ref = rest
    else:
        keep_ref, send0_ref, send1_ref, acc_ref, tile_ref = rest
    row_place = place_ref[0]
    acc_ref[...] = jnp.zeros(acc_ref.shape, F32)
    at = [pl.multiple_of(((row_place + d) % ROWS) * QUARTER, QUARTER) for d in (0, ROWS - 1, 1, 2)]
    half = OWNERS // 2

    def one_source(source, far_ref, far_source):
        for slot in range(CAP):
            span = slice(slot * QUARTER, (slot + 1) * QUARTER)
            tile_ref[slot, pl.ds(at[0], QUARTER), :] = own_ref[source, span, :]
            tile_ref[slot, pl.ds(at[1], QUARTER), :] = prev_ref[source, span, :]
            tile_ref[slot, pl.ds(at[2], QUARTER), :] = next_ref[source, span, :]
            tile_ref[slot, pl.ds(at[3], QUARTER), :] = far_ref[far_source, span, :]
        for slot in range(CAP):
            tile = tile_ref[slot]
            aux = meta_ref[source, 2 * slot]
            kept = meta_ref[source, 2 * slot + 1]
            green = green_ref[kept]
            if transposed:
                term = lax.dot_general(green, tile, (((1,), (1,)), ((), ())), preferred_element_type=F32)
                for low in range(4):
                    lanes = slice(low * BS, (low + 1) * BS)
                    acc_ref[aux, :, lanes] += term[low * BS : (low + 1) * BS, :]
            else:
                acc_ref[aux] += jnp.dot(tile, green, preferred_element_type=F32)

    @pl.loop(0, half)
    def _(source):
        one_source(source, far_a_ref, source)

    @pl.loop(0, half)
    def _(source):
        one_source(source + half, far_b_ref, source)

    bit_a = place_ref[1]
    bit_b = place_ref[2]

    def piece(a, b):
        return pl.multiple_of(jnp.where(b == 0, a, 3 - a) * QUARTER, QUARTER)

    for h, send_ref in ((0, send0_ref), (1, send1_ref)):
        kept_rows = []
        sent_rows = []
        for other in range(2):
            if h == 0:
                kept_rows.append(piece(bit_a, other))
                sent_rows.append(piece(1 - bit_a, other))
            else:
                kept_rows.append(piece(other, bit_b))
                sent_rows.append(piece(other, 1 - bit_b))

        @pl.loop(0, HALF)
        def _(p):
            levels = []
            for other in range(2):
                keep_ref[h, other, p] = acc_ref[p + h * HALF, pl.ds(kept_rows[other], QUARTER), :]
                codes, level = encode(acc_ref[p + h * HALF, pl.ds(sent_rows[other], QUARTER), :])
                send_ref[other, p] = codes
                levels.append(level)
            put_levels(send_ref, 0, p, levels[0])
            put_levels(send_ref, 1, p, levels[1])


def put_levels(ref, which, p, level):
    count = ref.shape[1] - 1
    at_row = lax.broadcasted_iota(jnp.int32, (QUARTER, ref.shape[-1]), 0) == p
    old = ref[which, count].astype(jnp.int32)
    ref[which, count] = jnp.where(at_row, level.astype(jnp.int32), old).astype(S16)


def get_levels(ref, which, p):
    count = ref.shape[1] - 1
    at_row = lax.broadcasted_iota(jnp.int32, (QUARTER, ref.shape[-1]), 0) == p
    rows = ref[which, count].astype(jnp.int32)
    return jnp.sum(jnp.where(at_row, rows, 0), axis=0, keepdims=True).astype(F32)


def contract(meta, place, quarters, green, transposed):
    own, prev, nxt, far_a, far_b = quarters
    vmem = pl.BlockSpec(memory_space=pltpu.VMEM)
    smem = pl.BlockSpec(memory_space=pltpu.SMEM)
    code = jax.ShapeDtypeStruct((2, HALF + 1, QUARTER, WIDE), S16)
    return pl.pallas_call(
        functools.partial(contract_body, transposed=transposed),
        in_specs=[smem, smem] + [vmem] * 6,
        out_specs=[vmem] * 3,
        out_shape=[jax.ShapeDtypeStruct((2, 2, HALF, QUARTER, WIDE), F32), code, code],
        scratch_shapes=[pltpu.VMEM((NP, BS, WIDE), F32), pltpu.VMEM((CAP, BS, BS), BF16)],
        compiler_params=params(48),
        name="contract_virt" if transposed else "contract_occ",
    )(meta, place, own, prev, nxt, far_a, far_b, green)


def halve_body(place_ref, keep_ref, got0_ref, got1_ref, left_ref, send0_ref, send1_ref):
    for h, got_ref, send_ref in ((0, got0_ref, send0_ref), (1, got1_ref, send1_ref)):
        mine = place_ref[2 - h]

        @pl.loop(0, HALF)
        def _(p):
            left_ref[h, p] = keep_ref[h, mine, p] + decode(got_ref[mine, p], get_levels(got_ref, mine, p))
            away = 1 - mine
            total = keep_ref[h, away, p] + decode(got_ref[away, p], get_levels(got_ref, away, p))
            codes, level = encode(total)
            send_ref[0, p] = codes
            put_levels(send_ref, 0, p, level)


def halve(place, keep, got0, got1, name):
    vmem = pl.BlockSpec(memory_space=pltpu.VMEM)
    smem = pl.BlockSpec(memory_space=pltpu.SMEM)
    code = jax.ShapeDtypeStruct((1, HALF + 1, QUARTER, WIDE), S16)
    return pl.pallas_call(
        halve_body,
        in_specs=[smem] + [vmem] * 3,
        out_specs=[vmem] * 3,
        out_shape=[jax.ShapeDtypeStruct((2, HALF, QUARTER, WIDE), F32), code, code],
        compiler_params=params(40),
        name=name,
    )(place, keep, got0, got1)


def finish_body(left_ref, got0_ref, got1_ref, out_ref, *, split):
    for h, got_ref in ((0, got0_ref), (1, got1_ref)):

        @pl.loop(0, HALF)
        def _(p):
            total = left_ref[h, p] + decode(got_ref[0, p], get_levels(got_ref, 0, p))
            codes, level = encode(total)
            if split:
                for low in range(4):
                    lanes = slice(low * BS, (low + 1) * BS)
                    out_ref[low, p + h * HALF] = codes[:, lanes]
                    put_levels(out_ref, low, p + h * HALF, level[:, lanes])
            else:
                out_ref[0, p + h * HALF] = codes
                put_levels(out_ref, 0, p + h * HALF, level)


def finish(left, got0, got1, split, name):
    vmem = pl.BlockSpec(memory_space=pltpu.VMEM)
    shape = (4, NP + 1, QUARTER, BS) if split else (1, NP + 1, QUARTER, WIDE)
    return pl.pallas_call(
        functools.partial(finish_body, split=split),
        in_specs=[vmem] * 3,
        out_specs=vmem,
        out_shape=jax.ShapeDtypeStruct(shape, S16),
        compiler_params=params(32),
        name=name,
    )(left, got0, got1)


def pair_body(low_ref, own_ref, one_ref, two_ref, three_ref, virt_ref, out_ref, occ_ref, vir_ref):
    here = low_ref[0]

    @pl.loop(0, NP)
    def _(p):
        values = decode(virt_ref[0, p], get_levels(virt_ref, 0, p))
        for low in range(4):
            vir_ref[p, low * QUARTER : (low + 1) * QUARTER, :] = values[:, low * BS : (low + 1) * BS]
        own = decode(own_ref[here, p], get_levels(own_ref, here, p))
        occ_ref[p, pl.ds(pl.multiple_of(here * QUARTER, QUARTER), QUARTER), :] = own
        for d, ref in ((1, one_ref), (2, two_ref), (3, three_ref)):
            source = (here + 4 - d) % 4
            part = decode(ref[0, p], get_levels(ref, 0, p))
            occ_ref[p, pl.ds(pl.multiple_of(source * QUARTER, QUARTER), QUARTER), :] = part

    @pl.loop(0, NP)
    def _(p):
        occ = occ_ref[p]
        for q in range(NP):
            out_ref[p, q : q + 1, :] = jnp.sum(occ * vir_ref[q], axis=0, keepdims=True)


def pair(low, own, others, virt):
    vmem = pl.BlockSpec(memory_space=pltpu.VMEM)
    smem = pl.BlockSpec(memory_space=pltpu.SMEM)
    return pl.pallas_call(
        pair_body,
        in_specs=[smem] + [vmem] * 5,
        out_specs=vmem,
        out_shape=jax.ShapeDtypeStruct((NP, NP, BS), F32),
        scratch_shapes=[pltpu.VMEM((NP, BS, BS), F32), pltpu.VMEM((NP, BS, BS), F32)],
        compiler_params=params(32),
        name="pair",
    )(low, own, *others, virt)


def rotate(size, step):
    return [(i, (i + step) % size) for i in range(size)]


def rotate_low(step):
    return [(c, c - c % 4 + (c + step) % 4) for c in range(COLS)]


def rotate_high(step):
    return [(c, (c + 4 * step) % COLS) for c in range(COLS)]


PAIRS_A = [(0, 1), (1, 0), (2, 3), (3, 2)]
PAIRS_B = [(0, 3), (3, 0), (1, 2), (2, 1)]


def index_of(row, col, layer):
    return (row * COLS + col) * LAYERS + layer


SWAP = [
    (index_of(r, c, l), index_of(c // 4, 4 * r + c % 4, l))
    for r in range(ROWS)
    for c in range(COLS)
    for l in range(LAYERS)
]


def tree_sum(values):
    rounds = (
        ("layer", [rotate(LAYERS, d) for d in (1, 2, 3)]),
        ("col", [rotate_low(d) for d in (1, 2, 3)]),
        ("row", [rotate(ROWS, d) for d in (1, 2, 3)]),
        ("col", [rotate_high(d) for d in (1, 2, 3)]),
    )
    for axis, perms in rounds:
        one, two, three = [lax.ppermute(values, axis, perm) for perm in perms]
        values = (values + two) + (one + three)
    return values


def on_device(blocks, block_aux, block_row, block_col, extents, occ_green, virt_green):
    layer_blocks = occ_green.shape[0] // BS
    row_place = lax.axis_index("row").astype(jnp.int32)
    col_place = lax.axis_index("col").astype(jnp.int32)
    layer_place = lax.axis_index("layer").astype(jnp.int32)
    bit_a = ((layer_place == 1) | (layer_place == 2)).astype(jnp.int32)
    bit_b = layer_place // 2
    place = jnp.stack([row_place, bit_a, bit_b])

    send = build_send(blocks, block_aux, block_row, block_col, extents, row_place[None], layer_blocks)
    own = lax.all_to_all(send, ("col", "layer"), 0, 0, tiled=True)
    meta = own[:, 2 * QUARTER, :4].astype(jnp.int32)
    prev = lax.ppermute(own, "row", rotate(ROWS, 1))
    nxt = lax.ppermute(own, "row", rotate(ROWS, -1))
    half = OWNERS // 2
    far_a = lax.ppermute(prev[:half], "row", rotate(ROWS, 1))
    far_b = lax.ppermute(nxt[half:], "row", rotate(ROWS, -1))
    quarters = (own, prev, nxt, far_a, far_b)

    virt_blocks = virt_green.reshape(layer_blocks, BS, WIDE).transpose(0, 2, 1)
    occ_blocks = occ_green.reshape(layer_blocks, BS, WIDE)

    v_keep, v_send0, v_send1 = contract(meta, place, quarters, virt_blocks, True)
    v_got0 = lax.ppermute(v_send0, "layer", PAIRS_A)
    v_got1 = lax.ppermute(v_send1, "layer", PAIRS_B)
    o_keep, o_send0, o_send1 = contract(meta, place, quarters, occ_blocks, False)
    o_got0 = lax.ppermute(o_send0, "layer", PAIRS_A)
    o_got1 = lax.ppermute(o_send1, "layer", PAIRS_B)
    v_left, v_send0, v_send1 = halve(place, v_keep, v_got0, v_got1, "halve_virt")
    v_got0 = lax.ppermute(v_send0, "layer", PAIRS_B)
    v_got1 = lax.ppermute(v_send1, "layer", PAIRS_A)
    o_left, o_send0, o_send1 = halve(place, o_keep, o_got0, o_got1, "halve_occ")
    o_got0 = lax.ppermute(o_send0, "layer", PAIRS_B)
    o_got1 = lax.ppermute(o_send1, "layer", PAIRS_A)
    virt = finish(v_left, v_got0, v_got1, False, "finish_virt")
    virt = lax.ppermute(virt, ALL, SWAP)
    occ = finish(o_left, o_got0, o_got1, True, "finish_occ")

    low = (col_place % 4)[None]
    others = []
    for d in (1, 2, 3):
        part = lax.dynamic_slice_in_dim(occ, (low[0] + d) % 4, 1, 0)
        others.append(lax.ppermute(part, "col", rotate_low(d)))
    partial = pair(low, occ, others, virt)
    return tree_sum(jnp.sum(partial, axis=-1))


def solution(mesh):
    in_specs = (
        P(("col", "layer"), None, None),
        P(("col", "layer")),
        P(("col", "layer")),
        P(("col", "layer")),
        P(("col", "layer")),
        P("layer", "row"),
        P("layer", "row"),
    )
    return jax.shard_map(on_device, mesh=mesh, in_specs=in_specs, out_specs=P(), check_vma=False)
```

time: 814 us -> 265 us (0.33)
  local copies, waits for them, and re-layouts: 195 us -> 15.2 us
  other arithmetic: 152 us -> 0.87 us
  waiting for transfers between devices: 216 us -> 82.4 us
  blocking collectives: 147 us -> 43.4 us
  Pallas kernels: 0 us -> 62.6 us
  matrix products: 57.5 us -> 0 us
  starting transfers between devices: 31.3 us -> 58.5 us
  between operations: 13.5 us -> 0.15 us
    gather x8 -> x0, local copies, waits for them, and re-layouts: 165 us -> none  [the longest x4 82.3 us: add_group(): virt_rows = virt_cols[row_index]]
    scatter-add x8 -> x0, other arithmetic: 146 us -> none  [the longest x4 73.3 us: add_group(): virt_total.at[aux_index].add(virt_term)]
    reduce_scatter x2 -> x0, waiting for transfers between devices: 122 us -> none  [the longest x1 64.1 us: on_device(): lax.psum_scatter(virt_total, 'layer', scatter_dimension=2, tiled=True)]
    all_to_all x3 -> x0, waiting for transfers between devices: 93.4 us -> none  [the longest x1 93.4 us: on_device(): lax.all_to_all(send_tiles.reshape(total_slots, tile_side, tile_side), ('c...]
    ppermute x0 -> x28, waiting for transfers between devices: none -> 82.4 us  [the longest x1 24.6 us: on_device(): prev = lax.ppermute(own, 'row', rotate(ROWS, 1))]
    psum x1 -> x0, blocking collectives: 72.8 us -> none  [on_device(): return lax.psum(chi_part, ('row', 'col', 'layer'))]
    pallas_call x0 -> x8, Pallas kernels: none -> 62.6 us  [the longest x2 44.3 us: contract(): pl.pallas_call(functools.partial(contract_body, transposed=transposed), i...]
    ppermute x0 -> x28, starting transfers between devices: none -> 58.5 us  [the longest x12 36.3 us: tree_sum(): one, two, three = [lax.ppermute(values, axis, perm) for perm in perms]]
  transfers between devices with their start and end apart: 5 -> 28, of which waited for: 3 -> 14; matrix products, arithmetic and copies ran while one was open for 3% -> 4% of each run, Pallas kernels for 0% -> 12%
where the time goes in v1:
time: 265 us; the launch traced here: 263 us
  waiting for transfers between devices  82.4 us (31%)
  Pallas kernels  62.6 us (24%)
  starting transfers between devices  58.5 us (22%)
  blocking collectives  43.4 us (16%)
  local copies, waits for them, and re-layouts  15.2 us (6%)
    pallas_call x2, Pallas kernels, contract(): pl.pallas_call(functools.partial(contract_body, transposed=transposed), i...  44.3 us
    all_to_all x1, blocking collectives, on_device(): own = lax.all_to_all(send, ('col', 'layer'), 0, 0, tiled=True)  43.4 us
    ppermute x12, starting transfers between devices, tree_sum(): one, two, three = [lax.ppermute(values, axis, perm) for perm in perms]  36.3 us
    ppermute x1, waiting for transfers between devices, on_device(): prev = lax.ppermute(own, 'row', rotate(ROWS, 1))  24.6 us
    ppermute x1, waiting for transfers between devices, on_device(): v_got0 = lax.ppermute(v_send0, 'layer', PAIRS_B)  20.7 us
    ppermute x12, waiting for transfers between devices, tree_sum(): one, two, three = [lax.ppermute(values, axis, perm) for perm in perms]  17.8 us
    ppermute x3, waiting for transfers between devices, on_device(): others.append(lax.ppermute(part, 'col', rotate_low(d)))  9.82 us
    ppermute x3, starting transfers between devices, on_device(): others.append(lax.ppermute(part, 'col', rotate_low(d)))  9.49 us
  transfers between devices with their start and end apart: 28, of which 14 were waited for; matrix products, arithmetic and copies ran while one was open for 4% of the time, Pallas kernels for 12%

profile of v1, /device:TPU:1, one launch (start us, length us, event | category | flops | bytes accessed | tf_op | source)
XLA Modules:
  0.0 263.1 jit_solution(17443767241634878131)
XLA Ops:
  0.0 1.8 copy-done.2
  1.8 0.7 copy-done.3
  2.5 0.7 copy-done.4
  3.1 0.7 copy-done.5
  3.8 0.7 copy-done.6
  4.4 3.3 %build_send.1 = bf16[64,72,128]{2,1,0:T(8,128)(2,1)S(1)} custom-call(s32[88]{0:T(128)S(1)} %copy-done.3, s32[88]{0:T(128)S(1)} %copy-done.4, s32[88]{0:T(128)S(1)} %copy-done.5, s32[88]{0:T(128)S(1)} %copy-done.6, s32[1]{0:T(128)} %bitcast.1.place_ref, bf16[88,128,128]{2,1,0:T(8,128)(2,1)S(1)} %copy-done.2), custom_call_target="tpu_custom_call" | custom-call | tf_op jit(solution)/shard_map/build_send/pallas_call | solution.py:72
  7.7 43.4 %all_to_all.5.own_ref = bf16[64,72,128]{2,1,0:T(8,128)(2,1)S(1)} all-to-all(bf16[64,72,128]{2,1,0:T(8,128)(2,1)S(1)} %build_send.1), channel_id=1, replica_groups=mesh['row'=4,'col'=16,'layer'=4] {'col','layer'}, dimensions={0} | all-to-all | bytes 2359296 | tf_op jit(solution)/shard_map/all_to_all | solution.py:329
  51.2 1.3 collective-permute-start
  52.5 1.4 collective-permute-start.1
  53.9 24.6 %collective-permute-done.prev_ref = bf16[64,72,128]{2,1,0:T(8,128)(2,1)S(1)} collective-permute-done((bf16[64,72,128]{2,1,0:T(8,128)(2,1)S(1)}, bf16[64,72,128]{2,1,0:T(8,128)(2,1)S(1)}, u32[]{:S(2)}, u32[]{:S(2)}) %collective-permute-start) | collective-permute-done | bytes 1179680 | tf_op jit(solution)/shard_map/ppermute | solution.py:331
  78.5 0.9 slice.13
  79.3 1.0 copy-done.7
  80.4 0.9 slice.14
  81.2 2.7 %collective-permute-start.3 = (bf16[32,72,128]{2,1,0:T(8,128)(2,1)}, bf16[32,72,128]{2,1,0:T(8,128)(2,1)S(1)}, u32[]{:S(2)}, u32[]{:S(2)}) collective-permute-start(bf16[32,72,128]{2,1,0:T(8,128)(2,1)} %slice.14), channel_id=1, source_target_pairs={{0,192},{64,0},{128,64},{192,128},{1,193},{65,1},{129,65},{193,129... | collective-permute-start | bytes 1769480 | tf_op jit(solution)/shard_map/ppermute | solution.py:335
  83.9 7.9 %copy.8 = bf16[40,128,512]{1,2,0:T(8,128)(2,1)} copy(bf16[40,128,512]{2,1,0:T(8,128)(2,1)} %bitcast.11) | data formatting | bytes 10485760 | tf_op jit(solution)/shard_map/reshape | solution.py:338
  91.9 1.3 collective-permute-done.2.far_a_ref
  93.2 1.0 collective-permute-done.3.far_b_ref
  94.2 23.7 %contract_virt.1 = (f32[2,2,12,32,512]{4,3,2,1,0:T(8,128)}, s16[2,13,32,512]{3,2,1,0:T(8,128)(2,1)S(1)}, s16[2,13,32,512]{3,2,1,0:T(8,128)(2,1)S(1)}) custom-call(s32[64,4]{1,0:T(8,128)S(1)} %bitcast.8, s32[3]{0:T(128)S(1)} %pad_add_fusion.place_ref, bf16[64,72,128]{2,1,0:T(8,128)(2,1)S(1)} %all_to_all.5.own_ref, ...), custom_call_target="tpu_custom_call" | custom-call | tf_op jit(solution)/shard_map/contract_virt/pallas_call | solution.py:173
  118.2 2.1 collective-permute-start.12
  120.2 20.6 %contract_occ.1 = (f32[2,2,12,32,512]{4,3,2,1,0:T(8,128)}, s16[2,13,32,512]{3,2,1,0:T(8,128)(2,1)S(1)}, s16[2,13,32,512]{3,2,1,0:T(8,128)(2,1)S(1)}) custom-call(s32[64,4]{1,0:T(8,128)S(1)} %bitcast.9, s32[3]{0:T(128)S(1)} %pad_add_fusion.place_ref, bf16[64,72,128]{2,1,0:T(8,128)(2,1)S(1)} %all_to_all.5.own_ref, ...), custom_call_target="tpu_custom_call" | custom-call | tf_op jit(solution)/shard_map/contract_occ/pallas_call | solution.py:173
  141.1 1.0 collective-permute-start.5
  142.0 2.6 halve_virt.1
  144.7 1.8 collective-permute-start.13
  146.5 20.7 %collective-permute-done.13.got0_ref = s16[1,13,32,512]{3,2,1,0:T(8,128)(2,1)S(1)} collective-permute-done((s16[1,13,32,512]{3,2,1,0:T(8,128)(2,1)S(1)}, s16[1,13,32,512]{3,2,1,0:T(8,128)(2,1)S(1)}, u32[]{:S(2)}, u32[]{:S(2)}) %collective-permute-start.13) | collective-permute-done | bytes 426016 | tf_op jit(solution)/shard_map/ppermute | solution.py:348
  167.2 1.6 finish_virt.1
  168.8 0.7 collective-permute-start.15
  169.5 3.5 %halve_occ.1 = (f32[2,12,32,512]{3,2,1,0:T(8,128)S(1)}, s16[1,13,32,512]{3,2,1,0:T(8,128)(2,1)}, s16[1,13,32,512]{3,2,1,0:T(8,128)(2,1)}) custom-call(s32[3]{0:T(128)S(1)} %pad_add_fusion.place_ref, f32[2,2,12,32,512]{4,3,2,1,0:T(8,128)S(1)} %copy-done, s16[2,13,32,512]{3,2,1,0:T(8,128)(2,1)S(1)} %collective-permute-done.4.got0_ref, ...), custom_call_target="tpu_custom_call" | custom-call | tf_op jit(solution)/shard_map/halve_occ/pallas_call | solution.py:202
  173.0 1.2 collective-permute-start.6
  174.2 7.3 %collective-permute-done.6.got0_ref = s16[1,13,32,512]{3,2,1,0:T(8,128)(2,1)} collective-permute-done((s16[1,13,32,512]{3,2,1,0:T(8,128)(2,1)}, s16[1,13,32,512]{3,2,1,0:T(8,128)(2,1)}, u32[]{:S(2)}, u32[]{:S(2)}) %collective-permute-start.6) | collective-permute-done | bytes 426016 | tf_op jit(solution)/shard_map/ppermute | solution.py:351
  181.5 3.0 %finish_occ.1.own_ref = s16[4,25,32,128]{3,2,1,0:T(8,128)(2,1)S(1)} custom-call(f32[2,12,32,512]{3,2,1,0:T(8,128)S(1)} %get-tuple-element.20.left_ref, s16[1,13,32,512]{3,2,1,0:T(8,128)(2,1)} %collective-permute-done.6.got0_ref, s16[1,13,32,512]{3,2,1,0:T(8,128)(2,1)} %collective-permute-done.7.got1_ref), custom_call_target="tpu_custom_call" | custom-call | tf_op jit(solution)/shard_map/finish_occ/pallas_call | solution.py:232
  184.6 7.0 %collective-permute-start.10 = (s16[1,25,32,128]{3,2,1,0:T(8,128)(2,1)S(1)}, s16[1,25,32,128]{3,2,1,0:T(8,128)(2,1)S(1)}, u32[]{:S(2)}, u32[]{:S(2)}) collective-permute-start(s16[1,25,32,128]{3,2,1,0:T(8,128)(2,1)S(1)} %get-tuple-element.29), channel_id=1, source_target_pairs={{0,12},{4,0},{8,4},{12,8},{16,28},{20,16},{24,20},{28,24},{32,44},... | collective-permute-start | bytes 614408 | tf_op jit(solution)/shard_map/ppermute | solution.py:361
  191.6 2.5 collective-permute-start.8
  194.1 5.5 %collective-permute-done.10.three_ref = s16[1,25,32,128]{3,2,1,0:T(8,128)(2,1)S(1)} collective-permute-done((s16[1,25,32,128]{3,2,1,0:T(8,128)(2,1)S(1)}, s16[1,25,32,128]{3,2,1,0:T(8,128)(2,1)S(1)}, u32[]{:S(2)}, u32[]{:S(2)}) %collective-permute-start.10) | collective-permute-done | bytes 204832 | tf_op jit(solution)/shard_map/ppermute | solution.py:361
  199.6 4.3 %collective-permute-done.9.two_ref = s16[1,25,32,128]{3,2,1,0:T(8,128)(2,1)S(1)} collective-permute-done((s16[1,25,32,128]{3,2,1,0:T(8,128)(2,1)S(1)}, s16[1,25,32,128]{3,2,1,0:T(8,128)(2,1)S(1)}, u32[]{:S(2)}, u32[]{:S(2)}) %collective-permute-start.9) | collective-permute-done | bytes 204832 | tf_op jit(solution)/shard_map/ppermute | solution.py:361
  203.9 4.3 %pair.1 = f32[24,24,128]{2,1,0:T(8,128)S(1)} custom-call(s32[1]{0:T(128)} %bitcast.low_ref, s16[4,25,32,128]{3,2,1,0:T(8,128)(2,1)S(1)} %finish_occ.1.own_ref, s16[1,25,32,128]{3,2,1,0:T(8,128)(2,1)S(1)} %collective-permute-done.8.one_ref, s16[1,25,32,128]{3,2,1,0:T(8,128)(2,1)S(1)} %collective-permute-done.9.two_ref, ...), custom_call_target="tpu_custom_call" | custom-call | tf_op jit(solution)/shard_map/pair/pallas_call | solution.py:267
  208.4 1.3 collective-permute-start.16
  209.7 1.1 collective-permute-start.17
  210.8 1.5 collective-permute-start.18
  212.5 1.2 collective-permute-done.17
  213.8 3.4 %collective-permute-start.20 = (f32[24,24]{1,0:T(8,128)S(1)}, f32[24,24]{1,0:T(8,128)S(1)}, u32[]{:S(2)}, u32[]{:S(2)}) collective-permute-start(f32[24,24]{1,0:T(8,128)S(1)} %add_add_fusion.3), channel_id=1, source_target_pairs={{0,4},{4,8},{8,12},{12,0},{16,20},{20,24},{24,28},{28,16},{32,36},... | collective-permute-start | bytes 6920 | tf_op jit(solution)/shard_map/ppermute | solution.py:314
  217.3 0.8 collective-permute-done.20
  218.1 11.9 %collective-permute-done.21 = f32[24,24]{1,0:T(8,128)S(1)} collective-permute-done((f32[24,24]{1,0:T(8,128)S(1)}, f32[24,24]{1,0:T(8,128)S(1)}, u32[]{:S(2)}, u32[]{:S(2)}) %collective-permute-start.21) | collective-permute-done | bytes 2336 | tf_op jit(solution)/shard_map/ppermute | solution.py:314
  230.1 19.5 %collective-permute-start.23 = (f32[24,24]{1,0:T(8,128)S(1)}, f32[24,24]{1,0:T(8,128)S(1)}, u32[]{:S(2)}, u32[]{:S(2)}) collective-permute-start(f32[24,24]{1,0:T(8,128)S(1)} %add_add_fusion.2), channel_id=1, source_target_pairs={{0,64},{64,128},{128,192},{192,0},{1,65},{65,129},{129,193},{193,1... | collective-permute-start | bytes 6920 | tf_op jit(solution)/shard_map/ppermute | solution.py:314
  249.6 0.9 collective-permute-done.23
  250.4 1.7 collective-permute-done.24
  252.1 5.7 %collective-permute-start.25 = (f32[24,24]{1,0:T(8,128)S(1)}, f32[24,24]{1,0:T(8,128)S(1)}, u32[]{:S(2)}, u32[]{:S(2)}) collective-permute-start(f32[24,24]{1,0:T(8,128)S(1)} %add_add_fusion.1), channel_id=1, source_target_pairs={{0,32},{4,36},{8,40},{12,44},{16,48},{20,52},{24,56},{28,60},{32,0... | collective-permute-start | bytes 6920 | tf_op jit(solution)/shard_map/ppermute | solution.py:314
  257.8 3.6 %collective-permute-start.27 = (f32[24,24]{1,0:T(8,128)S(1)}, f32[24,24]{1,0:T(8,128)S(1)}, u32[]{:S(2)}, u32[]{:S(2)}) collective-permute-start(f32[24,24]{1,0:T(8,128)S(1)} %add_add_fusion.1), channel_id=1, source_target_pairs={{0,48},{4,52},{8,56},{12,60},{16,0},{20,4},{24,8},{28,12},{32,16},... | collective-permute-start | bytes 6920 | tf_op jit(solution)/shard_map/ppermute | solution.py:314
  261.4 1.1 collective-permute-done.26
  (44 shorter events, 1.9 us)
Async XLA Ops:
  0.0 1.8 copy-start.2
  1.8 0.7 copy-start.3
  2.5 0.7 copy-start.4
  3.1 0.7 copy-start.5
  3.8 0.7 copy-start.6
  51.2 27.3 %collective-permute-start = (bf16[64,72,128]{2,1,0:T(8,128)(2,1)S(1)}, bf16[64,72,128]{2,1,0:T(8,128)(2,1)S(1)}, u32[]{:S(2)}, u32[]{:S(2)}) collective-permute-start(bf16[64,72,128]{2,1,0:T(8,128)(2,1)S(1)} %all_to_all.5.own_ref), channel_id=1, source_target_pairs={{0,64},{64,128},{128,192},{192,0},{1,65},{65,129},{129,193},{193,1... | collective-permute-start | bytes 3538952 | tf_op jit(solution)/shard_map/ppermute | solution.py:331
  52.5 26.9 %collective-permute-start.1 = (bf16[64,72,128]{2,1,0:T(8,128)(2,1)S(1)}, bf16[64,72,128]{2,1,0:T(8,128)(2,1)S(1)}, u32[]{:S(2)}, u32[]{:S(2)}) collective-permute-start(bf16[64,72,128]{2,1,0:T(8,128)(2,1)S(1)} %all_to_all.5.own_ref), channel_id=1, source_target_pairs={{0,192},{64,0},{128,64},{192,128},{1,193},{65,1},{129,65},{193,129... | collective-permute-start | bytes 3538952 | tf_op jit(solution)/shard_map/ppermute | solution.py:332
  79.3 13.9 %collective-permute-start.2 = (bf16[32,72,128]{2,1,0:T(8,128)(2,1)}, bf16[32,72,128]{2,1,0:T(8,128)(2,1)S(1)}, u32[]{:S(2)}, u32[]{:S(2)}) collective-permute-start(bf16[32,72,128]{2,1,0:T(8,128)(2,1)} %slice.13), channel_id=1, source_target_pairs={{0,64},{64,128},{128,192},{192,0},{1,65},{65,129},{129,193},{193,1... | collective-permute-start | bytes 1769480 | tf_op jit(solution)/shard_map/ppermute | solution.py:334
  79.3 1.0 copy-start.7
  81.2 13.0 %collective-permute-start.3 = (bf16[32,72,128]{2,1,0:T(8,128)(2,1)}, bf16[32,72,128]{2,1,0:T(8,128)(2,1)S(1)}, u32[]{:S(2)}, u32[]{:S(2)}) collective-permute-start(bf16[32,72,128]{2,1,0:T(8,128)(2,1)} %slice.14), channel_id=1, source_target_pairs={{0,192},{64,0},{128,64},{192,128},{1,193},{65,1},{129,65},{193,129... | collective-permute-start | bytes 1769480 | tf_op jit(solution)/shard_map/ppermute | solution.py:335
  117.9 24.2 %collective-permute-start.11 = (s16[2,13,32,512]{3,2,1,0:T(8,128)(2,1)S(1)}, s16[2,13,32,512]{3,2,1,0:T(8,128)(2,1)S(1)}, u32[]{:S(2)}, u32[]{:S(2)}) collective-permute-start(s16[2,13,32,512]{3,2,1,0:T(8,128)(2,1)S(1)} %get-tuple-element.24), channel_id=1, source_target_pairs={{0,1},{1,0},{2,3},{3,2},{4,5},{5,4},{6,7},{7,6},{8,9},{9,8},{10,11... | collective-permute-start | bytes 2555912 | tf_op jit(solution)/shard_map/ppermute | solution.py:342
  118.2 23.9 %collective-permute-start.12 = (s16[2,13,32,512]{3,2,1,0:T(8,128)(2,1)S(1)}, s16[2,13,32,512]{3,2,1,0:T(8,128)(2,1)S(1)}, u32[]{:S(2)}, u32[]{:S(2)}) collective-permute-start(s16[2,13,32,512]{3,2,1,0:T(8,128)(2,1)S(1)} %get-tuple-element.25), channel_id=1, source_target_pairs={{0,3},{3,0},{1,2},{2,1},{4,7},{7,4},{5,6},{6,5},{8,11},{11,8},{9,1... | collective-permute-start | bytes 2555912 | tf_op jit(solution)/shard_map/ppermute | solution.py:343
  120.2 21.8 %copy-start.1 = (f32[2,2,12,32,512]{4,3,2,1,0:T(8,128)S(1)}, f32[2,2,12,32,512]{4,3,2,1,0:T(8,128)}, u32[]{:S(2)}) copy-start(f32[2,2,12,32,512]{4,3,2,1,0:T(8,128)} %get-tuple-element.23.keep_ref) | copy-start | bytes 9437188
  140.9 28.6 %collective-permute-start.4 = (s16[2,13,32,512]{3,2,1,0:T(8,128)(2,1)S(1)}, s16[2,13,32,512]{3,2,1,0:T(8,128)(2,1)S(1)}, u32[]{:S(2)}, u32[]{:S(2)}) collective-permute-start(s16[2,13,32,512]{3,2,1,0:T(8,128)(2,1)S(1)} %get-tuple-element.18), channel_id=1, source_target_pairs={{0,1},{1,0},{2,3},{3,2},{4,5},{5,4},{6,7},{7,6},{8,9},{9,8},{10,11... | collective-permute-start | bytes 2555912 | tf_op jit(solution)/shard_map/ppermute | solution.py:345
  141.1 28.5 %collective-permute-start.5 = (s16[2,13,32,512]{3,2,1,0:T(8,128)(2,1)S(1)}, s16[2,13,32,512]{3,2,1,0:T(8,128)(2,1)S(1)}, u32[]{:S(2)}, u32[]{:S(2)}) collective-permute-start(s16[2,13,32,512]{3,2,1,0:T(8,128)(2,1)S(1)} %get-tuple-element.19), channel_id=1, source_target_pairs={{0,3},{3,0},{1,2},{2,1},{4,7},{7,4},{5,6},{6,5},{8,11},{11,8},{9,1... | collective-permute-start | bytes 2555912 | tf_op jit(solution)/shard_map/ppermute | solution.py:346
  144.7 22.5 %collective-permute-start.13 = (s16[1,13,32,512]{3,2,1,0:T(8,128)(2,1)S(1)}, s16[1,13,32,512]{3,2,1,0:T(8,128)(2,1)S(1)}, u32[]{:S(2)}, u32[]{:S(2)}) collective-permute-start(s16[1,13,32,512]{3,2,1,0:T(8,128)(2,1)S(1)} %get-tuple-element.27), channel_id=1, source_target_pairs={{0,3},{3,0},{1,2},{2,1},{4,7},{7,4},{5,6},{6,5},{8,11},{11,8},{9,1... | collective-permute-start | bytes 1277960 | tf_op jit(solution)/shard_map/ppermute | solution.py:348
  146.5 20.7 %collective-permute-start.14 = (s16[1,13,32,512]{3,2,1,0:T(8,128)(2,1)S(1)}, s16[1,13,32,512]{3,2,1,0:T(8,128)(2,1)S(1)}, u32[]{:S(2)}, u32[]{:S(2)}) collective-permute-start(s16[1,13,32,512]{3,2,1,0:T(8,128)(2,1)S(1)} %get-tuple-element.28), channel_id=1, source_target_pairs={{0,1},{1,0},{2,3},{3,2},{4,5},{5,4},{6,7},{7,6},{8,9},{9,8},{10,11... | collective-permute-start | bytes 1277960 | tf_op jit(solution)/shard_map/ppermute | solution.py:349
  167.2 2.3 copy-start
  168.8 35.1 %collective-permute-start.15 = (s16[1,25,32,512]{3,2,1,0:T(8,128)(2,1)S(1)}, s16[1,25,32,512]{3,2,1,0:T(8,128)(2,1)S(1)}, u32[]{:S(2)}, u32[]{:S(2)}) collective-permute-start(s16[1,25,32,512]{3,2,1,0:T(8,128)(2,1)S(1)} %finish_virt.1), channel_id=1, source_target_pairs={{0,0},{1,1},{2,2},{3,3},{4,4},{5,5},{6,6},{7,7},{8,8},{9,9},{10,10... | collective-permute-start | bytes 2457608 | tf_op jit(solution)/shard_map/ppermute | solution.py:354
  173.0 8.5 %collective-permute-start.6 = (s16[1,13,32,512]{3,2,1,0:T(8,128)(2,1)}, s16[1,13,32,512]{3,2,1,0:T(8,128)(2,1)}, u32[]{:S(2)}, u32[]{:S(2)}) collective-permute-start(s16[1,13,32,512]{3,2,1,0:T(8,128)(2,1)} %get-tuple-element.21), channel_id=1, source_target_pairs={{0,3},{3,0},{1,2},{2,1},{4,7},{7,4},{5,6},{6,5},{8,11},{11,8},{9,1... | collective-permute-start | bytes 1277960 | tf_op jit(solution)/shard_map/ppermute | solution.py:351
  174.2 7.3 %collective-permute-start.7 = (s16[1,13,32,512]{3,2,1,0:T(8,128)(2,1)}, s16[1,13,32,512]{3,2,1,0:T(8,128)(2,1)}, u32[]{:S(2)}, u32[]{:S(2)}) collective-permute-start(s16[1,13,32,512]{3,2,1,0:T(8,128)(2,1)} %get-tuple-element.22), channel_id=1, source_target_pairs={{0,1},{1,0},{2,3},{3,2},{4,5},{5,4},{6,7},{7,6},{8,9},{9,8},{10,11... | collective-permute-start | bytes 1277960 | tf_op jit(solution)/shard_map/ppermute | solution.py:352
  184.6 15.0 %collective-permute-start.10 = (s16[1,25,32,128]{3,2,1,0:T(8,128)(2,1)S(1)}, s16[1,25,32,128]{3,2,1,0:T(8,128)(2,1)S(1)}, u32[]{:S(2)}, u32[]{:S(2)}) collective-permute-start(s16[1,25,32,128]{3,2,1,0:T(8,128)(2,1)S(1)} %get-tuple-element.29), channel_id=1, source_target_pairs={{0,12},{4,0},{8,4},{12,8},{16,28},{20,16},{24,20},{28,24},{32,44},... | collective-permute-start | bytes 614408 | tf_op jit(solution)/shard_map/ppermute | solution.py:361
  191.6 8.0 %collective-permute-start.8 = (s16[1,25,32,128]{3,2,1,0:T(8,128)(2,1)S(1)}, s16[1,25,32,128]{3,2,1,0:T(8,128)(2,1)S(1)}, u32[]{:S(2)}, u32[]{:S(2)}) collective-permute-start(s16[1,25,32,128]{3,2,1,0:T(8,128)(2,1)S(1)} %get-tuple-element.31), channel_id=1, source_target_pairs={{0,4},{4,8},{8,12},{12,0},{16,20},{20,24},{24,28},{28,16},{32,36},... | collective-permute-start | bytes 614408 | tf_op jit(solution)/shard_map/ppermute | solution.py:361
  194.0 9.9 %collective-permute-start.9 = (s16[1,25,32,128]{3,2,1,0:T(8,128)(2,1)S(1)}, s16[1,25,32,128]{3,2,1,0:T(8,128)(2,1)S(1)}, u32[]{:S(2)}, u32[]{:S(2)}) collective-permute-start(s16[1,25,32,128]{3,2,1,0:T(8,128)(2,1)S(1)} %get-tuple-element.30), channel_id=1, source_target_pairs={{0,8},{4,12},{8,0},{12,4},{16,24},{20,28},{24,16},{28,20},{32,40},... | collective-permute-start | bytes 614408 | tf_op jit(solution)/shard_map/ppermute | solution.py:361
  208.4 4.1 %collective-permute-start.16 = (f32[24,24]{1,0:T(8,128)S(1)}, f32[24,24]{1,0:T(8,128)S(1)}, u32[]{:S(2)}, u32[]{:S(2)}) collective-permute-start(f32[24,24]{1,0:T(8,128)S(1)} %reduce_sum.9), channel_id=1, source_target_pairs={{0,2},{1,3},{2,0},{3,1},{4,6},{5,7},{6,4},{7,5},{8,10},{9,11},{10,... | collective-permute-start | bytes 6920 | tf_op jit(solution)/shard_map/ppermute | solution.py:314
  209.7 4.1 %collective-permute-start.17 = (f32[24,24]{1,0:T(8,128)S(1)}, f32[24,24]{1,0:T(8,128)S(1)}, u32[]{:S(2)}, u32[]{:S(2)}) collective-permute-start(f32[24,24]{1,0:T(8,128)S(1)} %reduce_sum.9), channel_id=1, source_target_pairs={{0,1},{1,2},{2,3},{3,0},{4,5},{5,6},{6,7},{7,4},{8,9},{9,10},{10,1... | collective-permute-start | bytes 6920 | tf_op jit(solution)/shard_map/ppermute | solution.py:314
  210.8 2.9 %collective-permute-start.18 = (f32[24,24]{1,0:T(8,128)S(1)}, f32[24,24]{1,0:T(8,128)S(1)}, u32[]{:S(2)}, u32[]{:S(2)}) collective-permute-start(f32[24,24]{1,0:T(8,128)S(1)} %reduce_sum.9), channel_id=1, source_target_pairs={{0,3},{1,0},{2,1},{3,2},{4,7},{5,4},{6,5},{7,6},{8,11},{9,8},{10,9... | collective-permute-start | bytes 6920 | tf_op jit(solution)/shard_map/ppermute | solution.py:314
  213.7 3.6 %collective-permute-start.19 = (f32[24,24]{1,0:T(8,128)S(1)}, f32[24,24]{1,0:T(8,128)S(1)}, u32[]{:S(2)}, u32[]{:S(2)}) collective-permute-start(f32[24,24]{1,0:T(8,128)S(1)} %add_add_fusion.3), channel_id=1, source_target_pairs={{0,8},{4,12},{8,0},{12,4},{16,24},{20,28},{24,16},{28,20},{32,40},... | collective-permute-start | bytes 6920 | tf_op jit(solution)/shard_map/ppermute | solution.py:314
  213.8 4.3 %collective-permute-start.20 = (f32[24,24]{1,0:T(8,128)S(1)}, f32[24,24]{1,0:T(8,128)S(1)}, u32[]{:S(2)}, u32[]{:S(2)}) collective-permute-start(f32[24,24]{1,0:T(8,128)S(1)} %add_add_fusion.3), channel_id=1, source_target_pairs={{0,4},{4,8},{8,12},{12,0},{16,20},{20,24},{24,28},{28,16},{32,36},... | collective-permute-start | bytes 6920 | tf_op jit(solution)/shard_map/ppermute | solution.py:314
  217.3 12.8 %collective-permute-start.21 = (f32[24,24]{1,0:T(8,128)S(1)}, f32[24,24]{1,0:T(8,128)S(1)}, u32[]{:S(2)}, u32[]{:S(2)}) collective-permute-start(f32[24,24]{1,0:T(8,128)S(1)} %add_add_fusion.3), channel_id=1, source_target_pairs={{0,12},{4,0},{8,4},{12,8},{16,28},{20,16},{24,20},{28,24},{32,44},... | collective-permute-start | bytes 6920 | tf_op jit(solution)/shard_map/ppermute | solution.py:314
  230.1 19.5 %collective-permute-start.22 = (f32[24,24]{1,0:T(8,128)S(1)}, f32[24,24]{1,0:T(8,128)S(1)}, u32[]{:S(2)}, u32[]{:S(2)}) collective-permute-start(f32[24,24]{1,0:T(8,128)S(1)} %add_add_fusion.2), channel_id=1, source_target_pairs={{0,128},{64,192},{128,0},{192,64},{1,129},{65,193},{129,1},{193,65... | collective-permute-start | bytes 6920 | tf_op jit(solution)/shard_map/ppermute | solution.py:314
  230.1 20.4 %collective-permute-start.23 = (f32[24,24]{1,0:T(8,128)S(1)}, f32[24,24]{1,0:T(8,128)S(1)}, u32[]{:S(2)}, u32[]{:S(2)}) collective-permute-start(f32[24,24]{1,0:T(8,128)S(1)} %add_add_fusion.2), channel_id=1, source_target_pairs={{0,64},{64,128},{128,192},{192,0},{1,65},{65,129},{129,193},{193,1... | collective-permute-start | bytes 6920 | tf_op jit(solution)/shard_map/ppermute | solution.py:314
  249.6 2.5 collective-permute-start.24
  252.1 9.3 %collective-permute-start.25 = (f32[24,24]{1,0:T(8,128)S(1)}, f32[24,24]{1,0:T(8,128)S(1)}, u32[]{:S(2)}, u32[]{:S(2)}) collective-permute-start(f32[24,24]{1,0:T(8,128)S(1)} %add_add_fusion.1), channel_id=1, source_target_pairs={{0,32},{4,36},{8,40},{12,44},{16,48},{20,52},{24,56},{28,60},{32,0... | collective-permute-start | bytes 6920 | tf_op jit(solution)/shard_map/ppermute | solution.py:314
  257.8 4.7 %collective-permute-start.26 = (f32[24,24]{1,0:T(8,128)S(1)}, f32[24,24]{1,0:T(8,128)S(1)}, u32[]{:S(2)}, u32[]{:S(2)}) collective-permute-start(f32[24,24]{1,0:T(8,128)S(1)} %add_add_fusion.1), channel_id=1, source_target_pairs={{0,16},{4,20},{8,24},{12,28},{16,32},{20,36},{24,40},{28,44},{32,4... | collective-permute-start | bytes 6920 | tf_op jit(solution)/shard_map/ppermute | solution.py:314
  257.8 4.7 %collective-permute-start.27 = (f32[24,24]{1,0:T(8,128)S(1)}, f32[24,24]{1,0:T(8,128)S(1)}, u32[]{:S(2)}, u32[]{:S(2)}) collective-permute-start(f32[24,24]{1,0:T(8,128)S(1)} %add_add_fusion.1), channel_id=1, source_target_pairs={{0,48},{4,52},{8,56},{12,60},{16,0},{20,4},{24,8},{28,12},{32,16},... | collective-permute-start | bytes 6920 | tf_op jit(solution)/shard_map/ppermute | solution.py:314

commit v2 on v1

v2 whole, which is shorter than its diff:
```python
import functools

import jax
import jax.numpy as jnp
from jax import lax
from jax.experimental import pallas as pl
from jax.experimental.pallas import tpu as pltpu
from jax.sharding import PartitionSpec as P

NP = 24
ROWS = 4
COLS = 16
LAYERS = 4
CAP = 2
OWNERS = COLS * LAYERS
BS = 128
QUARTER = BS // ROWS
WIDE = 512
HALF = NP // 2
TOP = 32700.0
STEPS = 64.0
ALL = ("row", "col", "layer")
F32 = jnp.float32
BF16 = jnp.bfloat16
S16 = jnp.int16


def params(mib):
    return pltpu.CompilerParams(vmem_limit_bytes=mib * 2**20)


def encode(block):
    peak = jnp.max(jnp.abs(block), axis=0, keepdims=True)
    level = jnp.ceil(jnp.log2(jnp.maximum(peak, 1e-30)) * STEPS)
    scaled = block * (jnp.exp2(level * (-1.0 / STEPS)) * TOP)
    return jnp.round(scaled).astype(jnp.int32).astype(S16), level


def decode(codes, level):
    return codes.astype(jnp.int32).astype(F32) * (jnp.exp2(level * (1.0 / STEPS)) * (1.0 / TOP))


class Plan:
    def __init__(self, quarters):
        self.quarters = quarters
        self.group = 4 // quarters
        self.rows = 8 * quarters * self.group
        self.blocks = HALF // self.group

    def coded(self, count):
        return count * self.rows + (count + 15) // 16 * 16


def at_block(plan, index):
    return pl.ds(pl.multiple_of(index * plan.rows, 16), plan.rows)


def level_rows(plan, count):
    return slice(count * plan.rows, plan.coded(count))


def put(ref, lead, plan, count, index, block):
    codes, level = encode(block)
    put_coded(ref, lead, plan, count, index, codes, level)


def put_coded(ref, lead, plan, count, index, codes, level):
    ref[(*lead, at_block(plan, index), slice(None))] = codes
    where = (*lead, level_rows(plan, count), slice(None))
    old = ref[where].astype(jnp.int32)
    here = lax.broadcasted_iota(jnp.int32, old.shape, 0) == index
    ref[where] = jnp.where(here, level.astype(jnp.int32), old).astype(S16)


def get(ref, lead, plan, count, index):
    codes = ref[(*lead, at_block(plan, index), slice(None))]
    rows = ref[(*lead, level_rows(plan, count), slice(None))].astype(jnp.int32)
    here = lax.broadcasted_iota(jnp.int32, rows.shape, 0) == index
    level = jnp.sum(jnp.where(here, rows, 0), axis=0, keepdims=True)
    return decode(codes, level.astype(F32))


def send_body(aux_ref, row_ref, col_ref, ext_ref, place_ref, blocks_ref, *rest, layer_blocks):
    del place_ref
    out_refs, count_ref = rest[:CAP], rest[CAP]
    for ref in out_refs:
        ref[...] = jnp.zeros(ref.shape, BF16)

    @pl.loop(0, OWNERS)
    def _(i):
        count_ref[i] = 0

    lane = lax.broadcasted_iota(jnp.int32, (QUARTER, BS), 1)
    meta_lane = lax.broadcasted_iota(jnp.int32, (8, BS), 1)

    @pl.loop(0, blocks_ref.shape[0])
    def _(i):
        col = col_ref[i]
        layer_of = col // layer_blocks
        kept = col - layer_of * layer_blocks
        owner = (row_ref[i] % 4 * 4 + row_ref[i] // 4) * LAYERS + layer_of
        used = count_ref[owner]
        count_ref[owner] = used + 1
        tile = jnp.where(lane < ext_ref[i], blocks_ref[i].astype(F32), 0.0).astype(BF16)
        meta = jnp.where(meta_lane == 0, aux_ref[i], jnp.where(meta_lane == 1, kept, 0)).astype(F32).astype(BF16)
        for slot, ref in enumerate(out_refs):

            @pl.when(used == slot)
            def _():
                ref[owner, :QUARTER, :] = tile
                ref[owner, QUARTER:, :] = meta


def build_send(blocks, block_aux, block_row, block_col, extents, row_place, layer_blocks):
    held = blocks.shape[0]
    shape = (OWNERS, QUARTER + 8, BS)
    return pl.pallas_call(
        functools.partial(send_body, layer_blocks=layer_blocks),
        grid_spec=pltpu.PrefetchScalarGridSpec(
            num_scalar_prefetch=5,
            grid=(1,),
            in_specs=[pl.BlockSpec((held, QUARTER, BS), lambda i, a, r, c, e, p: (0, p[0], 0))],
            out_specs=[pl.BlockSpec(shape, lambda i, a, r, c, e, p: (0, 0, 0))] * CAP,
            scratch_shapes=[pltpu.SMEM((OWNERS,), jnp.int32)],
        ),
        out_shape=[jax.ShapeDtypeStruct(shape, BF16)] * CAP,
        compiler_params=params(16),
        name="build_send",
    )(block_aux, block_row, block_col, extents, row_place, blocks)


def split_pieces(place_ref, plan, rows_of, keep_ref, send_refs):
    bit_a = place_ref[1]
    bit_b = place_ref[2]

    def piece(a, b):
        return jnp.where(b == 0, a, 3 - a)

    for h, send_ref in enumerate(send_refs):
        kept = [piece(bit_a, o) if h == 0 else piece(o, bit_b) for o in range(2)]
        sent = [piece(1 - bit_a, o) if h == 0 else piece(o, 1 - bit_b) for o in range(2)]

        @pl.loop(0, plan.blocks)
        def _(block):
            first = h * HALF + block * plan.group
            for other in range(2):
                keep_ref[h, other, block] = rows_of(first, kept[other])
                put(send_ref, (), plan, 2 * plan.blocks, other * plan.blocks + block, rows_of(first, sent[other]))


def virt_body(meta0_ref, meta1_ref, place_ref, *rest, plan, names):
    per_slot = len(names)
    tile_refs = [rest[:per_slot], rest[per_slot : 2 * per_slot]]
    green_ref, keep_ref, send0_ref, send1_ref, acc_ref = rest[2 * per_slot :]
    acc_ref[...] = jnp.zeros(acc_ref.shape, F32)
    half = OWNERS // 2

    for part in range(2):

        @pl.loop(0, half)
        def _(local):
            source = local + part * half
            for slot, meta_ref in enumerate((meta0_ref, meta1_ref)):
                refs = tile_refs[slot]
                parts = [ref[source, :QUARTER, :] for ref in refs[:3]] + [refs[3 + part][local, :QUARTER, :]]
                tile = jnp.concatenate(parts, axis=0)
                aux = meta_ref[source, 0]
                kept = meta_ref[source, 1]
                acc_ref[aux] += jnp.dot(tile, green_ref[kept], preferred_element_type=F32)

    def rows_of(first, piece):
        parts = []
        for j in range(plan.group):
            for quarter in range(plan.quarters):
                at = pl.multiple_of(quarter * QUARTER + piece * 8, 8)
                parts.append(acc_ref[first + j, pl.ds(at, 8), :])
        return jnp.concatenate(parts, axis=0)

    split_pieces(place_ref, plan, rows_of, keep_ref, (send0_ref, send1_ref))


def step_shapes(plan):
    return [
        jax.ShapeDtypeStruct((2, 2, plan.blocks, plan.rows, WIDE), F32),
        jax.ShapeDtypeStruct((plan.coded(2 * plan.blocks), WIDE), S16),
        jax.ShapeDtypeStruct((plan.coded(2 * plan.blocks), WIDE), S16),
    ]


VMEM = pl.BlockSpec(memory_space=pltpu.VMEM)
SMEM = pl.BlockSpec(memory_space=pltpu.SMEM)


def contract_virt(metas, place, slots, names, green, plan, name):
    tiles = [slot[n] for slot in slots for n in names]
    return pl.pallas_call(
        functools.partial(virt_body, plan=plan, names=names),
        in_specs=[SMEM] * 3 + [VMEM] * (len(tiles) + 1),
        out_specs=[VMEM] * 3,
        out_shape=step_shapes(plan),
        scratch_shapes=[pltpu.VMEM((NP, plan.quarters * QUARTER, WIDE), F32)],
        compiler_params=params(48),
        name=name,
    )(*metas, place, *tiles, green)


def occ_slot(meta_ref, place_ref, tile_refs, green_ref, acc_ref, tile_ref):
    own_ref, prev_ref, next_ref, far_a_ref, far_b_ref = tile_refs
    row_place = place_ref[0]
    at = [pl.multiple_of(((row_place + d) % ROWS) * QUARTER, QUARTER) for d in (0, ROWS - 1, 1, 2)]
    half = OWNERS // 2
    for part, far_ref in enumerate((far_a_ref, far_b_ref)):

        @pl.loop(0, half // 2)
        def _(step):
            for k in range(2):
                local = step * 2 + k
                source = local + part * half
                tile_ref[k, pl.ds(at[0], QUARTER), :] = own_ref[source, :QUARTER, :]
                tile_ref[k, pl.ds(at[1], QUARTER), :] = prev_ref[source, :QUARTER, :]
                tile_ref[k, pl.ds(at[2], QUARTER), :] = next_ref[source, :QUARTER, :]
                tile_ref[k, pl.ds(at[3], QUARTER), :] = far_ref[local, :QUARTER, :]
            for k in range(2):
                source = step * 2 + k + part * half
                aux = meta_ref[source, 0]
                kept = meta_ref[source, 1]
                term = lax.dot_general(
                    green_ref[kept], tile_ref[k], (((1,), (1,)), ((), ())), preferred_element_type=F32
                )
                for low in range(4):
                    lanes = slice(low * BS, (low + 1) * BS)
                    acc_ref[aux, :, lanes] += term[low * BS : (low + 1) * BS, :]


def occ_first_body(meta_ref, place_ref, *rest):
    tile_refs, (green_ref, out_ref, tile_ref) = rest[:5], rest[5:]
    out_ref[...] = jnp.zeros(out_ref.shape, F32)
    occ_slot(meta_ref, place_ref, tile_refs, green_ref, out_ref, tile_ref)


def occ_last_body(meta_ref, place_ref, *rest, plan):
    tile_refs, (green_ref, before_ref, keep_ref, send0_ref, send1_ref, acc_ref, tile_ref, sem) = rest[:5], rest[5:]
    load = pltpu.make_async_copy(before_ref, acc_ref, sem)
    load.start()
    load.wait()
    occ_slot(meta_ref, place_ref, tile_refs, green_ref, acc_ref, tile_ref)

    def rows_of(first, piece):
        parts = []
        for quarter in range(4):
            at = pl.multiple_of(quarter * QUARTER + piece * 8, 8)
            parts.append(acc_ref[first, pl.ds(at, 8), :])
        return jnp.concatenate(parts, axis=0)

    split_pieces(place_ref, plan, rows_of, keep_ref, (send0_ref, send1_ref))


ALL_QUARTERS = ("own", "prev", "next", "far_a", "far_b")
ACC = (NP, BS, WIDE)


def contract_occ_first(meta, place, slot, green):
    return pl.pallas_call(
        occ_first_body,
        in_specs=[SMEM] * 2 + [VMEM] * 6,
        out_specs=VMEM,
        out_shape=jax.ShapeDtypeStruct(ACC, F32),
        scratch_shapes=[pltpu.VMEM((2, BS, BS), BF16)],
        compiler_params=params(40),
        name="occ_first",
    )(meta, place, *[slot[n] for n in ALL_QUARTERS], green)


def contract_occ_last(meta, place, slot, green, before, plan):
    return pl.pallas_call(
        functools.partial(occ_last_body, plan=plan),
        in_specs=[SMEM] * 2 + [VMEM] * 6 + [pl.BlockSpec(memory_space=pl.ANY)],
        out_specs=[VMEM] * 3,
        out_shape=step_shapes(plan),
        scratch_shapes=[pltpu.VMEM(ACC, F32), pltpu.VMEM((2, BS, BS), BF16), pltpu.SemaphoreType.DMA(())],
        compiler_params=params(48),
        name="occ_last",
    )(meta, place, *[slot[n] for n in ALL_QUARTERS], green, before)


def halve_body(place_ref, keep_ref, got0_ref, got1_ref, left_ref, send0_ref, send1_ref, *, plan):
    for h, got_ref, send_ref in ((0, got0_ref, send0_ref), (1, got1_ref, send1_ref)):
        mine = place_ref[2 - h]
        away = 1 - mine

        @pl.loop(0, plan.blocks)
        def _(b):
            left_ref[h, b] = keep_ref[h, mine, b] + get(got_ref, (), plan, 2 * plan.blocks, mine * plan.blocks + b)
            total = keep_ref[h, away, b] + get(got_ref, (), plan, 2 * plan.blocks, away * plan.blocks + b)
            put(send_ref, (), plan, plan.blocks, b, total)


def halve(place, keep, got0, got1, plan, name):
    code = jax.ShapeDtypeStruct((plan.coded(plan.blocks), WIDE), S16)
    return pl.pallas_call(
        functools.partial(halve_body, plan=plan),
        in_specs=[SMEM] + [VMEM] * 3,
        out_specs=[VMEM] * 3,
        out_shape=[jax.ShapeDtypeStruct((2, plan.blocks, plan.rows, WIDE), F32), code, code],
        compiler_params=params(40),
        name=name,
    )(place, keep, got0, got1)


def finish_body(left_ref, got0_ref, got1_ref, out_ref, *, plan, split):
    count = 2 * plan.blocks
    for h, got_ref in ((0, got0_ref), (1, got1_ref)):

        @pl.loop(0, plan.blocks)
        def _(b):
            total = left_ref[h, b] + get(got_ref, (), plan, plan.blocks, b)
            index = h * plan.blocks + b
            if split:
                codes, level = encode(total)
                for low in range(4):
                    lanes = slice(low * BS, (low + 1) * BS)
                    put_coded(out_ref, (low,), plan, count, index, codes[:, lanes], level[:, lanes])
            else:
                put(out_ref, (), plan, count, index, total)


def finish(left, got0, got1, plan, split, name):
    rows = plan.coded(2 * plan.blocks)
    shape = (4, rows, BS) if split else (rows, WIDE)
    return pl.pallas_call(
        functools.partial(finish_body, plan=plan, split=split),
        in_specs=[VMEM] * 3,
        out_specs=VMEM,
        out_shape=jax.ShapeDtypeStruct(shape, S16),
        compiler_params=params(32),
        name=name,
    )(left, got0, got1)


def pair_body(place_ref, own_ref, one_ref, two_ref, three_ref, *rest, plans, shifts, occ_plan):
    virt_refs, (out_ref, occ_ref, vir_ref) = rest[: len(plans)], rest[len(plans) :]
    here = place_ref[0]
    high = place_ref[1]

    for ref, plan, shift in zip(virt_refs, plans, shifts):
        at = [((high + s) % 4) * 8 for s in shift]

        @pl.loop(0, 2 * plan.blocks)
        def _(b):
            values = get(ref, (), plan, 2 * plan.blocks, b)
            for j in range(plan.group):
                for k in range(plan.quarters):
                    rows = slice((j * plan.quarters + k) * 8, (j * plan.quarters + k + 1) * 8)
                    for low in range(4):
                        to = pl.ds(pl.multiple_of(low * QUARTER + at[k], 8), 8)
                        vir_ref[b * plan.group + j, to, :] = values[rows, low * BS : (low + 1) * BS]

    @pl.loop(0, NP)
    def _(p):
        own = get(own_ref, (here,), occ_plan, NP, p)
        occ_ref[p, pl.ds(pl.multiple_of(here * QUARTER, QUARTER), QUARTER), :] = own
        for d, ref in ((1, one_ref), (2, two_ref), (3, three_ref)):
            source = (here + 4 - d) % 4
            part = get(ref, (0,), occ_plan, NP, p)
            occ_ref[p, pl.ds(pl.multiple_of(source * QUARTER, QUARTER), QUARTER), :] = part

    @pl.loop(0, NP)
    def _(p):
        occ = occ_ref[p]
        for q in range(NP):
            out_ref[p, q : q + 1, :] = jnp.sum(occ * vir_ref[q], axis=0, keepdims=True)


def pair(place, own, others, virts, plans, shifts, occ_plan):
    return pl.pallas_call(
        functools.partial(pair_body, plans=plans, shifts=shifts, occ_plan=occ_plan),
        in_specs=[SMEM] + [VMEM] * (4 + len(virts)),
        out_specs=VMEM,
        out_shape=jax.ShapeDtypeStruct((NP, NP, BS), F32),
        scratch_shapes=[pltpu.VMEM((NP, BS, BS), F32), pltpu.VMEM((NP, BS, BS), F32)],
        compiler_params=params(32),
        name="pair",
    )(place, own, *others, *virts)


def rotate(size, step):
    return [(i, (i + step) % size) for i in range(size)]


def rotate_low(step):
    return [(c, c - c % 4 + (c + step) % 4) for c in range(COLS)]


def rotate_high(step):
    return [(c, (c + 4 * step) % COLS) for c in range(COLS)]


PAIRS_A = [(0, 1), (1, 0), (2, 3), (3, 2)]
PAIRS_B = [(0, 3), (3, 0), (1, 2), (2, 1)]


def index_of(row, col, layer):
    return (row * COLS + col) * LAYERS + layer


SWAP = [
    (index_of(r, c, l), index_of(c % 4, c // 4 * 4 + r, l))
    for r in range(ROWS)
    for c in range(COLS)
    for l in range(LAYERS)
]


def tree_sum(values):
    rounds = (
        ("layer", [rotate(LAYERS, d) for d in (1, 2, 3)]),
        ("col", [rotate_low(d) for d in (1, 2, 3)]),
        ("row", [rotate(ROWS, d) for d in (1, 2, 3)]),
        ("col", [rotate_high(d) for d in (1, 2, 3)]),
    )
    for axis, perms in rounds:
        one, two, three = [lax.ppermute(values, axis, perm) for perm in perms]
        values = (values + two) + (one + three)
    return values


def gather_rows(own):
    prev = lax.ppermute(own, "row", rotate(ROWS, 1))
    nxt = lax.ppermute(own, "row", rotate(ROWS, -1))
    half = OWNERS // 2
    far_a = lax.ppermute(prev[:half], "row", rotate(ROWS, 1))
    far_b = lax.ppermute(nxt[half:], "row", rotate(ROWS, -1))
    return {"own": own, "prev": prev, "next": nxt, "far_a": far_a, "far_b": far_b}


def layer_swap(send0, send1, perms):
    return lax.ppermute(send0, "layer", perms[0]), lax.ppermute(send1, "layer", perms[1])


FIRST = (PAIRS_A, PAIRS_B)
SECOND = (PAIRS_B, PAIRS_A)


def after(*values):
    return lax.optimization_barrier(values)


def on_device(blocks, block_aux, block_row, block_col, extents, occ_green, virt_green):
    layer_blocks = occ_green.shape[0] // BS
    row_place = lax.axis_index("row").astype(jnp.int32)
    col_place = lax.axis_index("col").astype(jnp.int32)
    layer_place = lax.axis_index("layer").astype(jnp.int32)
    bit_a = ((layer_place == 1) | (layer_place == 2)).astype(jnp.int32)
    bit_b = layer_place // 2
    place = jnp.stack([row_place, bit_a, bit_b])

    full = Plan(4)
    send0, send1 = build_send(blocks, block_aux, block_row, block_col, extents, row_place[None], layer_blocks)
    own0 = lax.all_to_all(send0, ("col", "layer"), 0, 0, tiled=True)
    own0, send1 = after(own0, send1)
    own1 = lax.all_to_all(send1, ("col", "layer"), 0, 0, tiled=True)
    virt_blocks = virt_green.reshape(layer_blocks, BS, WIDE)
    occ_blocks = occ_green.reshape(layer_blocks, BS, WIDE).transpose(0, 2, 1)
    slot0 = gather_rows(own0)
    own1, occ_blocks, slot0["far_a"], slot0["far_b"] = after(own1, occ_blocks, slot0["far_a"], slot0["far_b"])
    slot1 = gather_rows(own1)
    meta0, meta1 = [own[:, QUARTER, :2].astype(jnp.int32) for own in (own0, own1)]
    metas, slots = (meta0, meta1), (slot0, slot1)

    o_acc = contract_occ_first(meta0, place, slot0, occ_blocks)
    o_acc, virt_blocks = after(o_acc, virt_blocks)
    v_keep, v0, v1 = contract_virt(metas, place, slots, ALL_QUARTERS, virt_blocks, full, "contract_virt")
    v_got = layer_swap(v0, v1, FIRST)
    o_acc, v_keep = after(o_acc, v_keep)
    o_keep, o0, o1 = contract_occ_last(meta1, place, slot1, occ_blocks, o_acc, full)
    v_keep, o_keep = after(v_keep, o_keep)
    v_left, v0, v1 = halve(place, v_keep, *v_got, full, "halve_virt")
    v_got = layer_swap(v0, v1, SECOND)
    o0, o1, *v_got = after(o0, o1, *v_got)
    o_got = layer_swap(o0, o1, FIRST)
    virt = finish(v_left, *v_got, full, False, "finish_virt")
    virt, o_keep = after(virt, o_keep)
    virt = lax.ppermute(virt, ALL, SWAP)
    o_left, o0, o1 = halve(place, o_keep, *o_got, full, "halve_occ")
    o_got = layer_swap(o0, o1, SECOND)
    occ = finish(o_left, *o_got, full, True, "finish_occ")

    low = col_place // 4
    others = []
    for d in (1, 2, 3):
        part = lax.dynamic_slice_in_dim(occ, (low + d) % 4, 1, 0)
        others.append(lax.ppermute(part, "col", rotate_high(d)))
    here = jnp.stack([low, col_place % 4])
    partial = pair(here, occ, others, [virt], (full,), ((0, 3, 1, 2),), full)
    return tree_sum(jnp.sum(partial, axis=-1))


def solution(mesh):
    in_specs = (
        P(("col", "layer"), None, None),
        P(("col", "layer")),
        P(("col", "layer")),
        P(("col", "layer")),
        P(("col", "layer")),
        P("layer", "row"),
        P("layer", "row"),
    )
    return jax.shard_map(on_device, mesh=mesh, in_specs=in_specs, out_specs=P(), check_vma=False)
```

time: 265 us -> 260 us (0.981)
  local copies, waits for them, and re-layouts: 15.2 us -> 27 us
  waiting for transfers between devices: 82.4 us -> 71.5 us
  blocking collectives: 43.4 us -> 32.5 us
  Pallas kernels: 62.6 us -> 68.6 us
    ppermute x12, starting transfers between devices: 36.3 us -> 18.1 us  [tree_sum(): one, two, three = [lax.ppermute(values, axis, perm) for perm in perms]]
    ppermute x12, waiting for transfers between devices: 17.8 us -> 6.68 us  [tree_sum(): one, two, three = [lax.ppermute(values, axis, perm) for perm in perms]]
    unnamed x16 -> x38, local copies, waits for them, and re-layouts: 5.47 us -> 16.5 us
    all_to_all x1, blocking collectives: 43.4 us -> 32.5 us  [on_device(): own0 = lax.all_to_all(send0, ('col', 'layer'), 0, 0, tiled=True)]
    all_to_all x0 -> x1, starting transfers between devices: none -> 6.26 us  [on_device(): own1 = lax.all_to_all(send1, ('col', 'layer'), 0, 0, tiled=True)]
    ppermute x1, starting transfers between devices: 0.71 us -> 6.96 us  [on_device(): virt = lax.ppermute(virt, ALL, SWAP)]
    ppermute x15 -> x19, starting transfers between devices: 21.5 us -> 27.1 us  [the longest x3 8.9 us: on_device(): others.append(lax.ppermute(part, 'col', rotate_high(d)))]
    pallas_call x7 -> x8, Pallas kernels: 59.3 us -> 63.6 us  [the longest x1 20.8 us: contract_virt(): pl.pallas_call(functools.partial(virt_body, plan=plan, names=names), in_s...]
  transfers between devices with their start and end apart: 28 -> 33, of which waited for: 14 -> 15; matrix products, arithmetic and copies ran while one was open for 4% -> 4% of each run, Pallas kernels for 12% -> 13%
where the time goes in v2:
time: 260 us; the launch traced here: 259 us
  waiting for transfers between devices  71.5 us (28%)
  Pallas kernels  68.6 us (26%)
  starting transfers between devices  58.5 us (22%)
  blocking collectives  32.5 us (12%)
  local copies, waits for them, and re-layouts  27 us (10%)
    all_to_all x1, blocking collectives, on_device(): own0 = lax.all_to_all(send0, ('col', 'layer'), 0, 0, tiled=True)  32.5 us
    ppermute x2, waiting for transfers between devices, gather_rows(): prev = lax.ppermute(own, 'row', rotate(ROWS, 1))  27.3 us
    ppermute x4, waiting for transfers between devices, layer_swap(): lax.ppermute(send0, 'layer', perms[0])  21.2 us
    pallas_call x1, Pallas kernels, contract_virt(): pl.pallas_call(functools.partial(virt_body, plan=plan, names=names), in_s...  20.8 us
    ppermute x12, starting transfers between devices, tree_sum(): one, two, three = [lax.ppermute(values, axis, perm) for perm in perms]  18.1 us
    pallas_call x1, Pallas kernels, contract_occ_last(): pl.pallas_call(functools.partial(occ_last_body, plan=plan), in_specs=[SME...  17.7 us
    unnamed x38, local copies, waits for them, and re-layouts  16.5 us
    ppermute x3, waiting for transfers between devices, on_device(): others.append(lax.ppermute(part, 'col', rotate_high(d)))  16.3 us
  transfers between devices with their start and end apart: 33, of which 15 were waited for; matrix products, arithmetic and copies ran while one was open for 4% of the time, Pallas kernels for 13%

profile of v2, /device:TPU:1, one launch (start us, length us, event | category | flops | bytes accessed | tf_op | source)
XLA Modules:
  0.0 259.2 jit_solution(14682003525456361394)
XLA Ops:
  0.0 1.8 copy-done.4
  4.4 5.0 %build_send.1 = (bf16[64,40,128]{2,1,0:T(8,128)(2,1)S(1)}, bf16[64,40,128]{2,1,0:T(8,128)(2,1)}) custom-call(s32[88]{0:T(128)S(1)} %copy-done.15, s32[88]{0:T(128)S(1)} %copy-done.16, s32[88]{0:T(128)S(1)} %copy-done.17, s32[88]{0:T(128)S(1)} %copy-done.18, s32[1]{0:T(128)} %bitcast.2.place_ref, bf16[88,128,128]{2,1,0:T(8,128)(2,1)S(1)} %copy-done.4), custom_call_target="tpu_custom_call" | custom-call | tf_op jit(solution)/shard_map/build_send/pallas_call | solution.py:117
  9.4 32.5 %all_to_all.10.rest_0_ = bf16[64,40,128]{2,1,0:T(8,128)(2,1)S(1)} all-to-all(bf16[64,40,128]{2,1,0:T(8,128)(2,1)S(1)} %get-tuple-element.37), channel_id=1, replica_groups=mesh['row'=4,'col'=16,'layer'=4] {'col','layer'}, dimensions={0} | all-to-all | bytes 1310720 | tf_op jit(solution)/shard_map/all_to_all | solution.py:459
  41.9 6.3 %all-to-all-start.1 = ((bf16[64,40,128]{2,1,0:T(8,128)(2,1)}), bf16[64,40,128]{2,1,0:T(8,128)(2,1)S(1)}, u32[]{:S(2)}, u32[]{:S(2)}) async-start(bf16[64,40,128]{2,1,0:T(8,128)(2,1)} %get-tuple-element.40), calls=%async_computation.1 | async-start | bytes 1310720 | tf_op jit(solution)/shard_map/all_to_all | solution.py:461
  48.1 1.4 collective-permute-start
  49.5 1.5 collective-permute-start.1
  51.0 14.4 %collective-permute-done.rest_1_ = bf16[64,40,128]{2,1,0:T(8,128)(2,1)S(1)} collective-permute-done((bf16[64,40,128]{2,1,0:T(8,128)(2,1)S(1)}, bf16[64,40,128]{2,1,0:T(8,128)(2,1)S(1)}, u32[]{:S(2)}, u32[]{:S(2)}) %collective-permute-start) | collective-permute-done | bytes 655392 | tf_op jit(solution)/shard_map/ppermute | solution.py:428
  66.9 2.7 %collective-permute-start.3 = (bf16[32,40,128]{2,1,0:T(8,128)(2,1)}, bf16[32,40,128]{2,1,0:T(8,128)(2,1)S(1)}, u32[]{:S(2)}, u32[]{:S(2)}) collective-permute-start(bf16[32,40,128]{2,1,0:T(8,128)(2,1)} %slice.25), channel_id=1, source_target_pairs={{0,192},{64,0},{128,64},{192,128},{1,193},{65,1},{129,65},{193,129... | collective-permute-start | bytes 983048 | tf_op jit(solution)/shard_map/ppermute | solution.py:432
  69.6 7.8 %copy.22 = bf16[40,128,512]{1,2,0:T(8,128)(2,1)} copy(bf16[40,128,512]{2,1,0:T(8,128)(2,1)} %bitcast.16) | data formatting | bytes 10485760 | tf_op jit(solution)/shard_map/reshape | solution.py:463
  78.9 2.7 %collective-permute-start.5 = (bf16[64,40,128]{2,1,0:T(8,128)(2,1)S(1)}, bf16[64,40,128]{2,1,0:T(8,128)(2,1)}, u32[]{:S(2)}, u32[]{:S(2)}) collective-permute-start(bf16[64,40,128]{2,1,0:T(8,128)(2,1)S(1)} %all-to-all-done.1.rest_5_.rest_0_), channel_id=1, source_target_pairs={{0,192},{64,0},{128,64},{192,128},{1,193},{65,1},{129,65},{193,129... | collective-permute-start | bytes 1966088 | tf_op jit(solution)/shard_map/ppermute | solution.py:429
  81.7 12.9 %collective-permute-done.4.rest_6_.rest_1_ = bf16[64,40,128]{2,1,0:T(8,128)(2,1)S(1)} collective-permute-done((bf16[64,40,128]{2,1,0:T(8,128)(2,1)S(1)}, bf16[64,40,128]{2,1,0:T(8,128)(2,1)S(1)}, u32[]{:S(2)}, u32[]{:S(2)}) %collective-permute-start.4) | collective-permute-done | bytes 655392 | tf_op jit(solution)/shard_map/ppermute | solution.py:428
  94.7 1.0 slice.27
  95.7 2.7 %collective-permute-start.7 = (bf16[32,40,128]{2,1,0:T(8,128)(2,1)S(1)}, bf16[32,40,128]{2,1,0:T(8,128)(2,1)S(1)}, u32[]{:S(2)}, u32[]{:S(2)}) collective-permute-start(bf16[32,40,128]{2,1,0:T(8,128)(2,1)S(1)} %slice.27), channel_id=1, source_target_pairs={{0,192},{64,0},{128,64},{192,128},{1,193},{65,1},{129,65},{193,129... | collective-permute-start | bytes 983048 | tf_op jit(solution)/shard_map/ppermute | solution.py:432
  98.5 2.5 copy-done
  102.9 10.1 %occ_first.1.rest_6_ = f32[24,128,512]{2,1,0:T(8,128)S(1)} custom-call(s32[64,2]{1,0:T(8,128)S(1)} %bitcast.14, s32[3]{0:T(128)S(1)} %pad_add_fusion.1.place_ref, bf16[64,40,128]{2,1,0:T(8,128)(2,1)S(1)} %all_to_all.10.rest_0_, bf16[64,40,128]{2,1,0:T(8,128)(2,1)S(1)} %collective-permute-done.rest_1_, ...), custom_call_target="tpu_custom_call" | custom-call | tf_op jit(solution)/shard_map/occ_first/pallas_call | solution.py:263
  113.0 2.7 %copy-done.1 = f32[24,128,512]{2,1,0:T(8,128)} copy-done((f32[24,128,512]{2,1,0:T(8,128)}, f32[24,128,512]{2,1,0:T(8,128)S(1)}, u32[]{:S(2)}) %copy-start.1) | copy-done | bytes 6291480
  115.8 20.8 %contract_virt.1 = (f32[2,2,12,32,512]{4,3,2,1,0:T(8,128)}, s16[800,512]{1,0:T(8,128)(2,1)S(1)}, s16[800,512]{1,0:T(8,128)(2,1)}) custom-call(s32[64,2]{1,0:T(8,128)S(1)} %bitcast.15, s32[64,2]{1,0:T(8,128)S(1)} %bitcast.12, s32[3]{0:T(128)S(1)} %pad_add_fusion.1.place_ref, bf16[64,40,128]{2,1,0:T(8,128)(2,1)S(1)} %all_to_all.10.rest_0_, ...), custom_call_target="tpu_custom_call" | custom-call | tf_op jit(solution)/shard_map/contract_virt/pallas_call | solution.py:196
  136.6 1.6 collective-permute-start.8
  138.2 1.8 collective-permute-start.9
  140.0 17.7 %occ_last.1 = (f32[2,2,12,32,512]{4,3,2,1,0:T(8,128)}, s16[800,512]{1,0:T(8,128)(2,1)S(1)}, s16[800,512]{1,0:T(8,128)(2,1)S(1)}) custom-call(s32[64,2]{1,0:T(8,128)S(1)} %bitcast.13, s32[3]{0:T(128)S(1)} %pad_add_fusion.1.place_ref, bf16[64,40,128]{2,1,0:T(8,128)(2,1)S(1)} %all-to-all-done.1.rest_5_.rest_0_, ...), custom_call_target="tpu_custom_call" | custom-call | tf_op jit(solution)/shard_map/occ_last/pallas_call | solution.py:275
  157.8 2.5 halve_virt.1
  161.3 7.6 %collective-permute-done.10.got0_ref = s16[400,512]{1,0:T(8,128)(2,1)S(1)} collective-permute-done((s16[400,512]{1,0:T(8,128)(2,1)S(1)}, s16[400,512]{1,0:T(8,128)(2,1)S(1)}, u32[]{:S(2)}, u32[]{:S(2)}) %collective-permute-start.10) | collective-permute-done | bytes 409632 | tf_op jit(solution)/shard_map/ppermute | solution.py:437
  168.9 1.5 collective-permute-start.13
  170.3 1.5 finish_virt.1
  171.9 7.0 %collective-permute-start.19 = (s16[800,512]{1,0:T(8,128)(2,1)S(1)}, s16[800,512]{1,0:T(8,128)(2,1)}, u32[]{:S(2)}, u32[]{:S(2)}) collective-permute-start(s16[800,512]{1,0:T(8,128)(2,1)S(1)} %finish_virt.1), channel_id=1, source_target_pairs={{0,0},{1,1},{2,2},{3,3},{4,64},{5,65},{6,66},{7,67},{8,128},{9,129... | collective-permute-start | bytes 2457608 | tf_op jit(solution)/shard_map/ppermute | solution.py:483
  178.8 6.7 %collective-permute-done.12.got0_ref = s16[800,512]{1,0:T(8,128)(2,1)S(1)} collective-permute-done((s16[800,512]{1,0:T(8,128)(2,1)S(1)}, s16[800,512]{1,0:T(8,128)(2,1)S(1)}, u32[]{:S(2)}, u32[]{:S(2)}) %collective-permute-start.12) | collective-permute-done | bytes 819232 | tf_op jit(solution)/shard_map/ppermute | solution.py:437
  185.6 3.4 %halve_occ.1 = (f32[2,12,32,512]{3,2,1,0:T(8,128)S(1)}, s16[400,512]{1,0:T(8,128)(2,1)}, s16[400,512]{1,0:T(8,128)(2,1)}) custom-call(s32[3]{0:T(128)S(1)} %pad_add_fusion.1.place_ref, f32[2,2,12,32,512]{4,3,2,1,0:T(8,128)S(1)} %copy-done.2, s16[800,512]{1,0:T(8,128)(2,1)S(1)} %collective-permute-done.12.got0_ref, ...), custom_call_target="tpu_custom_call" | custom-call | tf_op jit(solution)/shard_map/halve_occ/pallas_call | solution.py:300
  188.9 1.3 collective-permute-start.14
  190.3 6.9 %collective-permute-done.14.got0_ref = s16[400,512]{1,0:T(8,128)(2,1)S(1)} collective-permute-done((s16[400,512]{1,0:T(8,128)(2,1)}, s16[400,512]{1,0:T(8,128)(2,1)S(1)}, u32[]{:S(2)}, u32[]{:S(2)}) %collective-permute-start.14) | collective-permute-done | bytes 409632 | tf_op jit(solution)/shard_map/ppermute | solution.py:437
  198.7 1.0 copy-done.12
  199.7 1.0 copy-done.14
  200.7 1.8 finish_occ.1.own_ref
  202.6 2.2 collective-permute-start.16
  204.7 3.5 %collective-permute-start.17 = (s16[1,800,128]{2,1,0:T(8,128)(2,1)S(1)}, s16[1,800,128]{2,1,0:T(8,128)(2,1)S(1)}, u32[]{:S(2)}, u32[]{:S(2)}) collective-permute-start(s16[1,800,128]{2,1,0:T(8,128)(2,1)S(1)} %get-tuple-element.70), channel_id=1, source_target_pairs={{0,32},{4,36},{8,40},{12,44},{16,48},{20,52},{24,56},{28,60},{32,0... | collective-permute-start | bytes 614408 | tf_op jit(solution)/shard_map/ppermute | solution.py:492
  208.3 3.2 %collective-permute-start.18 = (s16[1,800,128]{2,1,0:T(8,128)(2,1)S(1)}, s16[1,800,128]{2,1,0:T(8,128)(2,1)S(1)}, u32[]{:S(2)}, u32[]{:S(2)}) collective-permute-start(s16[1,800,128]{2,1,0:T(8,128)(2,1)S(1)} %get-tuple-element.69), channel_id=1, source_target_pairs={{0,48},{4,52},{8,56},{12,60},{16,0},{20,4},{24,8},{28,12},{32,16},... | collective-permute-start | bytes 614408 | tf_op jit(solution)/shard_map/ppermute | solution.py:492
  211.5 4.4 %collective-permute-done.17.two_ref = s16[1,800,128]{2,1,0:T(8,128)(2,1)S(1)} collective-permute-done((s16[1,800,128]{2,1,0:T(8,128)(2,1)S(1)}, s16[1,800,128]{2,1,0:T(8,128)(2,1)S(1)}, u32[]{:S(2)}, u32[]{:S(2)}) %collective-permute-start.17) | collective-permute-done | bytes 204832 | tf_op jit(solution)/shard_map/ppermute | solution.py:492
  215.9 12.0 %collective-permute-done.18.three_ref = s16[1,800,128]{2,1,0:T(8,128)(2,1)S(1)} collective-permute-done((s16[1,800,128]{2,1,0:T(8,128)(2,1)S(1)}, s16[1,800,128]{2,1,0:T(8,128)(2,1)S(1)}, u32[]{:S(2)}, u32[]{:S(2)}) %collective-permute-start.18) | collective-permute-done | bytes 204832 | tf_op jit(solution)/shard_map/ppermute | solution.py:492
  227.9 5.7 %pair.1 = f32[24,24,128]{2,1,0:T(8,128)S(1)} custom-call(s32[2]{0:T(128)S(1)} %pad_add_fusion.place_ref, s16[4,800,128]{2,1,0:T(8,128)(2,1)S(1)} %finish_occ.1.own_ref, s16[1,800,128]{2,1,0:T(8,128)(2,1)S(1)} %collective-permute-done.16.one_ref, s16[1,800,128]{2,1,0:T(8,128)(2,1)S(1)} %collective-permute-done.17.two_ref, ...), custom_call_target="tpu_custom_call" | custom-call | tf_op jit(solution)/shard_map/pair/pallas_call | solution.py:375
  234.3 1.4 collective-permute-start.21
  235.7 1.3 collective-permute-start.22
  238.3 4.5 %collective-permute-start.24 = (f32[24,24]{1,0:T(8,128)S(1)}, f32[24,24]{1,0:T(8,128)S(1)}, u32[]{:S(2)}, u32[]{:S(2)}) collective-permute-start(f32[24,24]{1,0:T(8,128)S(1)} %add_add_fusion.3), channel_id=1, source_target_pairs={{0,4},{4,8},{8,12},{12,0},{16,20},{20,24},{24,28},{28,16},{32,36},... | collective-permute-start | bytes 6920 | tf_op jit(solution)/shard_map/ppermute | solution.py:422
  243.6 2.3 collective-permute-done.25
  246.2 2.7 %collective-permute-start.28 = (f32[24,24]{1,0:T(8,128)S(1)}, f32[24,24]{1,0:T(8,128)S(1)}, u32[]{:S(2)}, u32[]{:S(2)}) collective-permute-start(f32[24,24]{1,0:T(8,128)S(1)} %add_add_fusion.2), channel_id=1, source_target_pairs={{0,192},{64,0},{128,64},{192,128},{1,193},{65,1},{129,65},{193,129... | collective-permute-start | bytes 6920 | tf_op jit(solution)/shard_map/ppermute | solution.py:422
  248.9 1.1 collective-permute-done.26
  250.1 3.9 %collective-permute-start.29 = (f32[24,24]{1,0:T(8,128)S(1)}, f32[24,24]{1,0:T(8,128)S(1)}, u32[]{:S(2)}, u32[]{:S(2)}) collective-permute-start(f32[24,24]{1,0:T(8,128)S(1)} %add_add_fusion.1), channel_id=1, source_target_pairs={{0,32},{4,36},{8,40},{12,44},{16,48},{20,52},{24,56},{28,60},{32,0... | collective-permute-start | bytes 6920 | tf_op jit(solution)/shard_map/ppermute | solution.py:422
  254.0 1.0 collective-permute-start.30
  254.9 2.6 collective-permute-start.31
  257.5 1.1 collective-permute-done.30
  (81 shorter events, 14.3 us)
Async XLA Ops:
  0.0 1.8 copy-start.4
  41.9 37.1 %all-to-all-start.1 = ((bf16[64,40,128]{2,1,0:T(8,128)(2,1)}), bf16[64,40,128]{2,1,0:T(8,128)(2,1)S(1)}, u32[]{:S(2)}, u32[]{:S(2)}) async-start(bf16[64,40,128]{2,1,0:T(8,128)(2,1)} %get-tuple-element.40), calls=%async_computation.1 | async-start | bytes 1310720 | tf_op jit(solution)/shard_map/all_to_all | solution.py:461
  48.1 17.3 %collective-permute-start = (bf16[64,40,128]{2,1,0:T(8,128)(2,1)S(1)}, bf16[64,40,128]{2,1,0:T(8,128)(2,1)S(1)}, u32[]{:S(2)}, u32[]{:S(2)}) collective-permute-start(bf16[64,40,128]{2,1,0:T(8,128)(2,1)S(1)} %all_to_all.10.rest_0_), channel_id=1, source_target_pairs={{0,64},{64,128},{128,192},{192,0},{1,65},{65,129},{129,193},{193,1... | collective-permute-start | bytes 1966088 | tf_op jit(solution)/shard_map/ppermute | solution.py:428
  49.5 16.7 %collective-permute-start.1 = (bf16[64,40,128]{2,1,0:T(8,128)(2,1)S(1)}, bf16[64,40,128]{2,1,0:T(8,128)(2,1)S(1)}, u32[]{:S(2)}, u32[]{:S(2)}) collective-permute-start(bf16[64,40,128]{2,1,0:T(8,128)(2,1)S(1)} %all_to_all.10.rest_0_), channel_id=1, source_target_pairs={{0,192},{64,0},{128,64},{192,128},{1,193},{65,1},{129,65},{193,129... | collective-permute-start | bytes 1966088 | tf_op jit(solution)/shard_map/ppermute | solution.py:429
  66.2 11.3 %collective-permute-start.2 = (bf16[32,40,128]{2,1,0:T(8,128)(2,1)}, bf16[32,40,128]{2,1,0:T(8,128)(2,1)S(1)}, u32[]{:S(2)}, u32[]{:S(2)}) collective-permute-start(bf16[32,40,128]{2,1,0:T(8,128)(2,1)} %slice.24), channel_id=1, source_target_pairs={{0,64},{64,128},{128,192},{192,0},{1,65},{65,129},{129,193},{193,1... | collective-permute-start | bytes 983048 | tf_op jit(solution)/shard_map/ppermute | solution.py:431
  66.9 11.2 %collective-permute-start.3 = (bf16[32,40,128]{2,1,0:T(8,128)(2,1)}, bf16[32,40,128]{2,1,0:T(8,128)(2,1)S(1)}, u32[]{:S(2)}, u32[]{:S(2)}) collective-permute-start(bf16[32,40,128]{2,1,0:T(8,128)(2,1)} %slice.25), channel_id=1, source_target_pairs={{0,192},{64,0},{128,64},{192,128},{1,193},{65,1},{129,65},{193,129... | collective-permute-start | bytes 983048 | tf_op jit(solution)/shard_map/ppermute | solution.py:432
  77.4 0.7 copy-start.5
  78.2 0.8 copy-start.8
  78.9 15.6 %collective-permute-start.4 = (bf16[64,40,128]{2,1,0:T(8,128)(2,1)S(1)}, bf16[64,40,128]{2,1,0:T(8,128)(2,1)S(1)}, u32[]{:S(2)}, u32[]{:S(2)}) collective-permute-start(bf16[64,40,128]{2,1,0:T(8,128)(2,1)S(1)} %all-to-all-done.1.rest_5_.rest_0_), channel_id=1, source_target_pairs={{0,64},{64,128},{128,192},{192,0},{1,65},{65,129},{129,193},{193,1... | collective-permute-start | bytes 1966088 | tf_op jit(solution)/shard_map/ppermute | solution.py:428
  78.9 15.8 %collective-permute-start.5 = (bf16[64,40,128]{2,1,0:T(8,128)(2,1)S(1)}, bf16[64,40,128]{2,1,0:T(8,128)(2,1)}, u32[]{:S(2)}, u32[]{:S(2)}) collective-permute-start(bf16[64,40,128]{2,1,0:T(8,128)(2,1)S(1)} %all-to-all-done.1.rest_5_.rest_0_), channel_id=1, source_target_pairs={{0,192},{64,0},{128,64},{192,128},{1,193},{65,1},{129,65},{193,129... | collective-permute-start | bytes 1966088 | tf_op jit(solution)/shard_map/ppermute | solution.py:429
  94.6 21.1 %collective-permute-start.6 = (bf16[32,40,128]{2,1,0:T(8,128)(2,1)S(1)}, bf16[32,40,128]{2,1,0:T(8,128)(2,1)S(1)}, u32[]{:S(2)}, u32[]{:S(2)}) collective-permute-start(bf16[32,40,128]{2,1,0:T(8,128)(2,1)S(1)} %slice.26), channel_id=1, source_target_pairs={{0,64},{64,128},{128,192},{192,0},{1,65},{65,129},{129,193},{193,1... | collective-permute-start | bytes 983048 | tf_op jit(solution)/shard_map/ppermute | solution.py:431
  95.7 20.0 %collective-permute-start.7 = (bf16[32,40,128]{2,1,0:T(8,128)(2,1)S(1)}, bf16[32,40,128]{2,1,0:T(8,128)(2,1)S(1)}, u32[]{:S(2)}, u32[]{:S(2)}) collective-permute-start(bf16[32,40,128]{2,1,0:T(8,128)(2,1)S(1)} %slice.27), channel_id=1, source_target_pairs={{0,192},{64,0},{128,64},{192,128},{1,193},{65,1},{129,65},{193,129... | collective-permute-start | bytes 983048 | tf_op jit(solution)/shard_map/ppermute | solution.py:432
  98.5 2.5 copy-start
  101.0 1.0 copy-start.6
  101.9 1.0 copy-start.9
  102.9 12.9 %copy-start.7 = (bf16[32,40,128]{2,1,0:T(8,128)(2,1)S(1)}, bf16[32,40,128]{2,1,0:T(8,128)(2,1)}, u32[]{:S(2)}) copy-start(bf16[32,40,128]{2,1,0:T(8,128)(2,1)} %copy-done.5) | copy-start | bytes 983044
  102.9 12.9 %copy-start.10 = (bf16[32,40,128]{2,1,0:T(8,128)(2,1)S(1)}, bf16[32,40,128]{2,1,0:T(8,128)(2,1)}, u32[]{:S(2)}) copy-start(bf16[32,40,128]{2,1,0:T(8,128)(2,1)} %copy-done.8) | copy-start | bytes 983044
  113.0 2.7 %copy-start.1 = (f32[24,128,512]{2,1,0:T(8,128)}, f32[24,128,512]{2,1,0:T(8,128)S(1)}, u32[]{:S(2)}) copy-start(f32[24,128,512]{2,1,0:T(8,128)S(1)} %occ_first.1.rest_6_) | copy-start | bytes 18874372
  136.6 21.2 %collective-permute-start.8 = (s16[800,512]{1,0:T(8,128)(2,1)S(1)}, s16[800,512]{1,0:T(8,128)(2,1)S(1)}, u32[]{:S(2)}, u32[]{:S(2)}) collective-permute-start(s16[800,512]{1,0:T(8,128)(2,1)S(1)} %get-tuple-element.52), channel_id=1, source_target_pairs={{0,1},{1,0},{2,3},{3,2},{4,5},{5,4},{6,7},{7,6},{8,9},{9,8},{10,11... | collective-permute-start | bytes 2457608 | tf_op jit(solution)/shard_map/ppermute | solution.py:437
  138.2 19.6 %collective-permute-start.9 = (s16[800,512]{1,0:T(8,128)(2,1)}, s16[800,512]{1,0:T(8,128)(2,1)S(1)}, u32[]{:S(2)}, u32[]{:S(2)}) collective-permute-start(s16[800,512]{1,0:T(8,128)(2,1)} %get-tuple-element.53), channel_id=1, source_target_pairs={{0,3},{3,0},{1,2},{2,1},{4,7},{7,4},{5,6},{6,5},{8,11},{11,8},{9,1... | collective-permute-start | bytes 2457608 | tf_op jit(solution)/shard_map/ppermute | solution.py:437
  140.0 17.8 %copy-start.3 = (f32[2,2,12,32,512]{4,3,2,1,0:T(8,128)S(1)}, f32[2,2,12,32,512]{4,3,2,1,0:T(8,128)}, u32[]{:S(2)}) copy-start(f32[2,2,12,32,512]{4,3,2,1,0:T(8,128)} %get-tuple-element.51.keep_ref) | copy-start | bytes 9437188
  157.8 27.8 %copy-start.2 = (f32[2,2,12,32,512]{4,3,2,1,0:T(8,128)S(1)}, f32[2,2,12,32,512]{4,3,2,1,0:T(8,128)}, u32[]{:S(2)}) copy-start(f32[2,2,12,32,512]{4,3,2,1,0:T(8,128)} %get-tuple-element.62.keep_ref) | copy-start | bytes 9437188
  160.3 8.5 %collective-permute-start.10 = (s16[400,512]{1,0:T(8,128)(2,1)S(1)}, s16[400,512]{1,0:T(8,128)(2,1)S(1)}, u32[]{:S(2)}, u32[]{:S(2)}) collective-permute-start(s16[400,512]{1,0:T(8,128)(2,1)S(1)} %get-tuple-element.57), channel_id=1, source_target_pairs={{0,3},{3,0},{1,2},{2,1},{4,7},{7,4},{5,6},{6,5},{8,11},{11,8},{9,1... | collective-permute-start | bytes 1228808 | tf_op jit(solution)/shard_map/ppermute | solution.py:437
  161.3 7.6 %collective-permute-start.11 = (s16[400,512]{1,0:T(8,128)(2,1)S(1)}, s16[400,512]{1,0:T(8,128)(2,1)S(1)}, u32[]{:S(2)}, u32[]{:S(2)}) collective-permute-start(s16[400,512]{1,0:T(8,128)(2,1)S(1)} %get-tuple-element.58), channel_id=1, source_target_pairs={{0,1},{1,0},{2,3},{3,2},{4,5},{5,4},{6,7},{7,6},{8,9},{9,8},{10,11... | collective-permute-start | bytes 1228808 | tf_op jit(solution)/shard_map/ppermute | solution.py:437
  168.9 16.7 %collective-permute-start.12 = (s16[800,512]{1,0:T(8,128)(2,1)S(1)}, s16[800,512]{1,0:T(8,128)(2,1)S(1)}, u32[]{:S(2)}, u32[]{:S(2)}) collective-permute-start(s16[800,512]{1,0:T(8,128)(2,1)S(1)} %get-tuple-element.63), channel_id=1, source_target_pairs={{0,1},{1,0},{2,3},{3,2},{4,5},{5,4},{6,7},{7,6},{8,9},{9,8},{10,11... | collective-permute-start | bytes 2457608 | tf_op jit(solution)/shard_map/ppermute | solution.py:437
  168.9 16.7 %collective-permute-start.13 = (s16[800,512]{1,0:T(8,128)(2,1)S(1)}, s16[800,512]{1,0:T(8,128)(2,1)S(1)}, u32[]{:S(2)}, u32[]{:S(2)}) collective-permute-start(s16[800,512]{1,0:T(8,128)(2,1)S(1)} %get-tuple-element.64), channel_id=1, source_target_pairs={{0,3},{3,0},{1,2},{2,1},{4,7},{7,4},{5,6},{6,5},{8,11},{11,8},{9,1... | collective-permute-start | bytes 2457608 | tf_op jit(solution)/shard_map/ppermute | solution.py:437
  171.9 39.7 %collective-permute-start.19 = (s16[800,512]{1,0:T(8,128)(2,1)S(1)}, s16[800,512]{1,0:T(8,128)(2,1)}, u32[]{:S(2)}, u32[]{:S(2)}) collective-permute-start(s16[800,512]{1,0:T(8,128)(2,1)S(1)} %finish_virt.1), channel_id=1, source_target_pairs={{0,0},{1,1},{2,2},{3,3},{4,64},{5,65},{6,66},{7,67},{8,128},{9,129... | collective-permute-start | bytes 2457608 | tf_op jit(solution)/shard_map/ppermute | solution.py:483
  188.9 8.2 %collective-permute-start.14 = (s16[400,512]{1,0:T(8,128)(2,1)}, s16[400,512]{1,0:T(8,128)(2,1)S(1)}, u32[]{:S(2)}, u32[]{:S(2)}) collective-permute-start(s16[400,512]{1,0:T(8,128)(2,1)} %get-tuple-element.66), channel_id=1, source_target_pairs={{0,3},{3,0},{1,2},{2,1},{4,7},{7,4},{5,6},{6,5},{8,11},{11,8},{9,1... | collective-permute-start | bytes 1228808 | tf_op jit(solution)/shard_map/ppermute | solution.py:437
  190.3 7.6 %collective-permute-start.15 = (s16[400,512]{1,0:T(8,128)(2,1)}, s16[400,512]{1,0:T(8,128)(2,1)S(1)}, u32[]{:S(2)}, u32[]{:S(2)}) collective-permute-start(s16[400,512]{1,0:T(8,128)(2,1)} %get-tuple-element.67), channel_id=1, source_target_pairs={{0,1},{1,0},{2,3},{3,2},{4,5},{5,4},{6,7},{7,6},{8,9},{9,8},{10,11... | collective-permute-start | bytes 1228808 | tf_op jit(solution)/shard_map/ppermute | solution.py:437
  197.2 0.7 copy-start.11
  197.9 0.8 copy-start.13
  198.7 1.0 copy-start.12
  199.7 1.0 copy-start.14
  202.6 9.0 %collective-permute-start.16 = (s16[1,800,128]{2,1,0:T(8,128)(2,1)S(1)}, s16[1,800,128]{2,1,0:T(8,128)(2,1)S(1)}, u32[]{:S(2)}, u32[]{:S(2)}) collective-permute-start(s16[1,800,128]{2,1,0:T(8,128)(2,1)S(1)} %get-tuple-element.71), channel_id=1, source_target_pairs={{0,16},{4,20},{8,24},{12,28},{16,32},{20,36},{24,40},{28,44},{32,4... | collective-permute-start | bytes 614408 | tf_op jit(solution)/shard_map/ppermute | solution.py:492
  204.7 11.2 %collective-permute-start.17 = (s16[1,800,128]{2,1,0:T(8,128)(2,1)S(1)}, s16[1,800,128]{2,1,0:T(8,128)(2,1)S(1)}, u32[]{:S(2)}, u32[]{:S(2)}) collective-permute-start(s16[1,800,128]{2,1,0:T(8,128)(2,1)S(1)} %get-tuple-element.70), channel_id=1, source_target_pairs={{0,32},{4,36},{8,40},{12,44},{16,48},{20,52},{24,56},{28,60},{32,0... | collective-permute-start | bytes 614408 | tf_op jit(solution)/shard_map/ppermute | solution.py:492
  208.3 19.6 %collective-permute-start.18 = (s16[1,800,128]{2,1,0:T(8,128)(2,1)S(1)}, s16[1,800,128]{2,1,0:T(8,128)(2,1)S(1)}, u32[]{:S(2)}, u32[]{:S(2)}) collective-permute-start(s16[1,800,128]{2,1,0:T(8,128)(2,1)S(1)} %get-tuple-element.69), channel_id=1, source_target_pairs={{0,48},{4,52},{8,56},{12,60},{16,0},{20,4},{24,8},{28,12},{32,16},... | collective-permute-start | bytes 614408 | tf_op jit(solution)/shard_map/ppermute | solution.py:492
  233.8 4.1 %collective-permute-start.20 = (f32[24,24]{1,0:T(8,128)S(1)}, f32[24,24]{1,0:T(8,128)S(1)}, u32[]{:S(2)}, u32[]{:S(2)}) collective-permute-start(f32[24,24]{1,0:T(8,128)S(1)} %reduce_sum.9), channel_id=1, source_target_pairs={{0,2},{1,3},{2,0},{3,1},{4,6},{5,7},{6,4},{7,5},{8,10},{9,11},{10,... | collective-permute-start | bytes 6920 | tf_op jit(solution)/shard_map/ppermute | solution.py:422
  234.3 3.8 %collective-permute-start.21 = (f32[24,24]{1,0:T(8,128)S(1)}, f32[24,24]{1,0:T(8,128)S(1)}, u32[]{:S(2)}, u32[]{:S(2)}) collective-permute-start(f32[24,24]{1,0:T(8,128)S(1)} %reduce_sum.9), channel_id=1, source_target_pairs={{0,1},{1,2},{2,3},{3,0},{4,5},{5,6},{6,7},{7,4},{8,9},{9,10},{10,1... | collective-permute-start | bytes 6920 | tf_op jit(solution)/shard_map/ppermute | solution.py:422
  235.7 2.5 collective-permute-start.22
  238.2 4.5 %collective-permute-start.23 = (f32[24,24]{1,0:T(8,128)S(1)}, f32[24,24]{1,0:T(8,128)S(1)}, u32[]{:S(2)}, u32[]{:S(2)}) collective-permute-start(f32[24,24]{1,0:T(8,128)S(1)} %add_add_fusion.3), channel_id=1, source_target_pairs={{0,8},{4,12},{8,0},{12,4},{16,24},{20,28},{24,16},{28,20},{32,40},... | collective-permute-start | bytes 6920 | tf_op jit(solution)/shard_map/ppermute | solution.py:422
  238.3 5.3 %collective-permute-start.24 = (f32[24,24]{1,0:T(8,128)S(1)}, f32[24,24]{1,0:T(8,128)S(1)}, u32[]{:S(2)}, u32[]{:S(2)}) collective-permute-start(f32[24,24]{1,0:T(8,128)S(1)} %add_add_fusion.3), channel_id=1, source_target_pairs={{0,4},{4,8},{8,12},{12,0},{16,20},{20,24},{24,28},{28,16},{32,36},... | collective-permute-start | bytes 6920 | tf_op jit(solution)/shard_map/ppermute | solution.py:422
  242.8 3.1 %collective-permute-start.25 = (f32[24,24]{1,0:T(8,128)S(1)}, f32[24,24]{1,0:T(8,128)S(1)}, u32[]{:S(2)}, u32[]{:S(2)}) collective-permute-start(f32[24,24]{1,0:T(8,128)S(1)} %add_add_fusion.3), channel_id=1, source_target_pairs={{0,12},{4,0},{8,4},{12,8},{16,28},{20,16},{24,20},{28,24},{32,44},... | collective-permute-start | bytes 6920 | tf_op jit(solution)/shard_map/ppermute | solution.py:422
  245.9 4.1 %collective-permute-start.26 = (f32[24,24]{1,0:T(8,128)S(1)}, f32[24,24]{1,0:T(8,128)S(1)}, u32[]{:S(2)}, u32[]{:S(2)}) collective-permute-start(f32[24,24]{1,0:T(8,128)S(1)} %add_add_fusion.2), channel_id=1, source_target_pairs={{0,128},{64,192},{128,0},{192,64},{1,129},{65,193},{129,1},{193,65... | collective-permute-start | bytes 6920 | tf_op jit(solution)/shard_map/ppermute | solution.py:422
  245.9 4.2 %collective-permute-start.27 = (f32[24,24]{1,0:T(8,128)S(1)}, f32[24,24]{1,0:T(8,128)S(1)}, u32[]{:S(2)}, u32[]{:S(2)}) collective-permute-start(f32[24,24]{1,0:T(8,128)S(1)} %add_add_fusion.2), channel_id=1, source_target_pairs={{0,64},{64,128},{128,192},{192,0},{1,65},{65,129},{129,193},{193,1... | collective-permute-start | bytes 6920 | tf_op jit(solution)/shard_map/ppermute | solution.py:422
  246.2 3.9 %collective-permute-start.28 = (f32[24,24]{1,0:T(8,128)S(1)}, f32[24,24]{1,0:T(8,128)S(1)}, u32[]{:S(2)}, u32[]{:S(2)}) collective-permute-start(f32[24,24]{1,0:T(8,128)S(1)} %add_add_fusion.2), channel_id=1, source_target_pairs={{0,192},{64,0},{128,64},{192,128},{1,193},{65,1},{129,65},{193,129... | collective-permute-start | bytes 6920 | tf_op jit(solution)/shard_map/ppermute | solution.py:422
  250.1 7.4 %collective-permute-start.29 = (f32[24,24]{1,0:T(8,128)S(1)}, f32[24,24]{1,0:T(8,128)S(1)}, u32[]{:S(2)}, u32[]{:S(2)}) collective-permute-start(f32[24,24]{1,0:T(8,128)S(1)} %add_add_fusion.1), channel_id=1, source_target_pairs={{0,32},{4,36},{8,40},{12,44},{16,48},{20,52},{24,56},{28,60},{32,0... | collective-permute-start | bytes 6920 | tf_op jit(solution)/shard_map/ppermute | solution.py:422
  254.0 4.7 %collective-permute-start.30 = (f32[24,24]{1,0:T(8,128)S(1)}, f32[24,24]{1,0:T(8,128)S(1)}, u32[]{:S(2)}, u32[]{:S(2)}) collective-permute-start(f32[24,24]{1,0:T(8,128)S(1)} %add_add_fusion.1), channel_id=1, source_target_pairs={{0,16},{4,20},{8,24},{12,28},{16,32},{20,36},{24,40},{28,44},{32,4... | collective-permute-start | bytes 6920 | tf_op jit(solution)/shard_map/ppermute | solution.py:422
  254.9 3.7 %collective-permute-start.31 = (f32[24,24]{1,0:T(8,128)S(1)}, f32[24,24]{1,0:T(8,128)S(1)}, u32[]{:S(2)}, u32[]{:S(2)}) collective-permute-start(f32[24,24]{1,0:T(8,128)S(1)} %add_add_fusion.1), channel_id=1, source_target_pairs={{0,48},{4,52},{8,56},{12,60},{16,0},{20,4},{24,8},{28,12},{32,16},... | collective-permute-start | bytes 6920 | tf_op jit(solution)/shard_map/ppermute | solution.py:422
  (4 other events, 2.6 us)

commit v3 on v2

v3 whole, which is shorter than its diff:
```python
import functools

import jax
import jax.numpy as jnp
from jax import lax
from jax.experimental import pallas as pl
from jax.experimental.pallas import tpu as pltpu
from jax.sharding import PartitionSpec as P

NP = 24
ROWS = 4
COLS = 16
LAYERS = 4
CAP = 2
OWNERS = COLS * LAYERS
BS = 128
QUARTER = BS // ROWS
WIDE = 512
HALF = NP // 2
TOP = 32700.0
STEPS = 64.0
ALL = ("row", "col", "layer")
F32 = jnp.float32
BF16 = jnp.bfloat16
S16 = jnp.int16


def params(mib):
    return pltpu.CompilerParams(vmem_limit_bytes=mib * 2**20)


def encode(block):
    peak = jnp.max(jnp.abs(block), axis=0, keepdims=True)
    level = jnp.ceil(jnp.log2(jnp.maximum(peak, 1e-30)) * STEPS)
    scaled = block * (jnp.exp2(level * (-1.0 / STEPS)) * TOP)
    return jnp.round(scaled).astype(jnp.int32).astype(S16), level


def decode(codes, level):
    return codes.astype(jnp.int32).astype(F32) * (jnp.exp2(level * (1.0 / STEPS)) * (1.0 / TOP))


class Plan:
    def __init__(self, quarters):
        self.quarters = quarters
        self.group = 4 // quarters
        self.rows = 8 * quarters * self.group
        self.blocks = HALF // self.group

    def levels(self, count):
        return (count + 15) // 16 * 16

    def coded(self, count):
        return count * self.rows + self.levels(count)


def at_block(plan, index):
    return pl.ds(pl.multiple_of(index * plan.rows, 16), plan.rows)


def level_rows(plan, count):
    return slice(count * plan.rows, plan.coded(count))


def read_scales(ref, lead, plan, count, scale_ref):
    level = ref[(*lead, level_rows(plan, count), slice(None))].astype(jnp.int32).astype(F32)
    scale_ref[: plan.levels(count), :] = jnp.exp2(level * (1.0 / STEPS)) * (1.0 / TOP)


def get(ref, lead, plan, index, scale_ref):
    codes = ref[(*lead, at_block(plan, index), slice(None))]
    return codes.astype(jnp.int32).astype(F32) * scale_ref[pl.ds(index, 1), :]


def put(ref, plan, index, block, level_ref):
    codes, level = encode(block)
    ref[at_block(plan, index), :] = codes
    level_ref[pl.ds(index, 1), :] = level


def put_levels(ref, plan, count, level_ref):
    level = level_ref[: plan.levels(count), :]
    ref[level_rows(plan, count), :] = level.astype(jnp.int32).astype(S16)


def send_body(aux_ref, row_ref, col_ref, ext_ref, tiles_ref, out_ref, count_ref, *, layer_blocks):
    out_ref[...] = jnp.zeros(out_ref.shape, BF16)

    @pl.loop(0, OWNERS)
    def _(i):
        count_ref[i] = 0

    lane = lax.broadcasted_iota(jnp.int32, (QUARTER, BS), 1)
    meta_lane = lax.broadcasted_iota(jnp.int32, (8, BS), 1)

    @pl.loop(0, tiles_ref.shape[0])
    def _(i):
        col = col_ref[i]
        layer_of = col // layer_blocks
        kept = col - layer_of * layer_blocks
        owner = (row_ref[i] % 4 * 4 + row_ref[i] // 4) * LAYERS + layer_of
        used = count_ref[owner]
        count_ref[owner] = used + 1
        tile = jnp.where(lane < ext_ref[i], tiles_ref[i].astype(F32), 0.0)
        out_ref[owner, pl.ds(pl.multiple_of(used * QUARTER, QUARTER), QUARTER), :] = tile.astype(BF16)
        old = out_ref[owner, CAP * QUARTER :, :].astype(F32)
        new = jnp.where(meta_lane == used * 2, aux_ref[i].astype(F32), old)
        new = jnp.where(meta_lane == used * 2 + 1, kept.astype(F32), new)
        out_ref[owner, CAP * QUARTER :, :] = new.astype(BF16)


def build_send(tiles, block_aux, block_row, block_col, extents, layer_blocks):
    return pl.pallas_call(
        functools.partial(send_body, layer_blocks=layer_blocks),
        in_specs=[SMEM] * 4 + [VMEM],
        out_specs=VMEM,
        out_shape=jax.ShapeDtypeStruct((OWNERS, CAP * QUARTER + 8, BS), BF16),
        scratch_shapes=[pltpu.SMEM((OWNERS,), jnp.int32)],
        compiler_params=params(8),
        name="build_send",
    )(block_aux, block_row, block_col, extents, tiles)


def split_pieces(place_ref, plan, rows_of, keep_ref, send_refs, level_ref):
    bit_a = place_ref[1]
    bit_b = place_ref[2]

    def piece(a, b):
        return jnp.where(b == 0, a, 3 - a)

    for h, send_ref in enumerate(send_refs):
        kept = [piece(bit_a, o) if h == 0 else piece(o, bit_b) for o in range(2)]
        sent = [piece(1 - bit_a, o) if h == 0 else piece(o, 1 - bit_b) for o in range(2)]

        @pl.loop(0, plan.blocks)
        def _(block):
            first = h * HALF + block * plan.group
            for other in range(2):
                keep_ref[h, other, block] = rows_of(first, kept[other])
                put(send_ref, plan, other * plan.blocks + block, rows_of(first, sent[other]), level_ref)

        put_levels(send_ref, plan, 2 * plan.blocks, level_ref)


def virt_near_body(meta_ref, own_ref, prev_ref, next_ref, green_ref, acc_ref):
    acc_ref[...] = jnp.zeros(acc_ref.shape, F32)

    @pl.loop(0, OWNERS // 2)
    def _(step):
        for source in (step * 2, step * 2 + 1):
            for slot in range(CAP):
                span = slice(slot * QUARTER, (slot + 1) * QUARTER)
                tile = jnp.concatenate([ref[source, span, :] for ref in (own_ref, prev_ref, next_ref)], axis=0)
                aux = meta_ref[source, 2 * slot]
                kept = meta_ref[source, 2 * slot + 1]
                acc_ref[aux] += jnp.dot(tile, green_ref[kept], preferred_element_type=F32)


def virt_far_body(
    meta_ref, place_ref, far_a_ref, far_b_ref, green_ref, near_ref, keep_ref, send0_ref, send1_ref, acc_ref, level_ref, *, plan
):
    acc_ref[...] = jnp.zeros(acc_ref.shape, F32)
    half = OWNERS // 2
    for part, far_ref in enumerate((far_a_ref, far_b_ref)):

        @pl.loop(0, half // 2)
        def _(step):
            for local in (step * 2, step * 2 + 1):
                source = part * half + local
                for slot in range(CAP):
                    tile = far_ref[local, slot * QUARTER : (slot + 1) * QUARTER, :]
                    aux = meta_ref[source, 2 * slot]
                    kept = meta_ref[source, 2 * slot + 1]
                    acc_ref[aux] += jnp.dot(tile, green_ref[kept], preferred_element_type=F32)

    def rows_of(first, piece):
        at = [pl.multiple_of(quarter * QUARTER + piece * 8, 8) for quarter in range(3)]
        parts = [near_ref[first, pl.ds(row, 8), :] for row in at]
        return jnp.concatenate(parts + [acc_ref[first, pl.ds(at[0], 8), :]], axis=0)

    split_pieces(place_ref, plan, rows_of, keep_ref, (send0_ref, send1_ref), level_ref)


def occ_body(
    meta_ref, place_ref, own_ref, prev_ref, next_ref, far_a_ref, far_b_ref, green_ref, *rest, plan
):
    keep_ref, send0_ref, send1_ref, acc_ref, tile_ref, level_ref = rest
    acc_ref[...] = jnp.zeros(acc_ref.shape, F32)
    row_place = place_ref[0]
    rows = [pl.multiple_of(((row_place + d) % ROWS) * QUARTER, QUARTER) for d in (0, ROWS - 1, 1, 2)]
    half = OWNERS // 2
    for part, far_ref in enumerate((far_a_ref, far_b_ref)):

        @pl.loop(0, half // 2)
        def _(step):
            visits = [(j, slot) for j in range(2) for slot in range(CAP)]
            for j, slot in visits:
                local = step * 2 + j
                source = part * half + local
                span = slice(slot * QUARTER, (slot + 1) * QUARTER)
                for ref, row in zip((own_ref, prev_ref, next_ref), rows):
                    tile_ref[CAP * j + slot, pl.ds(row, QUARTER), :] = ref[source, span, :]
                tile_ref[CAP * j + slot, pl.ds(rows[3], QUARTER), :] = far_ref[local, span, :]
            for j, slot in visits:
                source = part * half + step * 2 + j
                aux = meta_ref[source, 2 * slot]
                kept = meta_ref[source, 2 * slot + 1]
                term = lax.dot_general(
                    green_ref[kept], tile_ref[CAP * j + slot], (((1,), (1,)), ((), ())), preferred_element_type=F32
                )
                for low in range(4):
                    lanes = slice(low * BS, (low + 1) * BS)
                    acc_ref[aux, :, lanes] += term[low * BS : (low + 1) * BS, :]

    def rows_of(first, piece):
        at = [pl.multiple_of(quarter * QUARTER + piece * 8, 8) for quarter in range(4)]
        return jnp.concatenate([acc_ref[first, pl.ds(row, 8), :] for row in at], axis=0)

    split_pieces(place_ref, plan, rows_of, keep_ref, (send0_ref, send1_ref), level_ref)


VMEM = pl.BlockSpec(memory_space=pltpu.VMEM)
SMEM = pl.BlockSpec(memory_space=pltpu.SMEM)
NEAR = (NP, 3 * QUARTER, WIDE)


def step_shapes(plan):
    code = jax.ShapeDtypeStruct((plan.coded(2 * plan.blocks), WIDE), S16)
    return [jax.ShapeDtypeStruct((2, 2, plan.blocks, plan.rows, WIDE), F32), code, code]


def level_scratch(plan):
    return pltpu.VMEM((plan.levels(2 * plan.blocks), WIDE), F32)


def contract_virt_near(meta, quarters, green):
    return pl.pallas_call(
        virt_near_body,
        in_specs=[SMEM] + [VMEM] * 4,
        out_specs=VMEM,
        out_shape=jax.ShapeDtypeStruct(NEAR, F32),
        compiler_params=params(20),
        name="virt_near",
    )(meta, *quarters, green)


def contract_virt_far(meta, place, fars, green, near, plan):
    return pl.pallas_call(
        functools.partial(virt_far_body, plan=plan),
        in_specs=[SMEM] * 2 + [VMEM] * 4,
        out_specs=[VMEM] * 3,
        out_shape=step_shapes(plan),
        scratch_shapes=[pltpu.VMEM((NP, QUARTER, WIDE), F32), level_scratch(plan)],
        compiler_params=params(24),
        name="virt_far",
    )(meta, place, *fars, green, near)


def contract_occ(meta, place, quarters, green, plan):
    return pl.pallas_call(
        functools.partial(occ_body, plan=plan),
        in_specs=[SMEM] * 2 + [VMEM] * 6,
        out_specs=[VMEM] * 3,
        out_shape=step_shapes(plan),
        scratch_shapes=[pltpu.VMEM((NP, BS, WIDE), F32), pltpu.VMEM((2 * CAP, BS, BS), BF16), level_scratch(plan)],
        compiler_params=params(28),
        name="contract_occ",
    )(meta, place, *quarters, green)


def halve_body(place_ref, keep_ref, got0_ref, got1_ref, left_ref, send0_ref, send1_ref, level_ref, scale_ref, *, plan):
    for h, got_ref, send_ref in ((0, got0_ref, send0_ref), (1, got1_ref, send1_ref)):
        mine = place_ref[2 - h]
        away = 1 - mine
        read_scales(got_ref, (), plan, 2 * plan.blocks, scale_ref)

        @pl.loop(0, plan.blocks)
        def _(b):
            left_ref[h, b] = keep_ref[h, mine, b] + get(got_ref, (), plan, mine * plan.blocks + b, scale_ref)
            total = keep_ref[h, away, b] + get(got_ref, (), plan, away * plan.blocks + b, scale_ref)
            put(send_ref, plan, b, total, level_ref)

        put_levels(send_ref, plan, plan.blocks, level_ref)


def halve(place, keep, got0, got1, plan, name):
    code = jax.ShapeDtypeStruct((plan.coded(plan.blocks), WIDE), S16)
    return pl.pallas_call(
        functools.partial(halve_body, plan=plan),
        in_specs=[SMEM] + [VMEM] * 3,
        out_specs=[VMEM] * 3,
        out_shape=[jax.ShapeDtypeStruct((2, plan.blocks, plan.rows, WIDE), F32), code, code],
        scratch_shapes=[level_scratch(plan), level_scratch(plan)],
        compiler_params=params(16),
        name=name,
    )(place, keep, got0, got1)


def finish_body(left_ref, got0_ref, got1_ref, out_ref, level_ref, scale_ref, *, plan, split):
    count = 2 * plan.blocks
    for h, got_ref in ((0, got0_ref), (1, got1_ref)):
        read_scales(got_ref, (), plan, plan.blocks, scale_ref)

        @pl.loop(0, plan.blocks)
        def _(b):
            total = left_ref[h, b] + get(got_ref, (), plan, b, scale_ref)
            index = h * plan.blocks + b
            if split:
                codes, level = encode(total)
                for low in range(4):
                    out_ref[low, at_block(plan, index), :] = codes[:, low * BS : (low + 1) * BS]
                level_ref[pl.ds(index, 1), :] = level
            else:
                put(out_ref, plan, index, total, level_ref)

    if split:
        levels = level_ref[...].astype(jnp.int32).astype(S16)
        for low in range(4):
            out_ref[low, level_rows(plan, count), :] = levels[:, low * BS : (low + 1) * BS]
    else:
        put_levels(out_ref, plan, count, level_ref)


def finish(left, got0, got1, plan, split, name):
    rows = plan.coded(2 * plan.blocks)
    shape = (4, rows, BS) if split else (rows, WIDE)
    return pl.pallas_call(
        functools.partial(finish_body, plan=plan, split=split),
        in_specs=[VMEM] * 3,
        out_specs=VMEM,
        out_shape=jax.ShapeDtypeStruct(shape, S16),
        scratch_shapes=[level_scratch(plan), level_scratch(plan)],
        compiler_params=params(12),
        name=name,
    )(left, got0, got1)


def pair_body(place_ref, own_ref, one_ref, two_ref, three_ref, virt_ref, out_ref, occ_ref, vir_ref, wide_ref, thin_ref, *, plan):
    here = place_ref[0]
    high = place_ref[1]
    count = 2 * plan.blocks

    at = [((high + shift) % 4) * 8 for shift in (0, ROWS - 1, 1, 2)]
    read_scales(virt_ref, (), plan, count, wide_ref)

    @pl.loop(0, NP)
    def _(q):
        values = get(virt_ref, (), plan, q, wide_ref)
        for quarter in range(4):
            for low in range(4):
                to = pl.ds(pl.multiple_of(low * QUARTER + at[quarter], 8), 8)
                vir_ref[q, to, :] = values[quarter * 8 : (quarter + 1) * 8, low * BS : (low + 1) * BS]

    for d, ref in enumerate((own_ref, one_ref, two_ref, three_ref)):
        source = (here + 4 - d) % 4
        lead = (here,) if d == 0 else (0,)
        read_scales(ref, lead, plan, count, thin_ref)
        rows = pl.ds(pl.multiple_of(source * QUARTER, QUARTER), QUARTER)

        @pl.loop(0, NP)
        def _(p):
            occ_ref[p, rows, :] = get(ref, lead, plan, p, thin_ref)

    @pl.loop(0, NP)
    def _(p):
        occ = occ_ref[p]
        for q in range(NP):
            out_ref[p, q : q + 1, :] = jnp.sum(occ * vir_ref[q], axis=0, keepdims=True)


def pair(place, own, others, virt, plan):
    levels = plan.levels(2 * plan.blocks)
    return pl.pallas_call(
        functools.partial(pair_body, plan=plan),
        in_specs=[SMEM] + [VMEM] * 5,
        out_specs=VMEM,
        out_shape=jax.ShapeDtypeStruct((NP, NP, BS), F32),
        scratch_shapes=[
            pltpu.VMEM((NP, BS, BS), F32),
            pltpu.VMEM((NP, BS, BS), F32),
            pltpu.VMEM((levels, WIDE), F32),
            pltpu.VMEM((levels, BS), F32),
        ],
        compiler_params=params(16),
        name="pair",
    )(place, own, *others, virt)


def rotate(size, step):
    return [(i, (i + step) % size) for i in range(size)]


def rotate_low(step):
    return [(c, c - c % 4 + (c + step) % 4) for c in range(COLS)]


def rotate_high(step):
    return [(c, (c + 4 * step) % COLS) for c in range(COLS)]


PAIRS_A = [(0, 1), (1, 0), (2, 3), (3, 2)]
PAIRS_B = [(0, 3), (3, 0), (1, 2), (2, 1)]


def index_of(row, col, layer):
    return (row * COLS + col) * LAYERS + layer


SWAP = [
    (index_of(r, c, l), index_of(c % 4, c // 4 * 4 + r, l))
    for r in range(ROWS)
    for c in range(COLS)
    for l in range(LAYERS)
]


def tree_sum(values):
    rounds = (
        ("layer", [rotate(LAYERS, d) for d in (1, 2, 3)]),
        ("col", [rotate_low(d) for d in (1, 2, 3)]),
        ("row", [rotate(ROWS, d) for d in (1, 2, 3)]),
        ("col", [rotate_high(d) for d in (1, 2, 3)]),
    )
    for axis, perms in rounds:
        one, two, three = [lax.ppermute(values, axis, perm) for perm in perms]
        values = (values + two) + (one + three)
    return values


def layer_swap(send0, send1, perms):
    return lax.ppermute(send0, "layer", perms[0]), lax.ppermute(send1, "layer", perms[1])


FIRST = (PAIRS_A, PAIRS_B)
SECOND = (PAIRS_B, PAIRS_A)


def after(*values):
    return lax.optimization_barrier(values)


def on_device(blocks, block_aux, block_row, block_col, extents, occ_green, virt_green):
    layer_blocks = occ_green.shape[0] // BS
    row_place = lax.axis_index("row").astype(jnp.int32)
    col_place = lax.axis_index("col").astype(jnp.int32)
    layer_place = lax.axis_index("layer").astype(jnp.int32)
    bit_a = ((layer_place == 1) | (layer_place == 2)).astype(jnp.int32)
    bit_b = layer_place // 2
    place = jnp.stack([row_place, bit_a, bit_b])
    plan = Plan(4)

    tiles = lax.dynamic_slice_in_dim(blocks, row_place * QUARTER, QUARTER, 1)
    send = build_send(tiles, block_aux, block_row, block_col, extents, layer_blocks)
    own = lax.all_to_all(send, ("col", "layer"), 0, 0, tiled=True)
    meta = own[:, CAP * QUARTER, : 2 * CAP].astype(jnp.int32)
    virt_blocks = virt_green.reshape(layer_blocks, BS, WIDE)
    occ_blocks = occ_green.reshape(layer_blocks, BS, WIDE).transpose(0, 2, 1)

    half = OWNERS // 2
    prev = lax.ppermute(own, "row", rotate(ROWS, 1))
    nxt = lax.ppermute(own, "row", rotate(ROWS, -1))
    far_a = lax.ppermute(prev[:half], "row", rotate(ROWS, 1))
    far_b = lax.ppermute(nxt[half:], "row", rotate(ROWS, -1))

    prev, nxt, occ_blocks = after(prev, nxt, occ_blocks)
    v_near = contract_virt_near(meta, (own, prev, nxt), virt_blocks)
    v_keep, v0, v1 = contract_virt_far(meta, place, (far_a, far_b), virt_blocks, v_near, plan)
    v_got = layer_swap(v0, v1, FIRST)
    occ_blocks, v_keep = after(occ_blocks, v_keep)
    o_keep, o0, o1 = contract_occ(meta, place, (own, prev, nxt, far_a, far_b), occ_blocks, plan)
    o_got = layer_swap(o0, o1, FIRST)
    v_keep, o_keep = after(v_keep, o_keep)
    v_left, v0, v1 = halve(place, v_keep, *v_got, plan, "halve_virt")
    v_got = layer_swap(v0, v1, SECOND)
    virt = finish(v_left, *v_got, plan, False, "finish_virt")
    virt, o_keep = after(virt, o_keep)
    virt = lax.ppermute(virt, ALL, SWAP)
    o_left, o0, o1 = halve(place, o_keep, *o_got, plan, "halve_occ")
    o_got = layer_swap(o0, o1, SECOND)
    occ = finish(o_left, *o_got, plan, True, "finish_occ")

    low = col_place // 4
    others = []
    for d in (1, 2, 3):
        part = lax.dynamic_slice_in_dim(occ, (low + d) % 4, 1, 0)
        others.append(lax.ppermute(part, "col", rotate_high(d)))
    here = jnp.stack([low, col_place % 4])
    partial = pair(here, occ, others, virt, plan)
    return tree_sum(jnp.sum(partial, axis=-1))


def solution(mesh):
    in_specs = (
        P(("col", "layer"), None, None),
        P(("col", "layer")),
        P(("col", "layer")),
        P(("col", "layer")),
        P(("col", "layer")),
        P("layer", "row"),
        P("layer", "row"),
    )
    return jax.shard_map(on_device, mesh=mesh, in_specs=in_specs, out_specs=P(), check_vma=False)
```

time: 260 us -> 254 us (0.977)
  Pallas kernels: 68.6 us -> 50.5 us
  blocking collectives: 32.5 us -> 43.4 us
  local copies, waits for them, and re-layouts: 27 us -> 30.8 us
  waiting for transfers between devices: 71.5 us -> 67.9 us
    pallas_call x5, Pallas kernels: 59.4 us -> 42 us  [the longest x1 14 us: contract_occ(): pl.pallas_call(functools.partial(occ_body, plan=plan), in_specs=[SMEM] *...]
    ppermute x12, starting transfers between devices: 18.1 us -> 32.4 us  [tree_sum(): one, two, three = [lax.ppermute(values, axis, perm) for perm in perms]]
    all_to_all x1, blocking collectives: 32.5 us -> 43.4 us  [on_device(): own = lax.all_to_all(send, ('col', 'layer'), 0, 0, tiled=True)]
    ppermute x3, waiting for transfers between devices: 16.3 us -> 5.59 us  [on_device(): others.append(lax.ppermute(part, 'col', rotate_high(d)))]
    ppermute x4, waiting for transfers between devices: 21.2 us -> 29.4 us  [layer_swap(): lax.ppermute(send0, 'layer', perms[0])]
    all_to_all x1 -> x0, starting transfers between devices: 6.26 us -> none  [on_device(): own1 = lax.all_to_all(send1, ('col', 'layer'), 0, 0, tiled=True)]
    ppermute x8 -> x4, starting transfers between devices: 11.1 us -> 6.23 us  [the longest x1 2.49 us: on_device(): nxt = lax.ppermute(own, 'row', rotate(ROWS, -1))]
    ppermute x8 -> x4, waiting for transfers between devices: 27.3 us -> 23.5 us  [the longest x1 23.5 us: on_device(): prev = lax.ppermute(own, 'row', rotate(ROWS, 1))]
  transfers between devices with their start and end apart: 33 -> 28, of which waited for: 15 -> 16; matrix products, arithmetic and copies ran while one was open for 4% -> 5% of each run, Pallas kernels for 13% -> 13%
where the time goes in v3:
time: 254 us; the launch traced here: 252 us
  waiting for transfers between devices  67.9 us (27%)
  starting transfers between devices  57.6 us (23%)
  Pallas kernels  50.5 us (20%)
  blocking collectives  43.4 us (17%)
  local copies, waits for them, and re-layouts  30.8 us (12%)
    all_to_all x1, blocking collectives, on_device(): own = lax.all_to_all(send, ('col', 'layer'), 0, 0, tiled=True)  43.4 us
    ppermute x12, starting transfers between devices, tree_sum(): one, two, three = [lax.ppermute(values, axis, perm) for perm in perms]  32.4 us
    ppermute x4, waiting for transfers between devices, layer_swap(): lax.ppermute(send0, 'layer', perms[0])  29.4 us
    ppermute x1, waiting for transfers between devices, on_device(): prev = lax.ppermute(own, 'row', rotate(ROWS, 1))  23.5 us
    unnamed x46, local copies, waits for them, and re-layouts  20.2 us
    pallas_call x1, Pallas kernels, contract_occ(): pl.pallas_call(functools.partial(occ_body, plan=plan), in_specs=[SMEM] *...  14 us
    pallas_call x1, Pallas kernels, contract_virt_near(): pl.pallas_call(virt_near_body, in_specs=[SMEM] + [VMEM] * 4, out_specs=VM...  9.69 us
    pallas_call x1, Pallas kernels, contract_virt_far(): pl.pallas_call(functools.partial(virt_far_body, plan=plan), in_specs=[SME...  9.35 us
  transfers between devices with their start and end apart: 28, of which 16 were waited for; matrix products, arithmetic and copies ran while one was open for 5% of the time, Pallas kernels for 13%

profile of v3, /device:TPU:1, one launch (start us, length us, event | category | flops | bytes accessed | tf_op | source)
XLA Modules:
  0.0 252.4 jit_solution(14518180562959566701)
XLA Ops:
  0.0 1.8 copy-done
  4.5 3.3 %build_send.1 = bf16[64,72,128]{2,1,0:T(8,128)(2,1)S(1)} custom-call(s32[88]{0:T(128)S(1)} %copy-done.19, s32[88]{0:T(128)S(1)} %copy-done.20, s32[88]{0:T(128)S(1)} %copy-done.21, s32[88]{0:T(128)S(1)} %copy-done.22, bf16[88,32,128]{2,1,0:T(8,128)(2,1)S(1)} %constant_dynamic-slice_fusion.3.tiles_ref), custom_call_target="tpu_custom_call" | custom-call | tf_op jit(solution)/shard_map/build_send/pallas_call | solution.py:113
  7.9 43.4 %all_to_all.5.own_ref = bf16[64,72,128]{2,1,0:T(8,128)(2,1)S(1)} all-to-all(bf16[64,72,128]{2,1,0:T(8,128)(2,1)S(1)} %build_send.1), channel_id=1, replica_groups=mesh['row'=4,'col'=16,'layer'=4] {'col','layer'}, dimensions={0} | all-to-all | bytes 2359296 | tf_op jit(solution)/shard_map/all_to_all | solution.py:454
  51.3 1.3 collective-permute-start
  52.6 2.5 collective-permute-start.1
  55.1 23.5 %collective-permute-done.prev_ref = bf16[64,72,128]{2,1,0:T(8,128)(2,1)S(1)} collective-permute-done((bf16[64,72,128]{2,1,0:T(8,128)(2,1)S(1)}, bf16[64,72,128]{2,1,0:T(8,128)(2,1)S(1)}, u32[]{:S(2)}, u32[]{:S(2)}) %collective-permute-start) | collective-permute-done | bytes 1179680 | tf_op jit(solution)/shard_map/ppermute | solution.py:460
  81.2 2.4 collective-permute-start.3
  83.6 7.9 %copy.8 = bf16[40,128,512]{1,2,0:T(8,128)(2,1)} copy(bf16[40,128,512]{2,1,0:T(8,128)(2,1)} %bitcast.15) | data formatting | bytes 10485760 | tf_op jit(solution)/shard_map/reshape | solution.py:457
  91.6 0.9 slice_convert_fusion
  92.6 2.5 copy-done.1
  95.0 1.3 copy-done.5
  96.3 1.3 copy-done.8
  97.6 1.3 copy-done.11
  98.9 9.7 %virt_near.1.near_ref = f32[24,96,512]{2,1,0:T(8,128)S(1)} custom-call(s32[64,4]{1,0:T(8,128)S(1)} %bitcast.12, bf16[64,72,128]{2,1,0:T(8,128)(2,1)S(1)} %copy-done.5, bf16[64,72,128]{2,1,0:T(8,128)(2,1)S(1)} %copy-done.8, bf16[64,72,128]{2,1,0:T(8,128)(2,1)S(1)} %copy-done.11, bf16[40,128,512]{2,1,0:T(8,128)(2,1)S(1)} %bitcast.9), custom_call_target="tpu_custom_call" | custom-call | tf_op jit(solution)/shard_map/virt_near/pallas_call | solution.py:237
  108.6 2.5 copy-done.2
  111.1 9.3 %virt_far.1 = (f32[2,2,12,32,512]{4,3,2,1,0:T(8,128)S(1)}, s16[800,512]{1,0:T(8,128)(2,1)S(1)}, s16[800,512]{1,0:T(8,128)(2,1)S(1)}) custom-call(s32[64,4]{1,0:T(8,128)S(1)} %bitcast.13, s32[3]{0:T(128)S(1)} %pad_add_fusion.1.place_ref, bf16[32,72,128]{2,1,0:T(8,128)(2,1)S(1)} %collective-permute-done.2.far_a_ref, ...), custom_call_target="tpu_custom_call" | custom-call | tf_op jit(solution)/shard_map/virt_far/pallas_call | solution.py:248
  121.1 2.0 collective-permute-start.5
  123.1 14.0 %contract_occ.1 = (f32[2,2,12,32,512]{4,3,2,1,0:T(8,128)S(1)}, s16[800,512]{1,0:T(8,128)(2,1)S(1)}, s16[800,512]{1,0:T(8,128)(2,1)S(1)}) custom-call(s32[64,4]{1,0:T(8,128)S(1)} %bitcast.14, s32[3]{0:T(128)S(1)} %pad_add_fusion.1.place_ref, bf16[64,72,128]{2,1,0:T(8,128)(2,1)S(1)} %copy-done.6, bf16[64,72,128]{2,1,0:T(8,128)(2,1)S(1)} %copy-done.9, ...), custom_call_target="tpu_custom_call" | custom-call | tf_op jit(solution)/shard_map/contract_occ/pallas_call | solution.py:260
  138.6 1.8 halve_virt.1
  140.5 2.1 collective-permute-start.6
  142.6 23.1 %collective-permute-done.6.got0_ref = s16[400,512]{1,0:T(8,128)(2,1)S(1)} collective-permute-done((s16[400,512]{1,0:T(8,128)(2,1)S(1)}, s16[400,512]{1,0:T(8,128)(2,1)S(1)}, u32[]{:S(2)}, u32[]{:S(2)}) %collective-permute-start.6) | collective-permute-done | bytes 409632 | tf_op jit(solution)/shard_map/ppermute | solution.py:431
  165.7 2.0 finish_virt.1
  167.7 4.4 %collective-permute-start.15 = (s16[800,512]{1,0:T(8,128)(2,1)}, s16[800,512]{1,0:T(8,128)(2,1)}, u32[]{:S(2)}, u32[]{:S(2)}) collective-permute-start(s16[800,512]{1,0:T(8,128)(2,1)} %finish_virt.1), channel_id=1, source_target_pairs={{0,0},{1,1},{2,2},{3,3},{4,64},{5,65},{6,66},{7,67},{8,128},{9,129... | collective-permute-start | bytes 2457608 | tf_op jit(solution)/shard_map/ppermute | solution.py:477
  172.1 2.7 %halve_occ.1 = (f32[2,12,32,512]{3,2,1,0:T(8,128)S(1)}, s16[400,512]{1,0:T(8,128)(2,1)}, s16[400,512]{1,0:T(8,128)(2,1)}) custom-call(s32[3]{0:T(128)S(1)} %pad_add_fusion.1.place_ref, f32[2,2,12,32,512]{4,3,2,1,0:T(8,128)S(1)} %get-tuple-element.40.keep_ref, s16[800,512]{1,0:T(8,128)(2,1)S(1)} %collective-permute-done.8.got0_ref, ...), custom_call_target="tpu_custom_call" | custom-call | tf_op jit(solution)/shard_map/halve_occ/pallas_call | solution.py:288
  174.8 1.2 copy-done.15
  176.0 2.0 collective-permute-start.10
  177.9 6.3 %collective-permute-done.10.got0_ref = s16[400,512]{1,0:T(8,128)(2,1)S(1)} collective-permute-done((s16[400,512]{1,0:T(8,128)(2,1)}, s16[400,512]{1,0:T(8,128)(2,1)S(1)}, u32[]{:S(2)}, u32[]{:S(2)}) %collective-permute-start.10) | collective-permute-done | bytes 409632 | tf_op jit(solution)/shard_map/ppermute | solution.py:431
  185.1 1.4 copy-done.16
  186.5 2.1 finish_occ.1.own_ref
  190.3 2.1 collective-permute-start.12
  192.4 2.9 %collective-permute-start.13 = (s16[1,800,128]{2,1,0:T(8,128)(2,1)}, s16[1,800,128]{2,1,0:T(8,128)(2,1)S(1)}, u32[]{:S(2)}, u32[]{:S(2)}) collective-permute-start(s16[1,800,128]{2,1,0:T(8,128)(2,1)} %get-tuple-element.48), channel_id=1, source_target_pairs={{0,32},{4,36},{8,40},{12,44},{16,48},{20,52},{24,56},{28,60},{32,0... | collective-permute-start | bytes 614408 | tf_op jit(solution)/shard_map/ppermute | solution.py:486
  195.3 1.8 collective-permute-start.14
  197.2 5.5 %collective-permute-done.13.two_ref = s16[1,800,128]{2,1,0:T(8,128)(2,1)S(1)} collective-permute-done((s16[1,800,128]{2,1,0:T(8,128)(2,1)}, s16[1,800,128]{2,1,0:T(8,128)(2,1)S(1)}, u32[]{:S(2)}, u32[]{:S(2)}) %collective-permute-start.13) | collective-permute-done | bytes 204832 | tf_op jit(solution)/shard_map/ppermute | solution.py:486
  203.5 1.1 copy-done.14
  204.6 0.9 copy-done.18
  205.5 5.6 %pair.1 = f32[24,24,128]{2,1,0:T(8,128)S(1)} custom-call(s32[2]{0:T(128)S(1)} %pad_add_fusion.place_ref, s16[4,800,128]{2,1,0:T(8,128)(2,1)S(1)} %copy-done.14, s16[1,800,128]{2,1,0:T(8,128)(2,1)S(1)} %collective-permute-done.12.one_ref, s16[1,800,128]{2,1,0:T(8,128)(2,1)S(1)} %copy-done.18, s16[1,800,128]{2,1,0:T(8,128)(2,1)} %collective-permute-done.14.three_ref, ...), custom_call_target="tpu_custom_call" | custom-call | tf_op jit(solution)/shard_map/pair/pallas_call | solution.py:373
  211.3 1.0 collective-permute-start.16
  213.1 1.8 collective-permute-start.18
  216.3 11.2 %collective-permute-start.19 = (f32[24,24]{1,0:T(8,128)S(1)}, f32[24,24]{1,0:T(8,128)S(1)}, u32[]{:S(2)}, u32[]{:S(2)}) collective-permute-start(f32[24,24]{1,0:T(8,128)S(1)} %add_add_fusion.3), channel_id=1, source_target_pairs={{0,8},{4,12},{8,0},{12,4},{16,24},{20,28},{24,16},{28,20},{32,40},... | collective-permute-start | bytes 6920 | tf_op jit(solution)/shard_map/ppermute | solution.py:425
  227.5 7.0 %collective-permute-start.20 = (f32[24,24]{1,0:T(8,128)S(1)}, f32[24,24]{1,0:T(8,128)S(1)}, u32[]{:S(2)}, u32[]{:S(2)}) collective-permute-start(f32[24,24]{1,0:T(8,128)S(1)} %add_add_fusion.3), channel_id=1, source_target_pairs={{0,4},{4,8},{8,12},{12,0},{16,20},{20,24},{24,28},{28,16},{32,36},... | collective-permute-start | bytes 6920 | tf_op jit(solution)/shard_map/ppermute | solution.py:425
  235.3 2.3 collective-permute-done.21
  238.1 1.5 collective-permute-start.23
  239.6 1.4 collective-permute-start.24
  242.2 3.5 %collective-permute-start.25 = (f32[24,24]{1,0:T(8,128)S(1)}, f32[24,24]{1,0:T(8,128)S(1)}, u32[]{:S(2)}, u32[]{:S(2)}) collective-permute-start(f32[24,24]{1,0:T(8,128)S(1)} %add_add_fusion.1), channel_id=1, source_target_pairs={{0,32},{4,36},{8,40},{12,44},{16,48},{20,52},{24,56},{28,60},{32,0... | collective-permute-start | bytes 6920 | tf_op jit(solution)/shard_map/ppermute | solution.py:425
  245.7 2.5 collective-permute-start.26
  248.1 1.1 collective-permute-start.27
  249.3 1.1 collective-permute-done.26
  250.3 1.5 collective-permute-done.27
  (77 shorter events, 16.4 us)
Async XLA Ops:
  0.0 1.8 copy-start
  1.9 0.7 copy-start.19
  51.3 1.3 copy-start.4
  51.3 27.3 %collective-permute-start = (bf16[64,72,128]{2,1,0:T(8,128)(2,1)S(1)}, bf16[64,72,128]{2,1,0:T(8,128)(2,1)S(1)}, u32[]{:S(2)}, u32[]{:S(2)}) collective-permute-start(bf16[64,72,128]{2,1,0:T(8,128)(2,1)S(1)} %all_to_all.5.own_ref), channel_id=1, source_target_pairs={{0,64},{64,128},{128,192},{192,0},{1,65},{65,129},{129,193},{193,1... | collective-permute-start | bytes 3538952 | tf_op jit(solution)/shard_map/ppermute | solution.py:460
  52.6 26.9 %collective-permute-start.1 = (bf16[64,72,128]{2,1,0:T(8,128)(2,1)S(1)}, bf16[64,72,128]{2,1,0:T(8,128)(2,1)S(1)}, u32[]{:S(2)}, u32[]{:S(2)}) collective-permute-start(bf16[64,72,128]{2,1,0:T(8,128)(2,1)S(1)} %all_to_all.5.own_ref), channel_id=1, source_target_pairs={{0,192},{64,0},{128,64},{192,128},{1,193},{65,1},{129,65},{193,129... | collective-permute-start | bytes 3538952 | tf_op jit(solution)/shard_map/ppermute | solution.py:461
  78.6 1.2 copy-start.7
  79.5 29.0 %collective-permute-start.2 = (bf16[32,72,128]{2,1,0:T(8,128)(2,1)}, bf16[32,72,128]{2,1,0:T(8,128)(2,1)S(1)}, u32[]{:S(2)}, u32[]{:S(2)}) collective-permute-start(bf16[32,72,128]{2,1,0:T(8,128)(2,1)} %slice.13), channel_id=1, source_target_pairs={{0,64},{64,128},{128,192},{192,0},{1,65},{65,129},{129,193},{193,1... | collective-permute-start | bytes 1769480 | tf_op jit(solution)/shard_map/ppermute | solution.py:462
  79.8 1.3 copy-start.10
  81.2 27.4 %collective-permute-start.3 = (bf16[32,72,128]{2,1,0:T(8,128)(2,1)}, bf16[32,72,128]{2,1,0:T(8,128)(2,1)}, u32[]{:S(2)}, u32[]{:S(2)}) collective-permute-start(bf16[32,72,128]{2,1,0:T(8,128)(2,1)} %slice.14), channel_id=1, source_target_pairs={{0,192},{64,0},{128,64},{192,128},{1,193},{65,1},{129,65},{193,129... | collective-permute-start | bytes 1769480 | tf_op jit(solution)/shard_map/ppermute | solution.py:463
  92.6 2.5 copy-start.1
  95.0 1.3 copy-start.5
  96.3 1.3 copy-start.8
  97.6 1.3 copy-start.11
  98.9 24.2 %copy-start.3 = (bf16[40,128,512]{1,2,0:T(8,128)(2,1)S(1)}, bf16[40,128,512]{1,2,0:T(8,128)(2,1)}, u32[]{:S(2)}) copy-start(bf16[40,128,512]{1,2,0:T(8,128)(2,1)} %copy.8) | copy-start | bytes 15728644
  98.9 24.2 %copy-start.6 = (bf16[64,72,128]{2,1,0:T(8,128)(2,1)S(1)}, bf16[64,72,128]{2,1,0:T(8,128)(2,1)}, u32[]{:S(2)}) copy-start(bf16[64,72,128]{2,1,0:T(8,128)(2,1)} %copy-done.4) | copy-start | bytes 3538948
  98.9 24.2 %copy-start.9 = (bf16[64,72,128]{2,1,0:T(8,128)(2,1)S(1)}, bf16[64,72,128]{2,1,0:T(8,128)(2,1)}, u32[]{:S(2)}) copy-start(bf16[64,72,128]{2,1,0:T(8,128)(2,1)} %copy-done.7) | copy-start | bytes 3538948
  98.9 24.2 %copy-start.12 = (bf16[64,72,128]{2,1,0:T(8,128)(2,1)S(1)}, bf16[64,72,128]{2,1,0:T(8,128)(2,1)}, u32[]{:S(2)}) copy-start(bf16[64,72,128]{2,1,0:T(8,128)(2,1)} %copy-done.10) | copy-start | bytes 3538948
  108.6 2.5 copy-start.2
  120.4 17.7 %collective-permute-start.4 = (s16[800,512]{1,0:T(8,128)(2,1)S(1)}, s16[800,512]{1,0:T(8,128)(2,1)S(1)}, u32[]{:S(2)}, u32[]{:S(2)}) collective-permute-start(s16[800,512]{1,0:T(8,128)(2,1)S(1)} %get-tuple-element.34), channel_id=1, source_target_pairs={{0,1},{1,0},{2,3},{3,2},{4,5},{5,4},{6,7},{7,6},{8,9},{9,8},{10,11... | collective-permute-start | bytes 2457608 | tf_op jit(solution)/shard_map/ppermute | solution.py:431
  121.1 17.5 %collective-permute-start.5 = (s16[800,512]{1,0:T(8,128)(2,1)S(1)}, s16[800,512]{1,0:T(8,128)(2,1)S(1)}, u32[]{:S(2)}, u32[]{:S(2)}) collective-permute-start(s16[800,512]{1,0:T(8,128)(2,1)S(1)} %get-tuple-element.35), channel_id=1, source_target_pairs={{0,3},{3,0},{1,2},{2,1},{4,7},{7,4},{5,6},{6,5},{8,11},{11,8},{9,1... | collective-permute-start | bytes 2457608 | tf_op jit(solution)/shard_map/ppermute | solution.py:431
  137.1 35.0 %collective-permute-start.8 = (s16[800,512]{1,0:T(8,128)(2,1)S(1)}, s16[800,512]{1,0:T(8,128)(2,1)S(1)}, u32[]{:S(2)}, u32[]{:S(2)}) collective-permute-start(s16[800,512]{1,0:T(8,128)(2,1)S(1)} %get-tuple-element.41), channel_id=1, source_target_pairs={{0,1},{1,0},{2,3},{3,2},{4,5},{5,4},{6,7},{7,6},{8,9},{9,8},{10,11... | collective-permute-start | bytes 2457608 | tf_op jit(solution)/shard_map/ppermute | solution.py:431
  137.4 34.7 %collective-permute-start.9 = (s16[800,512]{1,0:T(8,128)(2,1)S(1)}, s16[800,512]{1,0:T(8,128)(2,1)S(1)}, u32[]{:S(2)}, u32[]{:S(2)}) collective-permute-start(s16[800,512]{1,0:T(8,128)(2,1)S(1)} %get-tuple-element.42), channel_id=1, source_target_pairs={{0,3},{3,0},{1,2},{2,1},{4,7},{7,4},{5,6},{6,5},{8,11},{11,8},{9,1... | collective-permute-start | bytes 2457608 | tf_op jit(solution)/shard_map/ppermute | solution.py:431
  140.5 25.2 %collective-permute-start.6 = (s16[400,512]{1,0:T(8,128)(2,1)S(1)}, s16[400,512]{1,0:T(8,128)(2,1)S(1)}, u32[]{:S(2)}, u32[]{:S(2)}) collective-permute-start(s16[400,512]{1,0:T(8,128)(2,1)S(1)} %get-tuple-element.37), channel_id=1, source_target_pairs={{0,3},{3,0},{1,2},{2,1},{4,7},{7,4},{5,6},{6,5},{8,11},{11,8},{9,1... | collective-permute-start | bytes 1228808 | tf_op jit(solution)/shard_map/ppermute | solution.py:431
  142.6 23.1 %collective-permute-start.7 = (s16[400,512]{1,0:T(8,128)(2,1)S(1)}, s16[400,512]{1,0:T(8,128)(2,1)S(1)}, u32[]{:S(2)}, u32[]{:S(2)}) collective-permute-start(s16[400,512]{1,0:T(8,128)(2,1)S(1)} %get-tuple-element.38), channel_id=1, source_target_pairs={{0,1},{1,0},{2,3},{3,2},{4,5},{5,4},{6,7},{7,6},{8,9},{9,8},{10,11... | collective-permute-start | bytes 1228808 | tf_op jit(solution)/shard_map/ppermute | solution.py:431
  167.7 35.8 %collective-permute-start.15 = (s16[800,512]{1,0:T(8,128)(2,1)}, s16[800,512]{1,0:T(8,128)(2,1)}, u32[]{:S(2)}, u32[]{:S(2)}) collective-permute-start(s16[800,512]{1,0:T(8,128)(2,1)} %finish_virt.1), channel_id=1, source_target_pairs={{0,0},{1,1},{2,2},{3,3},{4,64},{5,65},{6,66},{7,67},{8,128},{9,129... | collective-permute-start | bytes 2457608 | tf_op jit(solution)/shard_map/ppermute | solution.py:477
  174.8 1.2 copy-start.15
  176.0 8.2 %collective-permute-start.10 = (s16[400,512]{1,0:T(8,128)(2,1)}, s16[400,512]{1,0:T(8,128)(2,1)S(1)}, u32[]{:S(2)}, u32[]{:S(2)}) collective-permute-start(s16[400,512]{1,0:T(8,128)(2,1)} %get-tuple-element.44), channel_id=1, source_target_pairs={{0,3},{3,0},{1,2},{2,1},{4,7},{7,4},{5,6},{6,5},{8,11},{11,8},{9,1... | collective-permute-start | bytes 1228808 | tf_op jit(solution)/shard_map/ppermute | solution.py:431
  177.9 7.1 %collective-permute-start.11 = (s16[400,512]{1,0:T(8,128)(2,1)}, s16[400,512]{1,0:T(8,128)(2,1)}, u32[]{:S(2)}, u32[]{:S(2)}) collective-permute-start(s16[400,512]{1,0:T(8,128)(2,1)} %get-tuple-element.45), channel_id=1, source_target_pairs={{0,1},{1,0},{2,3},{3,2},{4,5},{5,4},{6,7},{7,6},{8,9},{9,8},{10,11... | collective-permute-start | bytes 1228808 | tf_op jit(solution)/shard_map/ppermute | solution.py:431
  185.1 1.4 copy-start.16
  189.4 0.9 copy-start.13
  190.3 6.9 %collective-permute-start.12 = (s16[1,800,128]{2,1,0:T(8,128)(2,1)}, s16[1,800,128]{2,1,0:T(8,128)(2,1)S(1)}, u32[]{:S(2)}, u32[]{:S(2)}) collective-permute-start(s16[1,800,128]{2,1,0:T(8,128)(2,1)} %get-tuple-element.49), channel_id=1, source_target_pairs={{0,16},{4,20},{8,24},{12,28},{16,32},{20,36},{24,40},{28,44},{32,4... | collective-permute-start | bytes 614408 | tf_op jit(solution)/shard_map/ppermute | solution.py:486
  192.4 10.4 %collective-permute-start.13 = (s16[1,800,128]{2,1,0:T(8,128)(2,1)}, s16[1,800,128]{2,1,0:T(8,128)(2,1)S(1)}, u32[]{:S(2)}, u32[]{:S(2)}) collective-permute-start(s16[1,800,128]{2,1,0:T(8,128)(2,1)} %get-tuple-element.48), channel_id=1, source_target_pairs={{0,32},{4,36},{8,40},{12,44},{16,48},{20,52},{24,56},{28,60},{32,0... | collective-permute-start | bytes 614408 | tf_op jit(solution)/shard_map/ppermute | solution.py:486
  195.3 8.2 %collective-permute-start.14 = (s16[1,800,128]{2,1,0:T(8,128)(2,1)S(1)}, s16[1,800,128]{2,1,0:T(8,128)(2,1)}, u32[]{:S(2)}, u32[]{:S(2)}) collective-permute-start(s16[1,800,128]{2,1,0:T(8,128)(2,1)S(1)} %get-tuple-element.47), channel_id=1, source_target_pairs={{0,48},{4,52},{8,56},{12,60},{16,0},{20,4},{24,8},{28,12},{32,16},... | collective-permute-start | bytes 614408 | tf_op jit(solution)/shard_map/ppermute | solution.py:486
  202.8 0.7 copy-start.17
  203.5 1.1 copy-start.14
  204.6 0.9 copy-start.18
  211.3 4.4 %collective-permute-start.16 = (f32[24,24]{1,0:T(8,128)S(1)}, f32[24,24]{1,0:T(8,128)S(1)}, u32[]{:S(2)}, u32[]{:S(2)}) collective-permute-start(f32[24,24]{1,0:T(8,128)S(1)} %reduce_sum.9), channel_id=1, source_target_pairs={{0,2},{1,3},{2,0},{3,1},{4,6},{5,7},{6,4},{7,5},{8,10},{9,11},{10,... | collective-permute-start | bytes 6920 | tf_op jit(solution)/shard_map/ppermute | solution.py:425
  212.3 4.0 %collective-permute-start.17 = (f32[24,24]{1,0:T(8,128)S(1)}, f32[24,24]{1,0:T(8,128)S(1)}, u32[]{:S(2)}, u32[]{:S(2)}) collective-permute-start(f32[24,24]{1,0:T(8,128)S(1)} %reduce_sum.9), channel_id=1, source_target_pairs={{0,1},{1,2},{2,3},{3,0},{4,5},{5,6},{6,7},{7,4},{8,9},{9,10},{10,1... | collective-permute-start | bytes 6920 | tf_op jit(solution)/shard_map/ppermute | solution.py:425
  213.1 3.1 %collective-permute-start.18 = (f32[24,24]{1,0:T(8,128)S(1)}, f32[24,24]{1,0:T(8,128)S(1)}, u32[]{:S(2)}, u32[]{:S(2)}) collective-permute-start(f32[24,24]{1,0:T(8,128)S(1)} %reduce_sum.9), channel_id=1, source_target_pairs={{0,3},{1,0},{2,1},{3,2},{4,7},{5,4},{6,5},{7,6},{8,11},{9,8},{10,9... | collective-permute-start | bytes 6920 | tf_op jit(solution)/shard_map/ppermute | solution.py:425
  216.3 18.2 %collective-permute-start.19 = (f32[24,24]{1,0:T(8,128)S(1)}, f32[24,24]{1,0:T(8,128)S(1)}, u32[]{:S(2)}, u32[]{:S(2)}) collective-permute-start(f32[24,24]{1,0:T(8,128)S(1)} %add_add_fusion.3), channel_id=1, source_target_pairs={{0,8},{4,12},{8,0},{12,4},{16,24},{20,28},{24,16},{28,20},{32,40},... | collective-permute-start | bytes 6920 | tf_op jit(solution)/shard_map/ppermute | solution.py:425
  227.5 7.8 %collective-permute-start.20 = (f32[24,24]{1,0:T(8,128)S(1)}, f32[24,24]{1,0:T(8,128)S(1)}, u32[]{:S(2)}, u32[]{:S(2)}) collective-permute-start(f32[24,24]{1,0:T(8,128)S(1)} %add_add_fusion.3), channel_id=1, source_target_pairs={{0,4},{4,8},{8,12},{12,0},{16,20},{20,24},{24,28},{28,16},{32,36},... | collective-permute-start | bytes 6920 | tf_op jit(solution)/shard_map/ppermute | solution.py:425
  234.5 3.1 %collective-permute-start.21 = (f32[24,24]{1,0:T(8,128)S(1)}, f32[24,24]{1,0:T(8,128)S(1)}, u32[]{:S(2)}, u32[]{:S(2)}) collective-permute-start(f32[24,24]{1,0:T(8,128)S(1)} %add_add_fusion.3), channel_id=1, source_target_pairs={{0,12},{4,0},{8,4},{12,8},{16,28},{20,16},{24,20},{28,24},{32,44},... | collective-permute-start | bytes 6920 | tf_op jit(solution)/shard_map/ppermute | solution.py:425
  237.6 4.1 %collective-permute-start.22 = (f32[24,24]{1,0:T(8,128)S(1)}, f32[24,24]{1,0:T(8,128)S(1)}, u32[]{:S(2)}, u32[]{:S(2)}) collective-permute-start(f32[24,24]{1,0:T(8,128)S(1)} %add_add_fusion.2), channel_id=1, source_target_pairs={{0,128},{64,192},{128,0},{192,64},{1,129},{65,193},{129,1},{193,65... | collective-permute-start | bytes 6920 | tf_op jit(solution)/shard_map/ppermute | solution.py:425
  238.1 4.0 %collective-permute-start.23 = (f32[24,24]{1,0:T(8,128)S(1)}, f32[24,24]{1,0:T(8,128)S(1)}, u32[]{:S(2)}, u32[]{:S(2)}) collective-permute-start(f32[24,24]{1,0:T(8,128)S(1)} %add_add_fusion.2), channel_id=1, source_target_pairs={{0,64},{64,128},{128,192},{192,0},{1,65},{65,129},{129,193},{193,1... | collective-permute-start | bytes 6920 | tf_op jit(solution)/shard_map/ppermute | solution.py:425
  239.6 2.5 %collective-permute-start.24 = (f32[24,24]{1,0:T(8,128)S(1)}, f32[24,24]{1,0:T(8,128)S(1)}, u32[]{:S(2)}, u32[]{:S(2)}) collective-permute-start(f32[24,24]{1,0:T(8,128)S(1)} %add_add_fusion.2), channel_id=1, source_target_pairs={{0,192},{64,0},{128,64},{192,128},{1,193},{65,1},{129,65},{193,129... | collective-permute-start | bytes 6920 | tf_op jit(solution)/shard_map/ppermute | solution.py:425
  242.2 7.1 %collective-permute-start.25 = (f32[24,24]{1,0:T(8,128)S(1)}, f32[24,24]{1,0:T(8,128)S(1)}, u32[]{:S(2)}, u32[]{:S(2)}) collective-permute-start(f32[24,24]{1,0:T(8,128)S(1)} %add_add_fusion.1), channel_id=1, source_target_pairs={{0,32},{4,36},{8,40},{12,44},{16,48},{20,52},{24,56},{28,60},{32,0... | collective-permute-start | bytes 6920 | tf_op jit(solution)/shard_map/ppermute | solution.py:425
  245.7 4.7 %collective-permute-start.26 = (f32[24,24]{1,0:T(8,128)S(1)}, f32[24,24]{1,0:T(8,128)S(1)}, u32[]{:S(2)}, u32[]{:S(2)}) collective-permute-start(f32[24,24]{1,0:T(8,128)S(1)} %add_add_fusion.1), channel_id=1, source_target_pairs={{0,16},{4,20},{8,24},{12,28},{16,32},{20,36},{24,40},{28,44},{32,4... | collective-permute-start | bytes 6920 | tf_op jit(solution)/shard_map/ppermute | solution.py:425
  248.1 3.7 %collective-permute-start.27 = (f32[24,24]{1,0:T(8,128)S(1)}, f32[24,24]{1,0:T(8,128)S(1)}, u32[]{:S(2)}, u32[]{:S(2)}) collective-permute-start(f32[24,24]{1,0:T(8,128)S(1)} %add_add_fusion.1), channel_id=1, source_target_pairs={{0,48},{4,52},{8,56},{12,60},{16,0},{20,4},{24,8},{28,12},{32,16},... | collective-permute-start | bytes 6920 | tf_op jit(solution)/shard_map/ppermute | solution.py:425
  (3 other events, 2.0 us)

commit v4 on v3

--- a/solution.py
+++ b/solution.py
@@ -142,43 +142,40 @@
         put_levels(send_ref, plan, 2 * plan.blocks, level_ref)
 
 
-def virt_near_body(meta_ref, own_ref, prev_ref, next_ref, green_ref, acc_ref):
+def virt_body(meta_ref, place_ref, *rest, plan):
+    sources, (keep_ref, send0_ref, send1_ref) = rest[:6], rest[6:9]
+    refs, (acc_ref, level_ref, sems) = rest[9:15], rest[15:]
+    loads = [pltpu.make_async_copy(src, dst, sems.at[i]) for i, (src, dst) in enumerate(zip(sources, refs))]
+    for load in loads:
+        load.start()
     acc_ref[...] = jnp.zeros(acc_ref.shape, F32)
-
-    @pl.loop(0, OWNERS // 2)
-    def _(step):
-        for source in (step * 2, step * 2 + 1):
-            for slot in range(CAP):
-                span = slice(slot * QUARTER, (slot + 1) * QUARTER)
-                tile = jnp.concatenate([ref[source, span, :] for ref in (own_ref, prev_ref, next_ref)], axis=0)
-                aux = meta_ref[source, 2 * slot]
-                kept = meta_ref[source, 2 * slot + 1]
-                acc_ref[aux] += jnp.dot(tile, green_ref[kept], preferred_element_type=F32)
-
-
-def virt_far_body(
-    meta_ref, place_ref, far_a_ref, far_b_ref, green_ref, near_ref, keep_ref, send0_ref, send1_ref, acc_ref, level_ref, *, plan
-):
-    acc_ref[...] = jnp.zeros(acc_ref.shape, F32)
+    for load in loads:
+        load.wait()
+    green_ref = refs[5]
     half = OWNERS // 2
-    for part, far_ref in enumerate((far_a_ref, far_b_ref)):
+    for part in range(2):
 
         @pl.loop(0, half // 2)
         def _(step):
             for local in (step * 2, step * 2 + 1):
                 source = part * half + local
                 for slot in range(CAP):
-                    tile = far_ref[local, slot * QUARTER : (slot + 1) * QUARTER, :]
+                    span = slice(slot * QUARTER, (slot + 1) * QUARTER)
+                    parts = [ref[source, span, :] for ref in refs[:3]] + [refs[3 + part][local, span, :]]
                     aux = meta_ref[source, 2 * slot]
                     kept = meta_ref[source, 2 * slot + 1]
+                    tile = jnp.concatenate(parts, axis=0)
                     acc_ref[aux] += jnp.dot(tile, green_ref[kept], preferred_element_type=F32)
 
+    split_pieces(place_ref, plan, piece_rows(acc_ref), keep_ref, (send0_ref, send1_ref), level_ref)
+
+
+def piece_rows(acc_ref):
     def rows_of(first, piece):
-        at = [pl.multiple_of(quarter * QUARTER + piece * 8, 8) for quarter in range(3)]
-        parts = [near_ref[first, pl.ds(row, 8), :] for row in at]
-        return jnp.concatenate(parts + [acc_ref[first, pl.ds(at[0], 8), :]], axis=0)
-
-    split_pieces(place_ref, plan, rows_of, keep_ref, (send0_ref, send1_ref), level_ref)
+        at = [pl.multiple_of(quarter * QUARTER + piece * 8, 8) for quarter in range(4)]
+        return jnp.concatenate([acc_ref[first, pl.ds(row, 8), :] for row in at], axis=0)
+
+    return rows_of
 
 
 def occ_body(
@@ -212,16 +209,12 @@
                     lanes = slice(low * BS, (low + 1) * BS)
                     acc_ref[aux, :, lanes] += term[low * BS : (low + 1) * BS, :]
 
-    def rows_of(first, piece):
-        at = [pl.multiple_of(quarter * QUARTER + piece * 8, 8) for quarter in range(4)]
-        return jnp.concatenate([acc_ref[first, pl.ds(row, 8), :] for row in at], axis=0)
-
-    split_pieces(place_ref, plan, rows_of, keep_ref, (send0_ref, send1_ref), level_ref)
+    split_pieces(place_ref, plan, piece_rows(acc_ref), keep_ref, (send0_ref, send1_ref), level_ref)
 
 
 VMEM = pl.BlockSpec(memory_space=pltpu.VMEM)
 SMEM = pl.BlockSpec(memory_space=pltpu.SMEM)
-NEAR = (NP, 3 * QUARTER, WIDE)
+ANY = pl.BlockSpec(memory_space=pl.ANY)
 
 
 def step_shapes(plan):
@@ -233,27 +226,18 @@
     return pltpu.VMEM((plan.levels(2 * plan.blocks), WIDE), F32)
 
 
-def contract_virt_near(meta, quarters, green):
-    return pl.pallas_call(
-        virt_near_body,
-        in_specs=[SMEM] + [VMEM] * 4,
-        out_specs=VMEM,
-        out_shape=jax.ShapeDtypeStruct(NEAR, F32),
-        compiler_params=params(20),
-        name="virt_near",
-    )(meta, *quarters, green)
-
-
-def contract_virt_far(meta, place, fars, green, near, plan):
-    return pl.pallas_call(
-        functools.partial(virt_far_body, plan=plan),
-        in_specs=[SMEM] * 2 + [VMEM] * 4,
+def contract_virt(meta, place, quarters, green, plan):
+    operands = [*quarters, green]
+    return pl.pallas_call(
+        functools.partial(virt_body, plan=plan),
+        in_specs=[SMEM] * 2 + [ANY] * 6,
         out_specs=[VMEM] * 3,
         out_shape=step_shapes(plan),
-        scratch_shapes=[pltpu.VMEM((NP, QUARTER, WIDE), F32), level_scratch(plan)],
-        compiler_params=params(24),
-        name="virt_far",
-    )(meta, place, *fars, green, near)
+        scratch_shapes=[pltpu.VMEM(x.shape, x.dtype) for x in operands]
+        + [pltpu.VMEM((NP, BS, WIDE), F32), level_scratch(plan), pltpu.SemaphoreType.DMA((6,))],
+        compiler_params=params(55),
+        name="contract_virt",
+    )(meta, place, *operands)
 
 
 def contract_occ(meta, place, quarters, green, plan):
@@ -459,23 +443,24 @@
     half = OWNERS // 2
     prev = lax.ppermute(own, "row", rotate(ROWS, 1))
     nxt = lax.ppermute(own, "row", rotate(ROWS, -1))
+    prev, nxt, occ_blocks = after(prev, nxt, occ_blocks)
     far_a = lax.ppermute(prev[:half], "row", rotate(ROWS, 1))
     far_b = lax.ppermute(nxt[half:], "row", rotate(ROWS, -1))
-
-    prev, nxt, occ_blocks = after(prev, nxt, occ_blocks)
-    v_near = contract_virt_near(meta, (own, prev, nxt), virt_blocks)
-    v_keep, v0, v1 = contract_virt_far(meta, place, (far_a, far_b), virt_blocks, v_near, plan)
+    quarters = (own, prev, nxt, far_a, far_b)
+
+    v_keep, v0, v1 = contract_virt(meta, place, quarters, virt_blocks, plan)
     v_got = layer_swap(v0, v1, FIRST)
     occ_blocks, v_keep = after(occ_blocks, v_keep)
-    o_keep, o0, o1 = contract_occ(meta, place, (own, prev, nxt, far_a, far_b), occ_blocks, plan)
+    o_keep, o0, o1 = contract_occ(meta, place, quarters, occ_blocks, plan)
     o_got = layer_swap(o0, o1, FIRST)
     v_keep, o_keep = after(v_keep, o_keep)
     v_left, v0, v1 = halve(place, v_keep, *v_got, plan, "halve_virt")
+    v0, v1, *o_got = after(v0, v1, *o_got)
     v_got = layer_swap(v0, v1, SECOND)
+    o_left, o0, o1 = halve(place, o_keep, *o_got, plan, "halve_occ")
+    o_left, *v_got = after(o_left, *v_got)
     virt = finish(v_left, *v_got, plan, False, "finish_virt")
-    virt, o_keep = after(virt, o_keep)
     virt = lax.ppermute(virt, ALL, SWAP)
-    o_left, o0, o1 = halve(place, o_keep, *o_got, plan, "halve_occ")
     o_got = layer_swap(o0, o1, SECOND)
     occ = finish(o_left, *o_got, plan, True, "finish_occ")
 

time: 254 us -> 251 us (0.988)
  starting transfers between devices: 57.6 us -> 64.3 us
  local copies, waits for them, and re-layouts: 30.8 us -> 24.5 us
  waiting for transfers between devices: 67.9 us -> 62.8 us
    unnamed x46 -> x36, local copies, waits for them, and re-layouts: 20.2 us -> 11.8 us
    ppermute x1, waiting for transfers between devices: 0.01 us -> 7.09 us  [on_device(): far_a = lax.ppermute(prev[:half], 'row', rotate(ROWS, 1))]
    ppermute x4, waiting for transfers between devices: 29.4 us -> 22.3 us  [layer_swap(): lax.ppermute(send0, 'layer', perms[0])]
    ppermute x1, waiting for transfers between devices: 23.5 us -> 16.9 us  [on_device(): prev = lax.ppermute(own, 'row', rotate(ROWS, 1))]
    ppermute x1, starting transfers between devices: 4.44 us -> 9.76 us  [on_device(): virt = lax.ppermute(virt, ALL, SWAP)]
    pallas_call x2 -> x1, Pallas kernels: 19 us -> 18.4 us  [contract_virt(): pl.pallas_call(functools.partial(virt_body, plan=plan), in_specs=[SMEM] *...]
  transfers between devices with their start and end apart: 28 -> 28, of which waited for: 16 -> 18; matrix products, arithmetic and copies ran while one was open for 5% -> 5% of each run, Pallas kernels for 13% -> 9%
where the time goes in v4:
time: 251 us; the launch traced here: 249 us
  starting transfers between devices  64.3 us (26%)
  waiting for transfers between devices  62.8 us (25%)
  Pallas kernels  50.9 us (20%)
  blocking collectives  43.5 us (17%)
  local copies, waits for them, and re-layouts  24.5 us (10%)
  other arithmetic  2.98 us (1%)
    all_to_all x1, blocking collectives, on_device(): own = lax.all_to_all(send, ('col', 'layer'), 0, 0, tiled=True)  43.5 us
    ppermute x12, starting transfers between devices, tree_sum(): one, two, three = [lax.ppermute(values, axis, perm) for perm in perms]  34.3 us
    ppermute x4, waiting for transfers between devices, layer_swap(): lax.ppermute(send0, 'layer', perms[0])  22.3 us
    pallas_call x1, Pallas kernels, contract_virt(): pl.pallas_call(functools.partial(virt_body, plan=plan), in_specs=[SMEM] *...  18.4 us
    ppermute x1, waiting for transfers between devices, on_device(): prev = lax.ppermute(own, 'row', rotate(ROWS, 1))  16.9 us
    pallas_call x1, Pallas kernels, contract_occ(): pl.pallas_call(functools.partial(occ_body, plan=plan), in_specs=[SMEM] *...  15 us
    unnamed x36, local copies, waits for them, and re-layouts  11.8 us
    ppermute x1, starting transfers between devices, on_device(): virt = lax.ppermute(virt, ALL, SWAP)  9.76 us
  transfers between devices with their start and end apart: 28, of which 18 were waited for; matrix products, arithmetic and copies ran while one was open for 5% of the time, Pallas kernels for 9%

profile of v4, /device:TPU:1, one launch (start us, length us, event | category | flops | bytes accessed | tf_op | source)
XLA Modules:
  0.0 249.1 jit_solution(9349377157409975702)
XLA Ops:
  0.0 1.8 copy-done
  4.5 3.3 %build_send.1 = bf16[64,72,128]{2,1,0:T(8,128)(2,1)S(1)} custom-call(s32[88]{0:T(128)S(1)} %copy-done.12, s32[88]{0:T(128)S(1)} %copy-done.13, s32[88]{0:T(128)S(1)} %copy-done.14, s32[88]{0:T(128)S(1)} %copy-done.15, bf16[88,32,128]{2,1,0:T(8,128)(2,1)S(1)} %constant_dynamic-slice_fusion.3.tiles_ref), custom_call_target="tpu_custom_call" | custom-call | tf_op jit(solution)/shard_map/build_send/pallas_call | solution.py:113
  7.9 43.5 %all_to_all.5.rest_0_.own_ref = bf16[64,72,128]{2,1,0:T(8,128)(2,1)} all-to-all(bf16[64,72,128]{2,1,0:T(8,128)(2,1)S(1)} %build_send.1), channel_id=1, replica_groups=mesh['row'=4,'col'=16,'layer'=4] {'col','layer'}, dimensions={0} | all-to-all | bytes 2359296 | tf_op jit(solution)/shard_map/all_to_all | solution.py:438
  51.4 1.3 collective-permute-start
  52.7 1.4 collective-permute-start.1
  54.1 7.9 %copy.8 = bf16[40,128,512]{1,2,0:T(8,128)(2,1)} copy(bf16[40,128,512]{2,1,0:T(8,128)(2,1)} %bitcast.14) | data formatting | bytes 10485760 | tf_op jit(solution)/shard_map/reshape | solution.py:441
  62.1 16.9 %collective-permute-done.rest_1_.prev_ref = bf16[64,72,128]{2,1,0:T(8,128)(2,1)} collective-permute-done((bf16[64,72,128]{2,1,0:T(8,128)(2,1)}, bf16[64,72,128]{2,1,0:T(8,128)(2,1)}, u32[]{:S(2)}, u32[]{:S(2)}) %collective-permute-start) | collective-permute-done | bytes 1179680 | tf_op jit(solution)/shard_map/ppermute | solution.py:444
  79.0 1.9 slice.10
  81.9 1.9 slice.11
  83.9 1.7 collective-permute-start.3
  86.2 1.5 slice_convert_fusion
  87.7 7.1 %collective-permute-done.2.rest_3_.far_a_ref = bf16[32,72,128]{2,1,0:T(8,128)(2,1)S(1)} collective-permute-done((bf16[32,72,128]{2,1,0:T(8,128)(2,1)}, bf16[32,72,128]{2,1,0:T(8,128)(2,1)S(1)}, u32[]{:S(2)}, u32[]{:S(2)}) %collective-permute-start.2) | collective-permute-done | bytes 589856 | tf_op jit(solution)/shard_map/ppermute | solution.py:447
  94.8 1.2 collective-permute-done.3.rest_4_.far_b_ref
  96.1 18.4 %contract_virt.1 = (f32[2,2,12,32,512]{4,3,2,1,0:T(8,128)}, s16[800,512]{1,0:T(8,128)(2,1)}, s16[800,512]{1,0:T(8,128)(2,1)}) custom-call(s32[64,4]{1,0:T(8,128)} %bitcast.12, s32[3]{0:T(128)} %pad_add_fusion.1.place_ref, bf16[64,72,128]{2,1,0:T(8,128)(2,1)} %all_to_all.5.rest_0_.own_ref, bf16[64,72,128]{2,1,0:T(8,128)(2,1)} %collective-permute-done.rest_1_.prev_ref, ...), custom_call_target="tpu_custom_call" | custom-call | tf_op jit(solution)/shard_map/contract_virt/pallas_call | solution.py:231
  114.9 2.1 collective-permute-start.5
  118.0 15.0 %contract_occ.1 = (f32[2,2,12,32,512]{4,3,2,1,0:T(8,128)S(1)}, s16[800,512]{1,0:T(8,128)(2,1)S(1)}, s16[800,512]{1,0:T(8,128)(2,1)S(1)}) custom-call(s32[64,4]{1,0:T(8,128)S(1)} %bitcast.13, s32[3]{0:T(128)S(1)} %copy-done.11, bf16[64,72,128]{2,1,0:T(8,128)(2,1)} %all_to_all.5.rest_0_.own_ref, bf16[64,72,128]{2,1,0:T(8,128)(2,1)} %collective-permute-done.rest_1_.prev_ref, ...), custom_call_target="tpu_custom_call" | custom-call | tf_op jit(solution)/shard_map/contract_occ/pallas_call | solution.py:244
  133.3 1.2 collective-permute-start.7
  134.5 1.8 halve_virt.1
  136.3 11.9 %collective-permute-done.6.got0_ref = s16[800,512]{1,0:T(8,128)(2,1)S(1)} collective-permute-done((s16[800,512]{1,0:T(8,128)(2,1)S(1)}, s16[800,512]{1,0:T(8,128)(2,1)S(1)}, u32[]{:S(2)}, u32[]{:S(2)}) %collective-permute-start.6) | collective-permute-done | bytes 819232 | tf_op jit(solution)/shard_map/ppermute | solution.py:415
  148.2 1.1 collective-permute-done.7.got1_ref
  149.3 1.8 collective-permute-start.8
  151.1 2.7 %halve_occ.1 = (f32[2,12,32,512]{3,2,1,0:T(8,128)S(1)}, s16[400,512]{1,0:T(8,128)(2,1)}, s16[400,512]{1,0:T(8,128)(2,1)}) custom-call(s32[3]{0:T(128)S(1)} %copy-done.11, f32[2,2,12,32,512]{4,3,2,1,0:T(8,128)S(1)} %get-tuple-element.38.keep_ref, s16[800,512]{1,0:T(8,128)(2,1)S(1)} %collective-permute-done.6.got0_ref, ...), custom_call_target="tpu_custom_call" | custom-call | tf_op jit(solution)/shard_map/halve_occ/pallas_call | solution.py:272
  153.8 1.2 copy-done.6
  154.9 4.0 %collective-permute-done.8.got0_ref = s16[400,512]{1,0:T(8,128)(2,1)S(1)} collective-permute-done((s16[400,512]{1,0:T(8,128)(2,1)S(1)}, s16[400,512]{1,0:T(8,128)(2,1)S(1)}, u32[]{:S(2)}, u32[]{:S(2)}) %collective-permute-start.8) | collective-permute-done | bytes 409632 | tf_op jit(solution)/shard_map/ppermute | solution.py:415
  158.9 1.9 finish_virt.1
  160.9 9.8 %collective-permute-start.15 = (s16[800,512]{1,0:T(8,128)(2,1)}, s16[800,512]{1,0:T(8,128)(2,1)}, u32[]{:S(2)}, u32[]{:S(2)}) collective-permute-start(s16[800,512]{1,0:T(8,128)(2,1)} %finish_virt.1), channel_id=1, source_target_pairs={{0,0},{1,1},{2,2},{3,3},{4,64},{5,65},{6,66},{7,67},{8,128},{9,129... | collective-permute-start | bytes 2457608 | tf_op jit(solution)/shard_map/ppermute | solution.py:463
  170.6 1.8 collective-permute-start.10
  172.5 6.4 %collective-permute-done.10.got0_ref = s16[400,512]{1,0:T(8,128)(2,1)S(1)} collective-permute-done((s16[400,512]{1,0:T(8,128)(2,1)}, s16[400,512]{1,0:T(8,128)(2,1)S(1)}, u32[]{:S(2)}, u32[]{:S(2)}) %collective-permute-start.10) | collective-permute-done | bytes 409632 | tf_op jit(solution)/shard_map/ppermute | solution.py:415
  179.6 1.4 copy-done.7
  181.0 2.1 finish_occ.1.own_ref
  184.8 2.6 %collective-permute-start.12 = (s16[1,800,128]{2,1,0:T(8,128)(2,1)}, s16[1,800,128]{2,1,0:T(8,128)(2,1)S(1)}, u32[]{:S(2)}, u32[]{:S(2)}) collective-permute-start(s16[1,800,128]{2,1,0:T(8,128)(2,1)} %get-tuple-element.59), channel_id=1, source_target_pairs={{0,16},{4,20},{8,24},{12,28},{16,32},{20,36},{24,40},{28,44},{32,4... | collective-permute-start | bytes 614408 | tf_op jit(solution)/shard_map/ppermute | solution.py:471
  187.5 2.4 collective-permute-start.13
  189.8 2.3 collective-permute-start.14
  192.2 5.3 %collective-permute-done.13.two_ref = s16[1,800,128]{2,1,0:T(8,128)(2,1)S(1)} collective-permute-done((s16[1,800,128]{2,1,0:T(8,128)(2,1)}, s16[1,800,128]{2,1,0:T(8,128)(2,1)S(1)}, u32[]{:S(2)}, u32[]{:S(2)}) %collective-permute-start.13) | collective-permute-done | bytes 204832 | tf_op jit(solution)/shard_map/ppermute | solution.py:471
  198.1 1.1 copy-done.2
  200.2 5.6 %pair.1 = f32[24,24,128]{2,1,0:T(8,128)S(1)} custom-call(s32[2]{0:T(128)S(1)} %pad_add_fusion.place_ref, s16[4,800,128]{2,1,0:T(8,128)(2,1)S(1)} %copy-done.2, s16[1,800,128]{2,1,0:T(8,128)(2,1)S(1)} %collective-permute-done.12.one_ref, s16[1,800,128]{2,1,0:T(8,128)(2,1)S(1)} %copy-done.10, s16[1,800,128]{2,1,0:T(8,128)(2,1)} %collective-permute-done.14.three_ref, ...), custom_call_target="tpu_custom_call" | custom-call | tf_op jit(solution)/shard_map/pair/pallas_call | solution.py:357
  206.2 1.2 collective-permute-start.17
  207.4 1.5 collective-permute-start.18
  208.9 1.2 collective-permute-done.16
  210.3 13.9 %collective-permute-start.19 = (f32[24,24]{1,0:T(8,128)S(1)}, f32[24,24]{1,0:T(8,128)S(1)}, u32[]{:S(2)}, u32[]{:S(2)}) collective-permute-start(f32[24,24]{1,0:T(8,128)S(1)} %add_add_fusion.3), channel_id=1, source_target_pairs={{0,8},{4,12},{8,0},{12,4},{16,24},{20,28},{24,16},{28,20},{32,40},... | collective-permute-start | bytes 6920 | tf_op jit(solution)/shard_map/ppermute | solution.py:409
  224.3 6.5 %collective-permute-start.20 = (f32[24,24]{1,0:T(8,128)S(1)}, f32[24,24]{1,0:T(8,128)S(1)}, u32[]{:S(2)}, u32[]{:S(2)}) collective-permute-start(f32[24,24]{1,0:T(8,128)S(1)} %add_add_fusion.3), channel_id=1, source_target_pairs={{0,4},{4,8},{8,12},{12,0},{16,20},{20,24},{24,28},{28,16},{32,36},... | collective-permute-start | bytes 6920 | tf_op jit(solution)/shard_map/ppermute | solution.py:409
  231.6 2.3 collective-permute-done.21
  233.9 2.2 collective-permute-start.23
  236.6 1.3 collective-permute-done.22
  238.9 4.6 %collective-permute-start.25 = (f32[24,24]{1,0:T(8,128)S(1)}, f32[24,24]{1,0:T(8,128)S(1)}, u32[]{:S(2)}, u32[]{:S(2)}) collective-permute-start(f32[24,24]{1,0:T(8,128)S(1)} %add_add_fusion.1), channel_id=1, source_target_pairs={{0,32},{4,36},{8,40},{12,44},{16,48},{20,52},{24,56},{28,60},{32,0... | collective-permute-start | bytes 6920 | tf_op jit(solution)/shard_map/ppermute | solution.py:409
  243.5 1.5 collective-permute-start.26
  245.0 2.1 collective-permute-start.27
  247.1 1.1 collective-permute-done.26
  (67 shorter events, 14.0 us)
Async XLA Ops:
  0.0 1.8 copy-start
  1.9 0.7 copy-start.12
  2.5 0.7 copy-start.13
  3.2 0.7 copy-start.14
  3.9 0.7 copy-start.15
  51.4 27.6 %collective-permute-start = (bf16[64,72,128]{2,1,0:T(8,128)(2,1)}, bf16[64,72,128]{2,1,0:T(8,128)(2,1)}, u32[]{:S(2)}, u32[]{:S(2)}) collective-permute-start(bf16[64,72,128]{2,1,0:T(8,128)(2,1)} %all_to_all.5.rest_0_.own_ref), channel_id=1, source_target_pairs={{0,64},{64,128},{128,192},{192,0},{1,65},{65,129},{129,193},{193,1... | collective-permute-start | bytes 3538952 | tf_op jit(solution)/shard_map/ppermute | solution.py:444
  52.7 26.3 %collective-permute-start.1 = (bf16[64,72,128]{2,1,0:T(8,128)(2,1)}, bf16[64,72,128]{2,1,0:T(8,128)(2,1)}, u32[]{:S(2)}, u32[]{:S(2)}) collective-permute-start(bf16[64,72,128]{2,1,0:T(8,128)(2,1)} %all_to_all.5.rest_0_.own_ref), channel_id=1, source_target_pairs={{0,192},{64,0},{128,64},{192,128},{1,193},{65,1},{129,65},{193,129... | collective-permute-start | bytes 3538952 | tf_op jit(solution)/shard_map/ppermute | solution.py:445
  81.0 13.9 %collective-permute-start.2 = (bf16[32,72,128]{2,1,0:T(8,128)(2,1)}, bf16[32,72,128]{2,1,0:T(8,128)(2,1)S(1)}, u32[]{:S(2)}, u32[]{:S(2)}) collective-permute-start(bf16[32,72,128]{2,1,0:T(8,128)(2,1)} %slice.10), channel_id=1, source_target_pairs={{0,64},{64,128},{128,192},{192,0},{1,65},{65,129},{129,193},{193,1... | collective-permute-start | bytes 1769480 | tf_op jit(solution)/shard_map/ppermute | solution.py:447
  83.9 12.2 %collective-permute-start.3 = (bf16[32,72,128]{2,1,0:T(8,128)(2,1)}, bf16[32,72,128]{2,1,0:T(8,128)(2,1)}, u32[]{:S(2)}, u32[]{:S(2)}) collective-permute-start(bf16[32,72,128]{2,1,0:T(8,128)(2,1)} %slice.11), channel_id=1, source_target_pairs={{0,192},{64,0},{128,64},{192,128},{1,193},{65,1},{129,65},{193,129... | collective-permute-start | bytes 1769480 | tf_op jit(solution)/shard_map/ppermute | solution.py:448
  94.8 1.2 copy-start.4
  96.0 20.9 %slice-start = ((s8[5242880]{0:T(1024)(128)(4,1)}), s8[4194304]{0:T(1024)(128)(4,1)S(1)}, s32[]{:S(2)}) async-start(s8[5242880]{0:T(1024)(128)(4,1)} %bitcast.9), calls=%async_computation.1 | async-start | bytes 8388608
  96.0 20.9 %slice-start.1 = ((s8[5242880]{0:T(1024)(128)(4,1)}), s8[1048576]{0:T(1024)(128)(4,1)S(1)}, s32[]{:S(2)}) async-start(s8[5242880]{0:T(1024)(128)(4,1)} %bitcast.9), calls=%async_computation.2 | async-start | bytes 2097152
  96.0 20.9 %copy-start.8 = (s32[64,1,4]{2,1,0:T(1,128)S(1)}, s32[64,1,4]{2,1,0:T(1,128)}, u32[]{:S(2)}) copy-start(s32[64,1,4]{2,1,0:T(1,128)} %slice_convert_fusion) | copy-start | bytes 3076
  96.0 20.9 %copy-start.11 = (s32[3]{0:T(128)S(1)}, s32[3]{0:T(128)}, u32[]{:S(2)}) copy-start(s32[3]{0:T(128)} %pad_add_fusion.1.place_ref) | copy-start | bytes 40
  114.5 20.0 %collective-permute-start.4 = (s16[800,512]{1,0:T(8,128)(2,1)}, s16[800,512]{1,0:T(8,128)(2,1)S(1)}, u32[]{:S(2)}, u32[]{:S(2)}) collective-permute-start(s16[800,512]{1,0:T(8,128)(2,1)} %get-tuple-element.40), channel_id=1, source_target_pairs={{0,1},{1,0},{2,3},{3,2},{4,5},{5,4},{6,7},{7,6},{8,9},{9,8},{10,11... | collective-permute-start | bytes 2457608 | tf_op jit(solution)/shard_map/ppermute | solution.py:415
  114.9 19.6 %copy-start.3 = (f32[2,2,12,32,512]{4,3,2,1,0:T(8,128)S(1)}, f32[2,2,12,32,512]{4,3,2,1,0:T(8,128)}, u32[]{:S(2)}) copy-start(f32[2,2,12,32,512]{4,3,2,1,0:T(8,128)} %get-tuple-element.39.keep_ref) | copy-start | bytes 9437188
  114.9 19.6 %collective-permute-start.5 = (s16[800,512]{1,0:T(8,128)(2,1)}, s16[800,512]{1,0:T(8,128)(2,1)S(1)}, u32[]{:S(2)}, u32[]{:S(2)}) collective-permute-start(s16[800,512]{1,0:T(8,128)(2,1)} %get-tuple-element.41), channel_id=1, source_target_pairs={{0,3},{3,0},{1,2},{2,1},{4,7},{7,4},{5,6},{6,5},{8,11},{11,8},{9,1... | collective-permute-start | bytes 2457608 | tf_op jit(solution)/shard_map/ppermute | solution.py:415
  116.9 1.1 copy-start.5
  133.1 15.1 %collective-permute-start.6 = (s16[800,512]{1,0:T(8,128)(2,1)S(1)}, s16[800,512]{1,0:T(8,128)(2,1)S(1)}, u32[]{:S(2)}, u32[]{:S(2)}) collective-permute-start(s16[800,512]{1,0:T(8,128)(2,1)S(1)} %get-tuple-element.44), channel_id=1, source_target_pairs={{0,1},{1,0},{2,3},{3,2},{4,5},{5,4},{6,7},{7,6},{8,9},{9,8},{10,11... | collective-permute-start | bytes 2457608 | tf_op jit(solution)/shard_map/ppermute | solution.py:415
  133.3 16.0 %collective-permute-start.7 = (s16[800,512]{1,0:T(8,128)(2,1)S(1)}, s16[800,512]{1,0:T(8,128)(2,1)S(1)}, u32[]{:S(2)}, u32[]{:S(2)}) collective-permute-start(s16[800,512]{1,0:T(8,128)(2,1)S(1)} %get-tuple-element.45), channel_id=1, source_target_pairs={{0,3},{3,0},{1,2},{2,1},{4,7},{7,4},{5,6},{6,5},{8,11},{11,8},{9,1... | collective-permute-start | bytes 2457608 | tf_op jit(solution)/shard_map/ppermute | solution.py:415
  149.3 9.6 %collective-permute-start.8 = (s16[400,512]{1,0:T(8,128)(2,1)S(1)}, s16[400,512]{1,0:T(8,128)(2,1)S(1)}, u32[]{:S(2)}, u32[]{:S(2)}) collective-permute-start(s16[400,512]{1,0:T(8,128)(2,1)S(1)} %get-tuple-element.49), channel_id=1, source_target_pairs={{0,3},{3,0},{1,2},{2,1},{4,7},{7,4},{5,6},{6,5},{8,11},{11,8},{9,1... | collective-permute-start | bytes 1228808 | tf_op jit(solution)/shard_map/ppermute | solution.py:415
  151.1 7.8 %collective-permute-start.9 = (s16[400,512]{1,0:T(8,128)(2,1)S(1)}, s16[400,512]{1,0:T(8,128)(2,1)S(1)}, u32[]{:S(2)}, u32[]{:S(2)}) collective-permute-start(s16[400,512]{1,0:T(8,128)(2,1)S(1)} %get-tuple-element.50), channel_id=1, source_target_pairs={{0,1},{1,0},{2,3},{3,2},{4,5},{5,4},{6,7},{7,6},{8,9},{9,8},{10,11... | collective-permute-start | bytes 1228808 | tf_op jit(solution)/shard_map/ppermute | solution.py:415
  153.8 1.2 copy-start.6
  160.9 37.3 %collective-permute-start.15 = (s16[800,512]{1,0:T(8,128)(2,1)}, s16[800,512]{1,0:T(8,128)(2,1)}, u32[]{:S(2)}, u32[]{:S(2)}) collective-permute-start(s16[800,512]{1,0:T(8,128)(2,1)} %finish_virt.1), channel_id=1, source_target_pairs={{0,0},{1,1},{2,2},{3,3},{4,64},{5,65},{6,66},{7,67},{8,128},{9,129... | collective-permute-start | bytes 2457608 | tf_op jit(solution)/shard_map/ppermute | solution.py:463
  170.6 8.3 %collective-permute-start.10 = (s16[400,512]{1,0:T(8,128)(2,1)}, s16[400,512]{1,0:T(8,128)(2,1)S(1)}, u32[]{:S(2)}, u32[]{:S(2)}) collective-permute-start(s16[400,512]{1,0:T(8,128)(2,1)} %get-tuple-element.52), channel_id=1, source_target_pairs={{0,3},{3,0},{1,2},{2,1},{4,7},{7,4},{5,6},{6,5},{8,11},{11,8},{9,1... | collective-permute-start | bytes 1228808 | tf_op jit(solution)/shard_map/ppermute | solution.py:415
  172.5 7.1 %collective-permute-start.11 = (s16[400,512]{1,0:T(8,128)(2,1)}, s16[400,512]{1,0:T(8,128)(2,1)}, u32[]{:S(2)}, u32[]{:S(2)}) collective-permute-start(s16[400,512]{1,0:T(8,128)(2,1)} %get-tuple-element.53), channel_id=1, source_target_pairs={{0,1},{1,0},{2,3},{3,2},{4,5},{5,4},{6,7},{7,6},{8,9},{9,8},{10,11... | collective-permute-start | bytes 1228808 | tf_op jit(solution)/shard_map/ppermute | solution.py:415
  179.6 1.4 copy-start.7
  183.9 0.9 copy-start.1
  184.8 7.3 %collective-permute-start.12 = (s16[1,800,128]{2,1,0:T(8,128)(2,1)}, s16[1,800,128]{2,1,0:T(8,128)(2,1)S(1)}, u32[]{:S(2)}, u32[]{:S(2)}) collective-permute-start(s16[1,800,128]{2,1,0:T(8,128)(2,1)} %get-tuple-element.59), channel_id=1, source_target_pairs={{0,16},{4,20},{8,24},{12,28},{16,32},{20,36},{24,40},{28,44},{32,4... | collective-permute-start | bytes 614408 | tf_op jit(solution)/shard_map/ppermute | solution.py:471
  187.5 10.0 %collective-permute-start.13 = (s16[1,800,128]{2,1,0:T(8,128)(2,1)}, s16[1,800,128]{2,1,0:T(8,128)(2,1)S(1)}, u32[]{:S(2)}, u32[]{:S(2)}) collective-permute-start(s16[1,800,128]{2,1,0:T(8,128)(2,1)} %get-tuple-element.58), channel_id=1, source_target_pairs={{0,32},{4,36},{8,40},{12,44},{16,48},{20,52},{24,56},{28,60},{32,0... | collective-permute-start | bytes 614408 | tf_op jit(solution)/shard_map/ppermute | solution.py:471
  189.8 8.3 %collective-permute-start.14 = (s16[1,800,128]{2,1,0:T(8,128)(2,1)S(1)}, s16[1,800,128]{2,1,0:T(8,128)(2,1)}, u32[]{:S(2)}, u32[]{:S(2)}) collective-permute-start(s16[1,800,128]{2,1,0:T(8,128)(2,1)S(1)} %get-tuple-element.57), channel_id=1, source_target_pairs={{0,48},{4,52},{8,56},{12,60},{16,0},{20,4},{24,8},{28,12},{32,16},... | collective-permute-start | bytes 614408 | tf_op jit(solution)/shard_map/ppermute | solution.py:471
  197.4 0.7 copy-start.9
  198.1 1.1 copy-start.2
  199.3 0.9 copy-start.10
  206.0 4.1 %collective-permute-start.16 = (f32[24,24]{1,0:T(8,128)S(1)}, f32[24,24]{1,0:T(8,128)S(1)}, u32[]{:S(2)}, u32[]{:S(2)}) collective-permute-start(f32[24,24]{1,0:T(8,128)S(1)} %reduce_sum.9), channel_id=1, source_target_pairs={{0,2},{1,3},{2,0},{3,1},{4,6},{5,7},{6,4},{7,5},{8,10},{9,11},{10,... | collective-permute-start | bytes 6920 | tf_op jit(solution)/shard_map/ppermute | solution.py:409
  206.2 4.0 %collective-permute-start.17 = (f32[24,24]{1,0:T(8,128)S(1)}, f32[24,24]{1,0:T(8,128)S(1)}, u32[]{:S(2)}, u32[]{:S(2)}) collective-permute-start(f32[24,24]{1,0:T(8,128)S(1)} %reduce_sum.9), channel_id=1, source_target_pairs={{0,1},{1,2},{2,3},{3,0},{4,5},{5,6},{6,7},{7,4},{8,9},{9,10},{10,1... | collective-permute-start | bytes 6920 | tf_op jit(solution)/shard_map/ppermute | solution.py:409
  207.4 2.9 %collective-permute-start.18 = (f32[24,24]{1,0:T(8,128)S(1)}, f32[24,24]{1,0:T(8,128)S(1)}, u32[]{:S(2)}, u32[]{:S(2)}) collective-permute-start(f32[24,24]{1,0:T(8,128)S(1)} %reduce_sum.9), channel_id=1, source_target_pairs={{0,3},{1,0},{2,1},{3,2},{4,7},{5,4},{6,5},{7,6},{8,11},{9,8},{10,9... | collective-permute-start | bytes 6920 | tf_op jit(solution)/shard_map/ppermute | solution.py:409
  210.3 20.4 %collective-permute-start.19 = (f32[24,24]{1,0:T(8,128)S(1)}, f32[24,24]{1,0:T(8,128)S(1)}, u32[]{:S(2)}, u32[]{:S(2)}) collective-permute-start(f32[24,24]{1,0:T(8,128)S(1)} %add_add_fusion.3), channel_id=1, source_target_pairs={{0,8},{4,12},{8,0},{12,4},{16,24},{20,28},{24,16},{28,20},{32,40},... | collective-permute-start | bytes 6920 | tf_op jit(solution)/shard_map/ppermute | solution.py:409
  224.3 7.3 %collective-permute-start.20 = (f32[24,24]{1,0:T(8,128)S(1)}, f32[24,24]{1,0:T(8,128)S(1)}, u32[]{:S(2)}, u32[]{:S(2)}) collective-permute-start(f32[24,24]{1,0:T(8,128)S(1)} %add_add_fusion.3), channel_id=1, source_target_pairs={{0,4},{4,8},{8,12},{12,0},{16,20},{20,24},{24,28},{28,16},{32,36},... | collective-permute-start | bytes 6920 | tf_op jit(solution)/shard_map/ppermute | solution.py:409
  230.7 3.1 %collective-permute-start.21 = (f32[24,24]{1,0:T(8,128)S(1)}, f32[24,24]{1,0:T(8,128)S(1)}, u32[]{:S(2)}, u32[]{:S(2)}) collective-permute-start(f32[24,24]{1,0:T(8,128)S(1)} %add_add_fusion.3), channel_id=1, source_target_pairs={{0,12},{4,0},{8,4},{12,8},{16,28},{20,16},{24,20},{28,24},{32,44},... | collective-permute-start | bytes 6920 | tf_op jit(solution)/shard_map/ppermute | solution.py:409
  233.9 4.0 %collective-permute-start.22 = (f32[24,24]{1,0:T(8,128)S(1)}, f32[24,24]{1,0:T(8,128)S(1)}, u32[]{:S(2)}, u32[]{:S(2)}) collective-permute-start(f32[24,24]{1,0:T(8,128)S(1)} %add_add_fusion.2), channel_id=1, source_target_pairs={{0,128},{64,192},{128,0},{192,64},{1,129},{65,193},{129,1},{193,65... | collective-permute-start | bytes 6920 | tf_op jit(solution)/shard_map/ppermute | solution.py:409
  233.9 4.0 %collective-permute-start.23 = (f32[24,24]{1,0:T(8,128)S(1)}, f32[24,24]{1,0:T(8,128)S(1)}, u32[]{:S(2)}, u32[]{:S(2)}) collective-permute-start(f32[24,24]{1,0:T(8,128)S(1)} %add_add_fusion.2), channel_id=1, source_target_pairs={{0,64},{64,128},{128,192},{192,0},{1,65},{65,129},{129,193},{193,1... | collective-permute-start | bytes 6920 | tf_op jit(solution)/shard_map/ppermute | solution.py:409
  236.1 2.8 %collective-permute-start.24 = (f32[24,24]{1,0:T(8,128)S(1)}, f32[24,24]{1,0:T(8,128)S(1)}, u32[]{:S(2)}, u32[]{:S(2)}) collective-permute-start(f32[24,24]{1,0:T(8,128)S(1)} %add_add_fusion.2), channel_id=1, source_target_pairs={{0,192},{64,0},{128,64},{192,128},{1,193},{65,1},{129,65},{193,129... | collective-permute-start | bytes 6920 | tf_op jit(solution)/shard_map/ppermute | solution.py:409
  238.9 8.2 %collective-permute-start.25 = (f32[24,24]{1,0:T(8,128)S(1)}, f32[24,24]{1,0:T(8,128)S(1)}, u32[]{:S(2)}, u32[]{:S(2)}) collective-permute-start(f32[24,24]{1,0:T(8,128)S(1)} %add_add_fusion.1), channel_id=1, source_target_pairs={{0,32},{4,36},{8,40},{12,44},{16,48},{20,52},{24,56},{28,60},{32,0... | collective-permute-start | bytes 6920 | tf_op jit(solution)/shard_map/ppermute | solution.py:409
  243.5 4.7 %collective-permute-start.26 = (f32[24,24]{1,0:T(8,128)S(1)}, f32[24,24]{1,0:T(8,128)S(1)}, u32[]{:S(2)}, u32[]{:S(2)}) collective-permute-start(f32[24,24]{1,0:T(8,128)S(1)} %add_add_fusion.1), channel_id=1, source_target_pairs={{0,16},{4,20},{8,24},{12,28},{16,32},{20,36},{24,40},{28,44},{32,4... | collective-permute-start | bytes 6920 | tf_op jit(solution)/shard_map/ppermute | solution.py:409
  245.0 3.4 %collective-permute-start.27 = (f32[24,24]{1,0:T(8,128)S(1)}, f32[24,24]{1,0:T(8,128)S(1)}, u32[]{:S(2)}, u32[]{:S(2)}) collective-permute-start(f32[24,24]{1,0:T(8,128)S(1)} %add_add_fusion.1), channel_id=1, source_target_pairs={{0,48},{4,52},{8,56},{12,60},{16,0},{20,4},{24,8},{28,12},{32,16},... | collective-permute-start | bytes 6920 | tf_op jit(solution)/shard_map/ppermute | solution.py:409

commit v5 on v4

--- a/solution.py
+++ b/solution.py
@@ -143,15 +143,15 @@
 
 
 def virt_body(meta_ref, place_ref, *rest, plan):
-    sources, (keep_ref, send0_ref, send1_ref) = rest[:6], rest[6:9]
-    refs, (acc_ref, level_ref, sems) = rest[9:15], rest[15:]
+    sources, (keep_ref, send0_ref, send1_ref) = rest[:8], rest[8:11]
+    refs, (acc_ref, level_ref, sems) = rest[11:19], rest[19:]
     loads = [pltpu.make_async_copy(src, dst, sems.at[i]) for i, (src, dst) in enumerate(zip(sources, refs))]
     for load in loads:
         load.start()
     acc_ref[...] = jnp.zeros(acc_ref.shape, F32)
     for load in loads:
         load.wait()
-    green_ref = refs[5]
+    own_ref, green_ref = refs[0], refs[7]
     half = OWNERS // 2
     for part in range(2):
 
@@ -161,7 +161,7 @@
                 source = part * half + local
                 for slot in range(CAP):
                     span = slice(slot * QUARTER, (slot + 1) * QUARTER)
-                    parts = [ref[source, span, :] for ref in refs[:3]] + [refs[3 + part][local, span, :]]
+                    parts = [own_ref[source, span, :]] + [ref[local, span, :] for ref in refs[1 + part : 7 : 2]]
                     aux = meta_ref[source, 2 * slot]
                     kept = meta_ref[source, 2 * slot + 1]
                     tile = jnp.concatenate(parts, axis=0)
@@ -179,14 +179,15 @@
 
 
 def occ_body(
-    meta_ref, place_ref, own_ref, prev_ref, next_ref, far_a_ref, far_b_ref, green_ref, *rest, plan
+    meta_ref, place_ref, own_ref, *rest, plan
 ):
+    halves, green_ref, rest = rest[:6], rest[6], rest[7:]
     keep_ref, send0_ref, send1_ref, acc_ref, tile_ref, level_ref = rest
     acc_ref[...] = jnp.zeros(acc_ref.shape, F32)
     row_place = place_ref[0]
     rows = [pl.multiple_of(((row_place + d) % ROWS) * QUARTER, QUARTER) for d in (0, ROWS - 1, 1, 2)]
     half = OWNERS // 2
-    for part, far_ref in enumerate((far_a_ref, far_b_ref)):
+    for part in range(2):
 
         @pl.loop(0, half // 2)
         def _(step):
@@ -195,9 +196,9 @@
                 local = step * 2 + j
                 source = part * half + local
                 span = slice(slot * QUARTER, (slot + 1) * QUARTER)
-                for ref, row in zip((own_ref, prev_ref, next_ref), rows):
-                    tile_ref[CAP * j + slot, pl.ds(row, QUARTER), :] = ref[source, span, :]
-                tile_ref[CAP * j + slot, pl.ds(rows[3], QUARTER), :] = far_ref[local, span, :]
+                tile_ref[CAP * j + slot, pl.ds(rows[0], QUARTER), :] = own_ref[source, span, :]
+                for ref, row in zip(halves[part::2], rows[1:]):
+                    tile_ref[CAP * j + slot, pl.ds(row, QUARTER), :] = ref[local, span, :]
             for j, slot in visits:
                 source = part * half + step * 2 + j
                 aux = meta_ref[source, 2 * slot]
@@ -230,11 +231,11 @@
     operands = [*quarters, green]
     return pl.pallas_call(
         functools.partial(virt_body, plan=plan),
-        in_specs=[SMEM] * 2 + [ANY] * 6,
+        in_specs=[SMEM] * 2 + [ANY] * 8,
         out_specs=[VMEM] * 3,
         out_shape=step_shapes(plan),
         scratch_shapes=[pltpu.VMEM(x.shape, x.dtype) for x in operands]
-        + [pltpu.VMEM((NP, BS, WIDE), F32), level_scratch(plan), pltpu.SemaphoreType.DMA((6,))],
+        + [pltpu.VMEM((NP, BS, WIDE), F32), level_scratch(plan), pltpu.SemaphoreType.DMA((8,))],
         compiler_params=params(55),
         name="contract_virt",
     )(meta, place, *operands)
@@ -243,7 +244,7 @@
 def contract_occ(meta, place, quarters, green, plan):
     return pl.pallas_call(
         functools.partial(occ_body, plan=plan),
-        in_specs=[SMEM] * 2 + [VMEM] * 6,
+        in_specs=[SMEM] * 2 + [VMEM] * 8,
         out_specs=[VMEM] * 3,
         out_shape=step_shapes(plan),
         scratch_shapes=[pltpu.VMEM((NP, BS, WIDE), F32), pltpu.VMEM((2 * CAP, BS, BS), BF16), level_scratch(plan)],
@@ -441,12 +442,16 @@
     occ_blocks = occ_green.reshape(layer_blocks, BS, WIDE).transpose(0, 2, 1)
 
     half = OWNERS // 2
-    prev = lax.ppermute(own, "row", rotate(ROWS, 1))
-    nxt = lax.ppermute(own, "row", rotate(ROWS, -1))
-    prev, nxt, occ_blocks = after(prev, nxt, occ_blocks)
-    far_a = lax.ppermute(prev[:half], "row", rotate(ROWS, 1))
-    far_b = lax.ppermute(nxt[half:], "row", rotate(ROWS, -1))
-    quarters = (own, prev, nxt, far_a, far_b)
+    own_a, own_b = own[:half], own[half:]
+    up, down = rotate(ROWS, 1), rotate(ROWS, -1)
+    prev_a = lax.ppermute(own_a, "row", up)
+    next_b = lax.ppermute(own_b, "row", down)
+    prev_a, next_b, own_a, own_b, occ_blocks = after(prev_a, next_b, own_a, own_b, occ_blocks)
+    far_a = lax.ppermute(prev_a, "row", up)
+    far_b = lax.ppermute(next_b, "row", down)
+    prev_b = lax.ppermute(own_b, "row", up)
+    next_a = lax.ppermute(own_a, "row", down)
+    quarters = (own, prev_a, prev_b, next_a, next_b, far_a, far_b)
 
     v_keep, v0, v1 = contract_virt(meta, place, quarters, virt_blocks, plan)
     v_got = layer_swap(v0, v1, FIRST)
@@ -458,10 +463,12 @@
     v0, v1, *o_got = after(v0, v1, *o_got)
     v_got = layer_swap(v0, v1, SECOND)
     o_left, o0, o1 = halve(place, o_keep, *o_got, plan, "halve_occ")
-    o_left, *v_got = after(o_left, *v_got)
+    o0, o1, *v_got = after(o0, o1, *v_got)
+    o_got = layer_swap(o0, o1, SECOND)
+    v_left, *o_got = after(v_left, *o_got)
     virt = finish(v_left, *v_got, plan, False, "finish_virt")
+    o_left, virt = after(o_left, virt)
     virt = lax.ppermute(virt, ALL, SWAP)
-    o_got = layer_swap(o0, o1, SECOND)
     occ = finish(o_left, *o_got, plan, True, "finish_occ")
 
     low = col_place // 4

time: 251 us -> 261 us (1.040)
  waiting for transfers between devices: 62.8 us -> 69.1 us
  starting transfers between devices: 64.3 us -> 69.5 us
    ppermute x3, waiting for transfers between devices: 5.27 us -> 11.3 us  [on_device(): others.append(lax.ppermute(part, 'col', rotate_high(d)))]
    slice x2 -> x1, local copies, waits for them, and re-layouts: 3.88 us -> 1.1 us  [on_device(): own_a, own_b = (own[:half], own[half:])]
    unnamed x36 -> x44, local copies, waits for them, and re-layouts: 11.8 us -> 14.5 us
    ppermute x4 -> x6, starting transfers between devices: 5.41 us -> 8.1 us  [the longest x1 2.69 us: on_device(): next_a = lax.ppermute(own_a, 'row', down)]
    ppermute x4 -> x6, waiting for transfers between devices: 25.2 us -> 23 us  [the longest x1 12.6 us: on_device(): prev_b = lax.ppermute(own_b, 'row', up)]
  transfers between devices with their start and end apart: 28 -> 30, of which waited for: 18 -> 15; matrix products, arithmetic and copies ran while one was open for 5% -> 4% of each run, Pallas kernels for 9% -> 7%
where the time goes in v5:
time: 261 us; the launch traced here: 259 us
  starting transfers between devices  69.5 us (27%)
  waiting for transfers between devices  69.1 us (26%)
  Pallas kernels  49.1 us (19%)
  blocking collectives  43.4 us (17%)
  local copies, waits for them, and re-layouts  24.4 us (9%)
  other arithmetic  3 us (1%)
    all_to_all x1, blocking collectives, on_device(): own = lax.all_to_all(send, ('col', 'layer'), 0, 0, tiled=True)  43.4 us
    ppermute x12, starting transfers between devices, tree_sum(): one, two, three = [lax.ppermute(values, axis, perm) for perm in perms]  36.7 us
    ppermute x4, waiting for transfers between devices, layer_swap(): lax.ppermute(send0, 'layer', perms[0])  24.7 us
    pallas_call x1, Pallas kernels, contract_virt(): pl.pallas_call(functools.partial(virt_body, plan=plan), in_specs=[SMEM] *...  18.8 us
    pallas_call x1, Pallas kernels, contract_occ(): pl.pallas_call(functools.partial(occ_body, plan=plan), in_specs=[SMEM] *...  14.7 us
    unnamed x44, local copies, waits for them, and re-layouts  14.5 us
    ppermute x1, waiting for transfers between devices, on_device(): prev_b = lax.ppermute(own_b, 'row', up)  12.6 us
    ppermute x1, starting transfers between devices, on_device(): virt = lax.ppermute(virt, ALL, SWAP)  11.9 us
  transfers between devices with their start and end apart: 30, of which 15 were waited for; matrix products, arithmetic and copies ran while one was open for 4% of the time, Pallas kernels for 7%

profile of v5, /device:TPU:1, one launch (start us, length us, event | category | flops | bytes accessed | tf_op | source)
XLA Modules:
  0.0 258.8 jit_solution(6452590714671281060)
XLA Ops:
  0.0 1.8 copy-done
  4.5 3.3 %build_send.1 = bf16[64,72,128]{2,1,0:T(8,128)(2,1)S(1)} custom-call(s32[88]{0:T(128)S(1)} %copy-done.16, s32[88]{0:T(128)S(1)} %copy-done.17, s32[88]{0:T(128)S(1)} %copy-done.18, s32[88]{0:T(128)S(1)} %copy-done.19, bf16[88,32,128]{2,1,0:T(8,128)(2,1)S(1)} %constant_dynamic-slice_fusion.3.tiles_ref), custom_call_target="tpu_custom_call" | custom-call | tf_op jit(solution)/shard_map/build_send/pallas_call | solution.py:113
  7.9 43.4 %all_to_all.5.rest_0_.own_ref = bf16[64,72,128]{2,1,0:T(8,128)(2,1)S(1)} all-to-all(bf16[64,72,128]{2,1,0:T(8,128)(2,1)S(1)} %build_send.1), channel_id=1, replica_groups=mesh['row'=4,'col'=16,'layer'=4] {'col','layer'}, dimensions={0} | all-to-all | bytes 2359296 | tf_op jit(solution)/shard_map/all_to_all | solution.py:439
  52.3 1.1 fusion
  53.4 1.3 collective-permute-start
  54.7 1.4 collective-permute-start.1
  56.2 7.9 %copy.8 = bf16[40,128,512]{1,2,0:T(8,128)(2,1)} copy(bf16[40,128,512]{2,1,0:T(8,128)(2,1)} %bitcast.14) | data formatting | bytes 10485760 | tf_op jit(solution)/shard_map/reshape | solution.py:442
  64.1 4.2 %collective-permute-done.rest_1_.rest_0_ = bf16[32,72,128]{2,1,0:T(8,128)(2,1)S(1)} collective-permute-done((bf16[32,72,128]{2,1,0:T(8,128)(2,1)}, bf16[32,72,128]{2,1,0:T(8,128)(2,1)S(1)}, u32[]{:S(2)}, u32[]{:S(2)}) %collective-permute-start) | collective-permute-done | bytes 589856 | tf_op jit(solution)/shard_map/ppermute | solution.py:447
  68.3 1.1 collective-permute-start.4
  69.4 1.6 collective-permute-start.5
  71.0 2.7 %collective-permute-start.3 = (bf16[32,72,128]{2,1,0:T(8,128)(2,1)}, bf16[32,72,128]{2,1,0:T(8,128)(2,1)}, u32[]{:S(2)}, u32[]{:S(2)}) collective-permute-start(bf16[32,72,128]{2,1,0:T(8,128)(2,1)} %get-tuple-element.42), channel_id=1, source_target_pairs={{0,192},{64,0},{128,64},{192,128},{1,193},{65,1},{129,65},{193,129... | collective-permute-start | bytes 1769480 | tf_op jit(solution)/shard_map/ppermute | solution.py:453
  74.3 1.5 slice_convert_fusion
  75.8 6.1 %collective-permute-done.4.rest_5_.rest_4_ = bf16[32,72,128]{2,1,0:T(8,128)(2,1)} collective-permute-done((bf16[32,72,128]{2,1,0:T(8,128)(2,1)S(1)}, bf16[32,72,128]{2,1,0:T(8,128)(2,1)}, u32[]{:S(2)}, u32[]{:S(2)}) %collective-permute-start.4) | collective-permute-done | bytes 589856 | tf_op jit(solution)/shard_map/ppermute | solution.py:450
  81.9 12.6 %collective-permute-done.2.rest_2_.rest_1_ = bf16[32,72,128]{2,1,0:T(8,128)(2,1)} collective-permute-done((bf16[32,72,128]{2,1,0:T(8,128)(2,1)}, bf16[32,72,128]{2,1,0:T(8,128)(2,1)}, u32[]{:S(2)}, u32[]{:S(2)}) %collective-permute-start.2) | collective-permute-done | bytes 589856 | tf_op jit(solution)/shard_map/ppermute | solution.py:452
  94.6 18.8 %contract_virt.1 = (f32[2,2,12,32,512]{4,3,2,1,0:T(8,128)}, s16[800,512]{1,0:T(8,128)(2,1)}, s16[800,512]{1,0:T(8,128)(2,1)}) custom-call(s32[64,4]{1,0:T(8,128)} %bitcast.12, s32[3]{0:T(128)} %pad_add_fusion.1.place_ref, bf16[64,72,128]{2,1,0:T(8,128)(2,1)} %copy-done.1, bf16[32,72,128]{2,1,0:T(8,128)(2,1)} %copy-done.6, ...), custom_call_target="tpu_custom_call" | custom-call | tf_op jit(solution)/shard_map/contract_virt/pallas_call | solution.py:232
  113.8 2.1 collective-permute-start.7
  115.9 1.1 copy-done.7
  117.0 14.7 %contract_occ.1 = (f32[2,2,12,32,512]{4,3,2,1,0:T(8,128)S(1)}, s16[800,512]{1,0:T(8,128)(2,1)S(1)}, s16[800,512]{1,0:T(8,128)(2,1)S(1)}) custom-call(s32[64,4]{1,0:T(8,128)S(1)} %bitcast.13, s32[3]{0:T(128)S(1)} %copy-done.15, bf16[64,72,128]{2,1,0:T(8,128)(2,1)S(1)} %copy-done.2, bf16[32,72,128]{2,1,0:T(8,128)(2,1)S(1)} %copy-done.7, ...), custom_call_target="tpu_custom_call" | custom-call | tf_op jit(solution)/shard_map/contract_occ/pallas_call | solution.py:245
  132.0 1.2 collective-permute-start.9
  133.2 1.8 halve_virt.1
  135.0 12.3 %collective-permute-done.8.got0_ref = s16[800,512]{1,0:T(8,128)(2,1)S(1)} collective-permute-done((s16[800,512]{1,0:T(8,128)(2,1)S(1)}, s16[800,512]{1,0:T(8,128)(2,1)S(1)}, u32[]{:S(2)}, u32[]{:S(2)}) %collective-permute-start.8) | collective-permute-done | bytes 819232 | tf_op jit(solution)/shard_map/ppermute | solution.py:416
  147.3 1.1 collective-permute-done.9.got1_ref
  148.4 2.4 collective-permute-start.10
  150.8 1.8 halve_occ.1
  152.5 1.2 copy-done.8
  153.7 3.8 %collective-permute-done.10.got0_ref = s16[400,512]{1,0:T(8,128)(2,1)S(1)} collective-permute-done((s16[400,512]{1,0:T(8,128)(2,1)S(1)}, s16[400,512]{1,0:T(8,128)(2,1)S(1)}, u32[]{:S(2)}, u32[]{:S(2)}) %collective-permute-start.10) | collective-permute-done | bytes 409632 | tf_op jit(solution)/shard_map/ppermute | solution.py:416
  157.6 1.7 collective-permute-start.12
  159.2 8.6 %collective-permute-done.12.got0_ref = s16[400,512]{1,0:T(8,128)(2,1)S(1)} collective-permute-done((s16[400,512]{1,0:T(8,128)(2,1)S(1)}, s16[400,512]{1,0:T(8,128)(2,1)S(1)}, u32[]{:S(2)}, u32[]{:S(2)}) %collective-permute-start.12) | collective-permute-done | bytes 409632 | tf_op jit(solution)/shard_map/ppermute | solution.py:416
  168.6 2.0 finish_virt.1
  170.6 11.9 %collective-permute-start.17 = (s16[800,512]{1,0:T(8,128)(2,1)}, s16[800,512]{1,0:T(8,128)(2,1)}, u32[]{:S(2)}, u32[]{:S(2)}) collective-permute-start(s16[800,512]{1,0:T(8,128)(2,1)} %finish_virt.1), channel_id=1, source_target_pairs={{0,0},{1,1},{2,2},{3,3},{4,64},{5,65},{6,66},{7,67},{8,128},{9,129... | collective-permute-start | bytes 2457608 | tf_op jit(solution)/shard_map/ppermute | solution.py:471
  182.6 1.4 copy-done.9
  185.0 1.1 finish_occ.1.own_ref
  188.9 1.6 collective-permute-start.15
  190.5 2.2 collective-permute-start.16
  192.7 9.0 %collective-permute-done.14.one_ref = s16[1,800,128]{2,1,0:T(8,128)(2,1)S(1)} collective-permute-done((s16[1,800,128]{2,1,0:T(8,128)(2,1)}, s16[1,800,128]{2,1,0:T(8,128)(2,1)S(1)}, u32[]{:S(2)}, u32[]{:S(2)}) %collective-permute-start.14) | collective-permute-done | bytes 204832 | tf_op jit(solution)/shard_map/ppermute | solution.py:478
  201.7 2.3 collective-permute-done.15.two_ref
  204.7 1.1 copy-done.4
  206.8 5.6 %pair.1 = f32[24,24,128]{2,1,0:T(8,128)S(1)} custom-call(s32[2]{0:T(128)S(1)} %pad_add_fusion.place_ref, s16[4,800,128]{2,1,0:T(8,128)(2,1)S(1)} %copy-done.4, s16[1,800,128]{2,1,0:T(8,128)(2,1)S(1)} %collective-permute-done.14.one_ref, s16[1,800,128]{2,1,0:T(8,128)(2,1)S(1)} %copy-done.14, s16[1,800,128]{2,1,0:T(8,128)(2,1)} %collective-permute-done.16.three_ref, ...), custom_call_target="tpu_custom_call" | custom-call | tf_op jit(solution)/shard_map/pair/pallas_call | solution.py:358
  212.7 2.7 %collective-permute-start.20 = (f32[24,24]{1,0:T(8,128)S(1)}, f32[24,24]{1,0:T(8,128)S(1)}, u32[]{:S(2)}, u32[]{:S(2)}) collective-permute-start(f32[24,24]{1,0:T(8,128)S(1)} %reduce_sum.9), channel_id=1, source_target_pairs={{0,3},{1,0},{2,1},{3,2},{4,7},{5,4},{6,5},{7,6},{8,11},{9,8},{10,9... | collective-permute-start | bytes 6920 | tf_op jit(solution)/shard_map/ppermute | solution.py:410
  215.4 1.3 collective-permute-done.18
  216.7 18.3 %collective-permute-start.21 = (f32[24,24]{1,0:T(8,128)S(1)}, f32[24,24]{1,0:T(8,128)S(1)}, u32[]{:S(2)}, u32[]{:S(2)}) collective-permute-start(f32[24,24]{1,0:T(8,128)S(1)} %add_add_fusion.3), channel_id=1, source_target_pairs={{0,8},{4,12},{8,0},{12,4},{16,24},{20,28},{24,16},{28,20},{32,40},... | collective-permute-start | bytes 6920 | tf_op jit(solution)/shard_map/ppermute | solution.py:410
  235.0 2.3 collective-permute-start.22
  238.3 2.1 collective-permute-done.23
  240.5 2.7 %collective-permute-start.26 = (f32[24,24]{1,0:T(8,128)S(1)}, f32[24,24]{1,0:T(8,128)S(1)}, u32[]{:S(2)}, u32[]{:S(2)}) collective-permute-start(f32[24,24]{1,0:T(8,128)S(1)} %add_add_fusion.2), channel_id=1, source_target_pairs={{0,192},{64,0},{128,64},{192,128},{1,193},{65,1},{129,65},{193,129... | collective-permute-start | bytes 6920 | tf_op jit(solution)/shard_map/ppermute | solution.py:410
  243.2 1.3 collective-permute-done.24
  244.5 5.8 %collective-permute-start.27 = (f32[24,24]{1,0:T(8,128)S(1)}, f32[24,24]{1,0:T(8,128)S(1)}, u32[]{:S(2)}, u32[]{:S(2)}) collective-permute-start(f32[24,24]{1,0:T(8,128)S(1)} %add_add_fusion.1), channel_id=1, source_target_pairs={{0,32},{4,36},{8,40},{12,44},{16,48},{20,52},{24,56},{28,60},{32,0... | collective-permute-start | bytes 6920 | tf_op jit(solution)/shard_map/ppermute | solution.py:410
  250.3 4.4 %collective-permute-start.28 = (f32[24,24]{1,0:T(8,128)S(1)}, f32[24,24]{1,0:T(8,128)S(1)}, u32[]{:S(2)}, u32[]{:S(2)}) collective-permute-start(f32[24,24]{1,0:T(8,128)S(1)} %add_add_fusion.1), channel_id=1, source_target_pairs={{0,16},{4,20},{8,24},{12,28},{16,32},{20,36},{24,40},{28,44},{32,4... | collective-permute-start | bytes 6920 | tf_op jit(solution)/shard_map/ppermute | solution.py:410
  255.5 2.7 %collective-permute-done.29 = f32[24,24]{1,0:T(8,128)S(1)} collective-permute-done((f32[24,24]{1,0:T(8,128)S(1)}, f32[24,24]{1,0:T(8,128)S(1)}, u32[]{:S(2)}, u32[]{:S(2)}) %collective-permute-start.29) | collective-permute-done | bytes 2336 | tf_op jit(solution)/shard_map/ppermute | solution.py:410
  (78 shorter events, 14.1 us)
Async XLA Ops:
  0.0 1.8 copy-start
  51.3 1.0 copy-start.1
  53.4 14.9 %collective-permute-start = (bf16[32,72,128]{2,1,0:T(8,128)(2,1)}, bf16[32,72,128]{2,1,0:T(8,128)(2,1)S(1)}, u32[]{:S(2)}, u32[]{:S(2)}) collective-permute-start(bf16[32,72,128]{2,1,0:T(8,128)(2,1)} %get-tuple-element.42), channel_id=1, source_target_pairs={{0,64},{64,128},{128,192},{192,0},{1,65},{65,129},{129,193},{193,1... | collective-permute-start | bytes 1769480 | tf_op jit(solution)/shard_map/ppermute | solution.py:447
  54.7 13.6 %collective-permute-start.1 = (bf16[32,72,128]{2,1,0:T(8,128)(2,1)}, bf16[32,72,128]{2,1,0:T(8,128)(2,1)}, u32[]{:S(2)}, u32[]{:S(2)}) collective-permute-start(bf16[32,72,128]{2,1,0:T(8,128)(2,1)} %get-tuple-element.41), channel_id=1, source_target_pairs={{0,192},{64,0},{128,64},{192,128},{1,193},{65,1},{129,65},{193,129... | collective-permute-start | bytes 1769480 | tf_op jit(solution)/shard_map/ppermute | solution.py:448
  68.3 26.3 %copy-start.6 = (bf16[32,72,128]{2,1,0:T(8,128)(2,1)}, bf16[32,72,128]{2,1,0:T(8,128)(2,1)S(1)}, u32[]{:S(2)}) copy-start(bf16[32,72,128]{2,1,0:T(8,128)(2,1)S(1)} %collective-permute-done.rest_1_.rest_0_) | copy-start | bytes 1769476
  68.3 13.7 %collective-permute-start.4 = (bf16[32,72,128]{2,1,0:T(8,128)(2,1)S(1)}, bf16[32,72,128]{2,1,0:T(8,128)(2,1)}, u32[]{:S(2)}, u32[]{:S(2)}) collective-permute-start(bf16[32,72,128]{2,1,0:T(8,128)(2,1)S(1)} %collective-permute-done.rest_1_.rest_0_), channel_id=1, source_target_pairs={{0,64},{64,128},{128,192},{192,0},{1,65},{65,129},{129,193},{193,1... | collective-permute-start | bytes 1769480 | tf_op jit(solution)/shard_map/ppermute | solution.py:450
  69.4 12.6 %collective-permute-start.5 = (bf16[32,72,128]{2,1,0:T(8,128)(2,1)}, bf16[32,72,128]{2,1,0:T(8,128)(2,1)}, u32[]{:S(2)}, u32[]{:S(2)}) collective-permute-start(bf16[32,72,128]{2,1,0:T(8,128)(2,1)} %collective-permute-done.1.rest_4_.rest_3_), channel_id=1, source_target_pairs={{0,192},{64,0},{128,64},{192,128},{1,193},{65,1},{129,65},{193,129... | collective-permute-start | bytes 1769480 | tf_op jit(solution)/shard_map/ppermute | solution.py:451
  71.0 23.6 %collective-permute-start.2 = (bf16[32,72,128]{2,1,0:T(8,128)(2,1)}, bf16[32,72,128]{2,1,0:T(8,128)(2,1)}, u32[]{:S(2)}, u32[]{:S(2)}) collective-permute-start(bf16[32,72,128]{2,1,0:T(8,128)(2,1)} %get-tuple-element.41), channel_id=1, source_target_pairs={{0,64},{64,128},{128,192},{192,0},{1,65},{65,129},{129,193},{193,1... | collective-permute-start | bytes 1769480 | tf_op jit(solution)/shard_map/ppermute | solution.py:452
  71.0 23.6 %collective-permute-start.3 = (bf16[32,72,128]{2,1,0:T(8,128)(2,1)}, bf16[32,72,128]{2,1,0:T(8,128)(2,1)}, u32[]{:S(2)}, u32[]{:S(2)}) collective-permute-start(bf16[32,72,128]{2,1,0:T(8,128)(2,1)} %get-tuple-element.42), channel_id=1, source_target_pairs={{0,192},{64,0},{128,64},{192,128},{1,193},{65,1},{129,65},{193,129... | collective-permute-start | bytes 1769480 | tf_op jit(solution)/shard_map/ppermute | solution.py:453
  94.6 21.3 %slice-start = ((s8[5242880]{0:T(1024)(128)(4,1)}), s8[4194304]{0:T(1024)(128)(4,1)S(1)}, s32[]{:S(2)}) async-start(s8[5242880]{0:T(1024)(128)(4,1)} %bitcast.9), calls=%async_computation.1 | async-start | bytes 8388608
  94.6 21.3 %slice-start.1 = ((s8[5242880]{0:T(1024)(128)(4,1)}), s8[1048576]{0:T(1024)(128)(4,1)S(1)}, s32[]{:S(2)}) async-start(s8[5242880]{0:T(1024)(128)(4,1)} %bitcast.9), calls=%async_computation.2 | async-start | bytes 2097152
  94.6 21.3 %copy-start.2 = (bf16[64,72,128]{2,1,0:T(8,128)(2,1)S(1)}, bf16[64,72,128]{2,1,0:T(8,128)(2,1)}, u32[]{:S(2)}) copy-start(bf16[64,72,128]{2,1,0:T(8,128)(2,1)} %copy-done.1) | copy-start | bytes 3538948
  94.6 21.3 %copy-start.12 = (s32[64,1,4]{2,1,0:T(1,128)S(1)}, s32[64,1,4]{2,1,0:T(1,128)}, u32[]{:S(2)}) copy-start(s32[64,1,4]{2,1,0:T(1,128)} %slice_convert_fusion) | copy-start | bytes 3076
  94.6 21.3 %copy-start.15 = (s32[3]{0:T(128)S(1)}, s32[3]{0:T(128)}, u32[]{:S(2)}) copy-start(s32[3]{0:T(128)} %pad_add_fusion.1.place_ref) | copy-start | bytes 40
  113.4 19.7 %collective-permute-start.6 = (s16[800,512]{1,0:T(8,128)(2,1)}, s16[800,512]{1,0:T(8,128)(2,1)S(1)}, u32[]{:S(2)}, u32[]{:S(2)}) collective-permute-start(s16[800,512]{1,0:T(8,128)(2,1)} %get-tuple-element.50), channel_id=1, source_target_pairs={{0,1},{1,0},{2,3},{3,2},{4,5},{5,4},{6,7},{7,6},{8,9},{9,8},{10,11... | collective-permute-start | bytes 2457608 | tf_op jit(solution)/shard_map/ppermute | solution.py:416
  113.8 19.4 %copy-start.5 = (f32[2,2,12,32,512]{4,3,2,1,0:T(8,128)S(1)}, f32[2,2,12,32,512]{4,3,2,1,0:T(8,128)}, u32[]{:S(2)}) copy-start(f32[2,2,12,32,512]{4,3,2,1,0:T(8,128)} %get-tuple-element.49.keep_ref) | copy-start | bytes 9437188
  113.8 19.4 %collective-permute-start.7 = (s16[800,512]{1,0:T(8,128)(2,1)}, s16[800,512]{1,0:T(8,128)(2,1)S(1)}, u32[]{:S(2)}, u32[]{:S(2)}) collective-permute-start(s16[800,512]{1,0:T(8,128)(2,1)} %get-tuple-element.51), channel_id=1, source_target_pairs={{0,3},{3,0},{1,2},{2,1},{4,7},{7,4},{5,6},{6,5},{8,11},{11,8},{9,1... | collective-permute-start | bytes 2457608 | tf_op jit(solution)/shard_map/ppermute | solution.py:416
  115.9 1.1 copy-start.7
  131.7 15.6 %collective-permute-start.8 = (s16[800,512]{1,0:T(8,128)(2,1)S(1)}, s16[800,512]{1,0:T(8,128)(2,1)S(1)}, u32[]{:S(2)}, u32[]{:S(2)}) collective-permute-start(s16[800,512]{1,0:T(8,128)(2,1)S(1)} %get-tuple-element.54), channel_id=1, source_target_pairs={{0,1},{1,0},{2,3},{3,2},{4,5},{5,4},{6,7},{7,6},{8,9},{9,8},{10,11... | collective-permute-start | bytes 2457608 | tf_op jit(solution)/shard_map/ppermute | solution.py:416
  132.0 16.4 %collective-permute-start.9 = (s16[800,512]{1,0:T(8,128)(2,1)S(1)}, s16[800,512]{1,0:T(8,128)(2,1)S(1)}, u32[]{:S(2)}, u32[]{:S(2)}) collective-permute-start(s16[800,512]{1,0:T(8,128)(2,1)S(1)} %get-tuple-element.55), channel_id=1, source_target_pairs={{0,3},{3,0},{1,2},{2,1},{4,7},{7,4},{5,6},{6,5},{8,11},{11,8},{9,1... | collective-permute-start | bytes 2457608 | tf_op jit(solution)/shard_map/ppermute | solution.py:416
  148.4 9.2 %collective-permute-start.10 = (s16[400,512]{1,0:T(8,128)(2,1)S(1)}, s16[400,512]{1,0:T(8,128)(2,1)S(1)}, u32[]{:S(2)}, u32[]{:S(2)}) collective-permute-start(s16[400,512]{1,0:T(8,128)(2,1)S(1)} %get-tuple-element.62), channel_id=1, source_target_pairs={{0,3},{3,0},{1,2},{2,1},{4,7},{7,4},{5,6},{6,5},{8,11},{11,8},{9,1... | collective-permute-start | bytes 1228808 | tf_op jit(solution)/shard_map/ppermute | solution.py:416
  150.7 6.8 %collective-permute-start.11 = (s16[400,512]{1,0:T(8,128)(2,1)S(1)}, s16[400,512]{1,0:T(8,128)(2,1)S(1)}, u32[]{:S(2)}, u32[]{:S(2)}) collective-permute-start(s16[400,512]{1,0:T(8,128)(2,1)S(1)} %get-tuple-element.63), channel_id=1, source_target_pairs={{0,1},{1,0},{2,3},{3,2},{4,5},{5,4},{6,7},{7,6},{8,9},{9,8},{10,11... | collective-permute-start | bytes 1228808 | tf_op jit(solution)/shard_map/ppermute | solution.py:416
  152.5 1.2 copy-start.8
  157.6 10.3 %collective-permute-start.12 = (s16[400,512]{1,0:T(8,128)(2,1)S(1)}, s16[400,512]{1,0:T(8,128)(2,1)S(1)}, u32[]{:S(2)}, u32[]{:S(2)}) collective-permute-start(s16[400,512]{1,0:T(8,128)(2,1)S(1)} %get-tuple-element.64), channel_id=1, source_target_pairs={{0,3},{3,0},{1,2},{2,1},{4,7},{7,4},{5,6},{6,5},{8,11},{11,8},{9,1... | collective-permute-start | bytes 1228808 | tf_op jit(solution)/shard_map/ppermute | solution.py:416
  159.2 8.6 %collective-permute-start.13 = (s16[400,512]{1,0:T(8,128)(2,1)S(1)}, s16[400,512]{1,0:T(8,128)(2,1)S(1)}, u32[]{:S(2)}, u32[]{:S(2)}) collective-permute-start(s16[400,512]{1,0:T(8,128)(2,1)S(1)} %get-tuple-element.65), channel_id=1, source_target_pairs={{0,1},{1,0},{2,3},{3,2},{4,5},{5,4},{6,7},{7,6},{8,9},{9,8},{10,11... | collective-permute-start | bytes 1228808 | tf_op jit(solution)/shard_map/ppermute | solution.py:416
  167.9 0.8 copy-start.10
  170.6 34.1 %collective-permute-start.17 = (s16[800,512]{1,0:T(8,128)(2,1)}, s16[800,512]{1,0:T(8,128)(2,1)}, u32[]{:S(2)}, u32[]{:S(2)}) collective-permute-start(s16[800,512]{1,0:T(8,128)(2,1)} %finish_virt.1), channel_id=1, source_target_pairs={{0,0},{1,1},{2,2},{3,3},{4,64},{5,65},{6,66},{7,67},{8,128},{9,129... | collective-permute-start | bytes 2457608 | tf_op jit(solution)/shard_map/ppermute | solution.py:471
  182.6 1.4 copy-start.9
  184.0 1.0 copy-start.11
  186.9 0.9 copy-start.3
  187.8 13.9 %collective-permute-start.14 = (s16[1,800,128]{2,1,0:T(8,128)(2,1)}, s16[1,800,128]{2,1,0:T(8,128)(2,1)S(1)}, u32[]{:S(2)}, u32[]{:S(2)}) collective-permute-start(s16[1,800,128]{2,1,0:T(8,128)(2,1)} %get-tuple-element.77), channel_id=1, source_target_pairs={{0,16},{4,20},{8,24},{12,28},{16,32},{20,36},{24,40},{28,44},{32,4... | collective-permute-start | bytes 614408 | tf_op jit(solution)/shard_map/ppermute | solution.py:478
  188.9 15.2 %collective-permute-start.15 = (s16[1,800,128]{2,1,0:T(8,128)(2,1)}, s16[1,800,128]{2,1,0:T(8,128)(2,1)S(1)}, u32[]{:S(2)}, u32[]{:S(2)}) collective-permute-start(s16[1,800,128]{2,1,0:T(8,128)(2,1)} %get-tuple-element.76), channel_id=1, source_target_pairs={{0,32},{4,36},{8,40},{12,44},{16,48},{20,52},{24,56},{28,60},{32,0... | collective-permute-start | bytes 614408 | tf_op jit(solution)/shard_map/ppermute | solution.py:478
  190.5 14.3 %collective-permute-start.16 = (s16[1,800,128]{2,1,0:T(8,128)(2,1)S(1)}, s16[1,800,128]{2,1,0:T(8,128)(2,1)}, u32[]{:S(2)}, u32[]{:S(2)}) collective-permute-start(s16[1,800,128]{2,1,0:T(8,128)(2,1)S(1)} %get-tuple-element.75), channel_id=1, source_target_pairs={{0,48},{4,52},{8,56},{12,60},{16,0},{20,4},{24,8},{28,12},{32,16},... | collective-permute-start | bytes 614408 | tf_op jit(solution)/shard_map/ppermute | solution.py:478
  204.0 0.7 copy-start.13
  204.7 1.1 copy-start.4
  205.9 0.9 copy-start.14
  212.5 4.1 %collective-permute-start.18 = (f32[24,24]{1,0:T(8,128)S(1)}, f32[24,24]{1,0:T(8,128)S(1)}, u32[]{:S(2)}, u32[]{:S(2)}) collective-permute-start(f32[24,24]{1,0:T(8,128)S(1)} %reduce_sum.9), channel_id=1, source_target_pairs={{0,2},{1,3},{2,0},{3,1},{4,6},{5,7},{6,4},{7,5},{8,10},{9,11},{10,... | collective-permute-start | bytes 6920 | tf_op jit(solution)/shard_map/ppermute | solution.py:410
  212.6 4.0 %collective-permute-start.19 = (f32[24,24]{1,0:T(8,128)S(1)}, f32[24,24]{1,0:T(8,128)S(1)}, u32[]{:S(2)}, u32[]{:S(2)}) collective-permute-start(f32[24,24]{1,0:T(8,128)S(1)} %reduce_sum.9), channel_id=1, source_target_pairs={{0,1},{1,2},{2,3},{3,0},{4,5},{5,6},{6,7},{7,4},{8,9},{9,10},{10,1... | collective-permute-start | bytes 6920 | tf_op jit(solution)/shard_map/ppermute | solution.py:410
  212.7 4.0 %collective-permute-start.20 = (f32[24,24]{1,0:T(8,128)S(1)}, f32[24,24]{1,0:T(8,128)S(1)}, u32[]{:S(2)}, u32[]{:S(2)}) collective-permute-start(f32[24,24]{1,0:T(8,128)S(1)} %reduce_sum.9), channel_id=1, source_target_pairs={{0,3},{1,0},{2,1},{3,2},{4,7},{5,4},{6,5},{7,6},{8,11},{9,8},{10,9... | collective-permute-start | bytes 6920 | tf_op jit(solution)/shard_map/ppermute | solution.py:410
  216.7 20.9 %collective-permute-start.21 = (f32[24,24]{1,0:T(8,128)S(1)}, f32[24,24]{1,0:T(8,128)S(1)}, u32[]{:S(2)}, u32[]{:S(2)}) collective-permute-start(f32[24,24]{1,0:T(8,128)S(1)} %add_add_fusion.3), channel_id=1, source_target_pairs={{0,8},{4,12},{8,0},{12,4},{16,24},{20,28},{24,16},{28,20},{32,40},... | collective-permute-start | bytes 6920 | tf_op jit(solution)/shard_map/ppermute | solution.py:410
  235.0 3.3 %collective-permute-start.22 = (f32[24,24]{1,0:T(8,128)S(1)}, f32[24,24]{1,0:T(8,128)S(1)}, u32[]{:S(2)}, u32[]{:S(2)}) collective-permute-start(f32[24,24]{1,0:T(8,128)S(1)} %add_add_fusion.3), channel_id=1, source_target_pairs={{0,4},{4,8},{8,12},{12,0},{16,20},{20,24},{24,28},{28,16},{32,36},... | collective-permute-start | bytes 6920 | tf_op jit(solution)/shard_map/ppermute | solution.py:410
  237.3 3.1 %collective-permute-start.23 = (f32[24,24]{1,0:T(8,128)S(1)}, f32[24,24]{1,0:T(8,128)S(1)}, u32[]{:S(2)}, u32[]{:S(2)}) collective-permute-start(f32[24,24]{1,0:T(8,128)S(1)} %add_add_fusion.3), channel_id=1, source_target_pairs={{0,12},{4,0},{8,4},{12,8},{16,28},{20,16},{24,20},{28,24},{32,44},... | collective-permute-start | bytes 6920 | tf_op jit(solution)/shard_map/ppermute | solution.py:410
  240.4 4.0 %collective-permute-start.24 = (f32[24,24]{1,0:T(8,128)S(1)}, f32[24,24]{1,0:T(8,128)S(1)}, u32[]{:S(2)}, u32[]{:S(2)}) collective-permute-start(f32[24,24]{1,0:T(8,128)S(1)} %add_add_fusion.2), channel_id=1, source_target_pairs={{0,128},{64,192},{128,0},{192,64},{1,129},{65,193},{129,1},{193,65... | collective-permute-start | bytes 6920 | tf_op jit(solution)/shard_map/ppermute | solution.py:410
  240.4 4.0 %collective-permute-start.25 = (f32[24,24]{1,0:T(8,128)S(1)}, f32[24,24]{1,0:T(8,128)S(1)}, u32[]{:S(2)}, u32[]{:S(2)}) collective-permute-start(f32[24,24]{1,0:T(8,128)S(1)} %add_add_fusion.2), channel_id=1, source_target_pairs={{0,64},{64,128},{128,192},{192,0},{1,65},{65,129},{129,193},{193,1... | collective-permute-start | bytes 6920 | tf_op jit(solution)/shard_map/ppermute | solution.py:410
  240.5 4.0 %collective-permute-start.26 = (f32[24,24]{1,0:T(8,128)S(1)}, f32[24,24]{1,0:T(8,128)S(1)}, u32[]{:S(2)}, u32[]{:S(2)}) collective-permute-start(f32[24,24]{1,0:T(8,128)S(1)} %add_add_fusion.2), channel_id=1, source_target_pairs={{0,192},{64,0},{128,64},{192,128},{1,193},{65,1},{129,65},{193,129... | collective-permute-start | bytes 6920 | tf_op jit(solution)/shard_map/ppermute | solution.py:410
  244.5 10.2 %collective-permute-start.27 = (f32[24,24]{1,0:T(8,128)S(1)}, f32[24,24]{1,0:T(8,128)S(1)}, u32[]{:S(2)}, u32[]{:S(2)}) collective-permute-start(f32[24,24]{1,0:T(8,128)S(1)} %add_add_fusion.1), channel_id=1, source_target_pairs={{0,32},{4,36},{8,40},{12,44},{16,48},{20,52},{24,56},{28,60},{32,0... | collective-permute-start | bytes 6920 | tf_op jit(solution)/shard_map/ppermute | solution.py:410
  250.3 5.2 %collective-permute-start.28 = (f32[24,24]{1,0:T(8,128)S(1)}, f32[24,24]{1,0:T(8,128)S(1)}, u32[]{:S(2)}, u32[]{:S(2)}) collective-permute-start(f32[24,24]{1,0:T(8,128)S(1)} %add_add_fusion.1), channel_id=1, source_target_pairs={{0,16},{4,20},{8,24},{12,28},{16,32},{20,36},{24,40},{28,44},{32,4... | collective-permute-start | bytes 6920 | tf_op jit(solution)/shard_map/ppermute | solution.py:410
  254.7 3.5 %collective-permute-start.29 = (f32[24,24]{1,0:T(8,128)S(1)}, f32[24,24]{1,0:T(8,128)S(1)}, u32[]{:S(2)}, u32[]{:S(2)}) collective-permute-start(f32[24,24]{1,0:T(8,128)S(1)} %add_add_fusion.1), channel_id=1, source_target_pairs={{0,48},{4,52},{8,56},{12,60},{16,0},{20,4},{24,8},{28,12},{32,16},... | collective-permute-start | bytes 6920 | tf_op jit(solution)/shard_map/ppermute | solution.py:410
  (4 other events, 2.6 us)

commit v6 on v5

--- a/solution.py
+++ b/solution.py
@@ -142,31 +142,44 @@
         put_levels(send_ref, plan, 2 * plan.blocks, level_ref)
 
 
-def virt_body(meta_ref, place_ref, *rest, plan):
-    sources, (keep_ref, send0_ref, send1_ref) = rest[:8], rest[8:11]
-    refs, (acc_ref, level_ref, sems) = rest[11:19], rest[19:]
-    loads = [pltpu.make_async_copy(src, dst, sems.at[i]) for i, (src, dst) in enumerate(zip(sources, refs))]
+def start_all(sources, targets, sems):
+    loads = [pltpu.make_async_copy(src, dst, sems.at[i]) for i, (src, dst) in enumerate(zip(sources, targets))]
     for load in loads:
         load.start()
+    return loads
+
+
+def add_virt(meta_ref, first, quarter_refs, green_ref, acc_ref):
+    @pl.loop(0, OWNERS // 4)
+    def _(step):
+        for local in (step * 2, step * 2 + 1):
+            for slot in range(CAP):
+                span = slice(slot * QUARTER, (slot + 1) * QUARTER)
+                tile = jnp.concatenate([ref[local, span, :] for ref in quarter_refs], axis=0)
+                aux = meta_ref[first + local, 2 * slot]
+                kept = meta_ref[first + local, 2 * slot + 1]
+                acc_ref[aux] += jnp.dot(tile, green_ref[kept], preferred_element_type=F32)
+
+
+def virt_first_body(meta_ref, *rest):
+    sources, out_ref, refs, (acc_ref, sems) = rest[:5], rest[5], rest[6:11], rest[11:]
+    loads = start_all(sources, refs, sems)
     acc_ref[...] = jnp.zeros(acc_ref.shape, F32)
     for load in loads:
         load.wait()
-    own_ref, green_ref = refs[0], refs[7]
-    half = OWNERS // 2
-    for part in range(2):
-
-        @pl.loop(0, half // 2)
-        def _(step):
-            for local in (step * 2, step * 2 + 1):
-                source = part * half + local
-                for slot in range(CAP):
-                    span = slice(slot * QUARTER, (slot + 1) * QUARTER)
-                    parts = [own_ref[source, span, :]] + [ref[local, span, :] for ref in refs[1 + part : 7 : 2]]
-                    aux = meta_ref[source, 2 * slot]
-                    kept = meta_ref[source, 2 * slot + 1]
-                    tile = jnp.concatenate(parts, axis=0)
-                    acc_ref[aux] += jnp.dot(tile, green_ref[kept], preferred_element_type=F32)
-
+    add_virt(meta_ref, 0, refs[:4], refs[4], acc_ref)
+    store = pltpu.make_async_copy(acc_ref, out_ref, sems.at[0])
+    store.start()
+    store.wait()
+
+
+def virt_last_body(meta_ref, place_ref, *rest, plan):
+    sources, (keep_ref, send0_ref, send1_ref) = rest[:6], rest[6:9]
+    refs, (level_ref, sems) = rest[9:15], rest[15:]
+    for load in start_all(sources, refs, sems):
+        load.wait()
+    acc_ref = refs[5]
+    add_virt(meta_ref, OWNERS // 2, refs[:4], refs[4], acc_ref)
     split_pieces(place_ref, plan, piece_rows(acc_ref), keep_ref, (send0_ref, send1_ref), level_ref)
 
 
@@ -178,27 +191,21 @@
     return rows_of
 
 
-def occ_body(
-    meta_ref, place_ref, own_ref, *rest, plan
-):
-    halves, green_ref, rest = rest[:6], rest[6], rest[7:]
-    keep_ref, send0_ref, send1_ref, acc_ref, tile_ref, level_ref = rest
+def occ_body(meta_ref, place_ref, *rest, plan):
+    parts, green_ref, (keep_ref, send0_ref, send1_ref, acc_ref, tile_ref, level_ref) = (rest[:4], rest[4:8]), rest[8], rest[9:]
     acc_ref[...] = jnp.zeros(acc_ref.shape, F32)
     row_place = place_ref[0]
     rows = [pl.multiple_of(((row_place + d) % ROWS) * QUARTER, QUARTER) for d in (0, ROWS - 1, 1, 2)]
     half = OWNERS // 2
+    visits = [(j, slot) for j in range(2) for slot in range(CAP)]
     for part in range(2):
 
         @pl.loop(0, half // 2)
         def _(step):
-            visits = [(j, slot) for j in range(2) for slot in range(CAP)]
             for j, slot in visits:
-                local = step * 2 + j
-                source = part * half + local
                 span = slice(slot * QUARTER, (slot + 1) * QUARTER)
-                tile_ref[CAP * j + slot, pl.ds(rows[0], QUARTER), :] = own_ref[source, span, :]
-                for ref, row in zip(halves[part::2], rows[1:]):
-                    tile_ref[CAP * j + slot, pl.ds(row, QUARTER), :] = ref[local, span, :]
+                for ref, row in zip(parts[part], rows):
+                    tile_ref[CAP * j + slot, pl.ds(row, QUARTER), :] = ref[step * 2 + j, span, :]
             for j, slot in visits:
                 source = part * half + step * 2 + j
                 aux = meta_ref[source, 2 * slot]
@@ -227,30 +234,49 @@
     return pltpu.VMEM((plan.levels(2 * plan.blocks), WIDE), F32)
 
 
-def contract_virt(meta, place, quarters, green, plan):
-    operands = [*quarters, green]
-    return pl.pallas_call(
-        functools.partial(virt_body, plan=plan),
-        in_specs=[SMEM] * 2 + [ANY] * 8,
+ACC = (NP, BS, WIDE)
+
+
+def scratch_like(operands):
+    return [pltpu.VMEM(x.shape, x.dtype) for x in operands]
+
+
+def contract_virt_first(meta, part, green):
+    operands = [*part, green]
+    return pl.pallas_call(
+        virt_first_body,
+        in_specs=[SMEM] + [ANY] * 5,
+        out_specs=ANY,
+        out_shape=jax.ShapeDtypeStruct(ACC, F32),
+        scratch_shapes=scratch_like(operands) + [pltpu.VMEM(ACC, F32), pltpu.SemaphoreType.DMA((5,))],
+        compiler_params=params(55),
+        name="virt_first",
+    )(meta, *operands)
+
+
+def contract_virt_last(meta, place, part, green, before, plan):
+    operands = [*part, green, before]
+    return pl.pallas_call(
+        functools.partial(virt_last_body, plan=plan),
+        in_specs=[SMEM] * 2 + [ANY] * 6,
         out_specs=[VMEM] * 3,
         out_shape=step_shapes(plan),
-        scratch_shapes=[pltpu.VMEM(x.shape, x.dtype) for x in operands]
-        + [pltpu.VMEM((NP, BS, WIDE), F32), level_scratch(plan), pltpu.SemaphoreType.DMA((8,))],
+        scratch_shapes=scratch_like(operands) + [level_scratch(plan), pltpu.SemaphoreType.DMA((6,))],
         compiler_params=params(55),
-        name="contract_virt",
+        name="virt_last",
     )(meta, place, *operands)
 
 
-def contract_occ(meta, place, quarters, green, plan):
+def contract_occ(meta, place, parts, green, plan):
     return pl.pallas_call(
         functools.partial(occ_body, plan=plan),
-        in_specs=[SMEM] * 2 + [VMEM] * 8,
+        in_specs=[SMEM] * 2 + [VMEM] * 9,
         out_specs=[VMEM] * 3,
         out_shape=step_shapes(plan),
-        scratch_shapes=[pltpu.VMEM((NP, BS, WIDE), F32), pltpu.VMEM((2 * CAP, BS, BS), BF16), level_scratch(plan)],
+        scratch_shapes=[pltpu.VMEM(ACC, F32), pltpu.VMEM((2 * CAP, BS, BS), BF16), level_scratch(plan)],
         compiler_params=params(28),
         name="contract_occ",
-    )(meta, place, *quarters, green)
+    )(meta, place, *parts[0], *parts[1], green)
 
 
 def halve_body(place_ref, keep_ref, got0_ref, got1_ref, left_ref, send0_ref, send1_ref, level_ref, scale_ref, *, plan):
@@ -442,33 +468,33 @@
     occ_blocks = occ_green.reshape(layer_blocks, BS, WIDE).transpose(0, 2, 1)
 
     half = OWNERS // 2
-    own_a, own_b = own[:half], own[half:]
+    own_a, own_b = own[:half, : CAP * QUARTER], own[half:, : CAP * QUARTER]
     up, down = rotate(ROWS, 1), rotate(ROWS, -1)
     prev_a = lax.ppermute(own_a, "row", up)
+    next_a = lax.ppermute(own_a, "row", down)
+    prev_a, next_a, own_b, occ_blocks = after(prev_a, next_a, own_b, occ_blocks)
+    far_a = lax.ppermute(prev_a, "row", up)
     next_b = lax.ppermute(own_b, "row", down)
-    prev_a, next_b, own_a, own_b, occ_blocks = after(prev_a, next_b, own_a, own_b, occ_blocks)
-    far_a = lax.ppermute(prev_a, "row", up)
+    far_a, next_b, own_b = after(far_a, next_b, own_b)
+    prev_b = lax.ppermute(own_b, "row", up)
     far_b = lax.ppermute(next_b, "row", down)
-    prev_b = lax.ppermute(own_b, "row", up)
-    next_a = lax.ppermute(own_a, "row", down)
-    quarters = (own, prev_a, prev_b, next_a, next_b, far_a, far_b)
-
-    v_keep, v0, v1 = contract_virt(meta, place, quarters, virt_blocks, plan)
+    part_a, part_b = (own_a, prev_a, next_a, far_a), (own_b, prev_b, next_b, far_b)
+
+    v_acc = contract_virt_first(meta, part_a, virt_blocks)
+    v_keep, v0, v1 = contract_virt_last(meta, place, part_b, virt_blocks, v_acc, plan)
     v_got = layer_swap(v0, v1, FIRST)
     occ_blocks, v_keep = after(occ_blocks, v_keep)
-    o_keep, o0, o1 = contract_occ(meta, place, quarters, occ_blocks, plan)
-    o_got = layer_swap(o0, o1, FIRST)
+    o_keep, o0, o1 = contract_occ(meta, place, (part_a, part_b), occ_blocks, plan)
     v_keep, o_keep = after(v_keep, o_keep)
     v_left, v0, v1 = halve(place, v_keep, *v_got, plan, "halve_virt")
-    v0, v1, *o_got = after(v0, v1, *o_got)
     v_got = layer_swap(v0, v1, SECOND)
+    o0, o1, *v_got = after(o0, o1, *v_got)
+    o_got = layer_swap(o0, o1, FIRST)
+    virt = finish(v_left, *v_got, plan, False, "finish_virt")
+    virt, o_keep = after(virt, o_keep)
+    virt = lax.ppermute(virt, ALL, SWAP)
     o_left, o0, o1 = halve(place, o_keep, *o_got, plan, "halve_occ")
-    o0, o1, *v_got = after(o0, o1, *v_got)
     o_got = layer_swap(o0, o1, SECOND)
-    v_left, *o_got = after(v_left, *o_got)
-    virt = finish(v_left, *v_got, plan, False, "finish_virt")
-    o_left, virt = after(o_left, virt)
-    virt = lax.ppermute(virt, ALL, SWAP)
     occ = finish(o_left, *o_got, plan, True, "finish_occ")
 
     low = col_place // 4

time: 261 us -> 240 us (0.920)
  waiting for transfers between devices: 69.1 us -> 51 us
  starting transfers between devices: 69.5 us -> 58.6 us
  Pallas kernels: 49.1 us -> 58.8 us
    ppermute x12, starting transfers between devices: 36.7 us -> 22.7 us  [tree_sum(): one, two, three = [lax.ppermute(values, axis, perm) for perm in perms]]
    ppermute x1, waiting for transfers between devices: 12.6 us -> 0.01 us  [on_device(): prev_b = lax.ppermute(own_b, 'row', up)]
    ppermute x4, waiting for transfers between devices: 24.7 us -> 16.1 us  [layer_swap(): lax.ppermute(send0, 'layer', perms[0])]
    pallas_call x1 -> x2, Pallas kernels: 18.8 us -> 26.4 us  [the longest x1 14.7 us: contract_virt_last(): pl.pallas_call(functools.partial(virt_last_body, plan=plan), in_specs=[SM...]
    ppermute x3, starting transfers between devices: 4.79 us -> 11.1 us  [on_device(): others.append(lax.ppermute(part, 'col', rotate_high(d)))]
    ppermute x1, waiting for transfers between devices: 6.13 us -> 9.78 us  [on_device(): far_a = lax.ppermute(prev_a, 'row', up)]
    ppermute x3, waiting for transfers between devices: 11.3 us -> 14.9 us  [on_device(): others.append(lax.ppermute(part, 'col', rotate_high(d)))]
    unnamed x44 -> x42, local copies, waits for them, and re-layouts: 14.5 us -> 12.5 us
  transfers between devices with their start and end apart: 30 -> 30, of which waited for: 15 -> 15; matrix products, arithmetic and copies ran while one was open for 4% -> 5% of each run, Pallas kernels for 7% -> 14%
where the time goes in v6:
time: 240 us; the launch traced here: 237 us
  Pallas kernels  58.8 us (24%)
  starting transfers between devices  58.6 us (24%)
  waiting for transfers between devices  51 us (21%)
  blocking collectives  43.4 us (18%)
  local copies, waits for them, and re-layouts  22.2 us (9%)
  other arithmetic  3.03 us (1%)
    all_to_all x1, blocking collectives, on_device(): own = lax.all_to_all(send, ('col', 'layer'), 0, 0, tiled=True)  43.4 us
    ppermute x12, starting transfers between devices, tree_sum(): one, two, three = [lax.ppermute(values, axis, perm) for perm in perms]  22.7 us
    ppermute x4, waiting for transfers between devices, layer_swap(): lax.ppermute(send0, 'layer', perms[0])  16.1 us
    pallas_call x1, Pallas kernels, contract_occ(): pl.pallas_call(functools.partial(occ_body, plan=plan), in_specs=[SMEM] *...  14.9 us
    ppermute x3, waiting for transfers between devices, on_device(): others.append(lax.ppermute(part, 'col', rotate_high(d)))  14.9 us
    pallas_call x1, Pallas kernels, contract_virt_last(): pl.pallas_call(functools.partial(virt_last_body, plan=plan), in_specs=[SM...  14.7 us
    unnamed x42, local copies, waits for them, and re-layouts  12.5 us
    pallas_call x1, Pallas kernels, contract_virt_first(): pl.pallas_call(virt_first_body, in_specs=[SMEM] + [ANY] * 5, out_specs=AN...  11.8 us
  transfers between devices with their start and end apart: 30, of which 15 were waited for; matrix products, arithmetic and copies ran while one was open for 5% of the time, Pallas kernels for 14%

profile of v6, /device:TPU:1, one launch (start us, length us, event | category | flops | bytes accessed | tf_op | source)
XLA Modules:
  0.0 237.3 jit_solution(5856139714434112721)
XLA Ops:
  0.0 1.8 copy-done
  4.5 3.3 %build_send.1 = bf16[64,72,128]{2,1,0:T(8,128)(2,1)S(1)} custom-call(s32[88]{0:T(128)S(1)} %copy-done.14, s32[88]{0:T(128)S(1)} %copy-done.15, s32[88]{0:T(128)S(1)} %copy-done.16, s32[88]{0:T(128)S(1)} %copy-done.17, bf16[88,32,128]{2,1,0:T(8,128)(2,1)S(1)} %constant_dynamic-slice_fusion.3.tiles_ref), custom_call_target="tpu_custom_call" | custom-call | tf_op jit(solution)/shard_map/build_send/pallas_call | solution.py:113
  7.9 43.4 %all_to_all.5 = bf16[64,72,128]{2,1,0:T(8,128)(2,1)S(1)} all-to-all(bf16[64,72,128]{2,1,0:T(8,128)(2,1)S(1)} %build_send.1), channel_id=1, replica_groups=mesh['row'=4,'col'=16,'layer'=4] {'col','layer'}, dimensions={0} | all-to-all | bytes 2359296 | tf_op jit(solution)/shard_map/all_to_all | solution.py:465
  51.3 1.1 copy-done.18
  53.3 1.3 collective-permute-start
  54.6 1.4 collective-permute-start.1
  56.1 7.8 %copy.8 = bf16[40,128,512]{1,2,0:T(8,128)(2,1)} copy(bf16[40,128,512]{2,1,0:T(8,128)(2,1)} %bitcast.17) | data formatting | bytes 10485760 | tf_op jit(solution)/shard_map/reshape | solution.py:468
  63.9 3.0 %collective-permute-done.rest_1_ = bf16[32,64,128]{2,1,0:T(8,128)(2,1)} collective-permute-done((bf16[32,64,128]{2,1,0:T(8,128)(2,1)}, bf16[32,64,128]{2,1,0:T(8,128)(2,1)}, u32[]{:S(2)}, u32[]{:S(2)}) %collective-permute-start) | collective-permute-done | bytes 524320 | tf_op jit(solution)/shard_map/ppermute | solution.py:473
  66.9 1.0 collective-permute-start.2
  67.9 1.7 collective-permute-start.3
  69.6 9.8 %collective-permute-done.2.rest_3_ = bf16[32,64,128]{2,1,0:T(8,128)(2,1)S(1)} collective-permute-done((bf16[32,64,128]{2,1,0:T(8,128)(2,1)}, bf16[32,64,128]{2,1,0:T(8,128)(2,1)S(1)}, u32[]{:S(2)}, u32[]{:S(2)}) %collective-permute-start.2) | collective-permute-done | bytes 524320 | tf_op jit(solution)/shard_map/ppermute | solution.py:476
  80.2 2.0 collective-permute-start.5
  82.8 1.5 slice_convert_fusion
  84.3 11.8 %virt_first.1.rest_5_ = f32[24,128,512]{2,1,0:T(8,128)} custom-call(s32[64,4]{1,0:T(8,128)} %bitcast.12, bf16[32,64,128]{2,1,0:T(8,128)(2,1)} %get-tuple-element.64.rest_0_, bf16[32,64,128]{2,1,0:T(8,128)(2,1)} %collective-permute-done.rest_1_, bf16[32,64,128]{2,1,0:T(8,128)(2,1)} %collective-permute-done.1.rest_2_, bf16[32,64,128]{2,1,0:T(8,128)(2,1)} %copy-done.6, ...), custom_call_target="tpu_custom_call" | custom-call | tf_op jit(solution)/shard_map/virt_first/pallas_call | solution.py:246
  96.2 14.7 %virt_last.1 = (f32[2,2,12,32,512]{4,3,2,1,0:T(8,128)}, s16[800,512]{1,0:T(8,128)(2,1)}, s16[800,512]{1,0:T(8,128)(2,1)}) custom-call(s32[64,4]{1,0:T(8,128)} %bitcast.13, s32[3]{0:T(128)} %pad_add_fusion.1.place_ref, bf16[32,64,128]{2,1,0:T(8,128)(2,1)} %copy-done.3, bf16[32,64,128]{2,1,0:T(8,128)(2,1)} %collective-permute-done.4.rest_1_.rest_5_, ...), custom_call_target="tpu_custom_call" | custom-call | tf_op jit(solution)/shard_map/virt_last/pallas_call | solution.py:259
  111.2 2.1 collective-permute-start.7
  113.4 14.9 %contract_occ.1 = (f32[2,2,12,32,512]{4,3,2,1,0:T(8,128)S(1)}, s16[800,512]{1,0:T(8,128)(2,1)S(1)}, s16[800,512]{1,0:T(8,128)(2,1)S(1)}) custom-call(s32[64,4]{1,0:T(8,128)S(1)} %bitcast.14, s32[3]{0:T(128)S(1)} %copy-done.13, bf16[32,64,128]{2,1,0:T(8,128)(2,1)} %get-tuple-element.64.rest_0_, bf16[32,64,128]{2,1,0:T(8,128)(2,1)} %collective-permute-done.rest_1_, ...), custom_call_target="tpu_custom_call" | custom-call | tf_op jit(solution)/shard_map/contract_occ/pallas_call | solution.py:271
  128.3 1.8 halve_virt.1
  130.1 1.9 collective-permute-start.8
  132.0 6.2 %collective-permute-done.8.got0_ref = s16[400,512]{1,0:T(8,128)(2,1)S(1)} collective-permute-done((s16[400,512]{1,0:T(8,128)(2,1)S(1)}, s16[400,512]{1,0:T(8,128)(2,1)S(1)}, u32[]{:S(2)}, u32[]{:S(2)}) %collective-permute-start.8) | collective-permute-done | bytes 409632 | tf_op jit(solution)/shard_map/ppermute | solution.py:442
  140.0 2.0 finish_virt.1
  142.0 10.5 %collective-permute-start.17 = (s16[800,512]{1,0:T(8,128)(2,1)}, s16[800,512]{1,0:T(8,128)(2,1)}, u32[]{:S(2)}, u32[]{:S(2)}) collective-permute-start(s16[800,512]{1,0:T(8,128)(2,1)} %finish_virt.1), channel_id=1, source_target_pairs={{0,0},{1,1},{2,2},{3,3},{4,64},{5,65},{6,66},{7,67},{8,128},{9,129... | collective-permute-start | bytes 2457608 | tf_op jit(solution)/shard_map/ppermute | solution.py:495
  152.4 3.0 %collective-permute-done.10.got0_ref = s16[800,512]{1,0:T(8,128)(2,1)S(1)} collective-permute-done((s16[800,512]{1,0:T(8,128)(2,1)S(1)}, s16[800,512]{1,0:T(8,128)(2,1)S(1)}, u32[]{:S(2)}, u32[]{:S(2)}) %collective-permute-start.10) | collective-permute-done | bytes 819232 | tf_op jit(solution)/shard_map/ppermute | solution.py:442
  155.4 2.6 %halve_occ.1 = (f32[2,12,32,512]{3,2,1,0:T(8,128)S(1)}, s16[400,512]{1,0:T(8,128)(2,1)}, s16[400,512]{1,0:T(8,128)(2,1)}) custom-call(s32[3]{0:T(128)S(1)} %copy-done.13, f32[2,2,12,32,512]{4,3,2,1,0:T(8,128)S(1)} %get-tuple-element.56.keep_ref, s16[800,512]{1,0:T(8,128)(2,1)S(1)} %collective-permute-done.10.got0_ref, ...), custom_call_target="tpu_custom_call" | custom-call | tf_op jit(solution)/shard_map/halve_occ/pallas_call | solution.py:299
  158.0 1.2 copy-done.8
  159.2 1.3 collective-permute-start.12
  160.5 6.9 %collective-permute-done.12.got0_ref = s16[400,512]{1,0:T(8,128)(2,1)S(1)} collective-permute-done((s16[400,512]{1,0:T(8,128)(2,1)}, s16[400,512]{1,0:T(8,128)(2,1)S(1)}, u32[]{:S(2)}, u32[]{:S(2)}) %collective-permute-start.12) | collective-permute-done | bytes 409632 | tf_op jit(solution)/shard_map/ppermute | solution.py:442
  167.6 1.4 copy-done.9
  169.1 2.1 finish_occ.1.own_ref
  172.9 5.3 %collective-permute-start.14 = (s16[1,800,128]{2,1,0:T(8,128)(2,1)}, s16[1,800,128]{2,1,0:T(8,128)(2,1)S(1)}, u32[]{:S(2)}, u32[]{:S(2)}) collective-permute-start(s16[1,800,128]{2,1,0:T(8,128)(2,1)} %get-tuple-element.67), channel_id=1, source_target_pairs={{0,16},{4,20},{8,24},{12,28},{16,32},{20,36},{24,40},{28,44},{32,4... | collective-permute-start | bytes 614408 | tf_op jit(solution)/shard_map/ppermute | solution.py:504
  178.2 3.4 %collective-permute-start.15 = (s16[1,800,128]{2,1,0:T(8,128)(2,1)}, s16[1,800,128]{2,1,0:T(8,128)(2,1)S(1)}, u32[]{:S(2)}, u32[]{:S(2)}) collective-permute-start(s16[1,800,128]{2,1,0:T(8,128)(2,1)} %get-tuple-element.66), channel_id=1, source_target_pairs={{0,32},{4,36},{8,40},{12,44},{16,48},{20,52},{24,56},{28,60},{32,0... | collective-permute-start | bytes 614408 | tf_op jit(solution)/shard_map/ppermute | solution.py:504
  181.6 2.4 %collective-permute-start.16 = (s16[1,800,128]{2,1,0:T(8,128)(2,1)S(1)}, s16[1,800,128]{2,1,0:T(8,128)(2,1)}, u32[]{:S(2)}, u32[]{:S(2)}) collective-permute-start(s16[1,800,128]{2,1,0:T(8,128)(2,1)S(1)} %get-tuple-element.65), channel_id=1, source_target_pairs={{0,48},{4,52},{8,56},{12,60},{16,0},{20,4},{24,8},{28,12},{32,16},... | collective-permute-start | bytes 614408 | tf_op jit(solution)/shard_map/ppermute | solution.py:504
  184.1 4.1 %collective-permute-done.15.two_ref = s16[1,800,128]{2,1,0:T(8,128)(2,1)S(1)} collective-permute-done((s16[1,800,128]{2,1,0:T(8,128)(2,1)}, s16[1,800,128]{2,1,0:T(8,128)(2,1)S(1)}, u32[]{:S(2)}, u32[]{:S(2)}) %collective-permute-start.15) | collective-permute-done | bytes 204832 | tf_op jit(solution)/shard_map/ppermute | solution.py:504
  188.9 10.8 %collective-permute-done.16.three_ref = s16[1,800,128]{2,1,0:T(8,128)(2,1)} collective-permute-done((s16[1,800,128]{2,1,0:T(8,128)(2,1)S(1)}, s16[1,800,128]{2,1,0:T(8,128)(2,1)}, u32[]{:S(2)}, u32[]{:S(2)}) %collective-permute-start.16) | collective-permute-done | bytes 204832 | tf_op jit(solution)/shard_map/ppermute | solution.py:504
  199.7 1.1 copy-done.2
  201.7 5.6 %pair.1 = f32[24,24,128]{2,1,0:T(8,128)S(1)} custom-call(s32[2]{0:T(128)S(1)} %pad_add_fusion.place_ref, s16[4,800,128]{2,1,0:T(8,128)(2,1)S(1)} %copy-done.2, s16[1,800,128]{2,1,0:T(8,128)(2,1)S(1)} %collective-permute-done.14.one_ref, s16[1,800,128]{2,1,0:T(8,128)(2,1)S(1)} %copy-done.12, s16[1,800,128]{2,1,0:T(8,128)(2,1)} %collective-permute-done.16.three_ref, ...), custom_call_target="tpu_custom_call" | custom-call | tf_op jit(solution)/shard_map/pair/pallas_call | solution.py:384
  207.5 1.5 collective-permute-start.18
  209.0 1.1 collective-permute-start.19
  210.0 1.6 collective-permute-start.20
  211.7 1.1 collective-permute-done.19
  212.7 1.0 collective-permute-start.21
  213.7 6.5 %collective-permute-start.22 = (f32[24,24]{1,0:T(8,128)S(1)}, f32[24,24]{1,0:T(8,128)S(1)}, u32[]{:S(2)}, u32[]{:S(2)}) collective-permute-start(f32[24,24]{1,0:T(8,128)S(1)} %add_add_fusion.3), channel_id=1, source_target_pairs={{0,4},{4,8},{8,12},{12,0},{16,20},{20,24},{24,28},{28,16},{32,36},... | collective-permute-start | bytes 6920 | tf_op jit(solution)/shard_map/ppermute | solution.py:436
  221.1 2.3 collective-permute-done.23
  224.2 2.2 collective-permute-start.26
  226.4 1.0 collective-permute-done.24
  227.6 4.5 %collective-permute-start.27 = (f32[24,24]{1,0:T(8,128)S(1)}, f32[24,24]{1,0:T(8,128)S(1)}, u32[]{:S(2)}, u32[]{:S(2)}) collective-permute-start(f32[24,24]{1,0:T(8,128)S(1)} %add_add_fusion.1), channel_id=1, source_target_pairs={{0,32},{4,36},{8,40},{12,44},{16,48},{20,52},{24,56},{28,60},{32,0... | collective-permute-start | bytes 6920 | tf_op jit(solution)/shard_map/ppermute | solution.py:436
  232.8 2.8 %collective-permute-start.29 = (f32[24,24]{1,0:T(8,128)S(1)}, f32[24,24]{1,0:T(8,128)S(1)}, u32[]{:S(2)}, u32[]{:S(2)}) collective-permute-start(f32[24,24]{1,0:T(8,128)S(1)} %add_add_fusion.1), channel_id=1, source_target_pairs={{0,48},{4,52},{8,56},{12,60},{16,0},{20,4},{24,8},{28,12},{32,16},... | collective-permute-start | bytes 6920 | tf_op jit(solution)/shard_map/ppermute | solution.py:436
  235.6 1.1 collective-permute-done.28
  (77 shorter events, 14.2 us)
Async XLA Ops:
  0.0 1.8 copy-start
  1.9 0.7 copy-start.14
  51.3 1.1 copy-start.18
  53.3 26.0 %copy-start.3 = (bf16[32,64,128]{2,1,0:T(8,128)(2,1)}, bf16[32,64,128]{2,1,0:T(8,128)(2,1)S(1)}, u32[]{:S(2)}) copy-start(bf16[32,64,128]{2,1,0:T(8,128)(2,1)S(1)} %get-tuple-element.37.rest_0_.rest_4_) | copy-start | bytes 1572868
  53.3 13.6 %collective-permute-start = (bf16[32,64,128]{2,1,0:T(8,128)(2,1)}, bf16[32,64,128]{2,1,0:T(8,128)(2,1)}, u32[]{:S(2)}, u32[]{:S(2)}) collective-permute-start(bf16[32,64,128]{2,1,0:T(8,128)(2,1)} %get-tuple-element.64.rest_0_), channel_id=1, source_target_pairs={{0,64},{64,128},{128,192},{192,0},{1,65},{65,129},{129,193},{193,1... | collective-permute-start | bytes 1572872 | tf_op jit(solution)/shard_map/ppermute | solution.py:473
  54.6 12.3 %collective-permute-start.1 = (bf16[32,64,128]{2,1,0:T(8,128)(2,1)}, bf16[32,64,128]{2,1,0:T(8,128)(2,1)}, u32[]{:S(2)}, u32[]{:S(2)}) collective-permute-start(bf16[32,64,128]{2,1,0:T(8,128)(2,1)} %get-tuple-element.64.rest_0_), channel_id=1, source_target_pairs={{0,192},{64,0},{128,64},{192,128},{1,193},{65,1},{129,65},{193,129... | collective-permute-start | bytes 1572872 | tf_op jit(solution)/shard_map/ppermute | solution.py:474
  66.9 12.5 %collective-permute-start.2 = (bf16[32,64,128]{2,1,0:T(8,128)(2,1)}, bf16[32,64,128]{2,1,0:T(8,128)(2,1)S(1)}, u32[]{:S(2)}, u32[]{:S(2)}) collective-permute-start(bf16[32,64,128]{2,1,0:T(8,128)(2,1)} %collective-permute-done.rest_1_), channel_id=1, source_target_pairs={{0,64},{64,128},{128,192},{192,0},{1,65},{65,129},{129,193},{193,1... | collective-permute-start | bytes 1572872 | tf_op jit(solution)/shard_map/ppermute | solution.py:476
  67.9 11.5 %collective-permute-start.3 = (bf16[32,64,128]{2,1,0:T(8,128)(2,1)S(1)}, bf16[32,64,128]{2,1,0:T(8,128)(2,1)}, u32[]{:S(2)}, u32[]{:S(2)}) collective-permute-start(bf16[32,64,128]{2,1,0:T(8,128)(2,1)S(1)} %get-tuple-element.37.rest_0_.rest_4_), channel_id=1, source_target_pairs={{0,192},{64,0},{128,64},{192,128},{1,193},{65,1},{129,65},{193,129... | collective-permute-start | bytes 1572872 | tf_op jit(solution)/shard_map/ppermute | solution.py:477
  79.4 0.8 copy-start.6
  79.4 16.8 %collective-permute-start.4 = (bf16[32,64,128]{2,1,0:T(8,128)(2,1)S(1)}, bf16[32,64,128]{2,1,0:T(8,128)(2,1)}, u32[]{:S(2)}, u32[]{:S(2)}) collective-permute-start(bf16[32,64,128]{2,1,0:T(8,128)(2,1)S(1)} %get-tuple-element.37.rest_0_.rest_4_), channel_id=1, source_target_pairs={{0,64},{64,128},{128,192},{192,0},{1,65},{65,129},{129,193},{193,1... | collective-permute-start | bytes 1572872 | tf_op jit(solution)/shard_map/ppermute | solution.py:479
  80.2 16.0 %collective-permute-start.5 = (bf16[32,64,128]{2,1,0:T(8,128)(2,1)}, bf16[32,64,128]{2,1,0:T(8,128)(2,1)}, u32[]{:S(2)}, u32[]{:S(2)}) collective-permute-start(bf16[32,64,128]{2,1,0:T(8,128)(2,1)} %collective-permute-done.3.rest_2_.rest_6_), channel_id=1, source_target_pairs={{0,192},{64,0},{128,64},{192,128},{1,193},{65,1},{129,65},{193,129... | collective-permute-start | bytes 1572872 | tf_op jit(solution)/shard_map/ppermute | solution.py:480
  84.3 29.0 %slice-start = ((s8[5242880]{0:T(1024)(128)(4,1)}), s8[4194304]{0:T(1024)(128)(4,1)S(1)}, s32[]{:S(2)}) async-start(s8[5242880]{0:T(1024)(128)(4,1)} %bitcast.9), calls=%async_computation.1 | async-start | bytes 8388608
  96.1 17.2 %slice-start.1 = ((s8[5242880]{0:T(1024)(128)(4,1)}), s8[1048576]{0:T(1024)(128)(4,1)S(1)}, s32[]{:S(2)}) async-start(s8[5242880]{0:T(1024)(128)(4,1)} %bitcast.9), calls=%async_computation.2 | async-start | bytes 2097152
  96.1 17.2 %copy-start.4 = (bf16[32,64,128]{2,1,0:T(8,128)(2,1)S(1)}, bf16[32,64,128]{2,1,0:T(8,128)(2,1)}, u32[]{:S(2)}) copy-start(bf16[32,64,128]{2,1,0:T(8,128)(2,1)} %copy-done.3) | copy-start | bytes 1572868
  96.1 17.2 %copy-start.10 = (s32[64,1,4]{2,1,0:T(1,128)S(1)}, s32[64,1,4]{2,1,0:T(1,128)}, u32[]{:S(2)}) copy-start(s32[64,1,4]{2,1,0:T(1,128)} %slice_convert_fusion) | copy-start | bytes 3076
  96.1 17.2 %copy-start.13 = (s32[3]{0:T(128)S(1)}, s32[3]{0:T(128)}, u32[]{:S(2)}) copy-start(s32[3]{0:T(128)} %pad_add_fusion.1.place_ref) | copy-start | bytes 40
  96.2 17.2 %copy-start.7 = (bf16[32,64,128]{2,1,0:T(8,128)(2,1)S(1)}, bf16[32,64,128]{2,1,0:T(8,128)(2,1)}, u32[]{:S(2)}) copy-start(bf16[32,64,128]{2,1,0:T(8,128)(2,1)} %copy-done.6) | copy-start | bytes 1572868
  110.9 17.4 %collective-permute-start.6 = (s16[800,512]{1,0:T(8,128)(2,1)}, s16[800,512]{1,0:T(8,128)(2,1)S(1)}, u32[]{:S(2)}, u32[]{:S(2)}) collective-permute-start(s16[800,512]{1,0:T(8,128)(2,1)} %get-tuple-element.46), channel_id=1, source_target_pairs={{0,1},{1,0},{2,3},{3,2},{4,5},{5,4},{6,7},{7,6},{8,9},{9,8},{10,11... | collective-permute-start | bytes 2457608 | tf_op jit(solution)/shard_map/ppermute | solution.py:442
  111.2 17.1 %collective-permute-start.7 = (s16[800,512]{1,0:T(8,128)(2,1)}, s16[800,512]{1,0:T(8,128)(2,1)S(1)}, u32[]{:S(2)}, u32[]{:S(2)}) collective-permute-start(s16[800,512]{1,0:T(8,128)(2,1)} %get-tuple-element.47), channel_id=1, source_target_pairs={{0,3},{3,0},{1,2},{2,1},{4,7},{7,4},{5,6},{6,5},{8,11},{11,8},{9,1... | collective-permute-start | bytes 2457608 | tf_op jit(solution)/shard_map/ppermute | solution.py:442
  113.3 15.0 %copy-start.5 = (f32[2,2,12,32,512]{4,3,2,1,0:T(8,128)S(1)}, f32[2,2,12,32,512]{4,3,2,1,0:T(8,128)}, u32[]{:S(2)}) copy-start(f32[2,2,12,32,512]{4,3,2,1,0:T(8,128)} %get-tuple-element.45.keep_ref) | copy-start | bytes 9437188
  130.1 8.1 %collective-permute-start.8 = (s16[400,512]{1,0:T(8,128)(2,1)S(1)}, s16[400,512]{1,0:T(8,128)(2,1)S(1)}, u32[]{:S(2)}, u32[]{:S(2)}) collective-permute-start(s16[400,512]{1,0:T(8,128)(2,1)S(1)} %get-tuple-element.51), channel_id=1, source_target_pairs={{0,3},{3,0},{1,2},{2,1},{4,7},{7,4},{5,6},{6,5},{8,11},{11,8},{9,1... | collective-permute-start | bytes 1228808 | tf_op jit(solution)/shard_map/ppermute | solution.py:442
  132.0 6.8 %collective-permute-start.9 = (s16[400,512]{1,0:T(8,128)(2,1)S(1)}, s16[400,512]{1,0:T(8,128)(2,1)S(1)}, u32[]{:S(2)}, u32[]{:S(2)}) collective-permute-start(s16[400,512]{1,0:T(8,128)(2,1)S(1)} %get-tuple-element.52), channel_id=1, source_target_pairs={{0,1},{1,0},{2,3},{3,2},{4,5},{5,4},{6,7},{7,6},{8,9},{9,8},{10,11... | collective-permute-start | bytes 1228808 | tf_op jit(solution)/shard_map/ppermute | solution.py:442
  138.8 16.6 %collective-permute-start.10 = (s16[800,512]{1,0:T(8,128)(2,1)S(1)}, s16[800,512]{1,0:T(8,128)(2,1)S(1)}, u32[]{:S(2)}, u32[]{:S(2)}) collective-permute-start(s16[800,512]{1,0:T(8,128)(2,1)S(1)} %get-tuple-element.57), channel_id=1, source_target_pairs={{0,1},{1,0},{2,3},{3,2},{4,5},{5,4},{6,7},{7,6},{8,9},{9,8},{10,11... | collective-permute-start | bytes 2457608 | tf_op jit(solution)/shard_map/ppermute | solution.py:442
  139.1 16.3 %collective-permute-start.11 = (s16[800,512]{1,0:T(8,128)(2,1)S(1)}, s16[800,512]{1,0:T(8,128)(2,1)S(1)}, u32[]{:S(2)}, u32[]{:S(2)}) collective-permute-start(s16[800,512]{1,0:T(8,128)(2,1)S(1)} %get-tuple-element.58), channel_id=1, source_target_pairs={{0,3},{3,0},{1,2},{2,1},{4,7},{7,4},{5,6},{6,5},{8,11},{11,8},{9,1... | collective-permute-start | bytes 2457608 | tf_op jit(solution)/shard_map/ppermute | solution.py:442
  142.0 42.1 %collective-permute-start.17 = (s16[800,512]{1,0:T(8,128)(2,1)}, s16[800,512]{1,0:T(8,128)(2,1)}, u32[]{:S(2)}, u32[]{:S(2)}) collective-permute-start(s16[800,512]{1,0:T(8,128)(2,1)} %finish_virt.1), channel_id=1, source_target_pairs={{0,0},{1,1},{2,2},{3,3},{4,64},{5,65},{6,66},{7,67},{8,128},{9,129... | collective-permute-start | bytes 2457608 | tf_op jit(solution)/shard_map/ppermute | solution.py:495
  158.0 1.2 copy-start.8
  159.2 8.2 %collective-permute-start.12 = (s16[400,512]{1,0:T(8,128)(2,1)}, s16[400,512]{1,0:T(8,128)(2,1)S(1)}, u32[]{:S(2)}, u32[]{:S(2)}) collective-permute-start(s16[400,512]{1,0:T(8,128)(2,1)} %get-tuple-element.60), channel_id=1, source_target_pairs={{0,3},{3,0},{1,2},{2,1},{4,7},{7,4},{5,6},{6,5},{8,11},{11,8},{9,1... | collective-permute-start | bytes 1228808 | tf_op jit(solution)/shard_map/ppermute | solution.py:442
  160.5 7.1 %collective-permute-start.13 = (s16[400,512]{1,0:T(8,128)(2,1)}, s16[400,512]{1,0:T(8,128)(2,1)}, u32[]{:S(2)}, u32[]{:S(2)}) collective-permute-start(s16[400,512]{1,0:T(8,128)(2,1)} %get-tuple-element.61), channel_id=1, source_target_pairs={{0,1},{1,0},{2,3},{3,2},{4,5},{5,4},{6,7},{7,6},{8,9},{9,8},{10,11... | collective-permute-start | bytes 1228808 | tf_op jit(solution)/shard_map/ppermute | solution.py:442
  167.6 1.4 copy-start.9
  172.0 0.9 copy-start.1
  172.9 11.2 %collective-permute-start.14 = (s16[1,800,128]{2,1,0:T(8,128)(2,1)}, s16[1,800,128]{2,1,0:T(8,128)(2,1)S(1)}, u32[]{:S(2)}, u32[]{:S(2)}) collective-permute-start(s16[1,800,128]{2,1,0:T(8,128)(2,1)} %get-tuple-element.67), channel_id=1, source_target_pairs={{0,16},{4,20},{8,24},{12,28},{16,32},{20,36},{24,40},{28,44},{32,4... | collective-permute-start | bytes 614408 | tf_op jit(solution)/shard_map/ppermute | solution.py:504
  178.2 10.0 %collective-permute-start.15 = (s16[1,800,128]{2,1,0:T(8,128)(2,1)}, s16[1,800,128]{2,1,0:T(8,128)(2,1)S(1)}, u32[]{:S(2)}, u32[]{:S(2)}) collective-permute-start(s16[1,800,128]{2,1,0:T(8,128)(2,1)} %get-tuple-element.66), channel_id=1, source_target_pairs={{0,32},{4,36},{8,40},{12,44},{16,48},{20,52},{24,56},{28,60},{32,0... | collective-permute-start | bytes 614408 | tf_op jit(solution)/shard_map/ppermute | solution.py:504
  181.6 18.0 %collective-permute-start.16 = (s16[1,800,128]{2,1,0:T(8,128)(2,1)S(1)}, s16[1,800,128]{2,1,0:T(8,128)(2,1)}, u32[]{:S(2)}, u32[]{:S(2)}) collective-permute-start(s16[1,800,128]{2,1,0:T(8,128)(2,1)S(1)} %get-tuple-element.65), channel_id=1, source_target_pairs={{0,48},{4,52},{8,56},{12,60},{16,0},{20,4},{24,8},{28,12},{32,16},... | collective-permute-start | bytes 614408 | tf_op jit(solution)/shard_map/ppermute | solution.py:504
  188.2 0.7 copy-start.11
  199.7 1.1 copy-start.2
  200.8 0.9 copy-start.12
  207.5 4.2 %collective-permute-start.18 = (f32[24,24]{1,0:T(8,128)S(1)}, f32[24,24]{1,0:T(8,128)S(1)}, u32[]{:S(2)}, u32[]{:S(2)}) collective-permute-start(f32[24,24]{1,0:T(8,128)S(1)} %reduce_sum.9), channel_id=1, source_target_pairs={{0,2},{1,3},{2,0},{3,1},{4,6},{5,7},{6,4},{7,5},{8,10},{9,11},{10,... | collective-permute-start | bytes 6920 | tf_op jit(solution)/shard_map/ppermute | solution.py:436
  209.0 3.8 %collective-permute-start.19 = (f32[24,24]{1,0:T(8,128)S(1)}, f32[24,24]{1,0:T(8,128)S(1)}, u32[]{:S(2)}, u32[]{:S(2)}) collective-permute-start(f32[24,24]{1,0:T(8,128)S(1)} %reduce_sum.9), channel_id=1, source_target_pairs={{0,1},{1,2},{2,3},{3,0},{4,5},{5,6},{6,7},{7,4},{8,9},{9,10},{10,1... | collective-permute-start | bytes 6920 | tf_op jit(solution)/shard_map/ppermute | solution.py:436
  210.0 2.7 %collective-permute-start.20 = (f32[24,24]{1,0:T(8,128)S(1)}, f32[24,24]{1,0:T(8,128)S(1)}, u32[]{:S(2)}, u32[]{:S(2)}) collective-permute-start(f32[24,24]{1,0:T(8,128)S(1)} %reduce_sum.9), channel_id=1, source_target_pairs={{0,3},{1,0},{2,1},{3,2},{4,7},{5,4},{6,5},{7,6},{8,11},{9,8},{10,9... | collective-permute-start | bytes 6920 | tf_op jit(solution)/shard_map/ppermute | solution.py:436
  212.7 7.5 %collective-permute-start.21 = (f32[24,24]{1,0:T(8,128)S(1)}, f32[24,24]{1,0:T(8,128)S(1)}, u32[]{:S(2)}, u32[]{:S(2)}) collective-permute-start(f32[24,24]{1,0:T(8,128)S(1)} %add_add_fusion.3), channel_id=1, source_target_pairs={{0,8},{4,12},{8,0},{12,4},{16,24},{20,28},{24,16},{28,20},{32,40},... | collective-permute-start | bytes 6920 | tf_op jit(solution)/shard_map/ppermute | solution.py:436
  213.7 7.4 %collective-permute-start.22 = (f32[24,24]{1,0:T(8,128)S(1)}, f32[24,24]{1,0:T(8,128)S(1)}, u32[]{:S(2)}, u32[]{:S(2)}) collective-permute-start(f32[24,24]{1,0:T(8,128)S(1)} %add_add_fusion.3), channel_id=1, source_target_pairs={{0,4},{4,8},{8,12},{12,0},{16,20},{20,24},{24,28},{28,16},{32,36},... | collective-permute-start | bytes 6920 | tf_op jit(solution)/shard_map/ppermute | solution.py:436
  220.3 3.1 %collective-permute-start.23 = (f32[24,24]{1,0:T(8,128)S(1)}, f32[24,24]{1,0:T(8,128)S(1)}, u32[]{:S(2)}, u32[]{:S(2)}) collective-permute-start(f32[24,24]{1,0:T(8,128)S(1)} %add_add_fusion.3), channel_id=1, source_target_pairs={{0,12},{4,0},{8,4},{12,8},{16,28},{20,16},{24,20},{28,24},{32,44},... | collective-permute-start | bytes 6920 | tf_op jit(solution)/shard_map/ppermute | solution.py:436
  223.4 4.1 %collective-permute-start.24 = (f32[24,24]{1,0:T(8,128)S(1)}, f32[24,24]{1,0:T(8,128)S(1)}, u32[]{:S(2)}, u32[]{:S(2)}) collective-permute-start(f32[24,24]{1,0:T(8,128)S(1)} %add_add_fusion.2), channel_id=1, source_target_pairs={{0,128},{64,192},{128,0},{192,64},{1,129},{65,193},{129,1},{193,65... | collective-permute-start | bytes 6920 | tf_op jit(solution)/shard_map/ppermute | solution.py:436
  223.7 3.8 %collective-permute-start.25 = (f32[24,24]{1,0:T(8,128)S(1)}, f32[24,24]{1,0:T(8,128)S(1)}, u32[]{:S(2)}, u32[]{:S(2)}) collective-permute-start(f32[24,24]{1,0:T(8,128)S(1)} %add_add_fusion.2), channel_id=1, source_target_pairs={{0,64},{64,128},{128,192},{192,0},{1,65},{65,129},{129,193},{193,1... | collective-permute-start | bytes 6920 | tf_op jit(solution)/shard_map/ppermute | solution.py:436
  224.2 3.4 %collective-permute-start.26 = (f32[24,24]{1,0:T(8,128)S(1)}, f32[24,24]{1,0:T(8,128)S(1)}, u32[]{:S(2)}, u32[]{:S(2)}) collective-permute-start(f32[24,24]{1,0:T(8,128)S(1)} %add_add_fusion.2), channel_id=1, source_target_pairs={{0,192},{64,0},{128,64},{192,128},{1,193},{65,1},{129,65},{193,129... | collective-permute-start | bytes 6920 | tf_op jit(solution)/shard_map/ppermute | solution.py:436
  227.6 8.0 %collective-permute-start.27 = (f32[24,24]{1,0:T(8,128)S(1)}, f32[24,24]{1,0:T(8,128)S(1)}, u32[]{:S(2)}, u32[]{:S(2)}) collective-permute-start(f32[24,24]{1,0:T(8,128)S(1)} %add_add_fusion.1), channel_id=1, source_target_pairs={{0,32},{4,36},{8,40},{12,44},{16,48},{20,52},{24,56},{28,60},{32,0... | collective-permute-start | bytes 6920 | tf_op jit(solution)/shard_map/ppermute | solution.py:436
  232.0 4.7 %collective-permute-start.28 = (f32[24,24]{1,0:T(8,128)S(1)}, f32[24,24]{1,0:T(8,128)S(1)}, u32[]{:S(2)}, u32[]{:S(2)}) collective-permute-start(f32[24,24]{1,0:T(8,128)S(1)} %add_add_fusion.1), channel_id=1, source_target_pairs={{0,16},{4,20},{8,24},{12,28},{16,32},{20,36},{24,40},{28,44},{32,4... | collective-permute-start | bytes 6920 | tf_op jit(solution)/shard_map/ppermute | solution.py:436
  232.8 3.9 %collective-permute-start.29 = (f32[24,24]{1,0:T(8,128)S(1)}, f32[24,24]{1,0:T(8,128)S(1)}, u32[]{:S(2)}, u32[]{:S(2)}) collective-permute-start(f32[24,24]{1,0:T(8,128)S(1)} %add_add_fusion.1), channel_id=1, source_target_pairs={{0,48},{4,52},{8,56},{12,60},{16,0},{20,4},{24,8},{28,12},{32,16},... | collective-permute-start | bytes 6920 | tf_op jit(solution)/shard_map/ppermute | solution.py:436
  (3 other events, 2.0 us)

commit v7 on v6

--- a/solution.py
+++ b/solution.py
@@ -175,12 +175,19 @@
 
 def virt_last_body(meta_ref, place_ref, *rest, plan):
     sources, (keep_ref, send0_ref, send1_ref) = rest[:6], rest[6:9]
-    refs, (level_ref, sems) = rest[9:15], rest[15:]
-    for load in start_all(sources, refs, sems):
+    refs, (acc_ref, level_ref, sems) = rest[9:15], rest[15:]
+    *loads, before = start_all(sources, refs, sems)
+    acc_ref[...] = jnp.zeros(acc_ref.shape, F32)
+    for load in loads:
         load.wait()
-    acc_ref = refs[5]
     add_virt(meta_ref, OWNERS // 2, refs[:4], refs[4], acc_ref)
-    split_pieces(place_ref, plan, piece_rows(acc_ref), keep_ref, (send0_ref, send1_ref), level_ref)
+    before.wait()
+    these, those = piece_rows(acc_ref), piece_rows(refs[5])
+
+    def rows_of(first, piece):
+        return these(first, piece) + those(first, piece)
+
+    split_pieces(place_ref, plan, rows_of, keep_ref, (send0_ref, send1_ref), level_ref)
 
 
 def piece_rows(acc_ref):
@@ -261,7 +268,7 @@
         in_specs=[SMEM] * 2 + [ANY] * 6,
         out_specs=[VMEM] * 3,
         out_shape=step_shapes(plan),
-        scratch_shapes=scratch_like(operands) + [level_scratch(plan), pltpu.SemaphoreType.DMA((6,))],
+        scratch_shapes=scratch_like(operands) + [pltpu.VMEM(ACC, F32), level_scratch(plan), pltpu.SemaphoreType.DMA((6,))],
         compiler_params=params(55),
         name="virt_last",
     )(meta, place, *operands)
@@ -307,43 +314,62 @@
     )(place, keep, got0, got1)
 
 
-def finish_body(left_ref, got0_ref, got1_ref, out_ref, level_ref, scale_ref, *, plan, split):
-    count = 2 * plan.blocks
-    for h, got_ref in ((0, got0_ref), (1, got1_ref)):
+def finish_blocks(left_ref, got_refs, scale_ref, plan, store):
+    for h, got_ref in enumerate(got_refs):
         read_scales(got_ref, (), plan, plan.blocks, scale_ref)
 
         @pl.loop(0, plan.blocks)
         def _(b):
-            total = left_ref[h, b] + get(got_ref, (), plan, b, scale_ref)
-            index = h * plan.blocks + b
-            if split:
-                codes, level = encode(total)
-                for low in range(4):
-                    out_ref[low, at_block(plan, index), :] = codes[:, low * BS : (low + 1) * BS]
-                level_ref[pl.ds(index, 1), :] = level
-            else:
-                put(out_ref, plan, index, total, level_ref)
-
-    if split:
-        levels = level_ref[...].astype(jnp.int32).astype(S16)
-        for low in range(4):
-            out_ref[low, level_rows(plan, count), :] = levels[:, low * BS : (low + 1) * BS]
-    else:
-        put_levels(out_ref, plan, count, level_ref)
-
-
-def finish(left, got0, got1, plan, split, name):
-    rows = plan.coded(2 * plan.blocks)
-    shape = (4, rows, BS) if split else (rows, WIDE)
-    return pl.pallas_call(
-        functools.partial(finish_body, plan=plan, split=split),
+            store(h * plan.blocks + b, left_ref[h, b] + get(got_ref, (), plan, b, scale_ref))
+
+
+def finish_virt_body(left_ref, got0_ref, got1_ref, out_ref, level_ref, scale_ref, *, plan):
+    def store(index, total):
+        put(out_ref, plan, index, total, level_ref)
+
+    finish_blocks(left_ref, (got0_ref, got1_ref), scale_ref, plan, store)
+    put_levels(out_ref, plan, 2 * plan.blocks, level_ref)
+
+
+def finish_occ_body(place_ref, left_ref, got0_ref, got1_ref, *rest, plan):
+    out_refs, (code_ref, level_ref, scale_ref) = rest[:4], rest[4:]
+    lanes = [pl.ds(pl.multiple_of((place_ref[0] + d) % 4 * BS, BS), BS) for d in range(4)]
+
+    def store(index, total):
+        codes, level = encode(total)
+        code_ref[...] = codes
+        level_ref[pl.ds(index, 1), :] = level
+        for out_ref, part in zip(out_refs, lanes):
+            out_ref[at_block(plan, index), :] = code_ref[:, part]
+
+    finish_blocks(left_ref, (got0_ref, got1_ref), scale_ref, plan, store)
+    for out_ref, part in zip(out_refs, lanes):
+        out_ref[level_rows(plan, 2 * plan.blocks), :] = level_ref[:, part].astype(jnp.int32).astype(S16)
+
+
+def finish_virt(left, got0, got1, plan):
+    return pl.pallas_call(
+        functools.partial(finish_virt_body, plan=plan),
         in_specs=[VMEM] * 3,
         out_specs=VMEM,
-        out_shape=jax.ShapeDtypeStruct(shape, S16),
+        out_shape=jax.ShapeDtypeStruct((plan.coded(2 * plan.blocks), WIDE), S16),
         scratch_shapes=[level_scratch(plan), level_scratch(plan)],
         compiler_params=params(12),
-        name=name,
+        name="finish_virt",
     )(left, got0, got1)
+
+
+def finish_occ(place, left, got0, got1, plan):
+    part = jax.ShapeDtypeStruct((plan.coded(2 * plan.blocks), BS), S16)
+    return pl.pallas_call(
+        functools.partial(finish_occ_body, plan=plan),
+        in_specs=[SMEM] + [VMEM] * 3,
+        out_specs=[VMEM] * 4,
+        out_shape=[part] * 4,
+        scratch_shapes=[pltpu.VMEM((plan.rows, WIDE), S16), level_scratch(plan), level_scratch(plan)],
+        compiler_params=params(12),
+        name="finish_occ",
+    )(place, left, got0, got1)
 
 
 def pair_body(place_ref, own_ref, one_ref, two_ref, three_ref, virt_ref, out_ref, occ_ref, vir_ref, wide_ref, thin_ref, *, plan):
@@ -364,13 +390,12 @@
 
     for d, ref in enumerate((own_ref, one_ref, two_ref, three_ref)):
         source = (here + 4 - d) % 4
-        lead = (here,) if d == 0 else (0,)
-        read_scales(ref, lead, plan, count, thin_ref)
+        read_scales(ref, (), plan, count, thin_ref)
         rows = pl.ds(pl.multiple_of(source * QUARTER, QUARTER), QUARTER)
 
         @pl.loop(0, NP)
         def _(p):
-            occ_ref[p, rows, :] = get(ref, lead, plan, p, thin_ref)
+            occ_ref[p, rows, :] = get(ref, (), plan, p, thin_ref)
 
     @pl.loop(0, NP)
     def _(p):
@@ -401,10 +426,6 @@
     return [(i, (i + step) % size) for i in range(size)]
 
 
-def rotate_low(step):
-    return [(c, c - c % 4 + (c + step) % 4) for c in range(COLS)]
-
-
 def rotate_high(step):
     return [(c, (c + 4 * step) % COLS) for c in range(COLS)]
 
@@ -425,16 +446,10 @@
 ]
 
 
-def tree_sum(values):
-    rounds = (
-        ("layer", [rotate(LAYERS, d) for d in (1, 2, 3)]),
-        ("col", [rotate_low(d) for d in (1, 2, 3)]),
-        ("row", [rotate(ROWS, d) for d in (1, 2, 3)]),
-        ("col", [rotate_high(d) for d in (1, 2, 3)]),
-    )
-    for axis, perms in rounds:
-        one, two, three = [lax.ppermute(values, axis, perm) for perm in perms]
-        values = (values + two) + (one + three)
+def sum_all(values):
+    for axes in ("col", ("row", "layer")):
+        copies = jnp.broadcast_to(values[None], (16, *values.shape))
+        values = jnp.sum(lax.all_to_all(copies, axes, 0, 0, tiled=True), axis=0)
     return values
 
 
@@ -472,7 +487,7 @@
     up, down = rotate(ROWS, 1), rotate(ROWS, -1)
     prev_a = lax.ppermute(own_a, "row", up)
     next_a = lax.ppermute(own_a, "row", down)
-    prev_a, next_a, own_b, occ_blocks = after(prev_a, next_a, own_b, occ_blocks)
+    prev_a, next_a, own_b, occ_blocks, meta = after(prev_a, next_a, own_b, occ_blocks, meta)
     far_a = lax.ppermute(prev_a, "row", up)
     next_b = lax.ppermute(own_b, "row", down)
     far_a, next_b, own_b = after(far_a, next_b, own_b)
@@ -490,21 +505,16 @@
     v_got = layer_swap(v0, v1, SECOND)
     o0, o1, *v_got = after(o0, o1, *v_got)
     o_got = layer_swap(o0, o1, FIRST)
-    virt = finish(v_left, *v_got, plan, False, "finish_virt")
+    virt = finish_virt(v_left, *v_got, plan)
     virt, o_keep = after(virt, o_keep)
     virt = lax.ppermute(virt, ALL, SWAP)
     o_left, o0, o1 = halve(place, o_keep, *o_got, plan, "halve_occ")
     o_got = layer_swap(o0, o1, SECOND)
-    occ = finish(o_left, *o_got, plan, True, "finish_occ")
-
-    low = col_place // 4
-    others = []
-    for d in (1, 2, 3):
-        part = lax.dynamic_slice_in_dim(occ, (low + d) % 4, 1, 0)
-        others.append(lax.ppermute(part, "col", rotate_high(d)))
-    here = jnp.stack([low, col_place % 4])
+    here = jnp.stack([col_place // 4, col_place % 4])
+    occ, *others = finish_occ(here, o_left, *o_got, plan)
+    others = [lax.ppermute(part, "col", rotate_high(d)) for d, part in zip((1, 2, 3), others)]
     partial = pair(here, occ, others, virt, plan)
-    return tree_sum(jnp.sum(partial, axis=-1))
+    return sum_all(jnp.sum(partial, axis=-1))
 
 
 def solution(mesh):

time: 240 us -> 232 us (0.967)
  blocking collectives: 43.4 us -> 69.9 us
  starting transfers between devices: 58.6 us -> 36 us
  waiting for transfers between devices: 51 us -> 43.9 us
  local copies, waits for them, and re-layouts: 22.2 us -> 18.9 us
    all_to_all x0 -> x2, blocking collectives: none -> 26.4 us  [sum_all(): values = jnp.sum(lax.all_to_all(copies, axes, 0, 0, tiled=True), axis=0)]
    ppermute x15 -> x3, starting transfers between devices: 33.8 us -> 11.2 us  [on_device(): lax.ppermute(part, 'col', rotate_high(d))]
    ppermute x15 -> x3, waiting for transfers between devices: 21.3 us -> 16 us  [on_device(): lax.ppermute(part, 'col', rotate_high(d))]
    unnamed x42 -> x36, local copies, waits for them, and re-layouts: 12.5 us -> 8.31 us
  transfers between devices with their start and end apart: 30 -> 18, of which waited for: 15 -> 9; matrix products, arithmetic and copies ran while one was open for 5% -> 4% of each run, Pallas kernels for 14% -> 15%
where the time goes in v7:
time: 232 us; the launch traced here: 231 us
  blocking collectives  69.9 us (30%)
  Pallas kernels  57.2 us (25%)
  waiting for transfers between devices  43.9 us (19%)
  starting transfers between devices  36 us (16%)
  local copies, waits for them, and re-layouts  18.9 us (8%)
  other arithmetic  4.46 us (2%)
    all_to_all x1, blocking collectives, on_device(): own = lax.all_to_all(send, ('col', 'layer'), 0, 0, tiled=True)  43.5 us
    all_to_all x2, blocking collectives, sum_all(): values = jnp.sum(lax.all_to_all(copies, axes, 0, 0, tiled=True), axis=0)  26.4 us
    ppermute x4, waiting for transfers between devices, layer_swap(): lax.ppermute(send0, 'layer', perms[0])  16 us
    ppermute x3, waiting for transfers between devices, on_device(): lax.ppermute(part, 'col', rotate_high(d))  16 us
    pallas_call x1, Pallas kernels, contract_occ(): pl.pallas_call(functools.partial(occ_body, plan=plan), in_specs=[SMEM] *...  14.9 us
    pallas_call x1, Pallas kernels, contract_virt_last(): pl.pallas_call(functools.partial(virt_last_body, plan=plan), in_specs=[SM...  13 us
    pallas_call x1, Pallas kernels, contract_virt_first(): pl.pallas_call(virt_first_body, in_specs=[SMEM] + [ANY] * 5, out_specs=AN...  11.7 us
    ppermute x3, starting transfers between devices, on_device(): lax.ppermute(part, 'col', rotate_high(d))  11.2 us
  transfers between devices with their start and end apart: 18, of which 9 were waited for; matrix products, arithmetic and copies ran while one was open for 4% of the time, Pallas kernels for 15%

profile of v7, /device:TPU:1, one launch (start us, length us, event | category | flops | bytes accessed | tf_op | source)
XLA Modules:
  0.0 230.7 jit_solution(16289277327757380752)
XLA Ops:
  0.0 1.8 copy-done
  1.9 0.6 copy-done.10
  2.5 0.7 copy-done.11
  3.2 0.7 copy-done.12
  3.9 0.7 copy-done.13
  4.5 3.3 %build_send.1 = bf16[64,72,128]{2,1,0:T(8,128)(2,1)S(1)} custom-call(s32[88]{0:T(128)S(1)} %copy-done.10, s32[88]{0:T(128)S(1)} %copy-done.11, s32[88]{0:T(128)S(1)} %copy-done.12, s32[88]{0:T(128)S(1)} %copy-done.13, bf16[88,32,128]{2,1,0:T(8,128)(2,1)S(1)} %constant_dynamic-slice_fusion.tiles_ref), custom_call_target="tpu_custom_call" | custom-call | tf_op jit(solution)/shard_map/build_send/pallas_call | solution.py:113
  7.9 43.5 %all_to_all.15 = bf16[64,72,128]{2,1,0:T(8,128)(2,1)} all-to-all(bf16[64,72,128]{2,1,0:T(8,128)(2,1)S(1)} %build_send.1), channel_id=1, replica_groups=mesh['row'=4,'col'=16,'layer'=4] {'col','layer'}, dimensions={0} | all-to-all | bytes 2359296 | tf_op jit(solution)/shard_map/all_to_all | solution.py:480
  51.4 2.1 fusion
  53.5 1.3 collective-permute-start
  54.8 1.4 collective-permute-start.1
  56.2 7.9 %copy.9 = bf16[40,128,512]{1,2,0:T(8,128)(2,1)} copy(bf16[40,128,512]{2,1,0:T(8,128)(2,1)} %bitcast.17) | data formatting | bytes 10485760 | tf_op jit(solution)/shard_map/reshape | solution.py:483
  64.1 1.5 slice_convert_fusion
  65.6 1.4 collective-permute-done.rest_1_
  67.0 1.0 collective-permute-start.2
  68.0 1.7 collective-permute-start.3
  69.7 9.8 %collective-permute-done.2.rest_3_ = bf16[32,64,128]{2,1,0:T(8,128)(2,1)S(1)} collective-permute-done((bf16[32,64,128]{2,1,0:T(8,128)(2,1)}, bf16[32,64,128]{2,1,0:T(8,128)(2,1)S(1)}, u32[]{:S(2)}, u32[]{:S(2)}) %collective-permute-start.2) | collective-permute-done | bytes 524320 | tf_op jit(solution)/shard_map/ppermute | solution.py:491
  79.6 0.7 copy-done.4
  80.3 2.0 collective-permute-start.5
  82.3 0.6 pad_add_fusion.1.place_ref
  82.8 11.7 %virt_first.1.rest_5_ = f32[24,128,512]{2,1,0:T(8,128)} custom-call(s32[64,4]{1,0:T(8,128)} %bitcast.12, bf16[32,64,128]{2,1,0:T(8,128)(2,1)} %get-tuple-element.74.rest_0_, bf16[32,64,128]{2,1,0:T(8,128)(2,1)} %collective-permute-done.rest_1_, bf16[32,64,128]{2,1,0:T(8,128)(2,1)} %collective-permute-done.1.rest_2_, bf16[32,64,128]{2,1,0:T(8,128)(2,1)} %copy-done.4, ...), custom_call_target="tpu_custom_call" | custom-call | tf_op jit(solution)/shard_map/virt_first/pallas_call | solution.py:253
  94.7 13.0 %virt_last.1 = (f32[2,2,12,32,512]{4,3,2,1,0:T(8,128)}, s16[800,512]{1,0:T(8,128)(2,1)}, s16[800,512]{1,0:T(8,128)(2,1)}) custom-call(s32[64,4]{1,0:T(8,128)} %bitcast.13, s32[3]{0:T(128)} %pad_add_fusion.1.place_ref, bf16[32,64,128]{2,1,0:T(8,128)(2,1)} %copy-done.1, bf16[32,64,128]{2,1,0:T(8,128)(2,1)} %collective-permute-done.4.rest_1_.rest_5_, ...), custom_call_target="tpu_custom_call" | custom-call | tf_op jit(solution)/shard_map/virt_last/pallas_call | solution.py:266
  108.0 2.1 collective-permute-start.7
  110.2 14.9 %contract_occ.1 = (f32[2,2,12,32,512]{4,3,2,1,0:T(8,128)S(1)}, s16[800,512]{1,0:T(8,128)(2,1)S(1)}, s16[800,512]{1,0:T(8,128)(2,1)S(1)}) custom-call(s32[64,4]{1,0:T(8,128)S(1)} %bitcast.14, s32[3]{0:T(128)S(1)} %copy-done.9, bf16[32,64,128]{2,1,0:T(8,128)(2,1)} %get-tuple-element.74.rest_0_, bf16[32,64,128]{2,1,0:T(8,128)(2,1)} %collective-permute-done.rest_1_, ...), custom_call_target="tpu_custom_call" | custom-call | tf_op jit(solution)/shard_map/contract_occ/pallas_call | solution.py:278
  125.1 1.8 halve_virt.1
  127.0 1.9 collective-permute-start.8
  128.8 6.2 %collective-permute-done.8.got0_ref = s16[400,512]{1,0:T(8,128)(2,1)S(1)} collective-permute-done((s16[400,512]{1,0:T(8,128)(2,1)S(1)}, s16[400,512]{1,0:T(8,128)(2,1)S(1)}, u32[]{:S(2)}, u32[]{:S(2)}) %collective-permute-start.8) | collective-permute-done | bytes 409632 | tf_op jit(solution)/shard_map/ppermute | solution.py:457
  135.1 0.6 collective-permute-done.9.got1_ref
  135.9 0.9 collective-permute-start.11
  136.8 2.0 finish_virt.1
  138.8 10.5 %collective-permute-start.17 = (s16[800,512]{1,0:T(8,128)(2,1)}, s16[800,512]{1,0:T(8,128)(2,1)}, u32[]{:S(2)}, u32[]{:S(2)}) collective-permute-start(s16[800,512]{1,0:T(8,128)(2,1)} %finish_virt.1), channel_id=1, source_target_pairs={{0,0},{1,1},{2,2},{3,3},{4,64},{5,65},{6,66},{7,67},{8,128},{9,129... | collective-permute-start | bytes 2457608 | tf_op jit(solution)/shard_map/ppermute | solution.py:510
  149.3 2.9 %collective-permute-done.10.got0_ref = s16[800,512]{1,0:T(8,128)(2,1)S(1)} collective-permute-done((s16[800,512]{1,0:T(8,128)(2,1)S(1)}, s16[800,512]{1,0:T(8,128)(2,1)S(1)}, u32[]{:S(2)}, u32[]{:S(2)}) %collective-permute-start.10) | collective-permute-done | bytes 819232 | tf_op jit(solution)/shard_map/ppermute | solution.py:457
  152.2 2.7 %halve_occ.1 = (f32[2,12,32,512]{3,2,1,0:T(8,128)S(1)}, s16[400,512]{1,0:T(8,128)(2,1)}, s16[400,512]{1,0:T(8,128)(2,1)}) custom-call(s32[3]{0:T(128)S(1)} %copy-done.9, f32[2,2,12,32,512]{4,3,2,1,0:T(8,128)S(1)} %get-tuple-element.62.keep_ref, s16[800,512]{1,0:T(8,128)(2,1)S(1)} %collective-permute-done.10.got0_ref, ...), custom_call_target="tpu_custom_call" | custom-call | tf_op jit(solution)/shard_map/halve_occ/pallas_call | solution.py:306
  154.9 1.2 copy-done.6
  156.1 1.3 collective-permute-start.12
  157.5 6.8 %collective-permute-done.12.got0_ref = s16[400,512]{1,0:T(8,128)(2,1)S(1)} collective-permute-done((s16[400,512]{1,0:T(8,128)(2,1)}, s16[400,512]{1,0:T(8,128)(2,1)S(1)}, u32[]{:S(2)}, u32[]{:S(2)}) %collective-permute-start.12) | collective-permute-done | bytes 409632 | tf_op jit(solution)/shard_map/ppermute | solution.py:457
  164.5 1.4 copy-done.7
  165.9 2.2 finish_occ.1
  168.2 5.4 %collective-permute-start.14 = (s16[800,128]{1,0:T(8,128)(2,1)S(1)}, s16[800,128]{1,0:T(8,128)(2,1)S(1)}, u32[]{:S(2)}, u32[]{:S(2)}) collective-permute-start(s16[800,128]{1,0:T(8,128)(2,1)S(1)} %get-tuple-element.69), channel_id=1, source_target_pairs={{0,16},{4,20},{8,24},{12,28},{16,32},{20,36},{24,40},{28,44},{32,4... | collective-permute-start | bytes 614408 | tf_op jit(solution)/shard_map/ppermute | solution.py:515
  173.6 3.4 %collective-permute-start.15 = (s16[800,128]{1,0:T(8,128)(2,1)S(1)}, s16[800,128]{1,0:T(8,128)(2,1)S(1)}, u32[]{:S(2)}, u32[]{:S(2)}) collective-permute-start(s16[800,128]{1,0:T(8,128)(2,1)S(1)} %get-tuple-element.70), channel_id=1, source_target_pairs={{0,32},{4,36},{8,40},{12,44},{16,48},{20,52},{24,56},{28,60},{32,0... | collective-permute-start | bytes 614408 | tf_op jit(solution)/shard_map/ppermute | solution.py:515
  177.0 2.4 %collective-permute-start.16 = (s16[800,128]{1,0:T(8,128)(2,1)S(1)}, s16[800,128]{1,0:T(8,128)(2,1)S(1)}, u32[]{:S(2)}, u32[]{:S(2)}) collective-permute-start(s16[800,128]{1,0:T(8,128)(2,1)S(1)} %get-tuple-element.71), channel_id=1, source_target_pairs={{0,48},{4,52},{8,56},{12,60},{16,0},{20,4},{24,8},{28,12},{32,16},... | collective-permute-start | bytes 614408 | tf_op jit(solution)/shard_map/ppermute | solution.py:515
  179.4 4.1 %collective-permute-done.15.two_ref = s16[800,128]{1,0:T(8,128)(2,1)S(1)} collective-permute-done((s16[800,128]{1,0:T(8,128)(2,1)S(1)}, s16[800,128]{1,0:T(8,128)(2,1)S(1)}, u32[]{:S(2)}, u32[]{:S(2)}) %collective-permute-start.15) | collective-permute-done | bytes 204832 | tf_op jit(solution)/shard_map/ppermute | solution.py:515
  183.5 11.9 %collective-permute-done.16.three_ref = s16[800,128]{1,0:T(8,128)(2,1)S(1)} collective-permute-done((s16[800,128]{1,0:T(8,128)(2,1)S(1)}, s16[800,128]{1,0:T(8,128)(2,1)S(1)}, u32[]{:S(2)}, u32[]{:S(2)}) %collective-permute-start.16) | collective-permute-done | bytes 204832 | tf_op jit(solution)/shard_map/ppermute | solution.py:515
  195.4 5.5 %pair.1 = f32[24,24,128]{2,1,0:T(8,128)S(1)} custom-call(s32[2]{0:T(128)S(1)} %pad_add_fusion.place_ref, s16[800,128]{1,0:T(8,128)(2,1)S(1)} %get-tuple-element.68.own_ref, s16[800,128]{1,0:T(8,128)(2,1)S(1)} %collective-permute-done.14.one_ref, s16[800,128]{1,0:T(8,128)(2,1)S(1)} %collective-permute-done.15.two_ref, ...), custom_call_target="tpu_custom_call" | custom-call | tf_op jit(solution)/shard_map/pair/pallas_call | solution.py:409
  201.2 17.1 %all_to_all.16 = f32[16,1,576]{2,1,0:T(1,128)S(1)} all-to-all(f32[16,1,576]{2,1,0:T(1,128)S(1)} %reshape.14), channel_id=1, replica_groups=mesh['row'=4,'col'=16,'layer'=4] {'col'}, dimensions={0} | all-to-all | bytes 73728 | tf_op jit(solution)/shard_map/all_to_all | solution.py:452
  218.8 0.7 reduce
  219.9 9.3 %all_to_all.17 = f32[16,1,576]{2,1,0:T(1,128)S(1)} all-to-all(f32[16,1,576]{2,1,0:T(1,128)S(1)} %reshape.16), channel_id=1, replica_groups=mesh['row'=4,'col'=16,'layer'=4] {'row','layer'}, dimensions={0} | all-to-all | bytes 73728 | tf_op jit(solution)/shard_map/all_to_all | solution.py:452
  229.2 0.7 reduce.1
  230.1 0.6 reduce_sum.29
  (51 shorter events, 2.5 us)
Async XLA Ops:
  0.0 1.8 copy-start
  1.9 0.7 copy-start.10
  2.5 0.7 copy-start.11
  3.2 0.7 copy-start.12
  3.9 0.7 copy-start.13
  53.5 26.0 %copy-start.1 = (bf16[32,64,128]{2,1,0:T(8,128)(2,1)}, bf16[32,64,128]{2,1,0:T(8,128)(2,1)S(1)}, u32[]{:S(2)}) copy-start(bf16[32,64,128]{2,1,0:T(8,128)(2,1)S(1)} %get-tuple-element.43.rest_0_.rest_4_) | copy-start | bytes 1572868
  53.5 13.6 %collective-permute-start = (bf16[32,64,128]{2,1,0:T(8,128)(2,1)}, bf16[32,64,128]{2,1,0:T(8,128)(2,1)}, u32[]{:S(2)}, u32[]{:S(2)}) collective-permute-start(bf16[32,64,128]{2,1,0:T(8,128)(2,1)} %get-tuple-element.74.rest_0_), channel_id=1, source_target_pairs={{0,64},{64,128},{128,192},{192,0},{1,65},{65,129},{129,193},{193,1... | collective-permute-start | bytes 1572872 | tf_op jit(solution)/shard_map/ppermute | solution.py:488
  54.8 12.3 %collective-permute-start.1 = (bf16[32,64,128]{2,1,0:T(8,128)(2,1)}, bf16[32,64,128]{2,1,0:T(8,128)(2,1)}, u32[]{:S(2)}, u32[]{:S(2)}) collective-permute-start(bf16[32,64,128]{2,1,0:T(8,128)(2,1)} %get-tuple-element.74.rest_0_), channel_id=1, source_target_pairs={{0,192},{64,0},{128,64},{192,128},{1,193},{65,1},{129,65},{193,129... | collective-permute-start | bytes 1572872 | tf_op jit(solution)/shard_map/ppermute | solution.py:489
  67.0 12.5 %collective-permute-start.2 = (bf16[32,64,128]{2,1,0:T(8,128)(2,1)}, bf16[32,64,128]{2,1,0:T(8,128)(2,1)S(1)}, u32[]{:S(2)}, u32[]{:S(2)}) collective-permute-start(bf16[32,64,128]{2,1,0:T(8,128)(2,1)} %collective-permute-done.rest_1_), channel_id=1, source_target_pairs={{0,64},{64,128},{128,192},{192,0},{1,65},{65,129},{129,193},{193,1... | collective-permute-start | bytes 1572872 | tf_op jit(solution)/shard_map/ppermute | solution.py:491
  68.0 11.5 %collective-permute-start.3 = (bf16[32,64,128]{2,1,0:T(8,128)(2,1)S(1)}, bf16[32,64,128]{2,1,0:T(8,128)(2,1)}, u32[]{:S(2)}, u32[]{:S(2)}) collective-permute-start(bf16[32,64,128]{2,1,0:T(8,128)(2,1)S(1)} %get-tuple-element.43.rest_0_.rest_4_), channel_id=1, source_target_pairs={{0,192},{64,0},{128,64},{192,128},{1,193},{65,1},{129,65},{193,129... | collective-permute-start | bytes 1572872 | tf_op jit(solution)/shard_map/ppermute | solution.py:492
  79.5 0.8 copy-start.4
  79.5 15.1 %collective-permute-start.4 = (bf16[32,64,128]{2,1,0:T(8,128)(2,1)S(1)}, bf16[32,64,128]{2,1,0:T(8,128)(2,1)}, u32[]{:S(2)}, u32[]{:S(2)}) collective-permute-start(bf16[32,64,128]{2,1,0:T(8,128)(2,1)S(1)} %get-tuple-element.43.rest_0_.rest_4_), channel_id=1, source_target_pairs={{0,64},{64,128},{128,192},{192,0},{1,65},{65,129},{129,193},{193,1... | collective-permute-start | bytes 1572872 | tf_op jit(solution)/shard_map/ppermute | solution.py:494
  80.3 14.3 %collective-permute-start.5 = (bf16[32,64,128]{2,1,0:T(8,128)(2,1)}, bf16[32,64,128]{2,1,0:T(8,128)(2,1)}, u32[]{:S(2)}, u32[]{:S(2)}) collective-permute-start(bf16[32,64,128]{2,1,0:T(8,128)(2,1)} %collective-permute-done.3.rest_2_.rest_6_), channel_id=1, source_target_pairs={{0,192},{64,0},{128,64},{192,128},{1,193},{65,1},{129,65},{193,129... | collective-permute-start | bytes 1572872 | tf_op jit(solution)/shard_map/ppermute | solution.py:495
  82.8 27.3 %slice-start = ((s8[5242880]{0:T(1024)(128)(4,1)}), s8[4194304]{0:T(1024)(128)(4,1)S(1)}, s32[]{:S(2)}) async-start(s8[5242880]{0:T(1024)(128)(4,1)} %bitcast.9), calls=%async_computation.3 | async-start | bytes 8388608
  94.6 15.5 %slice-start.1 = ((s8[5242880]{0:T(1024)(128)(4,1)}), s8[1048576]{0:T(1024)(128)(4,1)S(1)}, s32[]{:S(2)}) async-start(s8[5242880]{0:T(1024)(128)(4,1)} %bitcast.9), calls=%async_computation.4 | async-start | bytes 2097152
  94.6 15.5 %copy-start.2 = (bf16[32,64,128]{2,1,0:T(8,128)(2,1)S(1)}, bf16[32,64,128]{2,1,0:T(8,128)(2,1)}, u32[]{:S(2)}) copy-start(bf16[32,64,128]{2,1,0:T(8,128)(2,1)} %copy-done.1) | copy-start | bytes 1572868
  94.6 15.5 %copy-start.8 = (s32[64,1,4]{2,1,0:T(1,128)S(1)}, s32[64,1,4]{2,1,0:T(1,128)}, u32[]{:S(2)}) copy-start(s32[64,1,4]{2,1,0:T(1,128)} %slice_convert_fusion) | copy-start | bytes 3076
  94.6 15.5 %copy-start.9 = (s32[3]{0:T(128)S(1)}, s32[3]{0:T(128)}, u32[]{:S(2)}) copy-start(s32[3]{0:T(128)} %pad_add_fusion.1.place_ref) | copy-start | bytes 40
  94.6 15.5 %copy-start.5 = (bf16[32,64,128]{2,1,0:T(8,128)(2,1)S(1)}, bf16[32,64,128]{2,1,0:T(8,128)(2,1)}, u32[]{:S(2)}) copy-start(bf16[32,64,128]{2,1,0:T(8,128)(2,1)} %copy-done.4) | copy-start | bytes 1572868
  107.6 17.5 %collective-permute-start.6 = (s16[800,512]{1,0:T(8,128)(2,1)}, s16[800,512]{1,0:T(8,128)(2,1)S(1)}, u32[]{:S(2)}, u32[]{:S(2)}) collective-permute-start(s16[800,512]{1,0:T(8,128)(2,1)} %get-tuple-element.52), channel_id=1, source_target_pairs={{0,1},{1,0},{2,3},{3,2},{4,5},{5,4},{6,7},{7,6},{8,9},{9,8},{10,11... | collective-permute-start | bytes 2457608 | tf_op jit(solution)/shard_map/ppermute | solution.py:457
  108.0 17.1 %collective-permute-start.7 = (s16[800,512]{1,0:T(8,128)(2,1)}, s16[800,512]{1,0:T(8,128)(2,1)S(1)}, u32[]{:S(2)}, u32[]{:S(2)}) collective-permute-start(s16[800,512]{1,0:T(8,128)(2,1)} %get-tuple-element.53), channel_id=1, source_target_pairs={{0,3},{3,0},{1,2},{2,1},{4,7},{7,4},{5,6},{6,5},{8,11},{11,8},{9,1... | collective-permute-start | bytes 2457608 | tf_op jit(solution)/shard_map/ppermute | solution.py:457
  110.1 15.0 %copy-start.3 = (f32[2,2,12,32,512]{4,3,2,1,0:T(8,128)S(1)}, f32[2,2,12,32,512]{4,3,2,1,0:T(8,128)}, u32[]{:S(2)}) copy-start(f32[2,2,12,32,512]{4,3,2,1,0:T(8,128)} %get-tuple-element.51.keep_ref) | copy-start | bytes 9437188
  127.0 8.1 %collective-permute-start.8 = (s16[400,512]{1,0:T(8,128)(2,1)S(1)}, s16[400,512]{1,0:T(8,128)(2,1)S(1)}, u32[]{:S(2)}, u32[]{:S(2)}) collective-permute-start(s16[400,512]{1,0:T(8,128)(2,1)S(1)} %get-tuple-element.57), channel_id=1, source_target_pairs={{0,3},{3,0},{1,2},{2,1},{4,7},{7,4},{5,6},{6,5},{8,11},{11,8},{9,1... | collective-permute-start | bytes 1228808 | tf_op jit(solution)/shard_map/ppermute | solution.py:457
  128.8 6.8 %collective-permute-start.9 = (s16[400,512]{1,0:T(8,128)(2,1)S(1)}, s16[400,512]{1,0:T(8,128)(2,1)S(1)}, u32[]{:S(2)}, u32[]{:S(2)}) collective-permute-start(s16[400,512]{1,0:T(8,128)(2,1)S(1)} %get-tuple-element.58), channel_id=1, source_target_pairs={{0,1},{1,0},{2,3},{3,2},{4,5},{5,4},{6,7},{7,6},{8,9},{9,8},{10,11... | collective-permute-start | bytes 1228808 | tf_op jit(solution)/shard_map/ppermute | solution.py:457
  135.6 16.6 %collective-permute-start.10 = (s16[800,512]{1,0:T(8,128)(2,1)S(1)}, s16[800,512]{1,0:T(8,128)(2,1)S(1)}, u32[]{:S(2)}, u32[]{:S(2)}) collective-permute-start(s16[800,512]{1,0:T(8,128)(2,1)S(1)} %get-tuple-element.63), channel_id=1, source_target_pairs={{0,1},{1,0},{2,3},{3,2},{4,5},{5,4},{6,7},{7,6},{8,9},{9,8},{10,11... | collective-permute-start | bytes 2457608 | tf_op jit(solution)/shard_map/ppermute | solution.py:457
  135.9 16.3 %collective-permute-start.11 = (s16[800,512]{1,0:T(8,128)(2,1)S(1)}, s16[800,512]{1,0:T(8,128)(2,1)S(1)}, u32[]{:S(2)}, u32[]{:S(2)}) collective-permute-start(s16[800,512]{1,0:T(8,128)(2,1)S(1)} %get-tuple-element.64), channel_id=1, source_target_pairs={{0,3},{3,0},{1,2},{2,1},{4,7},{7,4},{5,6},{6,5},{8,11},{11,8},{9,1... | collective-permute-start | bytes 2457608 | tf_op jit(solution)/shard_map/ppermute | solution.py:457
  138.8 40.6 %collective-permute-start.17 = (s16[800,512]{1,0:T(8,128)(2,1)}, s16[800,512]{1,0:T(8,128)(2,1)}, u32[]{:S(2)}, u32[]{:S(2)}) collective-permute-start(s16[800,512]{1,0:T(8,128)(2,1)} %finish_virt.1), channel_id=1, source_target_pairs={{0,0},{1,1},{2,2},{3,3},{4,64},{5,65},{6,66},{7,67},{8,128},{9,129... | collective-permute-start | bytes 2457608 | tf_op jit(solution)/shard_map/ppermute | solution.py:510
  154.9 1.2 copy-start.6
  156.1 8.2 %collective-permute-start.12 = (s16[400,512]{1,0:T(8,128)(2,1)}, s16[400,512]{1,0:T(8,128)(2,1)S(1)}, u32[]{:S(2)}, u32[]{:S(2)}) collective-permute-start(s16[400,512]{1,0:T(8,128)(2,1)} %get-tuple-element.66), channel_id=1, source_target_pairs={{0,3},{3,0},{1,2},{2,1},{4,7},{7,4},{5,6},{6,5},{8,11},{11,8},{9,1... | collective-permute-start | bytes 1228808 | tf_op jit(solution)/shard_map/ppermute | solution.py:457
  157.4 7.1 %collective-permute-start.13 = (s16[400,512]{1,0:T(8,128)(2,1)}, s16[400,512]{1,0:T(8,128)(2,1)}, u32[]{:S(2)}, u32[]{:S(2)}) collective-permute-start(s16[400,512]{1,0:T(8,128)(2,1)} %get-tuple-element.67), channel_id=1, source_target_pairs={{0,1},{1,0},{2,3},{3,2},{4,5},{5,4},{6,7},{7,6},{8,9},{9,8},{10,11... | collective-permute-start | bytes 1228808 | tf_op jit(solution)/shard_map/ppermute | solution.py:457
  164.5 1.4 copy-start.7
  168.2 11.2 %collective-permute-start.14 = (s16[800,128]{1,0:T(8,128)(2,1)S(1)}, s16[800,128]{1,0:T(8,128)(2,1)S(1)}, u32[]{:S(2)}, u32[]{:S(2)}) collective-permute-start(s16[800,128]{1,0:T(8,128)(2,1)S(1)} %get-tuple-element.69), channel_id=1, source_target_pairs={{0,16},{4,20},{8,24},{12,28},{16,32},{20,36},{24,40},{28,44},{32,4... | collective-permute-start | bytes 614408 | tf_op jit(solution)/shard_map/ppermute | solution.py:515
  173.6 9.9 %collective-permute-start.15 = (s16[800,128]{1,0:T(8,128)(2,1)S(1)}, s16[800,128]{1,0:T(8,128)(2,1)S(1)}, u32[]{:S(2)}, u32[]{:S(2)}) collective-permute-start(s16[800,128]{1,0:T(8,128)(2,1)S(1)} %get-tuple-element.70), channel_id=1, source_target_pairs={{0,32},{4,36},{8,40},{12,44},{16,48},{20,52},{24,56},{28,60},{32,0... | collective-permute-start | bytes 614408 | tf_op jit(solution)/shard_map/ppermute | solution.py:515
  177.0 18.4 %collective-permute-start.16 = (s16[800,128]{1,0:T(8,128)(2,1)S(1)}, s16[800,128]{1,0:T(8,128)(2,1)S(1)}, u32[]{:S(2)}, u32[]{:S(2)}) collective-permute-start(s16[800,128]{1,0:T(8,128)(2,1)S(1)} %get-tuple-element.71), channel_id=1, source_target_pairs={{0,48},{4,52},{8,56},{12,60},{16,0},{20,4},{24,8},{28,12},{32,16},... | collective-permute-start | bytes 614408 | tf_op jit(solution)/shard_map/ppermute | solution.py:515

commit v8 on v7

--- a/solution.py
+++ b/solution.py
@@ -83,7 +83,12 @@
     ref[level_rows(plan, count), :] = level.astype(jnp.int32).astype(S16)
 
 
-def send_body(aux_ref, row_ref, col_ref, ext_ref, tiles_ref, out_ref, count_ref, *, layer_blocks):
+def send_body(
+    aux_ref, row_ref, col_ref, ext_ref, place_ref, blocks_ref, out_ref, count_ref, tiles_ref, sem, *, layer_blocks
+):
+    rows = pl.ds(pl.multiple_of(place_ref[0] * QUARTER, QUARTER), QUARTER)
+    load = pltpu.make_async_copy(blocks_ref.at[:, rows, :], tiles_ref, sem)
+    load.start()
     out_ref[...] = jnp.zeros(out_ref.shape, BF16)
 
     @pl.loop(0, OWNERS)
@@ -92,6 +97,7 @@
 
     lane = lax.broadcasted_iota(jnp.int32, (QUARTER, BS), 1)
     meta_lane = lax.broadcasted_iota(jnp.int32, (8, BS), 1)
+    load.wait()
 
     @pl.loop(0, tiles_ref.shape[0])
     def _(i):
@@ -109,16 +115,20 @@
         out_ref[owner, CAP * QUARTER :, :] = new.astype(BF16)
 
 
-def build_send(tiles, block_aux, block_row, block_col, extents, layer_blocks):
+def build_send(blocks, block_aux, block_row, block_col, extents, place, layer_blocks):
     return pl.pallas_call(
         functools.partial(send_body, layer_blocks=layer_blocks),
-        in_specs=[SMEM] * 4 + [VMEM],
+        in_specs=[SMEM] * 5 + [ANY],
         out_specs=VMEM,
         out_shape=jax.ShapeDtypeStruct((OWNERS, CAP * QUARTER + 8, BS), BF16),
-        scratch_shapes=[pltpu.SMEM((OWNERS,), jnp.int32)],
-        compiler_params=params(8),
+        scratch_shapes=[
+            pltpu.SMEM((OWNERS,), jnp.int32),
+            pltpu.VMEM((blocks.shape[0], QUARTER, BS), BF16),
+            pltpu.SemaphoreType.DMA(()),
+        ],
+        compiler_params=params(60),
         name="build_send",
-    )(block_aux, block_row, block_col, extents, tiles)
+    )(block_aux, block_row, block_col, extents, place, blocks)
 
 
 def split_pieces(place_ref, plan, rows_of, keep_ref, send_refs, level_ref):
@@ -132,7 +142,7 @@
         kept = [piece(bit_a, o) if h == 0 else piece(o, bit_b) for o in range(2)]
         sent = [piece(1 - bit_a, o) if h == 0 else piece(o, 1 - bit_b) for o in range(2)]
 
-        @pl.loop(0, plan.blocks)
+        @pl.loop(0, plan.blocks, unroll=2)
         def _(block):
             first = h * HALF + block * plan.group
             for other in range(2):
@@ -176,10 +186,12 @@
 def virt_last_body(meta_ref, place_ref, *rest, plan):
     sources, (keep_ref, send0_ref, send1_ref) = rest[:6], rest[6:9]
     refs, (acc_ref, level_ref, sems) = rest[9:15], rest[15:]
-    *loads, before = start_all(sources, refs, sems)
+    loads = start_all(sources[:5], refs, sems)
     acc_ref[...] = jnp.zeros(acc_ref.shape, F32)
     for load in loads:
         load.wait()
+    before = pltpu.make_async_copy(sources[5], refs[5], sems.at[5])
+    before.start()
     add_virt(meta_ref, OWNERS // 2, refs[:4], refs[4], acc_ref)
     before.wait()
     these, those = piece_rows(acc_ref), piece_rows(refs[5])
@@ -292,7 +304,7 @@
         away = 1 - mine
         read_scales(got_ref, (), plan, 2 * plan.blocks, scale_ref)
 
-        @pl.loop(0, plan.blocks)
+        @pl.loop(0, plan.blocks, unroll=2)
         def _(b):
             left_ref[h, b] = keep_ref[h, mine, b] + get(got_ref, (), plan, mine * plan.blocks + b, scale_ref)
             total = keep_ref[h, away, b] + get(got_ref, (), plan, away * plan.blocks + b, scale_ref)
@@ -318,7 +330,7 @@
     for h, got_ref in enumerate(got_refs):
         read_scales(got_ref, (), plan, plan.blocks, scale_ref)
 
-        @pl.loop(0, plan.blocks)
+        @pl.loop(0, plan.blocks, unroll=2)
         def _(b):
             store(h * plan.blocks + b, left_ref[h, b] + get(got_ref, (), plan, b, scale_ref))
 
@@ -372,30 +384,42 @@
     )(place, left, got0, got1)
 
 
-def pair_body(place_ref, own_ref, one_ref, two_ref, three_ref, virt_ref, out_ref, occ_ref, vir_ref, wide_ref, thin_ref, *, plan):
-    here = place_ref[0]
-    high = place_ref[1]
-    count = 2 * plan.blocks
-
-    at = [((high + shift) % 4) * 8 for shift in (0, ROWS - 1, 1, 2)]
-    read_scales(virt_ref, (), plan, count, wide_ref)
-
-    @pl.loop(0, NP)
+def decode_virt_body(place_ref, virt_ref, vir_ref, scale_ref, *, plan):
+    at = [((place_ref[1] + shift) % 4) * 8 for shift in (0, ROWS - 1, 1, 2)]
+    read_scales(virt_ref, (), plan, 2 * plan.blocks, scale_ref)
+
+    @pl.loop(0, NP, unroll=2)
     def _(q):
-        values = get(virt_ref, (), plan, q, wide_ref)
+        values = get(virt_ref, (), plan, q, scale_ref)
         for quarter in range(4):
             for low in range(4):
                 to = pl.ds(pl.multiple_of(low * QUARTER + at[quarter], 8), 8)
                 vir_ref[q, to, :] = values[quarter * 8 : (quarter + 1) * 8, low * BS : (low + 1) * BS]
 
+
+def decode_virt(place, virt, plan):
+    return pl.pallas_call(
+        functools.partial(decode_virt_body, plan=plan),
+        in_specs=[SMEM, VMEM],
+        out_specs=VMEM,
+        out_shape=jax.ShapeDtypeStruct((NP, BS, BS), F32),
+        scratch_shapes=[level_scratch(plan)],
+        compiler_params=params(8),
+        name="decode_virt",
+    )(place, virt)
+
+
+def pair_body(place_ref, own_ref, one_ref, two_ref, three_ref, vir_ref, out_ref, occ_ref, scale_ref, *, plan):
+    here = place_ref[0]
+
     for d, ref in enumerate((own_ref, one_ref, two_ref, three_ref)):
         source = (here + 4 - d) % 4
-        read_scales(ref, (), plan, count, thin_ref)
+        read_scales(ref, (), plan, 2 * plan.blocks, scale_ref)
         rows = pl.ds(pl.multiple_of(source * QUARTER, QUARTER), QUARTER)
 
-        @pl.loop(0, NP)
+        @pl.loop(0, NP, unroll=4)
         def _(p):
-            occ_ref[p, rows, :] = get(ref, (), plan, p, thin_ref)
+            occ_ref[p, rows, :] = get(ref, (), plan, p, scale_ref)
 
     @pl.loop(0, NP)
     def _(p):
@@ -404,22 +428,16 @@
             out_ref[p, q : q + 1, :] = jnp.sum(occ * vir_ref[q], axis=0, keepdims=True)
 
 
-def pair(place, own, others, virt, plan):
-    levels = plan.levels(2 * plan.blocks)
+def pair(place, own, others, vir, plan):
     return pl.pallas_call(
         functools.partial(pair_body, plan=plan),
         in_specs=[SMEM] + [VMEM] * 5,
         out_specs=VMEM,
         out_shape=jax.ShapeDtypeStruct((NP, NP, BS), F32),
-        scratch_shapes=[
-            pltpu.VMEM((NP, BS, BS), F32),
-            pltpu.VMEM((NP, BS, BS), F32),
-            pltpu.VMEM((levels, WIDE), F32),
-            pltpu.VMEM((levels, BS), F32),
-        ],
+        scratch_shapes=[pltpu.VMEM((NP, BS, BS), F32), pltpu.VMEM((plan.levels(2 * plan.blocks), BS), F32)],
         compiler_params=params(16),
         name="pair",
-    )(place, own, *others, virt)
+    )(place, own, *others, vir)
 
 
 def rotate(size, step):
@@ -475,15 +493,16 @@
     place = jnp.stack([row_place, bit_a, bit_b])
     plan = Plan(4)
 
-    tiles = lax.dynamic_slice_in_dim(blocks, row_place * QUARTER, QUARTER, 1)
-    send = build_send(tiles, block_aux, block_row, block_col, extents, layer_blocks)
+    send = build_send(blocks, block_aux, block_row, block_col, extents, row_place[None], layer_blocks)
     own = lax.all_to_all(send, ("col", "layer"), 0, 0, tiled=True)
-    meta = own[:, CAP * QUARTER, : 2 * CAP].astype(jnp.int32)
     virt_blocks = virt_green.reshape(layer_blocks, BS, WIDE)
     occ_blocks = occ_green.reshape(layer_blocks, BS, WIDE).transpose(0, 2, 1)
 
     half = OWNERS // 2
-    own_a, own_b = own[:half, : CAP * QUARTER], own[half:, : CAP * QUARTER]
+    own_a = own[:half, : CAP * QUARTER]
+    later, occ_blocks = after(own, occ_blocks)
+    own_b = later[half:, : CAP * QUARTER]
+    meta = later[:, CAP * QUARTER, : 2 * CAP].astype(jnp.int32)
     up, down = rotate(ROWS, 1), rotate(ROWS, -1)
     prev_a = lax.ppermute(own_a, "row", up)
     next_a = lax.ppermute(own_a, "row", down)
@@ -513,7 +532,7 @@
     here = jnp.stack([col_place // 4, col_place % 4])
     occ, *others = finish_occ(here, o_left, *o_got, plan)
     others = [lax.ppermute(part, "col", rotate_high(d)) for d, part in zip((1, 2, 3), others)]
-    partial = pair(here, occ, others, virt, plan)
+    partial = pair(here, occ, others, decode_virt(here, virt, plan), plan)
     return sum_all(jnp.sum(partial, axis=-1))
 
 

time: 232 us -> 222 us (0.957)
  local copies, waits for them, and re-layouts: 18.9 us -> 9.16 us
    unnamed x36 -> x38, local copies, waits for them, and re-layouts: 8.31 us -> 0.62 us
  transfers between devices with their start and end apart: 18 -> 18, of which waited for: 9 -> 10; matrix products, arithmetic and copies ran while one was open for 4% -> 4% of each run, Pallas kernels for 15% -> 14%
where the time goes in v8:
time: 222 us; the launch traced here: 221 us
  blocking collectives  69.9 us (31%)
  Pallas kernels  55.3 us (25%)
  waiting for transfers between devices  45.3 us (20%)
  starting transfers between devices  37.2 us (17%)
  local copies, waits for them, and re-layouts  9.16 us (4%)
  other arithmetic  3.62 us (2%)
    all_to_all x1, blocking collectives, on_device(): own = lax.all_to_all(send, ('col', 'layer'), 0, 0, tiled=True)  43.7 us
    all_to_all x2, blocking collectives, sum_all(): values = jnp.sum(lax.all_to_all(copies, axes, 0, 0, tiled=True), axis=0)  26.3 us
    ppermute x4, waiting for transfers between devices, layer_swap(): lax.ppermute(send0, 'layer', perms[0])  16.7 us
    ppermute x3, waiting for transfers between devices, on_device(): lax.ppermute(part, 'col', rotate_high(d))  15.2 us
    pallas_call x1, Pallas kernels, contract_occ(): pl.pallas_call(functools.partial(occ_body, plan=plan), in_specs=[SMEM] *...  13.9 us
    pallas_call x1, Pallas kernels, contract_virt_last(): pl.pallas_call(functools.partial(virt_last_body, plan=plan), in_specs=[SM...  12.6 us
    pallas_call x1, Pallas kernels, contract_virt_first(): pl.pallas_call(virt_first_body, in_specs=[SMEM] + [ANY] * 5, out_specs=AN...  11.7 us
    ppermute x1, starting transfers between devices, on_device(): virt = lax.ppermute(virt, ALL, SWAP)  10.9 us
  transfers between devices with their start and end apart: 18, of which 10 were waited for; matrix products, arithmetic and copies ran while one was open for 4% of the time, Pallas kernels for 14%

profile of v8, /device:TPU:1, one launch (start us, length us, event | category | flops | bytes accessed | tf_op | source)
XLA Modules:
  0.0 221.0 jit_solution(3387432739516421310)
XLA Ops:
  0.0 5.1 %build_send.1 = bf16[64,72,128]{2,1,0:T(8,128)(2,1)} custom-call(s32[88]{0:T(128)} %aux_ref.1, s32[88]{0:T(128)} %row_ref.1, s32[88]{0:T(128)} %col_ref.1, s32[88]{0:T(128)} %ext_ref.1, s32[1]{0:T(128)} %bitcast.2.place_ref, bf16[88,128,128]{2,1,0:T(8,128)(2,1)} %blocks_ref.1), custom_call_target="tpu_custom_call" | custom-call | tf_op jit(solution)/shard_map/build_send/pallas_call | solution.py:119
  5.1 43.7 %all_to_all.15 = bf16[64,72,128]{2,1,0:T(8,128)(2,1)S(1)} all-to-all(bf16[64,72,128]{2,1,0:T(8,128)(2,1)} %build_send.1), channel_id=1, replica_groups=mesh['row'=4,'col'=16,'layer'=4] {'col','layer'}, dimensions={0} | all-to-all | bytes 2359296 | tf_op jit(solution)/shard_map/all_to_all | solution.py:497
  48.8 1.4 collective-permute-start
  50.2 1.5 collective-permute-start.1
  51.7 7.9 %copy.9 = bf16[40,128,512]{1,2,0:T(8,128)(2,1)} copy(bf16[40,128,512]{2,1,0:T(8,128)(2,1)} %bitcast.17) | data formatting | bytes 10485760 | tf_op jit(solution)/shard_map/reshape | solution.py:499
  59.7 0.7 slice_convert_fusion
  60.4 1.8 collective-permute-done.rest_1_
  62.2 1.0 collective-permute-start.2
  63.2 1.8 collective-permute-start.3
  64.9 9.6 %collective-permute-done.2.rest_3_ = bf16[32,64,128]{2,1,0:T(8,128)(2,1)S(1)} collective-permute-done((bf16[32,64,128]{2,1,0:T(8,128)(2,1)S(1)}, bf16[32,64,128]{2,1,0:T(8,128)(2,1)S(1)}, u32[]{:S(2)}, u32[]{:S(2)}) %collective-permute-start.2) | collective-permute-done | bytes 524320 | tf_op jit(solution)/shard_map/ppermute | solution.py:510
  74.6 2.7 %collective-permute-start.5 = (bf16[32,64,128]{2,1,0:T(8,128)(2,1)S(1)}, bf16[32,64,128]{2,1,0:T(8,128)(2,1)}, u32[]{:S(2)}, u32[]{:S(2)}) collective-permute-start(bf16[32,64,128]{2,1,0:T(8,128)(2,1)S(1)} %collective-permute-done.3.rest_2_.rest_6_), channel_id=1, source_target_pairs={{0,192},{64,0},{128,64},{192,128},{1,193},{65,1},{129,65},{193,129... | collective-permute-start | bytes 1572872 | tf_op jit(solution)/shard_map/ppermute | solution.py:514
  77.3 0.6 pad_add_fusion.1.place_ref
  77.9 11.7 %virt_first.1.rest_5_ = f32[24,128,512]{2,1,0:T(8,128)} custom-call(s32[64,4]{1,0:T(8,128)} %bitcast.12, bf16[32,64,128]{2,1,0:T(8,128)(2,1)} %copy-done, bf16[32,64,128]{2,1,0:T(8,128)(2,1)} %copy-done.5, bf16[32,64,128]{2,1,0:T(8,128)(2,1)} %copy-done.7, bf16[32,64,128]{2,1,0:T(8,128)(2,1)} %copy-done.9, bf16[40,128,512]{2,1,0:T(8,128)(2,1)} %bitcast.15), custom_call_target="tpu_custom_call" | custom-call | tf_op jit(solution)/shard_map/virt_first/pallas_call | solution.py:265
  89.8 12.6 %virt_last.1 = (f32[2,2,12,32,512]{4,3,2,1,0:T(8,128)}, s16[800,512]{1,0:T(8,128)(2,1)}, s16[800,512]{1,0:T(8,128)(2,1)}) custom-call(s32[64,4]{1,0:T(8,128)} %bitcast.13, s32[3]{0:T(128)} %pad_add_fusion.1.place_ref, bf16[32,64,128]{2,1,0:T(8,128)(2,1)} %copy-done.2, bf16[32,64,128]{2,1,0:T(8,128)(2,1)} %collective-permute-done.4.rest_1_.rest_5_, ...), custom_call_target="tpu_custom_call" | custom-call | tf_op jit(solution)/shard_map/virt_last/pallas_call | solution.py:278
  102.4 0.4 collective-permute-start.6
  102.8 2.1 collective-permute-start.7
  105.0 13.9 %contract_occ.1 = (f32[2,2,12,32,512]{4,3,2,1,0:T(8,128)S(1)}, s16[800,512]{1,0:T(8,128)(2,1)S(1)}, s16[800,512]{1,0:T(8,128)(2,1)S(1)}) custom-call(s32[64,4]{1,0:T(8,128)S(1)} %bitcast.14, s32[3]{0:T(128)S(1)} %copy-done.14, bf16[32,64,128]{2,1,0:T(8,128)(2,1)S(1)} %copy-done.1, bf16[32,64,128]{2,1,0:T(8,128)(2,1)S(1)} %copy-done.6, ...), custom_call_target="tpu_custom_call" | custom-call | tf_op jit(solution)/shard_map/contract_occ/pallas_call | solution.py:290
  118.9 0.7 collective-permute-done.7.got1_ref
  119.5 1.5 halve_virt.1
  121.1 2.3 %collective-permute-start.8 = (s16[400,512]{1,0:T(8,128)(2,1)S(1)}, s16[400,512]{1,0:T(8,128)(2,1)S(1)}, u32[]{:S(2)}, u32[]{:S(2)}) collective-permute-start(s16[400,512]{1,0:T(8,128)(2,1)S(1)} %get-tuple-element.61), channel_id=1, source_target_pairs={{0,3},{3,0},{1,2},{2,1},{4,7},{7,4},{5,6},{6,5},{8,11},{11,8},{9,1... | collective-permute-start | bytes 1228808 | tf_op jit(solution)/shard_map/ppermute | solution.py:475
  123.3 5.8 %collective-permute-done.8.got0_ref = s16[400,512]{1,0:T(8,128)(2,1)S(1)} collective-permute-done((s16[400,512]{1,0:T(8,128)(2,1)S(1)}, s16[400,512]{1,0:T(8,128)(2,1)S(1)}, u32[]{:S(2)}, u32[]{:S(2)}) %collective-permute-start.8) | collective-permute-done | bytes 409632 | tf_op jit(solution)/shard_map/ppermute | solution.py:475
  129.2 1.0 collective-permute-done.9.got1_ref
  130.1 0.3 collective-permute-start.10
  130.4 0.9 collective-permute-start.11
  131.4 0.9 finish_virt.1
  132.2 10.9 %collective-permute-start.17 = (s16[800,512]{1,0:T(8,128)(2,1)S(1)}, s16[800,512]{1,0:T(8,128)(2,1)S(1)}, u32[]{:S(2)}, u32[]{:S(2)}) collective-permute-start(s16[800,512]{1,0:T(8,128)(2,1)S(1)} %finish_virt.1), channel_id=1, source_target_pairs={{0,0},{1,1},{2,2},{3,3},{4,64},{5,65},{6,66},{7,67},{8,128},{9,129... | collective-permute-start | bytes 2457608 | tf_op jit(solution)/shard_map/ppermute | solution.py:529
  143.1 3.6 %collective-permute-done.10.got0_ref = s16[800,512]{1,0:T(8,128)(2,1)S(1)} collective-permute-done((s16[800,512]{1,0:T(8,128)(2,1)S(1)}, s16[800,512]{1,0:T(8,128)(2,1)S(1)}, u32[]{:S(2)}, u32[]{:S(2)}) %collective-permute-start.10) | collective-permute-done | bytes 819232 | tf_op jit(solution)/shard_map/ppermute | solution.py:475
  146.8 2.4 %halve_occ.1 = (f32[2,12,32,512]{3,2,1,0:T(8,128)S(1)}, s16[400,512]{1,0:T(8,128)(2,1)}, s16[400,512]{1,0:T(8,128)(2,1)}) custom-call(s32[3]{0:T(128)S(1)} %copy-done.14, f32[2,2,12,32,512]{4,3,2,1,0:T(8,128)S(1)} %get-tuple-element.66.keep_ref, s16[800,512]{1,0:T(8,128)(2,1)S(1)} %collective-permute-done.10.got0_ref, ...), custom_call_target="tpu_custom_call" | custom-call | tf_op jit(solution)/shard_map/halve_occ/pallas_call | solution.py:318
  149.2 1.3 collective-permute-start.12
  150.5 7.2 %collective-permute-done.12.got0_ref = s16[400,512]{1,0:T(8,128)(2,1)} collective-permute-done((s16[400,512]{1,0:T(8,128)(2,1)}, s16[400,512]{1,0:T(8,128)(2,1)}, u32[]{:S(2)}, u32[]{:S(2)}) %collective-permute-start.12) | collective-permute-done | bytes 409632 | tf_op jit(solution)/shard_map/ppermute | solution.py:475
  157.8 0.4 collective-permute-done.13.got1_ref
  158.2 2.1 finish_occ.1
  160.3 4.7 %collective-permute-start.14 = (s16[800,128]{1,0:T(8,128)(2,1)S(1)}, s16[800,128]{1,0:T(8,128)(2,1)S(1)}, u32[]{:S(2)}, u32[]{:S(2)}) collective-permute-start(s16[800,128]{1,0:T(8,128)(2,1)S(1)} %get-tuple-element.73), channel_id=1, source_target_pairs={{0,16},{4,20},{8,24},{12,28},{16,32},{20,36},{24,40},{28,44},{32,4... | collective-permute-start | bytes 614408 | tf_op jit(solution)/shard_map/ppermute | solution.py:534
  165.0 3.5 %collective-permute-start.15 = (s16[800,128]{1,0:T(8,128)(2,1)S(1)}, s16[800,128]{1,0:T(8,128)(2,1)S(1)}, u32[]{:S(2)}, u32[]{:S(2)}) collective-permute-start(s16[800,128]{1,0:T(8,128)(2,1)S(1)} %get-tuple-element.74), channel_id=1, source_target_pairs={{0,32},{4,36},{8,40},{12,44},{16,48},{20,52},{24,56},{28,60},{32,0... | collective-permute-start | bytes 614408 | tf_op jit(solution)/shard_map/ppermute | solution.py:534
  168.4 2.5 %collective-permute-start.16 = (s16[800,128]{1,0:T(8,128)(2,1)S(1)}, s16[800,128]{1,0:T(8,128)(2,1)S(1)}, u32[]{:S(2)}, u32[]{:S(2)}) collective-permute-start(s16[800,128]{1,0:T(8,128)(2,1)S(1)} %get-tuple-element.75), channel_id=1, source_target_pairs={{0,48},{4,52},{8,56},{12,60},{16,0},{20,4},{24,8},{28,12},{32,16},... | collective-permute-start | bytes 614408 | tf_op jit(solution)/shard_map/ppermute | solution.py:534
  170.9 0.8 decode_virt.1.vir_ref
  171.7 2.2 %collective-permute-done.15.two_ref = s16[800,128]{1,0:T(8,128)(2,1)S(1)} collective-permute-done((s16[800,128]{1,0:T(8,128)(2,1)S(1)}, s16[800,128]{1,0:T(8,128)(2,1)S(1)}, u32[]{:S(2)}, u32[]{:S(2)}) %collective-permute-start.15) | collective-permute-done | bytes 204832 | tf_op jit(solution)/shard_map/ppermute | solution.py:534
  174.0 13.0 %collective-permute-done.16.three_ref = s16[800,128]{1,0:T(8,128)(2,1)S(1)} collective-permute-done((s16[800,128]{1,0:T(8,128)(2,1)S(1)}, s16[800,128]{1,0:T(8,128)(2,1)S(1)}, u32[]{:S(2)}, u32[]{:S(2)}) %collective-permute-start.16) | collective-permute-done | bytes 204832 | tf_op jit(solution)/shard_map/ppermute | solution.py:534
  187.0 4.3 %pair.1 = f32[24,24,128]{2,1,0:T(8,128)S(1)} custom-call(s32[2]{0:T(128)S(1)} %pad_add_fusion.place_ref, s16[800,128]{1,0:T(8,128)(2,1)S(1)} %get-tuple-element.72.own_ref, s16[800,128]{1,0:T(8,128)(2,1)S(1)} %collective-permute-done.14.one_ref, s16[800,128]{1,0:T(8,128)(2,1)S(1)} %collective-permute-done.15.two_ref, ...), custom_call_target="tpu_custom_call" | custom-call | tf_op jit(solution)/shard_map/pair/pallas_call | solution.py:432
  191.2 0.1 reduce_sum.27
  191.4 0.2 reshape.14
  191.6 17.0 %all_to_all.16 = f32[16,1,576]{2,1,0:T(1,128)S(1)} all-to-all(f32[16,1,576]{2,1,0:T(1,128)S(1)} %reshape.14), channel_id=1, replica_groups=mesh['row'=4,'col'=16,'layer'=4] {'col'}, dimensions={0} | all-to-all | bytes 73728 | tf_op jit(solution)/shard_map/all_to_all | solution.py:470
  208.6 0.5 broadcast.5
  209.1 0.7 reduce
  210.0 0.2 reshape.16
  210.2 9.3 %all_to_all.17 = f32[16,1,576]{2,1,0:T(1,128)S(1)} all-to-all(f32[16,1,576]{2,1,0:T(1,128)S(1)} %reshape.16), channel_id=1, replica_groups=mesh['row'=4,'col'=16,'layer'=4] {'row','layer'}, dimensions={0} | all-to-all | bytes 73728 | tf_op jit(solution)/shard_map/all_to_all | solution.py:470
  219.5 0.7 reduce.1
  220.3 0.6 reduce_sum.29
  (54 shorter events, 0.7 us)
Async XLA Ops:
  48.8 10.8 %copy-start = (bf16[32,64,128]{2,1,0:T(8,128)(2,1)}, bf16[32,64,128]{2,1,0:T(8,128)(2,1)S(1)}, u32[]{:S(2)}) copy-start(bf16[32,64,128]{2,1,0:T(8,128)(2,1)S(1)} %slice.12.rest_0_) | copy-start | bytes 1572868
  48.8 13.3 %collective-permute-start = (bf16[32,64,128]{2,1,0:T(8,128)(2,1)S(1)}, bf16[32,64,128]{2,1,0:T(8,128)(2,1)S(1)}, u32[]{:S(2)}, u32[]{:S(2)}) collective-permute-start(bf16[32,64,128]{2,1,0:T(8,128)(2,1)S(1)} %slice.12.rest_0_), channel_id=1, source_target_pairs={{0,64},{64,128},{128,192},{192,0},{1,65},{65,129},{129,193},{193,1... | collective-permute-start | bytes 1572872 | tf_op jit(solution)/shard_map/ppermute | solution.py:507
  50.2 12.0 %collective-permute-start.1 = (bf16[32,64,128]{2,1,0:T(8,128)(2,1)S(1)}, bf16[32,64,128]{2,1,0:T(8,128)(2,1)S(1)}, u32[]{:S(2)}, u32[]{:S(2)}) collective-permute-start(bf16[32,64,128]{2,1,0:T(8,128)(2,1)S(1)} %slice.12.rest_0_), channel_id=1, source_target_pairs={{0,192},{64,0},{128,64},{192,128},{1,193},{65,1},{129,65},{193,129... | collective-permute-start | bytes 1572872 | tf_op jit(solution)/shard_map/ppermute | solution.py:508
  59.7 29.9 %copy-start.2 = (bf16[32,64,128]{2,1,0:T(8,128)(2,1)}, bf16[32,64,128]{2,1,0:T(8,128)(2,1)S(1)}, u32[]{:S(2)}) copy-start(bf16[32,64,128]{2,1,0:T(8,128)(2,1)S(1)} %slice.10.rest_0_.rest_4_) | copy-start | bytes 1572868
  62.2 15.7 %copy-start.5 = (bf16[32,64,128]{2,1,0:T(8,128)(2,1)}, bf16[32,64,128]{2,1,0:T(8,128)(2,1)S(1)}, u32[]{:S(2)}) copy-start(bf16[32,64,128]{2,1,0:T(8,128)(2,1)S(1)} %collective-permute-done.rest_1_) | copy-start | bytes 1572868
  62.2 15.7 %copy-start.7 = (bf16[32,64,128]{2,1,0:T(8,128)(2,1)}, bf16[32,64,128]{2,1,0:T(8,128)(2,1)S(1)}, u32[]{:S(2)}) copy-start(bf16[32,64,128]{2,1,0:T(8,128)(2,1)S(1)} %collective-permute-done.1.rest_2_) | copy-start | bytes 1572868
  62.2 12.3 %collective-permute-start.2 = (bf16[32,64,128]{2,1,0:T(8,128)(2,1)S(1)}, bf16[32,64,128]{2,1,0:T(8,128)(2,1)S(1)}, u32[]{:S(2)}, u32[]{:S(2)}) collective-permute-start(bf16[32,64,128]{2,1,0:T(8,128)(2,1)S(1)} %collective-permute-done.rest_1_), channel_id=1, source_target_pairs={{0,64},{64,128},{128,192},{192,0},{1,65},{65,129},{129,193},{193,1... | collective-permute-start | bytes 1572872 | tf_op jit(solution)/shard_map/ppermute | solution.py:510
  63.2 11.4 %collective-permute-start.3 = (bf16[32,64,128]{2,1,0:T(8,128)(2,1)S(1)}, bf16[32,64,128]{2,1,0:T(8,128)(2,1)S(1)}, u32[]{:S(2)}, u32[]{:S(2)}) collective-permute-start(bf16[32,64,128]{2,1,0:T(8,128)(2,1)S(1)} %slice.10.rest_0_.rest_4_), channel_id=1, source_target_pairs={{0,192},{64,0},{128,64},{192,128},{1,193},{65,1},{129,65},{193,129... | collective-permute-start | bytes 1572872 | tf_op jit(solution)/shard_map/ppermute | solution.py:511
  74.5 3.3 %copy-start.9 = (bf16[32,64,128]{2,1,0:T(8,128)(2,1)}, bf16[32,64,128]{2,1,0:T(8,128)(2,1)S(1)}, u32[]{:S(2)}) copy-start(bf16[32,64,128]{2,1,0:T(8,128)(2,1)S(1)} %collective-permute-done.2.rest_3_) | copy-start | bytes 1572868
  74.5 15.1 %copy-start.11 = (bf16[32,64,128]{2,1,0:T(8,128)(2,1)}, bf16[32,64,128]{2,1,0:T(8,128)(2,1)S(1)}, u32[]{:S(2)}) copy-start(bf16[32,64,128]{2,1,0:T(8,128)(2,1)S(1)} %collective-permute-done.3.rest_2_.rest_6_) | copy-start | bytes 1572868
  74.5 15.2 %collective-permute-start.4 = (bf16[32,64,128]{2,1,0:T(8,128)(2,1)S(1)}, bf16[32,64,128]{2,1,0:T(8,128)(2,1)}, u32[]{:S(2)}, u32[]{:S(2)}) collective-permute-start(bf16[32,64,128]{2,1,0:T(8,128)(2,1)S(1)} %slice.10.rest_0_.rest_4_), channel_id=1, source_target_pairs={{0,64},{64,128},{128,192},{192,0},{1,65},{65,129},{129,193},{193,1... | collective-permute-start | bytes 1572872 | tf_op jit(solution)/shard_map/ppermute | solution.py:513
  74.6 15.1 %collective-permute-start.5 = (bf16[32,64,128]{2,1,0:T(8,128)(2,1)S(1)}, bf16[32,64,128]{2,1,0:T(8,128)(2,1)}, u32[]{:S(2)}, u32[]{:S(2)}) collective-permute-start(bf16[32,64,128]{2,1,0:T(8,128)(2,1)S(1)} %collective-permute-done.3.rest_2_.rest_6_), channel_id=1, source_target_pairs={{0,192},{64,0},{128,64},{192,128},{1,193},{65,1},{129,65},{193,129... | collective-permute-start | bytes 1572872 | tf_op jit(solution)/shard_map/ppermute | solution.py:514
  77.9 27.0 %slice-start = ((s8[5242880]{0:T(1024)(128)(4,1)}), s8[4194304]{0:T(1024)(128)(4,1)S(1)}, s32[]{:S(2)}) async-start(s8[5242880]{0:T(1024)(128)(4,1)} %bitcast.9), calls=%async_computation.3 | async-start | bytes 8388608
  89.6 15.2 %slice-start.1 = ((s8[5242880]{0:T(1024)(128)(4,1)}), s8[1048576]{0:T(1024)(128)(4,1)S(1)}, s32[]{:S(2)}) async-start(s8[5242880]{0:T(1024)(128)(4,1)} %bitcast.9), calls=%async_computation.4 | async-start | bytes 2097152
  89.7 15.2 %copy-start.1 = (bf16[32,64,128]{2,1,0:T(8,128)(2,1)S(1)}, bf16[32,64,128]{2,1,0:T(8,128)(2,1)}, u32[]{:S(2)}) copy-start(bf16[32,64,128]{2,1,0:T(8,128)(2,1)} %copy-done) | copy-start | bytes 1572868
  89.7 15.2 %copy-start.6 = (bf16[32,64,128]{2,1,0:T(8,128)(2,1)S(1)}, bf16[32,64,128]{2,1,0:T(8,128)(2,1)}, u32[]{:S(2)}) copy-start(bf16[32,64,128]{2,1,0:T(8,128)(2,1)} %copy-done.5) | copy-start | bytes 1572868
  89.7 15.2 %copy-start.8 = (bf16[32,64,128]{2,1,0:T(8,128)(2,1)S(1)}, bf16[32,64,128]{2,1,0:T(8,128)(2,1)}, u32[]{:S(2)}) copy-start(bf16[32,64,128]{2,1,0:T(8,128)(2,1)} %copy-done.7) | copy-start | bytes 1572868
  89.7 15.2 %copy-start.10 = (bf16[32,64,128]{2,1,0:T(8,128)(2,1)S(1)}, bf16[32,64,128]{2,1,0:T(8,128)(2,1)}, u32[]{:S(2)}) copy-start(bf16[32,64,128]{2,1,0:T(8,128)(2,1)} %copy-done.9) | copy-start | bytes 1572868
  89.7 15.2 %copy-start.13 = (s32[64,1,4]{2,1,0:T(1,128)S(1)}, s32[64,1,4]{2,1,0:T(1,128)}, u32[]{:S(2)}) copy-start(s32[64,1,4]{2,1,0:T(1,128)} %slice_convert_fusion) | copy-start | bytes 3076
  89.7 15.2 %copy-start.14 = (s32[3]{0:T(128)S(1)}, s32[3]{0:T(128)}, u32[]{:S(2)}) copy-start(s32[3]{0:T(128)} %pad_add_fusion.1.place_ref) | copy-start | bytes 40
  89.7 15.2 %copy-start.3 = (bf16[32,64,128]{2,1,0:T(8,128)(2,1)S(1)}, bf16[32,64,128]{2,1,0:T(8,128)(2,1)}, u32[]{:S(2)}) copy-start(bf16[32,64,128]{2,1,0:T(8,128)(2,1)} %copy-done.2) | copy-start | bytes 1572868
  89.7 15.2 %copy-start.12 = (bf16[32,64,128]{2,1,0:T(8,128)(2,1)S(1)}, bf16[32,64,128]{2,1,0:T(8,128)(2,1)}, u32[]{:S(2)}) copy-start(bf16[32,64,128]{2,1,0:T(8,128)(2,1)} %copy-done.11) | copy-start | bytes 1572868
  102.4 16.5 %collective-permute-start.6 = (s16[800,512]{1,0:T(8,128)(2,1)}, s16[800,512]{1,0:T(8,128)(2,1)S(1)}, u32[]{:S(2)}, u32[]{:S(2)}) collective-permute-start(s16[800,512]{1,0:T(8,128)(2,1)} %get-tuple-element.56), channel_id=1, source_target_pairs={{0,1},{1,0},{2,3},{3,2},{4,5},{5,4},{6,7},{7,6},{8,9},{9,8},{10,11... | collective-permute-start | bytes 2457608 | tf_op jit(solution)/shard_map/ppermute | solution.py:475
  102.8 16.7 %collective-permute-start.7 = (s16[800,512]{1,0:T(8,128)(2,1)}, s16[800,512]{1,0:T(8,128)(2,1)S(1)}, u32[]{:S(2)}, u32[]{:S(2)}) collective-permute-start(s16[800,512]{1,0:T(8,128)(2,1)} %get-tuple-element.57), channel_id=1, source_target_pairs={{0,3},{3,0},{1,2},{2,1},{4,7},{7,4},{5,6},{6,5},{8,11},{11,8},{9,1... | collective-permute-start | bytes 2457608 | tf_op jit(solution)/shard_map/ppermute | solution.py:475
  104.9 14.6 %copy-start.4 = (f32[2,2,12,32,512]{4,3,2,1,0:T(8,128)S(1)}, f32[2,2,12,32,512]{4,3,2,1,0:T(8,128)}, u32[]{:S(2)}) copy-start(f32[2,2,12,32,512]{4,3,2,1,0:T(8,128)} %get-tuple-element.55.keep_ref) | copy-start | bytes 9437188
  121.1 8.1 %collective-permute-start.8 = (s16[400,512]{1,0:T(8,128)(2,1)S(1)}, s16[400,512]{1,0:T(8,128)(2,1)S(1)}, u32[]{:S(2)}, u32[]{:S(2)}) collective-permute-start(s16[400,512]{1,0:T(8,128)(2,1)S(1)} %get-tuple-element.61), channel_id=1, source_target_pairs={{0,3},{3,0},{1,2},{2,1},{4,7},{7,4},{5,6},{6,5},{8,11},{11,8},{9,1... | collective-permute-start | bytes 1228808 | tf_op jit(solution)/shard_map/ppermute | solution.py:475
  123.3 6.8 %collective-permute-start.9 = (s16[400,512]{1,0:T(8,128)(2,1)S(1)}, s16[400,512]{1,0:T(8,128)(2,1)S(1)}, u32[]{:S(2)}, u32[]{:S(2)}) collective-permute-start(s16[400,512]{1,0:T(8,128)(2,1)S(1)} %get-tuple-element.62), channel_id=1, source_target_pairs={{0,1},{1,0},{2,3},{3,2},{4,5},{5,4},{6,7},{7,6},{8,9},{9,8},{10,11... | collective-permute-start | bytes 1228808 | tf_op jit(solution)/shard_map/ppermute | solution.py:475
  130.1 16.6 %collective-permute-start.10 = (s16[800,512]{1,0:T(8,128)(2,1)S(1)}, s16[800,512]{1,0:T(8,128)(2,1)S(1)}, u32[]{:S(2)}, u32[]{:S(2)}) collective-permute-start(s16[800,512]{1,0:T(8,128)(2,1)S(1)} %get-tuple-element.67), channel_id=1, source_target_pairs={{0,1},{1,0},{2,3},{3,2},{4,5},{5,4},{6,7},{7,6},{8,9},{9,8},{10,11... | collective-permute-start | bytes 2457608 | tf_op jit(solution)/shard_map/ppermute | solution.py:475
  130.4 16.3 %collective-permute-start.11 = (s16[800,512]{1,0:T(8,128)(2,1)S(1)}, s16[800,512]{1,0:T(8,128)(2,1)S(1)}, u32[]{:S(2)}, u32[]{:S(2)}) collective-permute-start(s16[800,512]{1,0:T(8,128)(2,1)S(1)} %get-tuple-element.68), channel_id=1, source_target_pairs={{0,3},{3,0},{1,2},{2,1},{4,7},{7,4},{5,6},{6,5},{8,11},{11,8},{9,1... | collective-permute-start | bytes 2457608 | tf_op jit(solution)/shard_map/ppermute | solution.py:475
  132.2 38.7 %collective-permute-start.17 = (s16[800,512]{1,0:T(8,128)(2,1)S(1)}, s16[800,512]{1,0:T(8,128)(2,1)S(1)}, u32[]{:S(2)}, u32[]{:S(2)}) collective-permute-start(s16[800,512]{1,0:T(8,128)(2,1)S(1)} %finish_virt.1), channel_id=1, source_target_pairs={{0,0},{1,1},{2,2},{3,3},{4,64},{5,65},{6,66},{7,67},{8,128},{9,129... | collective-permute-start | bytes 2457608 | tf_op jit(solution)/shard_map/ppermute | solution.py:529
  149.2 8.6 %collective-permute-start.12 = (s16[400,512]{1,0:T(8,128)(2,1)}, s16[400,512]{1,0:T(8,128)(2,1)}, u32[]{:S(2)}, u32[]{:S(2)}) collective-permute-start(s16[400,512]{1,0:T(8,128)(2,1)} %get-tuple-element.70), channel_id=1, source_target_pairs={{0,3},{3,0},{1,2},{2,1},{4,7},{7,4},{5,6},{6,5},{8,11},{11,8},{9,1... | collective-permute-start | bytes 1228808 | tf_op jit(solution)/shard_map/ppermute | solution.py:475
  150.5 7.7 %collective-permute-start.13 = (s16[400,512]{1,0:T(8,128)(2,1)}, s16[400,512]{1,0:T(8,128)(2,1)}, u32[]{:S(2)}, u32[]{:S(2)}) collective-permute-start(s16[400,512]{1,0:T(8,128)(2,1)} %get-tuple-element.71), channel_id=1, source_target_pairs={{0,1},{1,0},{2,3},{3,2},{4,5},{5,4},{6,7},{7,6},{8,9},{9,8},{10,11... | collective-permute-start | bytes 1228808 | tf_op jit(solution)/shard_map/ppermute | solution.py:475
  160.3 11.5 %collective-permute-start.14 = (s16[800,128]{1,0:T(8,128)(2,1)S(1)}, s16[800,128]{1,0:T(8,128)(2,1)S(1)}, u32[]{:S(2)}, u32[]{:S(2)}) collective-permute-start(s16[800,128]{1,0:T(8,128)(2,1)S(1)} %get-tuple-element.73), channel_id=1, source_target_pairs={{0,16},{4,20},{8,24},{12,28},{16,32},{20,36},{24,40},{28,44},{32,4... | collective-permute-start | bytes 614408 | tf_op jit(solution)/shard_map/ppermute | solution.py:534
  165.0 9.0 %collective-permute-start.15 = (s16[800,128]{1,0:T(8,128)(2,1)S(1)}, s16[800,128]{1,0:T(8,128)(2,1)S(1)}, u32[]{:S(2)}, u32[]{:S(2)}) collective-permute-start(s16[800,128]{1,0:T(8,128)(2,1)S(1)} %get-tuple-element.74), channel_id=1, source_target_pairs={{0,32},{4,36},{8,40},{12,44},{16,48},{20,52},{24,56},{28,60},{32,0... | collective-permute-start | bytes 614408 | tf_op jit(solution)/shard_map/ppermute | solution.py:534
  168.4 18.5 %collective-permute-start.16 = (s16[800,128]{1,0:T(8,128)(2,1)S(1)}, s16[800,128]{1,0:T(8,128)(2,1)S(1)}, u32[]{:S(2)}, u32[]{:S(2)}) collective-permute-start(s16[800,128]{1,0:T(8,128)(2,1)S(1)} %get-tuple-element.75), channel_id=1, source_target_pairs={{0,48},{4,52},{8,56},{12,60},{16,0},{20,4},{24,8},{28,12},{32,16},... | collective-permute-start | bytes 614408 | tf_op jit(solution)/shard_map/ppermute | solution.py:534

commit v9 on v8

--- a/solution.py
+++ b/solution.py
@@ -41,11 +41,12 @@
 
 
 class Plan:
-    def __init__(self, quarters):
+    def __init__(self, quarters, parts=1):
         self.quarters = quarters
+        self.parts = parts
         self.group = 4 // quarters
         self.rows = 8 * quarters * self.group
-        self.blocks = HALF // self.group
+        self.blocks = HALF // self.group // parts
 
     def levels(self, count):
         return (count + 15) // 16 * 16
@@ -131,25 +132,27 @@
     )(block_aux, block_row, block_col, extents, place, blocks)
 
 
-def split_pieces(place_ref, plan, rows_of, keep_ref, send_refs, level_ref):
+def split_pieces(place_ref, plan, rows_of, out_refs, level_ref):
     bit_a = place_ref[1]
     bit_b = place_ref[2]
 
     def piece(a, b):
         return jnp.where(b == 0, a, 3 - a)
 
-    for h, send_ref in enumerate(send_refs):
-        kept = [piece(bit_a, o) if h == 0 else piece(o, bit_b) for o in range(2)]
-        sent = [piece(1 - bit_a, o) if h == 0 else piece(o, 1 - bit_b) for o in range(2)]
-
-        @pl.loop(0, plan.blocks, unroll=2)
-        def _(block):
-            first = h * HALF + block * plan.group
-            for other in range(2):
-                keep_ref[h, other, block] = rows_of(first, kept[other])
-                put(send_ref, plan, other * plan.blocks + block, rows_of(first, sent[other]), level_ref)
-
-        put_levels(send_ref, plan, 2 * plan.blocks, level_ref)
+    for part in range(plan.parts):
+        keep_ref, *send_refs = out_refs[3 * part : 3 * part + 3]
+        for h, send_ref in enumerate(send_refs):
+            kept = [piece(bit_a, o) if h == 0 else piece(o, bit_b) for o in range(2)]
+            sent = [piece(1 - bit_a, o) if h == 0 else piece(o, 1 - bit_b) for o in range(2)]
+
+            @pl.loop(0, plan.blocks, unroll=2)
+            def _(block):
+                first = h * HALF + (part * plan.blocks + block) * plan.group
+                for other in range(2):
+                    keep_ref[h, other, block] = rows_of(first, kept[other])
+                    put(send_ref, plan, other * plan.blocks + block, rows_of(first, sent[other]), level_ref)
+
+            put_levels(send_ref, plan, 2 * plan.blocks, level_ref)
 
 
 def start_all(sources, targets, sems):
@@ -199,7 +202,7 @@
     def rows_of(first, piece):
         return these(first, piece) + those(first, piece)
 
-    split_pieces(place_ref, plan, rows_of, keep_ref, (send0_ref, send1_ref), level_ref)
+    split_pieces(place_ref, plan, rows_of, (keep_ref, send0_ref, send1_ref), level_ref)
 
 
 def piece_rows(acc_ref):
@@ -211,7 +214,8 @@
 
 
 def occ_body(meta_ref, place_ref, *rest, plan):
-    parts, green_ref, (keep_ref, send0_ref, send1_ref, acc_ref, tile_ref, level_ref) = (rest[:4], rest[4:8]), rest[8], rest[9:]
+    parts, green_ref = (rest[:4], rest[4:8]), rest[8]
+    out_refs, (acc_ref, tile_ref, level_ref) = rest[9:-3], rest[-3:]
     acc_ref[...] = jnp.zeros(acc_ref.shape, F32)
     row_place = place_ref[0]
     rows = [pl.multiple_of(((row_place + d) % ROWS) * QUARTER, QUARTER) for d in (0, ROWS - 1, 1, 2)]
@@ -236,7 +240,7 @@
                     lanes = slice(low * BS, (low + 1) * BS)
                     acc_ref[aux, :, lanes] += term[low * BS : (low + 1) * BS, :]
 
-    split_pieces(place_ref, plan, piece_rows(acc_ref), keep_ref, (send0_ref, send1_ref), level_ref)
+    split_pieces(place_ref, plan, piece_rows(acc_ref), out_refs, level_ref)
 
 
 VMEM = pl.BlockSpec(memory_space=pltpu.VMEM)
@@ -290,8 +294,8 @@
     return pl.pallas_call(
         functools.partial(occ_body, plan=plan),
         in_specs=[SMEM] * 2 + [VMEM] * 9,
-        out_specs=[VMEM] * 3,
-        out_shape=step_shapes(plan),
+        out_specs=[VMEM] * 3 * plan.parts,
+        out_shape=step_shapes(plan) * plan.parts,
         scratch_shapes=[pltpu.VMEM(ACC, F32), pltpu.VMEM((2 * CAP, BS, BS), BF16), level_scratch(plan)],
         compiler_params=params(28),
         name="contract_occ",
@@ -326,25 +330,28 @@
     )(place, keep, got0, got1)
 
 
-def finish_blocks(left_ref, got_refs, scale_ref, plan, store):
-    for h, got_ref in enumerate(got_refs):
-        read_scales(got_ref, (), plan, plan.blocks, scale_ref)
-
-        @pl.loop(0, plan.blocks, unroll=2)
-        def _(b):
-            store(h * plan.blocks + b, left_ref[h, b] + get(got_ref, (), plan, b, scale_ref))
+def finish_blocks(refs, scale_ref, plan, store):
+    for part in range(plan.parts):
+        left_ref, *got_refs = refs[3 * part : 3 * part + 3]
+        for h, got_ref in enumerate(got_refs):
+            read_scales(got_ref, (), plan, plan.blocks, scale_ref)
+
+            @pl.loop(0, plan.blocks, unroll=2)
+            def _(b):
+                total = left_ref[h, b] + get(got_ref, (), plan, b, scale_ref)
+                store((h * plan.parts + part) * plan.blocks + b, total)
 
 
 def finish_virt_body(left_ref, got0_ref, got1_ref, out_ref, level_ref, scale_ref, *, plan):
     def store(index, total):
         put(out_ref, plan, index, total, level_ref)
 
-    finish_blocks(left_ref, (got0_ref, got1_ref), scale_ref, plan, store)
+    finish_blocks((left_ref, got0_ref, got1_ref), scale_ref, plan, store)
     put_levels(out_ref, plan, 2 * plan.blocks, level_ref)
 
 
-def finish_occ_body(place_ref, left_ref, got0_ref, got1_ref, *rest, plan):
-    out_refs, (code_ref, level_ref, scale_ref) = rest[:4], rest[4:]
+def finish_occ_body(place_ref, *rest, plan, whole):
+    refs, out_refs, (code_ref, level_ref, scale_ref) = rest[:-7], rest[-7:-3], rest[-3:]
     lanes = [pl.ds(pl.multiple_of((place_ref[0] + d) % 4 * BS, BS), BS) for d in range(4)]
 
     def store(index, total):
@@ -354,9 +361,9 @@
         for out_ref, part in zip(out_refs, lanes):
             out_ref[at_block(plan, index), :] = code_ref[:, part]
 
-    finish_blocks(left_ref, (got0_ref, got1_ref), scale_ref, plan, store)
+    finish_blocks(refs, scale_ref, plan, store)
     for out_ref, part in zip(out_refs, lanes):
-        out_ref[level_rows(plan, 2 * plan.blocks), :] = level_ref[:, part].astype(jnp.int32).astype(S16)
+        out_ref[level_rows(whole, 2 * whole.blocks), :] = level_ref[:, part].astype(jnp.int32).astype(S16)
 
 
 def finish_virt(left, got0, got1, plan):
@@ -371,17 +378,17 @@
     )(left, got0, got1)
 
 
-def finish_occ(place, left, got0, got1, plan):
-    part = jax.ShapeDtypeStruct((plan.coded(2 * plan.blocks), BS), S16)
-    return pl.pallas_call(
-        functools.partial(finish_occ_body, plan=plan),
-        in_specs=[SMEM] + [VMEM] * 3,
+def finish_occ(place, sums, plan, whole):
+    part = jax.ShapeDtypeStruct((whole.coded(2 * whole.blocks), BS), S16)
+    return pl.pallas_call(
+        functools.partial(finish_occ_body, plan=plan, whole=whole),
+        in_specs=[SMEM] + [VMEM] * len(sums),
         out_specs=[VMEM] * 4,
         out_shape=[part] * 4,
-        scratch_shapes=[pltpu.VMEM((plan.rows, WIDE), S16), level_scratch(plan), level_scratch(plan)],
+        scratch_shapes=[pltpu.VMEM((plan.rows, WIDE), S16), level_scratch(whole), level_scratch(whole)],
         compiler_params=params(12),
         name="finish_occ",
-    )(place, left, got0, got1)
+    )(place, *sums)
 
 
 def decode_virt_body(place_ref, virt_ref, vir_ref, scale_ref, *, plan):
@@ -518,19 +525,25 @@
     v_keep, v0, v1 = contract_virt_last(meta, place, part_b, virt_blocks, v_acc, plan)
     v_got = layer_swap(v0, v1, FIRST)
     occ_blocks, v_keep = after(occ_blocks, v_keep)
-    o_keep, o0, o1 = contract_occ(meta, place, (part_a, part_b), occ_blocks, plan)
-    v_keep, o_keep = after(v_keep, o_keep)
+    halves = Plan(4, parts=2)
+    a_keep, a0, a1, b_keep, b0, b1 = contract_occ(meta, place, (part_a, part_b), occ_blocks, halves)
+    a_got = layer_swap(a0, a1, FIRST)
+    v_keep, a_keep, b_keep = after(v_keep, a_keep, b_keep)
     v_left, v0, v1 = halve(place, v_keep, *v_got, plan, "halve_virt")
     v_got = layer_swap(v0, v1, SECOND)
-    o0, o1, *v_got = after(o0, o1, *v_got)
-    o_got = layer_swap(o0, o1, FIRST)
+    a_keep, v_left = after(a_keep, v_left)
+    a_left, a0, a1 = halve(place, a_keep, *a_got, halves, "halve_occ_a")
+    a_left, *v_got = after(a_left, *v_got)
+    a0, a1, b0, b1, *v_got = after(a0, a1, b0, b1, *v_got)
+    b_got = layer_swap(b0, b1, FIRST)
+    a_got = layer_swap(a0, a1, SECOND)
     virt = finish_virt(v_left, *v_got, plan)
-    virt, o_keep = after(virt, o_keep)
+    virt, b_keep = after(virt, b_keep)
     virt = lax.ppermute(virt, ALL, SWAP)
-    o_left, o0, o1 = halve(place, o_keep, *o_got, plan, "halve_occ")
-    o_got = layer_swap(o0, o1, SECOND)
+    b_left, b0, b1 = halve(place, b_keep, *b_got, halves, "halve_occ_b")
+    b_got = layer_swap(b0, b1, SECOND)
     here = jnp.stack([col_place // 4, col_place % 4])
-    occ, *others = finish_occ(here, o_left, *o_got, plan)
+    occ, *others = finish_occ(here, (a_left, *a_got, b_left, *b_got), halves, plan)
     others = [lax.ppermute(part, "col", rotate_high(d)) for d, part in zip((1, 2, 3), others)]
     partial = pair(here, occ, others, decode_virt(here, virt, plan), plan)
     return sum_all(jnp.sum(partial, axis=-1))

time: 222 us -> 221 us (level)
  waiting for transfers between devices: 45.3 us -> 35.5 us
  blocking collectives: 69.9 us -> 79.3 us
    all_to_all x2, blocking collectives: 26.3 us -> 35.7 us  [sum_all(): values = jnp.sum(lax.all_to_all(copies, axes, 0, 0, tiled=True), axis=0)]
    ppermute x3, waiting for transfers between devices: 15.2 us -> 5.84 us  [on_device(): lax.ppermute(part, 'col', rotate_high(d))]
    ppermute x1, starting transfers between devices: 10.9 us -> 4.14 us  [on_device(): virt = lax.ppermute(virt, ALL, SWAP)]
    ppermute x4 -> x6, starting transfers between devices: 3.01 us -> 6.91 us  [layer_swap(): lax.ppermute(send1, 'layer', perms[1])]
    ppermute x4 -> x6, starting transfers between devices: 4.25 us -> 6.23 us  [layer_swap(): lax.ppermute(send0, 'layer', perms[0])]
    pallas_call x2 -> x3, Pallas kernels: 3.93 us -> 5.06 us  [halve(): pl.pallas_call(functools.partial(halve_body, plan=plan), in_specs=[SMEM]...]
    ppermute x4 -> x6, waiting for transfers between devices: 16.7 us -> 17 us  [layer_swap(): lax.ppermute(send0, 'layer', perms[0])]
  transfers between devices with their start and end apart: 18 -> 22, of which waited for: 10 -> 8; matrix products, arithmetic and copies ran while one was open for 4% -> 4% of each run, Pallas kernels for 14% -> 16%
where the time goes in v9:
time: 221 us
  blocking collectives  79.3 us (36%)
  Pallas kernels  56.5 us (26%)
  starting transfers between devices  36.2 us (16%)
  waiting for transfers between devices  35.5 us (16%)
  local copies, waits for them, and re-layouts  9.18 us (4%)
  other arithmetic  3.67 us (2%)
    all_to_all x1, blocking collectives, on_device(): own = lax.all_to_all(send, ('col', 'layer'), 0, 0, tiled=True)  43.7 us
    all_to_all x2, blocking collectives, sum_all(): values = jnp.sum(lax.all_to_all(copies, axes, 0, 0, tiled=True), axis=0)  35.7 us
    ppermute x6, waiting for transfers between devices, layer_swap(): lax.ppermute(send0, 'layer', perms[0])  17 us
    pallas_call x1, Pallas kernels, contract_occ(): pl.pallas_call(functools.partial(occ_body, plan=plan), in_specs=[SMEM] *...  14 us
    pallas_call x1, Pallas kernels, contract_virt_last(): pl.pallas_call(functools.partial(virt_last_body, plan=plan), in_specs=[SM...  12.7 us
    pallas_call x1, Pallas kernels, contract_virt_first(): pl.pallas_call(virt_first_body, in_specs=[SMEM] + [ANY] * 5, out_specs=AN...  11.7 us
    ppermute x3, starting transfers between devices, on_device(): lax.ppermute(part, 'col', rotate_high(d))  10.5 us
    ppermute x1, waiting for transfers between devices, on_device(): far_a = lax.ppermute(prev_a, 'row', up)  9.59 us
  transfers between devices with their start and end apart: 22, of which 8 were waited for; matrix products, arithmetic and copies ran while one was open for 4% of the time, Pallas kernels for 16%

profile of v9, /device:TPU:1, one launch (start us, length us, event | category | flops | bytes accessed | tf_op | source)
XLA Modules:
  0.0 220.8 jit_solution(13719357344399823667)
XLA Ops:
  0.0 5.1 %build_send.1 = bf16[64,72,128]{2,1,0:T(8,128)(2,1)} custom-call(s32[88]{0:T(128)} %aux_ref.1, s32[88]{0:T(128)} %row_ref.1, s32[88]{0:T(128)} %col_ref.1, s32[88]{0:T(128)} %ext_ref.1, s32[1]{0:T(128)} %bitcast.2.place_ref, bf16[88,128,128]{2,1,0:T(8,128)(2,1)} %blocks_ref.1), custom_call_target="tpu_custom_call" | custom-call | tf_op jit(solution)/shard_map/build_send/pallas_call | solution.py:120
  5.1 43.7 %all_to_all.15 = bf16[64,72,128]{2,1,0:T(8,128)(2,1)S(1)} all-to-all(bf16[64,72,128]{2,1,0:T(8,128)(2,1)} %build_send.1), channel_id=1, replica_groups=mesh['row'=4,'col'=16,'layer'=4] {'col','layer'}, dimensions={0} | all-to-all | bytes 2359296 | tf_op jit(solution)/shard_map/all_to_all | solution.py:504
  48.8 1.4 collective-permute-start
  50.2 1.5 collective-permute-start.1
  51.7 7.9 %copy.9 = bf16[40,128,512]{1,2,0:T(8,128)(2,1)} copy(bf16[40,128,512]{2,1,0:T(8,128)(2,1)} %bitcast.17) | data formatting | bytes 10485760 | tf_op jit(solution)/shard_map/reshape | solution.py:506
  59.7 0.7 slice_convert_fusion
  60.4 1.7 collective-permute-done.rest_1_
  62.1 1.0 collective-permute-start.2
  63.1 1.8 collective-permute-start.3
  64.9 9.6 %collective-permute-done.2.rest_3_ = bf16[32,64,128]{2,1,0:T(8,128)(2,1)S(1)} collective-permute-done((bf16[32,64,128]{2,1,0:T(8,128)(2,1)S(1)}, bf16[32,64,128]{2,1,0:T(8,128)(2,1)S(1)}, u32[]{:S(2)}, u32[]{:S(2)}) %collective-permute-start.2) | collective-permute-done | bytes 524320 | tf_op jit(solution)/shard_map/ppermute | solution.py:517
  74.6 2.7 %collective-permute-start.5 = (bf16[32,64,128]{2,1,0:T(8,128)(2,1)S(1)}, bf16[32,64,128]{2,1,0:T(8,128)(2,1)}, u32[]{:S(2)}, u32[]{:S(2)}) collective-permute-start(bf16[32,64,128]{2,1,0:T(8,128)(2,1)S(1)} %collective-permute-done.3.rest_2_.rest_6_), channel_id=1, source_target_pairs={{0,192},{64,0},{128,64},{192,128},{1,193},{65,1},{129,65},{193,129... | collective-permute-start | bytes 1572872 | tf_op jit(solution)/shard_map/ppermute | solution.py:521
  77.2 0.6 pad_add_fusion.1.place_ref
  77.9 11.7 %virt_first.1.rest_5_ = f32[24,128,512]{2,1,0:T(8,128)} custom-call(s32[64,4]{1,0:T(8,128)} %bitcast.12, bf16[32,64,128]{2,1,0:T(8,128)(2,1)} %copy-done, bf16[32,64,128]{2,1,0:T(8,128)(2,1)} %copy-done.5, bf16[32,64,128]{2,1,0:T(8,128)(2,1)} %copy-done.7, bf16[32,64,128]{2,1,0:T(8,128)(2,1)} %copy-done.9, bf16[40,128,512]{2,1,0:T(8,128)(2,1)} %bitcast.15), custom_call_target="tpu_custom_call" | custom-call | tf_op jit(solution)/shard_map/virt_first/pallas_call | solution.py:269
  89.7 12.7 %virt_last.1 = (f32[2,2,12,32,512]{4,3,2,1,0:T(8,128)}, s16[800,512]{1,0:T(8,128)(2,1)}, s16[800,512]{1,0:T(8,128)(2,1)}) custom-call(s32[64,4]{1,0:T(8,128)} %bitcast.13, s32[3]{0:T(128)} %pad_add_fusion.1.place_ref, bf16[32,64,128]{2,1,0:T(8,128)(2,1)} %copy-done.2, bf16[32,64,128]{2,1,0:T(8,128)(2,1)} %collective-permute-done.4.rest_1_.rest_5_, ...), custom_call_target="tpu_custom_call" | custom-call | tf_op jit(solution)/shard_map/virt_last/pallas_call | solution.py:282
  102.4 0.4 collective-permute-start.6
  102.8 2.1 collective-permute-start.7
  105.0 14.0 %contract_occ.1 = (f32[2,2,6,32,512]{4,3,2,1,0:T(8,128)S(1)}, s16[400,512]{1,0:T(8,128)(2,1)S(1)}, s16[400,512]{1,0:T(8,128)(2,1)S(1)}, f32[2,2,6,32,512]{4,3,2,...) custom-call(s32[64,4]{1,0:T(8,128)S(1)} %bitcast.14, s32[3]{0:T(128)S(1)} %copy-done.14, ...), custom_call_target="tpu_custom_call" | custom-call | tf_op jit(solution)/shard_map/contract_occ/pallas_call | solution.py:294
  118.9 0.3 collective-permute-start.8
  119.2 1.0 collective-permute-start.9
  120.2 1.5 halve_virt.1
  121.7 2.0 collective-permute-start.10
  123.8 4.1 %collective-permute-done.8.got0_ref = s16[400,512]{1,0:T(8,128)(2,1)S(1)} collective-permute-done((s16[400,512]{1,0:T(8,128)(2,1)S(1)}, s16[400,512]{1,0:T(8,128)(2,1)S(1)}, u32[]{:S(2)}, u32[]{:S(2)}) %collective-permute-start.8) | collective-permute-done | bytes 409632 | tf_op jit(solution)/shard_map/ppermute | solution.py:482
  127.9 1.3 collective-permute-done.9.got1_ref
  129.2 1.8 halve_occ_a.1
  130.9 7.0 %collective-permute-done.10.got0_ref = s16[400,512]{1,0:T(8,128)(2,1)S(1)} collective-permute-done((s16[400,512]{1,0:T(8,128)(2,1)S(1)}, s16[400,512]{1,0:T(8,128)(2,1)S(1)}, u32[]{:S(2)}, u32[]{:S(2)}) %collective-permute-start.10) | collective-permute-done | bytes 409632 | tf_op jit(solution)/shard_map/ppermute | solution.py:482
  138.0 3.4 %collective-permute-start.15 = (s16[400,512]{1,0:T(8,128)(2,1)S(1)}, s16[400,512]{1,0:T(8,128)(2,1)S(1)}, u32[]{:S(2)}, u32[]{:S(2)}) collective-permute-start(s16[400,512]{1,0:T(8,128)(2,1)S(1)} %get-tuple-element.96), channel_id=1, source_target_pairs={{0,3},{3,0},{1,2},{2,1},{4,7},{7,4},{5,6},{6,5},{8,11},{11,8},{9,1... | collective-permute-start | bytes 1228808 | tf_op jit(solution)/shard_map/ppermute | solution.py:482
  141.4 0.9 finish_virt.1
  142.2 4.1 %collective-permute-start.21 = (s16[800,512]{1,0:T(8,128)(2,1)S(1)}, s16[800,512]{1,0:T(8,128)(2,1)S(1)}, u32[]{:S(2)}, u32[]{:S(2)}) collective-permute-start(s16[800,512]{1,0:T(8,128)(2,1)S(1)} %finish_virt.1), channel_id=1, source_target_pairs={{0,0},{1,1},{2,2},{3,3},{4,64},{5,65},{6,66},{7,67},{8,128},{9,129... | collective-permute-start | bytes 2457608 | tf_op jit(solution)/shard_map/ppermute | solution.py:542
  146.4 0.9 collective-permute-start.12
  147.3 0.4 collective-permute-start.13
  147.7 1.8 halve_occ_b.1
  149.5 2.7 %collective-permute-start.16 = (s16[208,512]{1,0:T(8,128)(2,1)}, s16[208,512]{1,0:T(8,128)(2,1)}, u32[]{:S(2)}, u32[]{:S(2)}) collective-permute-start(s16[208,512]{1,0:T(8,128)(2,1)} %get-tuple-element.98), channel_id=1, source_target_pairs={{0,3},{3,0},{1,2},{2,1},{4,7},{7,4},{5,6},{6,5},{8,11},{11,8},{9,1... | collective-permute-start | bytes 638984 | tf_op jit(solution)/shard_map/ppermute | solution.py:482
  152.2 3.0 %collective-permute-done.12.rest_1_ = s16[208,512]{1,0:T(8,128)(2,1)S(1)} collective-permute-done((s16[208,512]{1,0:T(8,128)(2,1)}, s16[208,512]{1,0:T(8,128)(2,1)S(1)}, u32[]{:S(2)}, u32[]{:S(2)}) %collective-permute-start.12) | collective-permute-done | bytes 213024 | tf_op jit(solution)/shard_map/ppermute | solution.py:482
  155.2 2.9 %collective-permute-done.16.rest_4_ = s16[208,512]{1,0:T(8,128)(2,1)} collective-permute-done((s16[208,512]{1,0:T(8,128)(2,1)}, s16[208,512]{1,0:T(8,128)(2,1)}, u32[]{:S(2)}, u32[]{:S(2)}) %collective-permute-start.16) | collective-permute-done | bytes 213024 | tf_op jit(solution)/shard_map/ppermute | solution.py:482
  158.1 2.1 finish_occ.1
  160.2 5.0 %collective-permute-start.18 = (s16[800,128]{1,0:T(8,128)(2,1)S(1)}, s16[800,128]{1,0:T(8,128)(2,1)S(1)}, u32[]{:S(2)}, u32[]{:S(2)}) collective-permute-start(s16[800,128]{1,0:T(8,128)(2,1)S(1)} %get-tuple-element.101), channel_id=1, source_target_pairs={{0,16},{4,20},{8,24},{12,28},{16,32},{20,36},{24,40},{28,44},{32,4... | collective-permute-start | bytes 614408 | tf_op jit(solution)/shard_map/ppermute | solution.py:547
  165.3 3.3 %collective-permute-start.19 = (s16[800,128]{1,0:T(8,128)(2,1)S(1)}, s16[800,128]{1,0:T(8,128)(2,1)S(1)}, u32[]{:S(2)}, u32[]{:S(2)}) collective-permute-start(s16[800,128]{1,0:T(8,128)(2,1)S(1)} %get-tuple-element.102), channel_id=1, source_target_pairs={{0,32},{4,36},{8,40},{12,44},{16,48},{20,52},{24,56},{28,60},{32,0... | collective-permute-start | bytes 614408 | tf_op jit(solution)/shard_map/ppermute | solution.py:547
  168.6 2.2 collective-permute-start.20
  170.8 0.8 decode_virt.1.vir_ref
  171.6 5.8 %collective-permute-done.19.two_ref = s16[800,128]{1,0:T(8,128)(2,1)S(1)} collective-permute-done((s16[800,128]{1,0:T(8,128)(2,1)S(1)}, s16[800,128]{1,0:T(8,128)(2,1)S(1)}, u32[]{:S(2)}, u32[]{:S(2)}) %collective-permute-start.19) | collective-permute-done | bytes 204832 | tf_op jit(solution)/shard_map/ppermute | solution.py:547
  177.4 4.3 %pair.1 = f32[24,24,128]{2,1,0:T(8,128)S(1)} custom-call(s32[2]{0:T(128)S(1)} %pad_add_fusion.place_ref, s16[800,128]{1,0:T(8,128)(2,1)S(1)} %get-tuple-element.100.own_ref, s16[800,128]{1,0:T(8,128)(2,1)S(1)} %collective-permute-done.18.one_ref, s16[800,128]{1,0:T(8,128)(2,1)S(1)} %collective-permute-done.19.two_ref, ...), custom_call_target="tpu_custom_call" | custom-call | tf_op jit(solution)/shard_map/pair/pallas_call | solution.py:439
  181.9 0.2 reshape.14
  182.1 25.1 %all_to_all.16 = f32[16,1,576]{2,1,0:T(1,128)S(1)} all-to-all(f32[16,1,576]{2,1,0:T(1,128)S(1)} %reshape.14), channel_id=1, replica_groups=mesh['row'=4,'col'=16,'layer'=4] {'col'}, dimensions={0} | all-to-all | bytes 73728 | tf_op jit(solution)/shard_map/all_to_all | solution.py:477
  207.2 0.5 broadcast.5
  207.7 0.7 reduce
  208.8 10.5 %all_to_all.17 = f32[16,1,576]{2,1,0:T(1,128)S(1)} all-to-all(f32[16,1,576]{2,1,0:T(1,128)S(1)} %reshape.16), channel_id=1, replica_groups=mesh['row'=4,'col'=16,'layer'=4] {'row','layer'}, dimensions={0} | all-to-all | bytes 73728 | tf_op jit(solution)/shard_map/all_to_all | solution.py:477
  219.3 0.7 reduce.1
  220.2 0.6 reduce_sum.29
  (63 shorter events, 1.0 us)
Async XLA Ops:
  48.8 10.8 %copy-start = (bf16[32,64,128]{2,1,0:T(8,128)(2,1)}, bf16[32,64,128]{2,1,0:T(8,128)(2,1)S(1)}, u32[]{:S(2)}) copy-start(bf16[32,64,128]{2,1,0:T(8,128)(2,1)S(1)} %slice.12.rest_0_) | copy-start | bytes 1572868
  48.8 13.3 %collective-permute-start = (bf16[32,64,128]{2,1,0:T(8,128)(2,1)S(1)}, bf16[32,64,128]{2,1,0:T(8,128)(2,1)S(1)}, u32[]{:S(2)}, u32[]{:S(2)}) collective-permute-start(bf16[32,64,128]{2,1,0:T(8,128)(2,1)S(1)} %slice.12.rest_0_), channel_id=1, source_target_pairs={{0,64},{64,128},{128,192},{192,0},{1,65},{65,129},{129,193},{193,1... | collective-permute-start | bytes 1572872 | tf_op jit(solution)/shard_map/ppermute | solution.py:514
  50.2 12.0 %collective-permute-start.1 = (bf16[32,64,128]{2,1,0:T(8,128)(2,1)S(1)}, bf16[32,64,128]{2,1,0:T(8,128)(2,1)S(1)}, u32[]{:S(2)}, u32[]{:S(2)}) collective-permute-start(bf16[32,64,128]{2,1,0:T(8,128)(2,1)S(1)} %slice.12.rest_0_), channel_id=1, source_target_pairs={{0,192},{64,0},{128,64},{192,128},{1,193},{65,1},{129,65},{193,129... | collective-permute-start | bytes 1572872 | tf_op jit(solution)/shard_map/ppermute | solution.py:515
  59.7 29.9 %copy-start.2 = (bf16[32,64,128]{2,1,0:T(8,128)(2,1)}, bf16[32,64,128]{2,1,0:T(8,128)(2,1)S(1)}, u32[]{:S(2)}) copy-start(bf16[32,64,128]{2,1,0:T(8,128)(2,1)S(1)} %slice.10.rest_0_.rest_4_) | copy-start | bytes 1572868
  62.1 15.7 %copy-start.5 = (bf16[32,64,128]{2,1,0:T(8,128)(2,1)}, bf16[32,64,128]{2,1,0:T(8,128)(2,1)S(1)}, u32[]{:S(2)}) copy-start(bf16[32,64,128]{2,1,0:T(8,128)(2,1)S(1)} %collective-permute-done.rest_1_) | copy-start | bytes 1572868
  62.1 15.7 %copy-start.7 = (bf16[32,64,128]{2,1,0:T(8,128)(2,1)}, bf16[32,64,128]{2,1,0:T(8,128)(2,1)S(1)}, u32[]{:S(2)}) copy-start(bf16[32,64,128]{2,1,0:T(8,128)(2,1)S(1)} %collective-permute-done.1.rest_2_) | copy-start | bytes 1572868
  62.1 12.3 %collective-permute-start.2 = (bf16[32,64,128]{2,1,0:T(8,128)(2,1)S(1)}, bf16[32,64,128]{2,1,0:T(8,128)(2,1)S(1)}, u32[]{:S(2)}, u32[]{:S(2)}) collective-permute-start(bf16[32,64,128]{2,1,0:T(8,128)(2,1)S(1)} %collective-permute-done.rest_1_), channel_id=1, source_target_pairs={{0,64},{64,128},{128,192},{192,0},{1,65},{65,129},{129,193},{193,1... | collective-permute-start | bytes 1572872 | tf_op jit(solution)/shard_map/ppermute | solution.py:517
  63.1 11.4 %collective-permute-start.3 = (bf16[32,64,128]{2,1,0:T(8,128)(2,1)S(1)}, bf16[32,64,128]{2,1,0:T(8,128)(2,1)S(1)}, u32[]{:S(2)}, u32[]{:S(2)}) collective-permute-start(bf16[32,64,128]{2,1,0:T(8,128)(2,1)S(1)} %slice.10.rest_0_.rest_4_), channel_id=1, source_target_pairs={{0,192},{64,0},{128,64},{192,128},{1,193},{65,1},{129,65},{193,129... | collective-permute-start | bytes 1572872 | tf_op jit(solution)/shard_map/ppermute | solution.py:518
  74.5 3.4 %copy-start.9 = (bf16[32,64,128]{2,1,0:T(8,128)(2,1)}, bf16[32,64,128]{2,1,0:T(8,128)(2,1)S(1)}, u32[]{:S(2)}) copy-start(bf16[32,64,128]{2,1,0:T(8,128)(2,1)S(1)} %collective-permute-done.2.rest_3_) | copy-start | bytes 1572868
  74.5 15.1 %copy-start.11 = (bf16[32,64,128]{2,1,0:T(8,128)(2,1)}, bf16[32,64,128]{2,1,0:T(8,128)(2,1)S(1)}, u32[]{:S(2)}) copy-start(bf16[32,64,128]{2,1,0:T(8,128)(2,1)S(1)} %collective-permute-done.3.rest_2_.rest_6_) | copy-start | bytes 1572868
  74.5 15.2 %collective-permute-start.4 = (bf16[32,64,128]{2,1,0:T(8,128)(2,1)S(1)}, bf16[32,64,128]{2,1,0:T(8,128)(2,1)}, u32[]{:S(2)}, u32[]{:S(2)}) collective-permute-start(bf16[32,64,128]{2,1,0:T(8,128)(2,1)S(1)} %slice.10.rest_0_.rest_4_), channel_id=1, source_target_pairs={{0,64},{64,128},{128,192},{192,0},{1,65},{65,129},{129,193},{193,1... | collective-permute-start | bytes 1572872 | tf_op jit(solution)/shard_map/ppermute | solution.py:520
  74.6 15.1 %collective-permute-start.5 = (bf16[32,64,128]{2,1,0:T(8,128)(2,1)S(1)}, bf16[32,64,128]{2,1,0:T(8,128)(2,1)}, u32[]{:S(2)}, u32[]{:S(2)}) collective-permute-start(bf16[32,64,128]{2,1,0:T(8,128)(2,1)S(1)} %collective-permute-done.3.rest_2_.rest_6_), channel_id=1, source_target_pairs={{0,192},{64,0},{128,64},{192,128},{1,193},{65,1},{129,65},{193,129... | collective-permute-start | bytes 1572872 | tf_op jit(solution)/shard_map/ppermute | solution.py:521
  77.9 27.0 %slice-start = ((s8[5242880]{0:T(1024)(128)(4,1)}), s8[4194304]{0:T(1024)(128)(4,1)S(1)}, s32[]{:S(2)}) async-start(s8[5242880]{0:T(1024)(128)(4,1)} %bitcast.9), calls=%async_computation.3 | async-start | bytes 8388608
  89.6 15.2 %slice-start.1 = ((s8[5242880]{0:T(1024)(128)(4,1)}), s8[1048576]{0:T(1024)(128)(4,1)S(1)}, s32[]{:S(2)}) async-start(s8[5242880]{0:T(1024)(128)(4,1)} %bitcast.9), calls=%async_computation.4 | async-start | bytes 2097152
  89.6 15.2 %copy-start.1 = (bf16[32,64,128]{2,1,0:T(8,128)(2,1)S(1)}, bf16[32,64,128]{2,1,0:T(8,128)(2,1)}, u32[]{:S(2)}) copy-start(bf16[32,64,128]{2,1,0:T(8,128)(2,1)} %copy-done) | copy-start | bytes 1572868
  89.6 15.2 %copy-start.6 = (bf16[32,64,128]{2,1,0:T(8,128)(2,1)S(1)}, bf16[32,64,128]{2,1,0:T(8,128)(2,1)}, u32[]{:S(2)}) copy-start(bf16[32,64,128]{2,1,0:T(8,128)(2,1)} %copy-done.5) | copy-start | bytes 1572868
  89.7 15.2 %copy-start.8 = (bf16[32,64,128]{2,1,0:T(8,128)(2,1)S(1)}, bf16[32,64,128]{2,1,0:T(8,128)(2,1)}, u32[]{:S(2)}) copy-start(bf16[32,64,128]{2,1,0:T(8,128)(2,1)} %copy-done.7) | copy-start | bytes 1572868
  89.7 15.2 %copy-start.10 = (bf16[32,64,128]{2,1,0:T(8,128)(2,1)S(1)}, bf16[32,64,128]{2,1,0:T(8,128)(2,1)}, u32[]{:S(2)}) copy-start(bf16[32,64,128]{2,1,0:T(8,128)(2,1)} %copy-done.9) | copy-start | bytes 1572868
  89.7 15.2 %copy-start.13 = (s32[64,1,4]{2,1,0:T(1,128)S(1)}, s32[64,1,4]{2,1,0:T(1,128)}, u32[]{:S(2)}) copy-start(s32[64,1,4]{2,1,0:T(1,128)} %slice_convert_fusion) | copy-start | bytes 3076
  89.7 15.2 %copy-start.14 = (s32[3]{0:T(128)S(1)}, s32[3]{0:T(128)}, u32[]{:S(2)}) copy-start(s32[3]{0:T(128)} %pad_add_fusion.1.place_ref) | copy-start | bytes 40
  89.7 15.2 %copy-start.3 = (bf16[32,64,128]{2,1,0:T(8,128)(2,1)S(1)}, bf16[32,64,128]{2,1,0:T(8,128)(2,1)}, u32[]{:S(2)}) copy-start(bf16[32,64,128]{2,1,0:T(8,128)(2,1)} %copy-done.2) | copy-start | bytes 1572868
  89.7 15.2 %copy-start.12 = (bf16[32,64,128]{2,1,0:T(8,128)(2,1)S(1)}, bf16[32,64,128]{2,1,0:T(8,128)(2,1)}, u32[]{:S(2)}) copy-start(bf16[32,64,128]{2,1,0:T(8,128)(2,1)} %copy-done.11) | copy-start | bytes 1572868
  102.4 17.8 %collective-permute-start.6 = (s16[800,512]{1,0:T(8,128)(2,1)}, s16[800,512]{1,0:T(8,128)(2,1)S(1)}, u32[]{:S(2)}, u32[]{:S(2)}) collective-permute-start(s16[800,512]{1,0:T(8,128)(2,1)} %get-tuple-element.72), channel_id=1, source_target_pairs={{0,1},{1,0},{2,3},{3,2},{4,5},{5,4},{6,7},{7,6},{8,9},{9,8},{10,11... | collective-permute-start | bytes 2457608 | tf_op jit(solution)/shard_map/ppermute | solution.py:482
  102.8 17.4 %collective-permute-start.7 = (s16[800,512]{1,0:T(8,128)(2,1)}, s16[800,512]{1,0:T(8,128)(2,1)S(1)}, u32[]{:S(2)}, u32[]{:S(2)}) collective-permute-start(s16[800,512]{1,0:T(8,128)(2,1)} %get-tuple-element.73), channel_id=1, source_target_pairs={{0,3},{3,0},{1,2},{2,1},{4,7},{7,4},{5,6},{6,5},{8,11},{11,8},{9,1... | collective-permute-start | bytes 2457608 | tf_op jit(solution)/shard_map/ppermute | solution.py:482
  105.0 15.2 %copy-start.4 = (f32[2,2,12,32,512]{4,3,2,1,0:T(8,128)S(1)}, f32[2,2,12,32,512]{4,3,2,1,0:T(8,128)}, u32[]{:S(2)}) copy-start(f32[2,2,12,32,512]{4,3,2,1,0:T(8,128)} %get-tuple-element.71.keep_ref) | copy-start | bytes 9437188
  118.9 9.0 %collective-permute-start.8 = (s16[400,512]{1,0:T(8,128)(2,1)S(1)}, s16[400,512]{1,0:T(8,128)(2,1)S(1)}, u32[]{:S(2)}, u32[]{:S(2)}) collective-permute-start(s16[400,512]{1,0:T(8,128)(2,1)S(1)} %get-tuple-element.76), channel_id=1, source_target_pairs={{0,1},{1,0},{2,3},{3,2},{4,5},{5,4},{6,7},{7,6},{8,9},{9,8},{10,11... | collective-permute-start | bytes 1228808 | tf_op jit(solution)/shard_map/ppermute | solution.py:482
  119.2 10.0 %collective-permute-start.9 = (s16[400,512]{1,0:T(8,128)(2,1)S(1)}, s16[400,512]{1,0:T(8,128)(2,1)S(1)}, u32[]{:S(2)}, u32[]{:S(2)}) collective-permute-start(s16[400,512]{1,0:T(8,128)(2,1)S(1)} %get-tuple-element.77), channel_id=1, source_target_pairs={{0,3},{3,0},{1,2},{2,1},{4,7},{7,4},{5,6},{6,5},{8,11},{11,8},{9,1... | collective-permute-start | bytes 1228808 | tf_op jit(solution)/shard_map/ppermute | solution.py:482
  121.7 16.2 %collective-permute-start.10 = (s16[400,512]{1,0:T(8,128)(2,1)S(1)}, s16[400,512]{1,0:T(8,128)(2,1)S(1)}, u32[]{:S(2)}, u32[]{:S(2)}) collective-permute-start(s16[400,512]{1,0:T(8,128)(2,1)S(1)} %get-tuple-element.79), channel_id=1, source_target_pairs={{0,3},{3,0},{1,2},{2,1},{4,7},{7,4},{5,6},{6,5},{8,11},{11,8},{9,1... | collective-permute-start | bytes 1228808 | tf_op jit(solution)/shard_map/ppermute | solution.py:482
  123.7 14.2 %collective-permute-start.11 = (s16[400,512]{1,0:T(8,128)(2,1)S(1)}, s16[400,512]{1,0:T(8,128)(2,1)S(1)}, u32[]{:S(2)}, u32[]{:S(2)}) collective-permute-start(s16[400,512]{1,0:T(8,128)(2,1)S(1)} %get-tuple-element.80), channel_id=1, source_target_pairs={{0,1},{1,0},{2,3},{3,2},{4,5},{5,4},{6,7},{7,6},{8,9},{9,8},{10,11... | collective-permute-start | bytes 1228808 | tf_op jit(solution)/shard_map/ppermute | solution.py:482
  137.9 9.7 %collective-permute-start.14 = (s16[400,512]{1,0:T(8,128)(2,1)S(1)}, s16[400,512]{1,0:T(8,128)(2,1)S(1)}, u32[]{:S(2)}, u32[]{:S(2)}) collective-permute-start(s16[400,512]{1,0:T(8,128)(2,1)S(1)} %get-tuple-element.95), channel_id=1, source_target_pairs={{0,1},{1,0},{2,3},{3,2},{4,5},{5,4},{6,7},{7,6},{8,9},{9,8},{10,11... | collective-permute-start | bytes 1228808 | tf_op jit(solution)/shard_map/ppermute | solution.py:482
  138.0 9.7 %collective-permute-start.15 = (s16[400,512]{1,0:T(8,128)(2,1)S(1)}, s16[400,512]{1,0:T(8,128)(2,1)S(1)}, u32[]{:S(2)}, u32[]{:S(2)}) collective-permute-start(s16[400,512]{1,0:T(8,128)(2,1)S(1)} %get-tuple-element.96), channel_id=1, source_target_pairs={{0,3},{3,0},{1,2},{2,1},{4,7},{7,4},{5,6},{6,5},{8,11},{11,8},{9,1... | collective-permute-start | bytes 1228808 | tf_op jit(solution)/shard_map/ppermute | solution.py:482
  142.2 28.6 %collective-permute-start.21 = (s16[800,512]{1,0:T(8,128)(2,1)S(1)}, s16[800,512]{1,0:T(8,128)(2,1)S(1)}, u32[]{:S(2)}, u32[]{:S(2)}) collective-permute-start(s16[800,512]{1,0:T(8,128)(2,1)S(1)} %finish_virt.1), channel_id=1, source_target_pairs={{0,0},{1,1},{2,2},{3,3},{4,64},{5,65},{6,66},{7,67},{8,128},{9,129... | collective-permute-start | bytes 2457608 | tf_op jit(solution)/shard_map/ppermute | solution.py:542
  146.4 8.8 %collective-permute-start.12 = (s16[208,512]{1,0:T(8,128)(2,1)}, s16[208,512]{1,0:T(8,128)(2,1)S(1)}, u32[]{:S(2)}, u32[]{:S(2)}) collective-permute-start(s16[208,512]{1,0:T(8,128)(2,1)} %get-tuple-element.88), channel_id=1, source_target_pairs={{0,3},{3,0},{1,2},{2,1},{4,7},{7,4},{5,6},{6,5},{8,11},{11,8},{9,1... | collective-permute-start | bytes 638984 | tf_op jit(solution)/shard_map/ppermute | solution.py:482
  147.3 7.9 %collective-permute-start.13 = (s16[208,512]{1,0:T(8,128)(2,1)}, s16[208,512]{1,0:T(8,128)(2,1)}, u32[]{:S(2)}, u32[]{:S(2)}) collective-permute-start(s16[208,512]{1,0:T(8,128)(2,1)} %get-tuple-element.89), channel_id=1, source_target_pairs={{0,1},{1,0},{2,3},{3,2},{4,5},{5,4},{6,7},{7,6},{8,9},{9,8},{10,11... | collective-permute-start | bytes 638984 | tf_op jit(solution)/shard_map/ppermute | solution.py:482
  149.5 8.6 %collective-permute-start.16 = (s16[208,512]{1,0:T(8,128)(2,1)}, s16[208,512]{1,0:T(8,128)(2,1)}, u32[]{:S(2)}, u32[]{:S(2)}) collective-permute-start(s16[208,512]{1,0:T(8,128)(2,1)} %get-tuple-element.98), channel_id=1, source_target_pairs={{0,3},{3,0},{1,2},{2,1},{4,7},{7,4},{5,6},{6,5},{8,11},{11,8},{9,1... | collective-permute-start | bytes 638984 | tf_op jit(solution)/shard_map/ppermute | solution.py:482
  152.1 6.0 %collective-permute-start.17 = (s16[208,512]{1,0:T(8,128)(2,1)}, s16[208,512]{1,0:T(8,128)(2,1)}, u32[]{:S(2)}, u32[]{:S(2)}) collective-permute-start(s16[208,512]{1,0:T(8,128)(2,1)} %get-tuple-element.99), channel_id=1, source_target_pairs={{0,1},{1,0},{2,3},{3,2},{4,5},{5,4},{6,7},{7,6},{8,9},{9,8},{10,11... | collective-permute-start | bytes 638984 | tf_op jit(solution)/shard_map/ppermute | solution.py:482
  160.2 11.4 %collective-permute-start.18 = (s16[800,128]{1,0:T(8,128)(2,1)S(1)}, s16[800,128]{1,0:T(8,128)(2,1)S(1)}, u32[]{:S(2)}, u32[]{:S(2)}) collective-permute-start(s16[800,128]{1,0:T(8,128)(2,1)S(1)} %get-tuple-element.101), channel_id=1, source_target_pairs={{0,16},{4,20},{8,24},{12,28},{16,32},{20,36},{24,40},{28,44},{32,4... | collective-permute-start | bytes 614408 | tf_op jit(solution)/shard_map/ppermute | solution.py:547
  165.3 12.2 %collective-permute-start.19 = (s16[800,128]{1,0:T(8,128)(2,1)S(1)}, s16[800,128]{1,0:T(8,128)(2,1)S(1)}, u32[]{:S(2)}, u32[]{:S(2)}) collective-permute-start(s16[800,128]{1,0:T(8,128)(2,1)S(1)} %get-tuple-element.102), channel_id=1, source_target_pairs={{0,32},{4,36},{8,40},{12,44},{16,48},{20,52},{24,56},{28,60},{32,0... | collective-permute-start | bytes 614408 | tf_op jit(solution)/shard_map/ppermute | solution.py:547
  168.6 8.9 %collective-permute-start.20 = (s16[800,128]{1,0:T(8,128)(2,1)S(1)}, s16[800,128]{1,0:T(8,128)(2,1)S(1)}, u32[]{:S(2)}, u32[]{:S(2)}) collective-permute-start(s16[800,128]{1,0:T(8,128)(2,1)S(1)} %get-tuple-element.103), channel_id=1, source_target_pairs={{0,48},{4,52},{8,56},{12,60},{16,0},{20,4},{24,8},{28,12},{32,16},... | collective-permute-start | bytes 614408 | tf_op jit(solution)/shard_map/ppermute | solution.py:547

commit v10 on v9

--- a/solution.py
+++ b/solution.py
@@ -41,12 +41,12 @@
 
 
 class Plan:
-    def __init__(self, quarters, parts=1):
+    def __init__(self, quarters, first=0, blocks=None):
         self.quarters = quarters
-        self.parts = parts
         self.group = 4 // quarters
         self.rows = 8 * quarters * self.group
-        self.blocks = HALF // self.group // parts
+        self.first = first
+        self.blocks = blocks or HALF // self.group
 
     def levels(self, count):
         return (count + 15) // 16 * 16
@@ -132,14 +132,14 @@
     )(block_aux, block_row, block_col, extents, place, blocks)
 
 
-def split_pieces(place_ref, plan, rows_of, out_refs, level_ref):
+def split_pieces(place_ref, plans, rows_of, out_refs, level_ref):
     bit_a = place_ref[1]
     bit_b = place_ref[2]
 
     def piece(a, b):
         return jnp.where(b == 0, a, 3 - a)
 
-    for part in range(plan.parts):
+    for part, plan in enumerate(plans):
         keep_ref, *send_refs = out_refs[3 * part : 3 * part + 3]
         for h, send_ref in enumerate(send_refs):
             kept = [piece(bit_a, o) if h == 0 else piece(o, bit_b) for o in range(2)]
@@ -147,7 +147,7 @@
 
             @pl.loop(0, plan.blocks, unroll=2)
             def _(block):
-                first = h * HALF + (part * plan.blocks + block) * plan.group
+                first = h * HALF + (plan.first + block) * plan.group
                 for other in range(2):
                     keep_ref[h, other, block] = rows_of(first, kept[other])
                     put(send_ref, plan, other * plan.blocks + block, rows_of(first, sent[other]), level_ref)
@@ -202,7 +202,7 @@
     def rows_of(first, piece):
         return these(first, piece) + those(first, piece)
 
-    split_pieces(place_ref, plan, rows_of, (keep_ref, send0_ref, send1_ref), level_ref)
+    split_pieces(place_ref, (plan,), rows_of, (keep_ref, send0_ref, send1_ref), level_ref)
 
 
 def piece_rows(acc_ref):
@@ -213,7 +213,7 @@
     return rows_of
 
 
-def occ_body(meta_ref, place_ref, *rest, plan):
+def occ_body(meta_ref, place_ref, *rest, plans):
     parts, green_ref = (rest[:4], rest[4:8]), rest[8]
     out_refs, (acc_ref, tile_ref, level_ref) = rest[9:-3], rest[-3:]
     acc_ref[...] = jnp.zeros(acc_ref.shape, F32)
@@ -240,7 +240,7 @@
                     lanes = slice(low * BS, (low + 1) * BS)
                     acc_ref[aux, :, lanes] += term[low * BS : (low + 1) * BS, :]
 
-    split_pieces(place_ref, plan, piece_rows(acc_ref), out_refs, level_ref)
+    split_pieces(place_ref, plans, piece_rows(acc_ref), out_refs, level_ref)
 
 
 VMEM = pl.BlockSpec(memory_space=pltpu.VMEM)
@@ -290,13 +290,13 @@
     )(meta, place, *operands)
 
 
-def contract_occ(meta, place, parts, green, plan):
-    return pl.pallas_call(
-        functools.partial(occ_body, plan=plan),
+def contract_occ(meta, place, parts, green, plans):
+    return pl.pallas_call(
+        functools.partial(occ_body, plans=plans),
         in_specs=[SMEM] * 2 + [VMEM] * 9,
-        out_specs=[VMEM] * 3 * plan.parts,
-        out_shape=step_shapes(plan) * plan.parts,
-        scratch_shapes=[pltpu.VMEM(ACC, F32), pltpu.VMEM((2 * CAP, BS, BS), BF16), level_scratch(plan)],
+        out_specs=[VMEM] * 3 * len(plans),
+        out_shape=[shape for plan in plans for shape in step_shapes(plan)],
+        scratch_shapes=[pltpu.VMEM(ACC, F32), pltpu.VMEM((2 * CAP, BS, BS), BF16), level_scratch(plans[-1])],
         compiler_params=params(28),
         name="contract_occ",
     )(meta, place, *parts[0], *parts[1], green)
@@ -330,8 +330,8 @@
     )(place, keep, got0, got1)
 
 
-def finish_blocks(refs, scale_ref, plan, store):
-    for part in range(plan.parts):
+def finish_blocks(refs, scale_ref, plans, store):
+    for part, plan in enumerate(plans):
         left_ref, *got_refs = refs[3 * part : 3 * part + 3]
         for h, got_ref in enumerate(got_refs):
             read_scales(got_ref, (), plan, plan.blocks, scale_ref)
@@ -339,18 +339,18 @@
             @pl.loop(0, plan.blocks, unroll=2)
             def _(b):
                 total = left_ref[h, b] + get(got_ref, (), plan, b, scale_ref)
-                store((h * plan.parts + part) * plan.blocks + b, total)
+                store(h * HALF // plan.group + plan.first + b, total)
 
 
 def finish_virt_body(left_ref, got0_ref, got1_ref, out_ref, level_ref, scale_ref, *, plan):
     def store(index, total):
         put(out_ref, plan, index, total, level_ref)
 
-    finish_blocks((left_ref, got0_ref, got1_ref), scale_ref, plan, store)
+    finish_blocks((left_ref, got0_ref, got1_ref), scale_ref, (plan,), store)
     put_levels(out_ref, plan, 2 * plan.blocks, level_ref)
 
 
-def finish_occ_body(place_ref, *rest, plan, whole):
+def finish_occ_body(place_ref, *rest, plans, whole):
     refs, out_refs, (code_ref, level_ref, scale_ref) = rest[:-7], rest[-7:-3], rest[-3:]
     lanes = [pl.ds(pl.multiple_of((place_ref[0] + d) % 4 * BS, BS), BS) for d in range(4)]
 
@@ -359,9 +359,9 @@
         code_ref[...] = codes
         level_ref[pl.ds(index, 1), :] = level
         for out_ref, part in zip(out_refs, lanes):
-            out_ref[at_block(plan, index), :] = code_ref[:, part]
-
-    finish_blocks(refs, scale_ref, plan, store)
+            out_ref[at_block(whole, index), :] = code_ref[:, part]
+
+    finish_blocks(refs, scale_ref, plans, store)
     for out_ref, part in zip(out_refs, lanes):
         out_ref[level_rows(whole, 2 * whole.blocks), :] = level_ref[:, part].astype(jnp.int32).astype(S16)
 
@@ -378,14 +378,14 @@
     )(left, got0, got1)
 
 
-def finish_occ(place, sums, plan, whole):
+def finish_occ(place, sums, plans, whole):
     part = jax.ShapeDtypeStruct((whole.coded(2 * whole.blocks), BS), S16)
     return pl.pallas_call(
-        functools.partial(finish_occ_body, plan=plan, whole=whole),
+        functools.partial(finish_occ_body, plans=plans, whole=whole),
         in_specs=[SMEM] + [VMEM] * len(sums),
         out_specs=[VMEM] * 4,
         out_shape=[part] * 4,
-        scratch_shapes=[pltpu.VMEM((plan.rows, WIDE), S16), level_scratch(whole), level_scratch(whole)],
+        scratch_shapes=[pltpu.VMEM((whole.rows, WIDE), S16), level_scratch(whole), level_scratch(whole)],
         compiler_params=params(12),
         name="finish_occ",
     )(place, *sums)
@@ -525,14 +525,15 @@
     v_keep, v0, v1 = contract_virt_last(meta, place, part_b, virt_blocks, v_acc, plan)
     v_got = layer_swap(v0, v1, FIRST)
     occ_blocks, v_keep = after(occ_blocks, v_keep)
-    halves = Plan(4, parts=2)
-    a_keep, a0, a1, b_keep, b0, b1 = contract_occ(meta, place, (part_a, part_b), occ_blocks, halves)
+    small, large = parts = Plan(4, 0, 4), Plan(4, 4, 8)
+    a_keep, a0, a1, b_keep, b0, b1 = contract_occ(meta, place, (part_a, part_b), occ_blocks, parts)
     a_got = layer_swap(a0, a1, FIRST)
     v_keep, a_keep, b_keep = after(v_keep, a_keep, b_keep)
     v_left, v0, v1 = halve(place, v_keep, *v_got, plan, "halve_virt")
+    v0, v1, *a_got = after(v0, v1, *a_got)
     v_got = layer_swap(v0, v1, SECOND)
     a_keep, v_left = after(a_keep, v_left)
-    a_left, a0, a1 = halve(place, a_keep, *a_got, halves, "halve_occ_a")
+    a_left, a0, a1 = halve(place, a_keep, *a_got, small, "halve_occ_a")
     a_left, *v_got = after(a_left, *v_got)
     a0, a1, b0, b1, *v_got = after(a0, a1, b0, b1, *v_got)
     b_got = layer_swap(b0, b1, FIRST)
@@ -540,11 +541,12 @@
     virt = finish_virt(v_left, *v_got, plan)
     virt, b_keep = after(virt, b_keep)
     virt = lax.ppermute(virt, ALL, SWAP)
-    b_left, b0, b1 = halve(place, b_keep, *b_got, halves, "halve_occ_b")
+    b_left, b0, b1 = halve(place, b_keep, *b_got, large, "halve_occ_b")
     b_got = layer_swap(b0, b1, SECOND)
     here = jnp.stack([col_place // 4, col_place % 4])
-    occ, *others = finish_occ(here, (a_left, *a_got, b_left, *b_got), halves, plan)
-    others = [lax.ppermute(part, "col", rotate_high(d)) for d, part in zip((1, 2, 3), others)]
+    occ, *others = finish_occ(here, (a_left, *a_got, b_left, *b_got), parts, plan)
+    far = lax.ppermute(others[1], "col", rotate_high(2))
+    others = [lax.ppermute(others[0], "col", rotate_high(1)), far, lax.ppermute(others[2], "col", rotate_high(3))]
     partial = pair(here, occ, others, decode_virt(here, virt, plan), plan)
     return sum_all(jnp.sum(partial, axis=-1))
 

time: 221 us -> 221 us (level)
  blocking collectives: 79.3 us -> 69.6 us
  waiting for transfers between devices: 35.5 us -> 43.6 us
    all_to_all x2, blocking collectives: 35.7 us -> 25.9 us  [sum_all(): values = jnp.sum(lax.all_to_all(copies, axes, 0, 0, tiled=True), axis=0)]
    ppermute x3, waiting for transfers between devices: 5.84 us -> 14.5 us  [the longest x1 8.5 us: on_device(): lax.ppermute(others[2], 'col', rotate_high(3))]
    ppermute x1, starting transfers between devices: 4.14 us -> 11.3 us  [on_device(): virt = lax.ppermute(virt, ALL, SWAP)]
    ppermute x3, starting transfers between devices: 10.5 us -> 6.28 us  [the longest x1 3.38 us: on_device(): far = lax.ppermute(others[1], 'col', rotate_high(2))]
    ppermute x6, waiting for transfers between devices: 17 us -> 14.7 us  [layer_swap(): lax.ppermute(send0, 'layer', perms[0])]
  transfers between devices with their start and end apart: 22 -> 22, of which waited for: 8 -> 10; matrix products, arithmetic and copies ran while one was open for 4% -> 4% of each run, Pallas kernels for 16% -> 16%
where the time goes in v10:
time: 221 us; the launch traced here: 220 us
  blocking collectives  69.6 us (31%)
  Pallas kernels  56.5 us (26%)
  waiting for transfers between devices  43.6 us (20%)
  starting transfers between devices  37.3 us (17%)
  local copies, waits for them, and re-layouts  9.18 us (4%)
  other arithmetic  3.67 us (2%)
    all_to_all x1, blocking collectives, on_device(): own = lax.all_to_all(send, ('col', 'layer'), 0, 0, tiled=True)  43.7 us
    all_to_all x2, blocking collectives, sum_all(): values = jnp.sum(lax.all_to_all(copies, axes, 0, 0, tiled=True), axis=0)  25.9 us
    ppermute x6, waiting for transfers between devices, layer_swap(): lax.ppermute(send0, 'layer', perms[0])  14.7 us
    pallas_call x1, Pallas kernels, contract_occ(): pl.pallas_call(functools.partial(occ_body, plans=plans), in_specs=[SMEM]...  13.9 us
    pallas_call x1, Pallas kernels, contract_virt_last(): pl.pallas_call(functools.partial(virt_last_body, plan=plan), in_specs=[SM...  12.7 us
    pallas_call x1, Pallas kernels, contract_virt_first(): pl.pallas_call(virt_first_body, in_specs=[SMEM] + [ANY] * 5, out_specs=AN...  11.7 us
    ppermute x1, starting transfers between devices, on_device(): virt = lax.ppermute(virt, ALL, SWAP)  11.3 us
    ppermute x1, waiting for transfers between devices, on_device(): far_a = lax.ppermute(prev_a, 'row', up)  9.59 us
  transfers between devices with their start and end apart: 22, of which 10 were waited for; matrix products, arithmetic and copies ran while one was open for 4% of the time, Pallas kernels for 16%

profile of v10, /device:TPU:1, one launch (start us, length us, event | category | flops | bytes accessed | tf_op | source)
XLA Modules:
  0.0 220.2 jit_solution(1268477990663917907)
XLA Ops:
  0.0 5.1 %build_send.1 = bf16[64,72,128]{2,1,0:T(8,128)(2,1)} custom-call(s32[88]{0:T(128)} %aux_ref.1, s32[88]{0:T(128)} %row_ref.1, s32[88]{0:T(128)} %col_ref.1, s32[88]{0:T(128)} %ext_ref.1, s32[1]{0:T(128)} %bitcast.2.place_ref, bf16[88,128,128]{2,1,0:T(8,128)(2,1)} %blocks_ref.1), custom_call_target="tpu_custom_call" | custom-call | tf_op jit(solution)/shard_map/build_send/pallas_call | solution.py:120
  5.1 43.7 %all_to_all.15 = bf16[64,72,128]{2,1,0:T(8,128)(2,1)S(1)} all-to-all(bf16[64,72,128]{2,1,0:T(8,128)(2,1)} %build_send.1), channel_id=1, replica_groups=mesh['row'=4,'col'=16,'layer'=4] {'col','layer'}, dimensions={0} | all-to-all | bytes 2359296 | tf_op jit(solution)/shard_map/all_to_all | solution.py:504
  48.8 1.4 collective-permute-start
  50.2 1.5 collective-permute-start.1
  51.7 7.9 %copy.9 = bf16[40,128,512]{1,2,0:T(8,128)(2,1)} copy(bf16[40,128,512]{2,1,0:T(8,128)(2,1)} %bitcast.17) | data formatting | bytes 10485760 | tf_op jit(solution)/shard_map/reshape | solution.py:506
  59.7 0.7 slice_convert_fusion
  60.4 1.7 collective-permute-done.rest_1_
  62.1 1.0 collective-permute-start.2
  63.1 1.8 collective-permute-start.3
  64.9 9.6 %collective-permute-done.2.rest_3_ = bf16[32,64,128]{2,1,0:T(8,128)(2,1)S(1)} collective-permute-done((bf16[32,64,128]{2,1,0:T(8,128)(2,1)S(1)}, bf16[32,64,128]{2,1,0:T(8,128)(2,1)S(1)}, u32[]{:S(2)}, u32[]{:S(2)}) %collective-permute-start.2) | collective-permute-done | bytes 524320 | tf_op jit(solution)/shard_map/ppermute | solution.py:517
  74.6 2.7 %collective-permute-start.5 = (bf16[32,64,128]{2,1,0:T(8,128)(2,1)S(1)}, bf16[32,64,128]{2,1,0:T(8,128)(2,1)}, u32[]{:S(2)}, u32[]{:S(2)}) collective-permute-start(bf16[32,64,128]{2,1,0:T(8,128)(2,1)S(1)} %collective-permute-done.3.rest_2_.rest_6_), channel_id=1, source_target_pairs={{0,192},{64,0},{128,64},{192,128},{1,193},{65,1},{129,65},{193,129... | collective-permute-start | bytes 1572872 | tf_op jit(solution)/shard_map/ppermute | solution.py:521
  77.2 0.6 pad_add_fusion.1.place_ref
  77.9 11.7 %virt_first.1.rest_5_ = f32[24,128,512]{2,1,0:T(8,128)} custom-call(s32[64,4]{1,0:T(8,128)} %bitcast.12, bf16[32,64,128]{2,1,0:T(8,128)(2,1)} %copy-done, bf16[32,64,128]{2,1,0:T(8,128)(2,1)} %copy-done.5, bf16[32,64,128]{2,1,0:T(8,128)(2,1)} %copy-done.7, bf16[32,64,128]{2,1,0:T(8,128)(2,1)} %copy-done.9, bf16[40,128,512]{2,1,0:T(8,128)(2,1)} %bitcast.15), custom_call_target="tpu_custom_call" | custom-call | tf_op jit(solution)/shard_map/virt_first/pallas_call | solution.py:269
  89.7 12.7 %virt_last.1 = (f32[2,2,12,32,512]{4,3,2,1,0:T(8,128)}, s16[800,512]{1,0:T(8,128)(2,1)}, s16[800,512]{1,0:T(8,128)(2,1)}) custom-call(s32[64,4]{1,0:T(8,128)} %bitcast.13, s32[3]{0:T(128)} %pad_add_fusion.1.place_ref, bf16[32,64,128]{2,1,0:T(8,128)(2,1)} %copy-done.2, bf16[32,64,128]{2,1,0:T(8,128)(2,1)} %collective-permute-done.4.rest_1_.rest_5_, ...), custom_call_target="tpu_custom_call" | custom-call | tf_op jit(solution)/shard_map/virt_last/pallas_call | solution.py:282
  102.4 0.4 collective-permute-start.6
  102.8 2.1 collective-permute-start.7
  105.0 13.9 %contract_occ.1 = (f32[2,2,4,32,512]{4,3,2,1,0:T(8,128)S(1)}, s16[272,512]{1,0:T(8,128)(2,1)S(1)}, s16[272,512]{1,0:T(8,128)(2,1)S(1)}, f32[2,2,8,32,512]{4,3,2,...) custom-call(s32[64,4]{1,0:T(8,128)S(1)} %bitcast.14, s32[3]{0:T(128)S(1)} %copy-done.14, ...), custom_call_target="tpu_custom_call" | custom-call | tf_op jit(solution)/shard_map/contract_occ/pallas_call | solution.py:294
  118.9 0.3 collective-permute-start.8
  119.2 1.0 collective-permute-start.9
  120.2 1.5 halve_virt.1
  121.7 4.0 %collective-permute-done.8.got0_ref = s16[272,512]{1,0:T(8,128)(2,1)S(1)} collective-permute-done((s16[272,512]{1,0:T(8,128)(2,1)S(1)}, s16[272,512]{1,0:T(8,128)(2,1)S(1)}, u32[]{:S(2)}, u32[]{:S(2)}) %collective-permute-start.8) | collective-permute-done | bytes 278560 | tf_op jit(solution)/shard_map/ppermute | solution.py:482
  125.8 1.4 collective-permute-done.9.got1_ref
  127.2 2.6 %collective-permute-start.10 = (s16[400,512]{1,0:T(8,128)(2,1)S(1)}, s16[400,512]{1,0:T(8,128)(2,1)S(1)}, u32[]{:S(2)}, u32[]{:S(2)}) collective-permute-start(s16[400,512]{1,0:T(8,128)(2,1)S(1)} %get-tuple-element.87), channel_id=1, source_target_pairs={{0,3},{3,0},{1,2},{2,1},{4,7},{7,4},{5,6},{6,5},{8,11},{11,8},{9,1... | collective-permute-start | bytes 1228808 | tf_op jit(solution)/shard_map/ppermute | solution.py:482
  129.8 1.6 halve_occ_a.1
  131.3 4.2 %collective-permute-done.10.got0_ref = s16[400,512]{1,0:T(8,128)(2,1)S(1)} collective-permute-done((s16[400,512]{1,0:T(8,128)(2,1)S(1)}, s16[400,512]{1,0:T(8,128)(2,1)S(1)}, u32[]{:S(2)}, u32[]{:S(2)}) %collective-permute-start.10) | collective-permute-done | bytes 409632 | tf_op jit(solution)/shard_map/ppermute | solution.py:482
  135.6 1.7 collective-permute-done.11.got1_ref
  137.3 1.5 collective-permute-start.15
  138.8 0.8 finish_virt.1
  139.7 11.3 %collective-permute-start.21 = (s16[800,512]{1,0:T(8,128)(2,1)S(1)}, s16[800,512]{1,0:T(8,128)(2,1)S(1)}, u32[]{:S(2)}, u32[]{:S(2)}) collective-permute-start(s16[800,512]{1,0:T(8,128)(2,1)S(1)} %finish_virt.1), channel_id=1, source_target_pairs={{0,0},{1,1},{2,2},{3,3},{4,64},{5,65},{6,66},{7,67},{8,128},{9,129... | collective-permute-start | bytes 2457608 | tf_op jit(solution)/shard_map/ppermute | solution.py:543
  151.0 2.0 halve_occ_b.1
  152.9 2.7 %collective-permute-start.12 = (s16[144,512]{1,0:T(8,128)(2,1)}, s16[144,512]{1,0:T(8,128)(2,1)}, u32[]{:S(2)}, u32[]{:S(2)}) collective-permute-start(s16[144,512]{1,0:T(8,128)(2,1)} %get-tuple-element.96), channel_id=1, source_target_pairs={{0,3},{3,0},{1,2},{2,1},{4,7},{7,4},{5,6},{6,5},{8,11},{11,8},{9,1... | collective-permute-start | bytes 442376 | tf_op jit(solution)/shard_map/ppermute | solution.py:482
  155.6 0.9 collective-permute-start.13
  156.5 6.4 %collective-permute-done.12.rest_1_ = s16[144,512]{1,0:T(8,128)(2,1)} collective-permute-done((s16[144,512]{1,0:T(8,128)(2,1)}, s16[144,512]{1,0:T(8,128)(2,1)}, u32[]{:S(2)}, u32[]{:S(2)}) %collective-permute-start.12) | collective-permute-done | bytes 147488 | tf_op jit(solution)/shard_map/ppermute | solution.py:482
  162.9 2.1 finish_occ.1
  165.0 1.6 collective-permute-start.18
  166.6 3.4 %collective-permute-start.19 = (s16[800,128]{1,0:T(8,128)(2,1)S(1)}, s16[800,128]{1,0:T(8,128)(2,1)S(1)}, u32[]{:S(2)}, u32[]{:S(2)}) collective-permute-start(s16[800,128]{1,0:T(8,128)(2,1)S(1)} %get-tuple-element.110), channel_id=1, source_target_pairs={{0,32},{4,36},{8,40},{12,44},{16,48},{20,52},{24,56},{28,60},{32,0... | collective-permute-start | bytes 614408 | tf_op jit(solution)/shard_map/ppermute | solution.py:548
  169.9 1.3 collective-permute-start.20
  171.3 0.8 decode_virt.1.vir_ref
  172.1 1.2 collective-permute-done.18.one_ref
  173.3 4.8 %collective-permute-done.19.two_ref = s16[800,128]{1,0:T(8,128)(2,1)S(1)} collective-permute-done((s16[800,128]{1,0:T(8,128)(2,1)S(1)}, s16[800,128]{1,0:T(8,128)(2,1)S(1)}, u32[]{:S(2)}, u32[]{:S(2)}) %collective-permute-start.19) | collective-permute-done | bytes 204832 | tf_op jit(solution)/shard_map/ppermute | solution.py:548
  178.1 8.5 %collective-permute-done.20.three_ref = s16[800,128]{1,0:T(8,128)(2,1)S(1)} collective-permute-done((s16[800,128]{1,0:T(8,128)(2,1)S(1)}, s16[800,128]{1,0:T(8,128)(2,1)S(1)}, u32[]{:S(2)}, u32[]{:S(2)}) %collective-permute-start.20) | collective-permute-done | bytes 204832 | tf_op jit(solution)/shard_map/ppermute | solution.py:549
  186.6 4.3 %pair.1 = f32[24,24,128]{2,1,0:T(8,128)S(1)} custom-call(s32[2]{0:T(128)S(1)} %pad_add_fusion.place_ref, s16[800,128]{1,0:T(8,128)(2,1)S(1)} %get-tuple-element.108.own_ref, s16[800,128]{1,0:T(8,128)(2,1)S(1)} %collective-permute-done.18.one_ref, s16[800,128]{1,0:T(8,128)(2,1)S(1)} %collective-permute-done.19.two_ref, ...), custom_call_target="tpu_custom_call" | custom-call | tf_op jit(solution)/shard_map/pair/pallas_call | solution.py:439
  191.2 15.8 %all_to_all.16 = f32[16,1,576]{2,1,0:T(1,128)S(1)} all-to-all(f32[16,1,576]{2,1,0:T(1,128)S(1)} %reshape.14), channel_id=1, replica_groups=mesh['row'=4,'col'=16,'layer'=4] {'col'}, dimensions={0} | all-to-all | bytes 73728 | tf_op jit(solution)/shard_map/all_to_all | solution.py:477
  207.0 0.5 broadcast.5
  207.5 0.7 reduce
  208.6 10.1 %all_to_all.17 = f32[16,1,576]{2,1,0:T(1,128)S(1)} all-to-all(f32[16,1,576]{2,1,0:T(1,128)S(1)} %reshape.16), channel_id=1, replica_groups=mesh['row'=4,'col'=16,'layer'=4] {'row','layer'}, dimensions={0} | all-to-all | bytes 73728 | tf_op jit(solution)/shard_map/all_to_all | solution.py:477
  218.7 0.7 reduce.1
  219.6 0.6 reduce_sum.29
  (63 shorter events, 1.1 us)
Async XLA Ops:
  48.8 10.8 %copy-start = (bf16[32,64,128]{2,1,0:T(8,128)(2,1)}, bf16[32,64,128]{2,1,0:T(8,128)(2,1)S(1)}, u32[]{:S(2)}) copy-start(bf16[32,64,128]{2,1,0:T(8,128)(2,1)S(1)} %slice.12.rest_0_) | copy-start | bytes 1572868
  48.8 13.3 %collective-permute-start = (bf16[32,64,128]{2,1,0:T(8,128)(2,1)S(1)}, bf16[32,64,128]{2,1,0:T(8,128)(2,1)S(1)}, u32[]{:S(2)}, u32[]{:S(2)}) collective-permute-start(bf16[32,64,128]{2,1,0:T(8,128)(2,1)S(1)} %slice.12.rest_0_), channel_id=1, source_target_pairs={{0,64},{64,128},{128,192},{192,0},{1,65},{65,129},{129,193},{193,1... | collective-permute-start | bytes 1572872 | tf_op jit(solution)/shard_map/ppermute | solution.py:514
  50.2 12.0 %collective-permute-start.1 = (bf16[32,64,128]{2,1,0:T(8,128)(2,1)S(1)}, bf16[32,64,128]{2,1,0:T(8,128)(2,1)S(1)}, u32[]{:S(2)}, u32[]{:S(2)}) collective-permute-start(bf16[32,64,128]{2,1,0:T(8,128)(2,1)S(1)} %slice.12.rest_0_), channel_id=1, source_target_pairs={{0,192},{64,0},{128,64},{192,128},{1,193},{65,1},{129,65},{193,129... | collective-permute-start | bytes 1572872 | tf_op jit(solution)/shard_map/ppermute | solution.py:515
  59.7 29.9 %copy-start.2 = (bf16[32,64,128]{2,1,0:T(8,128)(2,1)}, bf16[32,64,128]{2,1,0:T(8,128)(2,1)S(1)}, u32[]{:S(2)}) copy-start(bf16[32,64,128]{2,1,0:T(8,128)(2,1)S(1)} %slice.10.rest_0_.rest_4_) | copy-start | bytes 1572868
  62.1 15.7 %copy-start.5 = (bf16[32,64,128]{2,1,0:T(8,128)(2,1)}, bf16[32,64,128]{2,1,0:T(8,128)(2,1)S(1)}, u32[]{:S(2)}) copy-start(bf16[32,64,128]{2,1,0:T(8,128)(2,1)S(1)} %collective-permute-done.rest_1_) | copy-start | bytes 1572868
  62.1 15.7 %copy-start.7 = (bf16[32,64,128]{2,1,0:T(8,128)(2,1)}, bf16[32,64,128]{2,1,0:T(8,128)(2,1)S(1)}, u32[]{:S(2)}) copy-start(bf16[32,64,128]{2,1,0:T(8,128)(2,1)S(1)} %collective-permute-done.1.rest_2_) | copy-start | bytes 1572868
  62.1 12.3 %collective-permute-start.2 = (bf16[32,64,128]{2,1,0:T(8,128)(2,1)S(1)}, bf16[32,64,128]{2,1,0:T(8,128)(2,1)S(1)}, u32[]{:S(2)}, u32[]{:S(2)}) collective-permute-start(bf16[32,64,128]{2,1,0:T(8,128)(2,1)S(1)} %collective-permute-done.rest_1_), channel_id=1, source_target_pairs={{0,64},{64,128},{128,192},{192,0},{1,65},{65,129},{129,193},{193,1... | collective-permute-start | bytes 1572872 | tf_op jit(solution)/shard_map/ppermute | solution.py:517
  63.1 11.4 %collective-permute-start.3 = (bf16[32,64,128]{2,1,0:T(8,128)(2,1)S(1)}, bf16[32,64,128]{2,1,0:T(8,128)(2,1)S(1)}, u32[]{:S(2)}, u32[]{:S(2)}) collective-permute-start(bf16[32,64,128]{2,1,0:T(8,128)(2,1)S(1)} %slice.10.rest_0_.rest_4_), channel_id=1, source_target_pairs={{0,192},{64,0},{128,64},{192,128},{1,193},{65,1},{129,65},{193,129... | collective-permute-start | bytes 1572872 | tf_op jit(solution)/shard_map/ppermute | solution.py:518
  74.5 3.4 %copy-start.9 = (bf16[32,64,128]{2,1,0:T(8,128)(2,1)}, bf16[32,64,128]{2,1,0:T(8,128)(2,1)S(1)}, u32[]{:S(2)}) copy-start(bf16[32,64,128]{2,1,0:T(8,128)(2,1)S(1)} %collective-permute-done.2.rest_3_) | copy-start | bytes 1572868
  74.5 15.1 %copy-start.11 = (bf16[32,64,128]{2,1,0:T(8,128)(2,1)}, bf16[32,64,128]{2,1,0:T(8,128)(2,1)S(1)}, u32[]{:S(2)}) copy-start(bf16[32,64,128]{2,1,0:T(8,128)(2,1)S(1)} %collective-permute-done.3.rest_2_.rest_6_) | copy-start | bytes 1572868
  74.5 15.2 %collective-permute-start.4 = (bf16[32,64,128]{2,1,0:T(8,128)(2,1)S(1)}, bf16[32,64,128]{2,1,0:T(8,128)(2,1)}, u32[]{:S(2)}, u32[]{:S(2)}) collective-permute-start(bf16[32,64,128]{2,1,0:T(8,128)(2,1)S(1)} %slice.10.rest_0_.rest_4_), channel_id=1, source_target_pairs={{0,64},{64,128},{128,192},{192,0},{1,65},{65,129},{129,193},{193,1... | collective-permute-start | bytes 1572872 | tf_op jit(solution)/shard_map/ppermute | solution.py:520
  74.6 15.1 %collective-permute-start.5 = (bf16[32,64,128]{2,1,0:T(8,128)(2,1)S(1)}, bf16[32,64,128]{2,1,0:T(8,128)(2,1)}, u32[]{:S(2)}, u32[]{:S(2)}) collective-permute-start(bf16[32,64,128]{2,1,0:T(8,128)(2,1)S(1)} %collective-permute-done.3.rest_2_.rest_6_), channel_id=1, source_target_pairs={{0,192},{64,0},{128,64},{192,128},{1,193},{65,1},{129,65},{193,129... | collective-permute-start | bytes 1572872 | tf_op jit(solution)/shard_map/ppermute | solution.py:521
  77.9 27.0 %slice-start = ((s8[5242880]{0:T(1024)(128)(4,1)}), s8[4194304]{0:T(1024)(128)(4,1)S(1)}, s32[]{:S(2)}) async-start(s8[5242880]{0:T(1024)(128)(4,1)} %bitcast.9), calls=%async_computation.3 | async-start | bytes 8388608
  89.6 15.2 %slice-start.1 = ((s8[5242880]{0:T(1024)(128)(4,1)}), s8[1048576]{0:T(1024)(128)(4,1)S(1)}, s32[]{:S(2)}) async-start(s8[5242880]{0:T(1024)(128)(4,1)} %bitcast.9), calls=%async_computation.4 | async-start | bytes 2097152
  89.6 15.2 %copy-start.1 = (bf16[32,64,128]{2,1,0:T(8,128)(2,1)S(1)}, bf16[32,64,128]{2,1,0:T(8,128)(2,1)}, u32[]{:S(2)}) copy-start(bf16[32,64,128]{2,1,0:T(8,128)(2,1)} %copy-done) | copy-start | bytes 1572868
  89.6 15.2 %copy-start.6 = (bf16[32,64,128]{2,1,0:T(8,128)(2,1)S(1)}, bf16[32,64,128]{2,1,0:T(8,128)(2,1)}, u32[]{:S(2)}) copy-start(bf16[32,64,128]{2,1,0:T(8,128)(2,1)} %copy-done.5) | copy-start | bytes 1572868
  89.7 15.2 %copy-start.8 = (bf16[32,64,128]{2,1,0:T(8,128)(2,1)S(1)}, bf16[32,64,128]{2,1,0:T(8,128)(2,1)}, u32[]{:S(2)}) copy-start(bf16[32,64,128]{2,1,0:T(8,128)(2,1)} %copy-done.7) | copy-start | bytes 1572868
  89.7 15.2 %copy-start.10 = (bf16[32,64,128]{2,1,0:T(8,128)(2,1)S(1)}, bf16[32,64,128]{2,1,0:T(8,128)(2,1)}, u32[]{:S(2)}) copy-start(bf16[32,64,128]{2,1,0:T(8,128)(2,1)} %copy-done.9) | copy-start | bytes 1572868
  89.7 15.2 %copy-start.13 = (s32[64,1,4]{2,1,0:T(1,128)S(1)}, s32[64,1,4]{2,1,0:T(1,128)}, u32[]{:S(2)}) copy-start(s32[64,1,4]{2,1,0:T(1,128)} %slice_convert_fusion) | copy-start | bytes 3076
  89.7 15.2 %copy-start.14 = (s32[3]{0:T(128)S(1)}, s32[3]{0:T(128)}, u32[]{:S(2)}) copy-start(s32[3]{0:T(128)} %pad_add_fusion.1.place_ref) | copy-start | bytes 40
  89.7 15.2 %copy-start.3 = (bf16[32,64,128]{2,1,0:T(8,128)(2,1)S(1)}, bf16[32,64,128]{2,1,0:T(8,128)(2,1)}, u32[]{:S(2)}) copy-start(bf16[32,64,128]{2,1,0:T(8,128)(2,1)} %copy-done.2) | copy-start | bytes 1572868
  89.7 15.2 %copy-start.12 = (bf16[32,64,128]{2,1,0:T(8,128)(2,1)S(1)}, bf16[32,64,128]{2,1,0:T(8,128)(2,1)}, u32[]{:S(2)}) copy-start(bf16[32,64,128]{2,1,0:T(8,128)(2,1)} %copy-done.11) | copy-start | bytes 1572868
  102.4 17.8 %collective-permute-start.6 = (s16[800,512]{1,0:T(8,128)(2,1)}, s16[800,512]{1,0:T(8,128)(2,1)S(1)}, u32[]{:S(2)}, u32[]{:S(2)}) collective-permute-start(s16[800,512]{1,0:T(8,128)(2,1)} %get-tuple-element.76), channel_id=1, source_target_pairs={{0,1},{1,0},{2,3},{3,2},{4,5},{5,4},{6,7},{7,6},{8,9},{9,8},{10,11... | collective-permute-start | bytes 2457608 | tf_op jit(solution)/shard_map/ppermute | solution.py:482
  102.8 17.4 %collective-permute-start.7 = (s16[800,512]{1,0:T(8,128)(2,1)}, s16[800,512]{1,0:T(8,128)(2,1)S(1)}, u32[]{:S(2)}, u32[]{:S(2)}) collective-permute-start(s16[800,512]{1,0:T(8,128)(2,1)} %get-tuple-element.77), channel_id=1, source_target_pairs={{0,3},{3,0},{1,2},{2,1},{4,7},{7,4},{5,6},{6,5},{8,11},{11,8},{9,1... | collective-permute-start | bytes 2457608 | tf_op jit(solution)/shard_map/ppermute | solution.py:482
  105.0 15.2 %copy-start.4 = (f32[2,2,12,32,512]{4,3,2,1,0:T(8,128)S(1)}, f32[2,2,12,32,512]{4,3,2,1,0:T(8,128)}, u32[]{:S(2)}) copy-start(f32[2,2,12,32,512]{4,3,2,1,0:T(8,128)} %get-tuple-element.75.keep_ref) | copy-start | bytes 9437188
  118.9 6.9 %collective-permute-start.8 = (s16[272,512]{1,0:T(8,128)(2,1)S(1)}, s16[272,512]{1,0:T(8,128)(2,1)S(1)}, u32[]{:S(2)}, u32[]{:S(2)}) collective-permute-start(s16[272,512]{1,0:T(8,128)(2,1)S(1)} %get-tuple-element.82), channel_id=1, source_target_pairs={{0,1},{1,0},{2,3},{3,2},{4,5},{5,4},{6,7},{7,6},{8,9},{9,8},{10,11... | collective-permute-start | bytes 835592 | tf_op jit(solution)/shard_map/ppermute | solution.py:482
  119.2 8.0 %collective-permute-start.9 = (s16[272,512]{1,0:T(8,128)(2,1)S(1)}, s16[272,512]{1,0:T(8,128)(2,1)S(1)}, u32[]{:S(2)}, u32[]{:S(2)}) collective-permute-start(s16[272,512]{1,0:T(8,128)(2,1)S(1)} %get-tuple-element.83), channel_id=1, source_target_pairs={{0,3},{3,0},{1,2},{2,1},{4,7},{7,4},{5,6},{6,5},{8,11},{11,8},{9,1... | collective-permute-start | bytes 835592 | tf_op jit(solution)/shard_map/ppermute | solution.py:482
  127.2 8.4 %collective-permute-start.10 = (s16[400,512]{1,0:T(8,128)(2,1)S(1)}, s16[400,512]{1,0:T(8,128)(2,1)S(1)}, u32[]{:S(2)}, u32[]{:S(2)}) collective-permute-start(s16[400,512]{1,0:T(8,128)(2,1)S(1)} %get-tuple-element.87), channel_id=1, source_target_pairs={{0,3},{3,0},{1,2},{2,1},{4,7},{7,4},{5,6},{6,5},{8,11},{11,8},{9,1... | collective-permute-start | bytes 1228808 | tf_op jit(solution)/shard_map/ppermute | solution.py:482
  129.8 7.5 %collective-permute-start.11 = (s16[400,512]{1,0:T(8,128)(2,1)S(1)}, s16[400,512]{1,0:T(8,128)(2,1)S(1)}, u32[]{:S(2)}, u32[]{:S(2)}) collective-permute-start(s16[400,512]{1,0:T(8,128)(2,1)S(1)} %get-tuple-element.88), channel_id=1, source_target_pairs={{0,1},{1,0},{2,3},{3,2},{4,5},{5,4},{6,7},{7,6},{8,9},{9,8},{10,11... | collective-permute-start | bytes 1228808 | tf_op jit(solution)/shard_map/ppermute | solution.py:482
  137.3 13.6 %collective-permute-start.14 = (s16[528,512]{1,0:T(8,128)(2,1)S(1)}, s16[528,512]{1,0:T(8,128)(2,1)S(1)}, u32[]{:S(2)}, u32[]{:S(2)}) collective-permute-start(s16[528,512]{1,0:T(8,128)(2,1)S(1)} %get-tuple-element.103), channel_id=1, source_target_pairs={{0,1},{1,0},{2,3},{3,2},{4,5},{5,4},{6,7},{7,6},{8,9},{9,8},{10,11... | collective-permute-start | bytes 1622024 | tf_op jit(solution)/shard_map/ppermute | solution.py:482
  137.3 13.6 %collective-permute-start.15 = (s16[528,512]{1,0:T(8,128)(2,1)S(1)}, s16[528,512]{1,0:T(8,128)(2,1)S(1)}, u32[]{:S(2)}, u32[]{:S(2)}) collective-permute-start(s16[528,512]{1,0:T(8,128)(2,1)S(1)} %get-tuple-element.104), channel_id=1, source_target_pairs={{0,3},{3,0},{1,2},{2,1},{4,7},{7,4},{5,6},{6,5},{8,11},{11,8},{9,1... | collective-permute-start | bytes 1622024 | tf_op jit(solution)/shard_map/ppermute | solution.py:482
  139.7 31.6 %collective-permute-start.21 = (s16[800,512]{1,0:T(8,128)(2,1)S(1)}, s16[800,512]{1,0:T(8,128)(2,1)S(1)}, u32[]{:S(2)}, u32[]{:S(2)}) collective-permute-start(s16[800,512]{1,0:T(8,128)(2,1)S(1)} %finish_virt.1), channel_id=1, source_target_pairs={{0,0},{1,1},{2,2},{3,3},{4,64},{5,65},{6,66},{7,67},{8,128},{9,129... | collective-permute-start | bytes 2457608 | tf_op jit(solution)/shard_map/ppermute | solution.py:543
  152.9 10.0 %collective-permute-start.16 = (s16[272,512]{1,0:T(8,128)(2,1)}, s16[272,512]{1,0:T(8,128)(2,1)S(1)}, u32[]{:S(2)}, u32[]{:S(2)}) collective-permute-start(s16[272,512]{1,0:T(8,128)(2,1)} %get-tuple-element.106), channel_id=1, source_target_pairs={{0,3},{3,0},{1,2},{2,1},{4,7},{7,4},{5,6},{6,5},{8,11},{11,8},{9,1... | collective-permute-start | bytes 835592 | tf_op jit(solution)/shard_map/ppermute | solution.py:482
  152.9 10.0 %collective-permute-start.17 = (s16[272,512]{1,0:T(8,128)(2,1)}, s16[272,512]{1,0:T(8,128)(2,1)}, u32[]{:S(2)}, u32[]{:S(2)}) collective-permute-start(s16[272,512]{1,0:T(8,128)(2,1)} %get-tuple-element.107), channel_id=1, source_target_pairs={{0,1},{1,0},{2,3},{3,2},{4,5},{5,4},{6,7},{7,6},{8,9},{9,8},{10,11... | collective-permute-start | bytes 835592 | tf_op jit(solution)/shard_map/ppermute | solution.py:482
  152.9 10.0 %collective-permute-start.12 = (s16[144,512]{1,0:T(8,128)(2,1)}, s16[144,512]{1,0:T(8,128)(2,1)}, u32[]{:S(2)}, u32[]{:S(2)}) collective-permute-start(s16[144,512]{1,0:T(8,128)(2,1)} %get-tuple-element.96), channel_id=1, source_target_pairs={{0,3},{3,0},{1,2},{2,1},{4,7},{7,4},{5,6},{6,5},{8,11},{11,8},{9,1... | collective-permute-start | bytes 442376 | tf_op jit(solution)/shard_map/ppermute | solution.py:482
  155.6 7.3 %collective-permute-start.13 = (s16[144,512]{1,0:T(8,128)(2,1)}, s16[144,512]{1,0:T(8,128)(2,1)}, u32[]{:S(2)}, u32[]{:S(2)}) collective-permute-start(s16[144,512]{1,0:T(8,128)(2,1)} %get-tuple-element.97), channel_id=1, source_target_pairs={{0,1},{1,0},{2,3},{3,2},{4,5},{5,4},{6,7},{7,6},{8,9},{9,8},{10,11... | collective-permute-start | bytes 442376 | tf_op jit(solution)/shard_map/ppermute | solution.py:482
  165.0 8.3 %collective-permute-start.18 = (s16[800,128]{1,0:T(8,128)(2,1)S(1)}, s16[800,128]{1,0:T(8,128)(2,1)S(1)}, u32[]{:S(2)}, u32[]{:S(2)}) collective-permute-start(s16[800,128]{1,0:T(8,128)(2,1)S(1)} %get-tuple-element.109), channel_id=1, source_target_pairs={{0,16},{4,20},{8,24},{12,28},{16,32},{20,36},{24,40},{28,44},{32,4... | collective-permute-start | bytes 614408 | tf_op jit(solution)/shard_map/ppermute | solution.py:549
  166.6 11.5 %collective-permute-start.19 = (s16[800,128]{1,0:T(8,128)(2,1)S(1)}, s16[800,128]{1,0:T(8,128)(2,1)S(1)}, u32[]{:S(2)}, u32[]{:S(2)}) collective-permute-start(s16[800,128]{1,0:T(8,128)(2,1)S(1)} %get-tuple-element.110), channel_id=1, source_target_pairs={{0,32},{4,36},{8,40},{12,44},{16,48},{20,52},{24,56},{28,60},{32,0... | collective-permute-start | bytes 614408 | tf_op jit(solution)/shard_map/ppermute | solution.py:548
  169.9 16.6 %collective-permute-start.20 = (s16[800,128]{1,0:T(8,128)(2,1)S(1)}, s16[800,128]{1,0:T(8,128)(2,1)S(1)}, u32[]{:S(2)}, u32[]{:S(2)}) collective-permute-start(s16[800,128]{1,0:T(8,128)(2,1)S(1)} %get-tuple-element.111), channel_id=1, source_target_pairs={{0,48},{4,52},{8,56},{12,60},{16,0},{20,4},{24,8},{28,12},{32,16},... | collective-permute-start | bytes 614408 | tf_op jit(solution)/shard_map/ppermute | solution.py:549

commit v11 on v10

--- a/solution.py
+++ b/solution.py
@@ -100,7 +100,7 @@
     meta_lane = lax.broadcasted_iota(jnp.int32, (8, BS), 1)
     load.wait()
 
-    @pl.loop(0, tiles_ref.shape[0])
+    @pl.loop(0, tiles_ref.shape[0], unroll=2)
     def _(i):
         col = col_ref[i]
         layer_of = col // layer_blocks
@@ -163,9 +163,9 @@
 
 
 def add_virt(meta_ref, first, quarter_refs, green_ref, acc_ref):
-    @pl.loop(0, OWNERS // 4)
+    @pl.loop(0, OWNERS // 8)
     def _(step):
-        for local in (step * 2, step * 2 + 1):
+        for local in [step * 4 + k for k in range(4)]:
             for slot in range(CAP):
                 span = slice(slot * QUARTER, (slot + 1) * QUARTER)
                 tile = jnp.concatenate([ref[local, span, :] for ref in quarter_refs], axis=0)

time: 221 us -> 219 us (level)
  Pallas kernels: 56.5 us -> 53.5 us
  waiting for transfers between devices: 43.6 us -> 46.3 us
    ppermute x1, waiting for transfers between devices: 4.78 us -> 9.8 us  [on_device(): far = lax.ppermute(others[1], 'col', rotate_high(2))]
    ppermute x1, waiting for transfers between devices: 8.5 us -> 6.01 us  [on_device(): lax.ppermute(others[2], 'col', rotate_high(3))]
  transfers between devices with their start and end apart: 22 -> 22, of which waited for: 10 -> 10; matrix products, arithmetic and copies ran while one was open for 4% -> 4% of each run, Pallas kernels for 16% -> 15%
where the time goes in v11:
time: 219 us; the launch traced here: 218 us
  blocking collectives  67.9 us (31%)
  Pallas kernels  53.5 us (24%)
  waiting for transfers between devices  46.3 us (21%)
  starting transfers between devices  37.4 us (17%)
  local copies, waits for them, and re-layouts  9.18 us (4%)
  other arithmetic  3.67 us (2%)
    all_to_all x1, blocking collectives, on_device(): own = lax.all_to_all(send, ('col', 'layer'), 0, 0, tiled=True)  43.7 us
    all_to_all x2, blocking collectives, sum_all(): values = jnp.sum(lax.all_to_all(copies, axes, 0, 0, tiled=True), axis=0)  24.3 us
    ppermute x6, waiting for transfers between devices, layer_swap(): lax.ppermute(send0, 'layer', perms[0])  14.7 us
    pallas_call x1, Pallas kernels, contract_occ(): pl.pallas_call(functools.partial(occ_body, plans=plans), in_specs=[SMEM]...  13.9 us
    pallas_call x1, Pallas kernels, contract_virt_last(): pl.pallas_call(functools.partial(virt_last_body, plan=plan), in_specs=[SM...  11.4 us
    ppermute x1, starting transfers between devices, on_device(): virt = lax.ppermute(virt, ALL, SWAP)  11.3 us
    pallas_call x1, Pallas kernels, contract_virt_first(): pl.pallas_call(virt_first_body, in_specs=[SMEM] + [ANY] * 5, out_specs=AN...  10.5 us
    ppermute x1, waiting for transfers between devices, on_device(): far = lax.ppermute(others[1], 'col', rotate_high(2))  9.8 us
  transfers between devices with their start and end apart: 22, of which 10 were waited for; matrix products, arithmetic and copies ran while one was open for 4% of the time, Pallas kernels for 15%

profile of v11, /device:TPU:1, one launch (start us, length us, event | category | flops | bytes accessed | tf_op | source)
XLA Modules:
  0.0 218.4 jit_solution(7325409436472221081)
XLA Ops:
  0.0 4.6 %build_send.1 = bf16[64,72,128]{2,1,0:T(8,128)(2,1)} custom-call(s32[88]{0:T(128)} %aux_ref.1, s32[88]{0:T(128)} %row_ref.1, s32[88]{0:T(128)} %col_ref.1, s32[88]{0:T(128)} %ext_ref.1, s32[1]{0:T(128)} %bitcast.2.place_ref, bf16[88,128,128]{2,1,0:T(8,128)(2,1)} %blocks_ref.1), custom_call_target="tpu_custom_call" | custom-call | tf_op jit(solution)/shard_map/build_send/pallas_call | solution.py:120
  4.6 43.7 %all_to_all.15 = bf16[64,72,128]{2,1,0:T(8,128)(2,1)S(1)} all-to-all(bf16[64,72,128]{2,1,0:T(8,128)(2,1)} %build_send.1), channel_id=1, replica_groups=mesh['row'=4,'col'=16,'layer'=4] {'col','layer'}, dimensions={0} | all-to-all | bytes 2359296 | tf_op jit(solution)/shard_map/all_to_all | solution.py:504
  48.4 1.4 collective-permute-start
  49.7 1.5 collective-permute-start.1
  51.3 7.9 %copy.9 = bf16[40,128,512]{1,2,0:T(8,128)(2,1)} copy(bf16[40,128,512]{2,1,0:T(8,128)(2,1)} %bitcast.17) | data formatting | bytes 10485760 | tf_op jit(solution)/shard_map/reshape | solution.py:506
  59.3 0.7 slice_convert_fusion
  60.0 1.7 collective-permute-done.rest_1_
  61.7 1.0 collective-permute-start.2
  62.7 1.8 collective-permute-start.3
  64.5 9.6 %collective-permute-done.2.rest_3_ = bf16[32,64,128]{2,1,0:T(8,128)(2,1)S(1)} collective-permute-done((bf16[32,64,128]{2,1,0:T(8,128)(2,1)S(1)}, bf16[32,64,128]{2,1,0:T(8,128)(2,1)S(1)}, u32[]{:S(2)}, u32[]{:S(2)}) %collective-permute-start.2) | collective-permute-done | bytes 524320 | tf_op jit(solution)/shard_map/ppermute | solution.py:517
  74.1 2.7 %collective-permute-start.5 = (bf16[32,64,128]{2,1,0:T(8,128)(2,1)S(1)}, bf16[32,64,128]{2,1,0:T(8,128)(2,1)}, u32[]{:S(2)}, u32[]{:S(2)}) collective-permute-start(bf16[32,64,128]{2,1,0:T(8,128)(2,1)S(1)} %collective-permute-done.3.rest_2_.rest_6_), channel_id=1, source_target_pairs={{0,192},{64,0},{128,64},{192,128},{1,193},{65,1},{129,65},{193,129... | collective-permute-start | bytes 1572872 | tf_op jit(solution)/shard_map/ppermute | solution.py:521
  76.8 0.6 pad_add_fusion.1.place_ref
  77.4 10.5 %virt_first.1.rest_5_ = f32[24,128,512]{2,1,0:T(8,128)} custom-call(s32[64,4]{1,0:T(8,128)} %bitcast.12, bf16[32,64,128]{2,1,0:T(8,128)(2,1)} %copy-done, bf16[32,64,128]{2,1,0:T(8,128)(2,1)} %copy-done.5, bf16[32,64,128]{2,1,0:T(8,128)(2,1)} %copy-done.7, bf16[32,64,128]{2,1,0:T(8,128)(2,1)} %copy-done.9, bf16[40,128,512]{2,1,0:T(8,128)(2,1)} %bitcast.15), custom_call_target="tpu_custom_call" | custom-call | tf_op jit(solution)/shard_map/virt_first/pallas_call | solution.py:269
  88.1 11.4 %virt_last.1 = (f32[2,2,12,32,512]{4,3,2,1,0:T(8,128)}, s16[800,512]{1,0:T(8,128)(2,1)}, s16[800,512]{1,0:T(8,128)(2,1)}) custom-call(s32[64,4]{1,0:T(8,128)} %bitcast.13, s32[3]{0:T(128)} %pad_add_fusion.1.place_ref, bf16[32,64,128]{2,1,0:T(8,128)(2,1)} %copy-done.2, bf16[32,64,128]{2,1,0:T(8,128)(2,1)} %collective-permute-done.4.rest_1_.rest_5_, ...), custom_call_target="tpu_custom_call" | custom-call | tf_op jit(solution)/shard_map/virt_last/pallas_call | solution.py:282
  99.5 0.4 collective-permute-start.6
  99.9 2.1 collective-permute-start.7
  102.1 13.9 %contract_occ.1 = (f32[2,2,4,32,512]{4,3,2,1,0:T(8,128)S(1)}, s16[272,512]{1,0:T(8,128)(2,1)S(1)}, s16[272,512]{1,0:T(8,128)(2,1)S(1)}, f32[2,2,8,32,512]{4,3,2,...) custom-call(s32[64,4]{1,0:T(8,128)S(1)} %bitcast.14, s32[3]{0:T(128)S(1)} %copy-done.14, ...), custom_call_target="tpu_custom_call" | custom-call | tf_op jit(solution)/shard_map/contract_occ/pallas_call | solution.py:294
  116.0 0.3 collective-permute-start.8
  116.3 1.0 collective-permute-start.9
  117.3 1.5 halve_virt.1
  118.8 4.0 %collective-permute-done.8.got0_ref = s16[272,512]{1,0:T(8,128)(2,1)S(1)} collective-permute-done((s16[272,512]{1,0:T(8,128)(2,1)S(1)}, s16[272,512]{1,0:T(8,128)(2,1)S(1)}, u32[]{:S(2)}, u32[]{:S(2)}) %collective-permute-start.8) | collective-permute-done | bytes 278560 | tf_op jit(solution)/shard_map/ppermute | solution.py:482
  122.8 1.5 collective-permute-done.9.got1_ref
  124.3 2.6 %collective-permute-start.10 = (s16[400,512]{1,0:T(8,128)(2,1)S(1)}, s16[400,512]{1,0:T(8,128)(2,1)S(1)}, u32[]{:S(2)}, u32[]{:S(2)}) collective-permute-start(s16[400,512]{1,0:T(8,128)(2,1)S(1)} %get-tuple-element.87), channel_id=1, source_target_pairs={{0,3},{3,0},{1,2},{2,1},{4,7},{7,4},{5,6},{6,5},{8,11},{11,8},{9,1... | collective-permute-start | bytes 1228808 | tf_op jit(solution)/shard_map/ppermute | solution.py:482
  126.9 1.6 halve_occ_a.1
  128.4 4.2 %collective-permute-done.10.got0_ref = s16[400,512]{1,0:T(8,128)(2,1)S(1)} collective-permute-done((s16[400,512]{1,0:T(8,128)(2,1)S(1)}, s16[400,512]{1,0:T(8,128)(2,1)S(1)}, u32[]{:S(2)}, u32[]{:S(2)}) %collective-permute-start.10) | collective-permute-done | bytes 409632 | tf_op jit(solution)/shard_map/ppermute | solution.py:482
  132.7 1.8 collective-permute-done.11.got1_ref
  134.4 1.5 collective-permute-start.15
  135.9 0.8 finish_virt.1
  136.8 11.3 %collective-permute-start.21 = (s16[800,512]{1,0:T(8,128)(2,1)S(1)}, s16[800,512]{1,0:T(8,128)(2,1)S(1)}, u32[]{:S(2)}, u32[]{:S(2)}) collective-permute-start(s16[800,512]{1,0:T(8,128)(2,1)S(1)} %finish_virt.1), channel_id=1, source_target_pairs={{0,0},{1,1},{2,2},{3,3},{4,64},{5,65},{6,66},{7,67},{8,128},{9,129... | collective-permute-start | bytes 2457608 | tf_op jit(solution)/shard_map/ppermute | solution.py:543
  148.1 2.0 halve_occ_b.1
  150.1 2.7 %collective-permute-start.12 = (s16[144,512]{1,0:T(8,128)(2,1)}, s16[144,512]{1,0:T(8,128)(2,1)}, u32[]{:S(2)}, u32[]{:S(2)}) collective-permute-start(s16[144,512]{1,0:T(8,128)(2,1)} %get-tuple-element.96), channel_id=1, source_target_pairs={{0,3},{3,0},{1,2},{2,1},{4,7},{7,4},{5,6},{6,5},{8,11},{11,8},{9,1... | collective-permute-start | bytes 442376 | tf_op jit(solution)/shard_map/ppermute | solution.py:482
  152.8 0.9 collective-permute-start.13
  153.7 6.5 %collective-permute-done.12.rest_1_ = s16[144,512]{1,0:T(8,128)(2,1)} collective-permute-done((s16[144,512]{1,0:T(8,128)(2,1)}, s16[144,512]{1,0:T(8,128)(2,1)}, u32[]{:S(2)}, u32[]{:S(2)}) %collective-permute-start.12) | collective-permute-done | bytes 147488 | tf_op jit(solution)/shard_map/ppermute | solution.py:482
  160.2 2.1 finish_occ.1
  162.3 2.2 %collective-permute-start.18 = (s16[800,128]{1,0:T(8,128)(2,1)S(1)}, s16[800,128]{1,0:T(8,128)(2,1)S(1)}, u32[]{:S(2)}, u32[]{:S(2)}) collective-permute-start(s16[800,128]{1,0:T(8,128)(2,1)S(1)} %get-tuple-element.109), channel_id=1, source_target_pairs={{0,16},{4,20},{8,24},{12,28},{16,32},{20,36},{24,40},{28,44},{32,4... | collective-permute-start | bytes 614408 | tf_op jit(solution)/shard_map/ppermute | solution.py:549
  164.5 3.3 %collective-permute-start.19 = (s16[800,128]{1,0:T(8,128)(2,1)S(1)}, s16[800,128]{1,0:T(8,128)(2,1)S(1)}, u32[]{:S(2)}, u32[]{:S(2)}) collective-permute-start(s16[800,128]{1,0:T(8,128)(2,1)S(1)} %get-tuple-element.110), channel_id=1, source_target_pairs={{0,32},{4,36},{8,40},{12,44},{16,48},{20,52},{24,56},{28,60},{32,0... | collective-permute-start | bytes 614408 | tf_op jit(solution)/shard_map/ppermute | solution.py:548
  167.8 0.8 collective-permute-start.20
  168.6 0.8 decode_virt.1.vir_ref
  169.4 1.2 collective-permute-done.18.one_ref
  170.6 9.8 %collective-permute-done.19.two_ref = s16[800,128]{1,0:T(8,128)(2,1)S(1)} collective-permute-done((s16[800,128]{1,0:T(8,128)(2,1)S(1)}, s16[800,128]{1,0:T(8,128)(2,1)S(1)}, u32[]{:S(2)}, u32[]{:S(2)}) %collective-permute-start.19) | collective-permute-done | bytes 204832 | tf_op jit(solution)/shard_map/ppermute | solution.py:548
  180.4 6.0 %collective-permute-done.20.three_ref = s16[800,128]{1,0:T(8,128)(2,1)S(1)} collective-permute-done((s16[800,128]{1,0:T(8,128)(2,1)S(1)}, s16[800,128]{1,0:T(8,128)(2,1)S(1)}, u32[]{:S(2)}, u32[]{:S(2)}) %collective-permute-start.20) | collective-permute-done | bytes 204832 | tf_op jit(solution)/shard_map/ppermute | solution.py:549
  186.4 4.3 %pair.1 = f32[24,24,128]{2,1,0:T(8,128)S(1)} custom-call(s32[2]{0:T(128)S(1)} %pad_add_fusion.place_ref, s16[800,128]{1,0:T(8,128)(2,1)S(1)} %get-tuple-element.108.own_ref, s16[800,128]{1,0:T(8,128)(2,1)S(1)} %collective-permute-done.18.one_ref, s16[800,128]{1,0:T(8,128)(2,1)S(1)} %collective-permute-done.19.two_ref, ...), custom_call_target="tpu_custom_call" | custom-call | tf_op jit(solution)/shard_map/pair/pallas_call | solution.py:439
  191.0 13.7 %all_to_all.16 = f32[16,1,576]{2,1,0:T(1,128)S(1)} all-to-all(f32[16,1,576]{2,1,0:T(1,128)S(1)} %reshape.14), channel_id=1, replica_groups=mesh['row'=4,'col'=16,'layer'=4] {'col'}, dimensions={0} | all-to-all | bytes 73728 | tf_op jit(solution)/shard_map/all_to_all | solution.py:477
  204.7 0.5 broadcast.5
  205.2 0.7 reduce
  206.3 10.6 %all_to_all.17 = f32[16,1,576]{2,1,0:T(1,128)S(1)} all-to-all(f32[16,1,576]{2,1,0:T(1,128)S(1)} %reshape.16), channel_id=1, replica_groups=mesh['row'=4,'col'=16,'layer'=4] {'row','layer'}, dimensions={0} | all-to-all | bytes 73728 | tf_op jit(solution)/shard_map/all_to_all | solution.py:477
  216.9 0.7 reduce.1
  217.8 0.6 reduce_sum.29
  (63 shorter events, 1.1 us)
Async XLA Ops:
  48.4 10.8 %copy-start = (bf16[32,64,128]{2,1,0:T(8,128)(2,1)}, bf16[32,64,128]{2,1,0:T(8,128)(2,1)S(1)}, u32[]{:S(2)}) copy-start(bf16[32,64,128]{2,1,0:T(8,128)(2,1)S(1)} %slice.12.rest_0_) | copy-start | bytes 1572868
  48.4 13.3 %collective-permute-start = (bf16[32,64,128]{2,1,0:T(8,128)(2,1)S(1)}, bf16[32,64,128]{2,1,0:T(8,128)(2,1)S(1)}, u32[]{:S(2)}, u32[]{:S(2)}) collective-permute-start(bf16[32,64,128]{2,1,0:T(8,128)(2,1)S(1)} %slice.12.rest_0_), channel_id=1, source_target_pairs={{0,64},{64,128},{128,192},{192,0},{1,65},{65,129},{129,193},{193,1... | collective-permute-start | bytes 1572872 | tf_op jit(solution)/shard_map/ppermute | solution.py:514
  49.7 12.0 %collective-permute-start.1 = (bf16[32,64,128]{2,1,0:T(8,128)(2,1)S(1)}, bf16[32,64,128]{2,1,0:T(8,128)(2,1)S(1)}, u32[]{:S(2)}, u32[]{:S(2)}) collective-permute-start(bf16[32,64,128]{2,1,0:T(8,128)(2,1)S(1)} %slice.12.rest_0_), channel_id=1, source_target_pairs={{0,192},{64,0},{128,64},{192,128},{1,193},{65,1},{129,65},{193,129... | collective-permute-start | bytes 1572872 | tf_op jit(solution)/shard_map/ppermute | solution.py:515
  59.2 28.7 %copy-start.2 = (bf16[32,64,128]{2,1,0:T(8,128)(2,1)}, bf16[32,64,128]{2,1,0:T(8,128)(2,1)S(1)}, u32[]{:S(2)}) copy-start(bf16[32,64,128]{2,1,0:T(8,128)(2,1)S(1)} %slice.10.rest_0_.rest_4_) | copy-start | bytes 1572868
  61.7 15.7 %copy-start.5 = (bf16[32,64,128]{2,1,0:T(8,128)(2,1)}, bf16[32,64,128]{2,1,0:T(8,128)(2,1)S(1)}, u32[]{:S(2)}) copy-start(bf16[32,64,128]{2,1,0:T(8,128)(2,1)S(1)} %collective-permute-done.rest_1_) | copy-start | bytes 1572868
  61.7 15.7 %copy-start.7 = (bf16[32,64,128]{2,1,0:T(8,128)(2,1)}, bf16[32,64,128]{2,1,0:T(8,128)(2,1)S(1)}, u32[]{:S(2)}) copy-start(bf16[32,64,128]{2,1,0:T(8,128)(2,1)S(1)} %collective-permute-done.1.rest_2_) | copy-start | bytes 1572868
  61.7 12.3 %collective-permute-start.2 = (bf16[32,64,128]{2,1,0:T(8,128)(2,1)S(1)}, bf16[32,64,128]{2,1,0:T(8,128)(2,1)S(1)}, u32[]{:S(2)}, u32[]{:S(2)}) collective-permute-start(bf16[32,64,128]{2,1,0:T(8,128)(2,1)S(1)} %collective-permute-done.rest_1_), channel_id=1, source_target_pairs={{0,64},{64,128},{128,192},{192,0},{1,65},{65,129},{129,193},{193,1... | collective-permute-start | bytes 1572872 | tf_op jit(solution)/shard_map/ppermute | solution.py:517
  62.7 11.4 %collective-permute-start.3 = (bf16[32,64,128]{2,1,0:T(8,128)(2,1)S(1)}, bf16[32,64,128]{2,1,0:T(8,128)(2,1)S(1)}, u32[]{:S(2)}, u32[]{:S(2)}) collective-permute-start(bf16[32,64,128]{2,1,0:T(8,128)(2,1)S(1)} %slice.10.rest_0_.rest_4_), channel_id=1, source_target_pairs={{0,192},{64,0},{128,64},{192,128},{1,193},{65,1},{129,65},{193,129... | collective-permute-start | bytes 1572872 | tf_op jit(solution)/shard_map/ppermute | solution.py:518
  74.0 3.4 %copy-start.9 = (bf16[32,64,128]{2,1,0:T(8,128)(2,1)}, bf16[32,64,128]{2,1,0:T(8,128)(2,1)S(1)}, u32[]{:S(2)}) copy-start(bf16[32,64,128]{2,1,0:T(8,128)(2,1)S(1)} %collective-permute-done.2.rest_3_) | copy-start | bytes 1572868
  74.1 13.9 %copy-start.11 = (bf16[32,64,128]{2,1,0:T(8,128)(2,1)}, bf16[32,64,128]{2,1,0:T(8,128)(2,1)S(1)}, u32[]{:S(2)}) copy-start(bf16[32,64,128]{2,1,0:T(8,128)(2,1)S(1)} %collective-permute-done.3.rest_2_.rest_6_) | copy-start | bytes 1572868
  74.1 14.0 %collective-permute-start.4 = (bf16[32,64,128]{2,1,0:T(8,128)(2,1)S(1)}, bf16[32,64,128]{2,1,0:T(8,128)(2,1)}, u32[]{:S(2)}, u32[]{:S(2)}) collective-permute-start(bf16[32,64,128]{2,1,0:T(8,128)(2,1)S(1)} %slice.10.rest_0_.rest_4_), channel_id=1, source_target_pairs={{0,64},{64,128},{128,192},{192,0},{1,65},{65,129},{129,193},{193,1... | collective-permute-start | bytes 1572872 | tf_op jit(solution)/shard_map/ppermute | solution.py:520
  74.1 13.9 %collective-permute-start.5 = (bf16[32,64,128]{2,1,0:T(8,128)(2,1)S(1)}, bf16[32,64,128]{2,1,0:T(8,128)(2,1)}, u32[]{:S(2)}, u32[]{:S(2)}) collective-permute-start(bf16[32,64,128]{2,1,0:T(8,128)(2,1)S(1)} %collective-permute-done.3.rest_2_.rest_6_), channel_id=1, source_target_pairs={{0,192},{64,0},{128,64},{192,128},{1,193},{65,1},{129,65},{193,129... | collective-permute-start | bytes 1572872 | tf_op jit(solution)/shard_map/ppermute | solution.py:521
  77.4 24.5 %slice-start = ((s8[5242880]{0:T(1024)(128)(4,1)}), s8[4194304]{0:T(1024)(128)(4,1)S(1)}, s32[]{:S(2)}) async-start(s8[5242880]{0:T(1024)(128)(4,1)} %bitcast.9), calls=%async_computation.3 | async-start | bytes 8388608
  88.0 14.0 %slice-start.1 = ((s8[5242880]{0:T(1024)(128)(4,1)}), s8[1048576]{0:T(1024)(128)(4,1)S(1)}, s32[]{:S(2)}) async-start(s8[5242880]{0:T(1024)(128)(4,1)} %bitcast.9), calls=%async_computation.4 | async-start | bytes 2097152
  88.0 14.0 %copy-start.1 = (bf16[32,64,128]{2,1,0:T(8,128)(2,1)S(1)}, bf16[32,64,128]{2,1,0:T(8,128)(2,1)}, u32[]{:S(2)}) copy-start(bf16[32,64,128]{2,1,0:T(8,128)(2,1)} %copy-done) | copy-start | bytes 1572868
  88.0 14.0 %copy-start.6 = (bf16[32,64,128]{2,1,0:T(8,128)(2,1)S(1)}, bf16[32,64,128]{2,1,0:T(8,128)(2,1)}, u32[]{:S(2)}) copy-start(bf16[32,64,128]{2,1,0:T(8,128)(2,1)} %copy-done.5) | copy-start | bytes 1572868
  88.0 14.0 %copy-start.8 = (bf16[32,64,128]{2,1,0:T(8,128)(2,1)S(1)}, bf16[32,64,128]{2,1,0:T(8,128)(2,1)}, u32[]{:S(2)}) copy-start(bf16[32,64,128]{2,1,0:T(8,128)(2,1)} %copy-done.7) | copy-start | bytes 1572868
  88.0 14.0 %copy-start.10 = (bf16[32,64,128]{2,1,0:T(8,128)(2,1)S(1)}, bf16[32,64,128]{2,1,0:T(8,128)(2,1)}, u32[]{:S(2)}) copy-start(bf16[32,64,128]{2,1,0:T(8,128)(2,1)} %copy-done.9) | copy-start | bytes 1572868
  88.0 14.0 %copy-start.13 = (s32[64,1,4]{2,1,0:T(1,128)S(1)}, s32[64,1,4]{2,1,0:T(1,128)}, u32[]{:S(2)}) copy-start(s32[64,1,4]{2,1,0:T(1,128)} %slice_convert_fusion) | copy-start | bytes 3076
  88.0 14.0 %copy-start.14 = (s32[3]{0:T(128)S(1)}, s32[3]{0:T(128)}, u32[]{:S(2)}) copy-start(s32[3]{0:T(128)} %pad_add_fusion.1.place_ref) | copy-start | bytes 40
  88.1 14.0 %copy-start.3 = (bf16[32,64,128]{2,1,0:T(8,128)(2,1)S(1)}, bf16[32,64,128]{2,1,0:T(8,128)(2,1)}, u32[]{:S(2)}) copy-start(bf16[32,64,128]{2,1,0:T(8,128)(2,1)} %copy-done.2) | copy-start | bytes 1572868
  88.1 14.0 %copy-start.12 = (bf16[32,64,128]{2,1,0:T(8,128)(2,1)S(1)}, bf16[32,64,128]{2,1,0:T(8,128)(2,1)}, u32[]{:S(2)}) copy-start(bf16[32,64,128]{2,1,0:T(8,128)(2,1)} %copy-done.11) | copy-start | bytes 1572868
  99.5 17.8 %collective-permute-start.6 = (s16[800,512]{1,0:T(8,128)(2,1)}, s16[800,512]{1,0:T(8,128)(2,1)S(1)}, u32[]{:S(2)}, u32[]{:S(2)}) collective-permute-start(s16[800,512]{1,0:T(8,128)(2,1)} %get-tuple-element.76), channel_id=1, source_target_pairs={{0,1},{1,0},{2,3},{3,2},{4,5},{5,4},{6,7},{7,6},{8,9},{9,8},{10,11... | collective-permute-start | bytes 2457608 | tf_op jit(solution)/shard_map/ppermute | solution.py:482
  99.9 17.4 %collective-permute-start.7 = (s16[800,512]{1,0:T(8,128)(2,1)}, s16[800,512]{1,0:T(8,128)(2,1)S(1)}, u32[]{:S(2)}, u32[]{:S(2)}) collective-permute-start(s16[800,512]{1,0:T(8,128)(2,1)} %get-tuple-element.77), channel_id=1, source_target_pairs={{0,3},{3,0},{1,2},{2,1},{4,7},{7,4},{5,6},{6,5},{8,11},{11,8},{9,1... | collective-permute-start | bytes 2457608 | tf_op jit(solution)/shard_map/ppermute | solution.py:482
  102.0 15.2 %copy-start.4 = (f32[2,2,12,32,512]{4,3,2,1,0:T(8,128)S(1)}, f32[2,2,12,32,512]{4,3,2,1,0:T(8,128)}, u32[]{:S(2)}) copy-start(f32[2,2,12,32,512]{4,3,2,1,0:T(8,128)} %get-tuple-element.75.keep_ref) | copy-start | bytes 9437188
  116.0 6.8 %collective-permute-start.8 = (s16[272,512]{1,0:T(8,128)(2,1)S(1)}, s16[272,512]{1,0:T(8,128)(2,1)S(1)}, u32[]{:S(2)}, u32[]{:S(2)}) collective-permute-start(s16[272,512]{1,0:T(8,128)(2,1)S(1)} %get-tuple-element.82), channel_id=1, source_target_pairs={{0,1},{1,0},{2,3},{3,2},{4,5},{5,4},{6,7},{7,6},{8,9},{9,8},{10,11... | collective-permute-start | bytes 835592 | tf_op jit(solution)/shard_map/ppermute | solution.py:482
  116.3 8.0 %collective-permute-start.9 = (s16[272,512]{1,0:T(8,128)(2,1)S(1)}, s16[272,512]{1,0:T(8,128)(2,1)S(1)}, u32[]{:S(2)}, u32[]{:S(2)}) collective-permute-start(s16[272,512]{1,0:T(8,128)(2,1)S(1)} %get-tuple-element.83), channel_id=1, source_target_pairs={{0,3},{3,0},{1,2},{2,1},{4,7},{7,4},{5,6},{6,5},{8,11},{11,8},{9,1... | collective-permute-start | bytes 835592 | tf_op jit(solution)/shard_map/ppermute | solution.py:482
  124.3 8.4 %collective-permute-start.10 = (s16[400,512]{1,0:T(8,128)(2,1)S(1)}, s16[400,512]{1,0:T(8,128)(2,1)S(1)}, u32[]{:S(2)}, u32[]{:S(2)}) collective-permute-start(s16[400,512]{1,0:T(8,128)(2,1)S(1)} %get-tuple-element.87), channel_id=1, source_target_pairs={{0,3},{3,0},{1,2},{2,1},{4,7},{7,4},{5,6},{6,5},{8,11},{11,8},{9,1... | collective-permute-start | bytes 1228808 | tf_op jit(solution)/shard_map/ppermute | solution.py:482
  126.9 7.5 %collective-permute-start.11 = (s16[400,512]{1,0:T(8,128)(2,1)S(1)}, s16[400,512]{1,0:T(8,128)(2,1)S(1)}, u32[]{:S(2)}, u32[]{:S(2)}) collective-permute-start(s16[400,512]{1,0:T(8,128)(2,1)S(1)} %get-tuple-element.88), channel_id=1, source_target_pairs={{0,1},{1,0},{2,3},{3,2},{4,5},{5,4},{6,7},{7,6},{8,9},{9,8},{10,11... | collective-permute-start | bytes 1228808 | tf_op jit(solution)/shard_map/ppermute | solution.py:482
  134.4 13.7 %collective-permute-start.14 = (s16[528,512]{1,0:T(8,128)(2,1)S(1)}, s16[528,512]{1,0:T(8,128)(2,1)S(1)}, u32[]{:S(2)}, u32[]{:S(2)}) collective-permute-start(s16[528,512]{1,0:T(8,128)(2,1)S(1)} %get-tuple-element.103), channel_id=1, source_target_pairs={{0,1},{1,0},{2,3},{3,2},{4,5},{5,4},{6,7},{7,6},{8,9},{9,8},{10,11... | collective-permute-start | bytes 1622024 | tf_op jit(solution)/shard_map/ppermute | solution.py:482
  134.4 13.7 %collective-permute-start.15 = (s16[528,512]{1,0:T(8,128)(2,1)S(1)}, s16[528,512]{1,0:T(8,128)(2,1)S(1)}, u32[]{:S(2)}, u32[]{:S(2)}) collective-permute-start(s16[528,512]{1,0:T(8,128)(2,1)S(1)} %get-tuple-element.104), channel_id=1, source_target_pairs={{0,3},{3,0},{1,2},{2,1},{4,7},{7,4},{5,6},{6,5},{8,11},{11,8},{9,1... | collective-permute-start | bytes 1622024 | tf_op jit(solution)/shard_map/ppermute | solution.py:482
  136.8 31.8 %collective-permute-start.21 = (s16[800,512]{1,0:T(8,128)(2,1)S(1)}, s16[800,512]{1,0:T(8,128)(2,1)S(1)}, u32[]{:S(2)}, u32[]{:S(2)}) collective-permute-start(s16[800,512]{1,0:T(8,128)(2,1)S(1)} %finish_virt.1), channel_id=1, source_target_pairs={{0,0},{1,1},{2,2},{3,3},{4,64},{5,65},{6,66},{7,67},{8,128},{9,129... | collective-permute-start | bytes 2457608 | tf_op jit(solution)/shard_map/ppermute | solution.py:543
  150.1 10.1 %collective-permute-start.16 = (s16[272,512]{1,0:T(8,128)(2,1)}, s16[272,512]{1,0:T(8,128)(2,1)S(1)}, u32[]{:S(2)}, u32[]{:S(2)}) collective-permute-start(s16[272,512]{1,0:T(8,128)(2,1)} %get-tuple-element.106), channel_id=1, source_target_pairs={{0,3},{3,0},{1,2},{2,1},{4,7},{7,4},{5,6},{6,5},{8,11},{11,8},{9,1... | collective-permute-start | bytes 835592 | tf_op jit(solution)/shard_map/ppermute | solution.py:482
  150.1 10.1 %collective-permute-start.17 = (s16[272,512]{1,0:T(8,128)(2,1)}, s16[272,512]{1,0:T(8,128)(2,1)}, u32[]{:S(2)}, u32[]{:S(2)}) collective-permute-start(s16[272,512]{1,0:T(8,128)(2,1)} %get-tuple-element.107), channel_id=1, source_target_pairs={{0,1},{1,0},{2,3},{3,2},{4,5},{5,4},{6,7},{7,6},{8,9},{9,8},{10,11... | collective-permute-start | bytes 835592 | tf_op jit(solution)/shard_map/ppermute | solution.py:482
  150.1 10.1 %collective-permute-start.12 = (s16[144,512]{1,0:T(8,128)(2,1)}, s16[144,512]{1,0:T(8,128)(2,1)}, u32[]{:S(2)}, u32[]{:S(2)}) collective-permute-start(s16[144,512]{1,0:T(8,128)(2,1)} %get-tuple-element.96), channel_id=1, source_target_pairs={{0,3},{3,0},{1,2},{2,1},{4,7},{7,4},{5,6},{6,5},{8,11},{11,8},{9,1... | collective-permute-start | bytes 442376 | tf_op jit(solution)/shard_map/ppermute | solution.py:482
  152.8 7.4 %collective-permute-start.13 = (s16[144,512]{1,0:T(8,128)(2,1)}, s16[144,512]{1,0:T(8,128)(2,1)}, u32[]{:S(2)}, u32[]{:S(2)}) collective-permute-start(s16[144,512]{1,0:T(8,128)(2,1)} %get-tuple-element.97), channel_id=1, source_target_pairs={{0,1},{1,0},{2,3},{3,2},{4,5},{5,4},{6,7},{7,6},{8,9},{9,8},{10,11... | collective-permute-start | bytes 442376 | tf_op jit(solution)/shard_map/ppermute | solution.py:482
  162.3 8.3 %collective-permute-start.18 = (s16[800,128]{1,0:T(8,128)(2,1)S(1)}, s16[800,128]{1,0:T(8,128)(2,1)S(1)}, u32[]{:S(2)}, u32[]{:S(2)}) collective-permute-start(s16[800,128]{1,0:T(8,128)(2,1)S(1)} %get-tuple-element.109), channel_id=1, source_target_pairs={{0,16},{4,20},{8,24},{12,28},{16,32},{20,36},{24,40},{28,44},{32,4... | collective-permute-start | bytes 614408 | tf_op jit(solution)/shard_map/ppermute | solution.py:549
  164.5 15.9 %collective-permute-start.19 = (s16[800,128]{1,0:T(8,128)(2,1)S(1)}, s16[800,128]{1,0:T(8,128)(2,1)S(1)}, u32[]{:S(2)}, u32[]{:S(2)}) collective-permute-start(s16[800,128]{1,0:T(8,128)(2,1)S(1)} %get-tuple-element.110), channel_id=1, source_target_pairs={{0,32},{4,36},{8,40},{12,44},{16,48},{20,52},{24,56},{28,60},{32,0... | collective-permute-start | bytes 614408 | tf_op jit(solution)/shard_map/ppermute | solution.py:548
  167.8 18.6 %collective-permute-start.20 = (s16[800,128]{1,0:T(8,128)(2,1)S(1)}, s16[800,128]{1,0:T(8,128)(2,1)S(1)}, u32[]{:S(2)}, u32[]{:S(2)}) collective-permute-start(s16[800,128]{1,0:T(8,128)(2,1)S(1)} %get-tuple-element.111), channel_id=1, source_target_pairs={{0,48},{4,52},{8,56},{12,60},{16,0},{20,4},{24,8},{28,12},{32,16},... | collective-permute-start | bytes 614408 | tf_op jit(solution)/shard_map/ppermute | solution.py:549
